TPU v7x, 32 devices: a whole 2x2x4 slice. The times are simulated.
32 devices in a mesh: dp: 16 (over z, y, x), strip: 2 (over core).
Axes of the slice: x: 2, y: 2, z: 4, core: 2. Of those that a mesh axis runs over, the one named last changes fastest.
Arguments:
- weights: float32 [10952704], P(('dp', 'strip'))
- blocks: float32 [512, 128, 128], P('dp'), may hold values from -0.1875 to 0.1875
- stat_left: float32 [512, 128, 128], P('dp')
- stat_right: float32 [512, 128, 128], P('dp')
- root_left: float32 [512, 128, 128], P('dp')
- root_right: float32 [512, 128, 128], P('dp')
- first_moment: float32 [10952704], P(('dp', 'strip')), may hold values from -0.0029296875 to 0.0029296875
- second_moment: float32 [10952704], P(('dp', 'strip')), may hold values from 1.4404297e-07 to 5.7861325e-07
- image: bfloat16 [16, 257, 768], P('dp'), may hold values from -6 to 6
- camera: int32 [16], P('dp'), may hold values from 0 to 31
- samples: int32 [16, 3, 16, 512], P('dp', None, None, 'strip'), may hold values from 0 to 2047
- ray_pixel: int32 [16, 512], P('dp', 'strip'), may hold values from 0 to 4095
- target: float32 [16, 3, 4096], P('dp'), may hold values from 0 to 1
- valid: int32 [16, 4096], P('dp'), may hold values 0 or 1
Outputs:
- loss: float32 [], replicated
- new_weights: float32 [10952704], P(('dp', 'strip'))
- new_first: float32 [10952704], P(('dp', 'strip'))
- new_second: float32 [10952704], P(('dp', 'strip'))
- new_blocks: float32 [512, 128, 128], P('dp')
- block_grads: float32 [512, 128, 128], P('dp')
- new_left: float32 [512, 128, 128], P('dp')
- new_right: float32 [512, 128, 128], P('dp')
- block_rms: float32 [512], P('dp')
All inputs are finite; a program needn't handle non-finite values. No bound on the sum of `valid` on one device may be relied on, other than what follows from the above.
Results may differ from a plain program's by a relative error of at most 0.007.
The roundings to bfloat16 on the way count: a program that leaves them out, or rounds other values in their place, can miss the bound.
Values may be sent and summed in bfloat16 or wider, within the bound.
A program may use at most 320 MiB of HBM per device.

v0:
```python
import math

import jax
import jax.numpy as jnp
from jax import lax
from jax.sharding import PartitionSpec as P

D = 1024
HEAD_DIM = 64
HID = 4096
DI = 768
CH = 80
DEC_HID = 64
BLOCK = 128
PR = 8
TC = 32
S = 16
NCAM = 32
ADAM_STEP = 10


NORM_EPS = 1e-05
ADAM_RATE = 0.015
BETA_FIRST = 0.9
BETA_SECOND = 0.95
ADAM_EPS = 1e-08
WEIGHT_DECAY = 0.1
STAT_DECAY = 0.9
SHAMPOO_RATE = 0.01
RMS_EPS = 1e-06
HIGHEST_MODE = lax.Precision.HIGHEST
group_heads = 4


def with_halo(block, sides, width):
    for axis, dim in sides:
        count = lax.axis_size(axis)
        forward = [(i, i + 1) for i in range(count - 1)]
        backward = [(target, source) for source, target in forward]
        low = lax.ppermute(
            lax.slice_in_dim(block, block.shape[dim] - width, None, axis=dim), axis, forward
        )
        high = lax.ppermute(lax.slice_in_dim(block, 0, width, axis=dim), axis, backward)
        block = jnp.concatenate([low, block, high], axis=dim)
    return block


def segments(plane_rows):
    return (
        ("query_cross", (D, D)),
        ("keyval_cross", (DI, 2 * D)),
        ("out_cross", (D, D)),
        ("qkv_self", (D, 3 * D)),
        ("out_self", (D, D)),
        ("deconv", (D, 16 * CH)),
        ("decode_in", (CH, DEC_HID)),
        ("decode_out", (DEC_HID, 4)),
        ("modulate", (NCAM, 6, D)),
        ("triplane", (3, plane_rows, TC, D)),
    )


def unflatten(flat, plane_rows):
    parts = {}
    offset = 0
    for label, shape in segments(plane_rows):
        length = math.prod(shape)
        parts[label] = flat[offset : offset + length].reshape(shape)
        offset += length
    return parts


def unblock(tiles):
    rows_one, cols_one = (D // BLOCK, HID // BLOCK)
    half = rows_one * cols_one
    leading_value = (
        tiles[:half].reshape(rows_one, cols_one, BLOCK, BLOCK).transpose(0, 2, 1, 3).reshape(D, HID)
    )
    trailing_value = (
        tiles[half:].reshape(cols_one, rows_one, BLOCK, BLOCK).transpose(0, 2, 1, 3).reshape(HID, D)
    )
    return (leading_value, trailing_value)


def regroup_blocks(leading_value, trailing_value):
    rows_one, cols_one = (D // BLOCK, HID // BLOCK)
    upper = (
        leading_value.reshape(rows_one, BLOCK, cols_one, BLOCK)
        .transpose(0, 2, 1, 3)
        .reshape(-1, BLOCK, BLOCK)
    )
    lower = (
        trailing_value.reshape(cols_one, BLOCK, rows_one, BLOCK)
        .transpose(0, 2, 1, 3)
        .reshape(-1, BLOCK, BLOCK)
    )
    return jnp.concatenate([upper, lower], 0)


def product(left, right):
    return jnp.dot(left, right, preferred_element_type=jnp.float32)


def product_back(left, right):
    return lax.dot_general(
        left, right, (((left.ndim - 1,), (1,)), ((), ())), preferred_element_type=jnp.float32
    )


def weight_grad(left, right):
    return lax.dot_general(
        left, right, (((0,), (0,)), ((), ())), preferred_element_type=jnp.float32
    )


def norm_mod(stream, scale, shift):
    centred = stream - jnp.mean(stream, -1, keepdims=True)
    spread = jnp.mean(centred * centred, -1, keepdims=True)
    return centred * lax.rsqrt(spread + NORM_EPS) * (1.0 + scale) + shift


def gelu_tanh(value):
    return jax.nn.gelu(value, approximate=True)


def assemble(ydc):
    planes, rows, cols, _ = ydc.shape
    inner = rows - 2
    kernel = ydc.reshape(planes, rows, cols, 4, 4, -1)
    even = kernel[:, 1 : inner + 1, :, 1] + kernel[:, 0:inner, :, 3]
    odd = kernel[:, 1 : inner + 1, :, 2] + kernel[:, 2 : inner + 2, :, 0]
    tall = jnp.stack([even, odd], 2)
    wide = jnp.pad(tall, ((0, 0), (0, 0), (0, 0), (1, 1), (0, 0), (0, 0)))
    left_cols = wide[:, :, :, 1 : cols + 1, 1] + wide[:, :, :, 0:cols, 3]
    right_cols = wide[:, :, :, 1 : cols + 1, 2] + wide[:, :, :, 2 : cols + 2, 0]
    return jnp.stack([left_cols, right_cols], 4).reshape(planes, 2 * inner, 2 * cols, -1)


def render_loss(output, pixel, target, valid):
    sigma = jax.nn.softplus(output[..., 0])
    colour = jax.nn.sigmoid(output[..., 1:])
    absorb = 4.0 / S * sigma
    before = jnp.cumsum(absorb, 0) - absorb
    weight = jnp.exp(-before) * (1.0 - jnp.exp(-absorb))
    colour_sum = jnp.sum(weight[..., None] * colour, 0)
    mask = jnp.take(valid, pixel).astype(jnp.float32)
    wanted = jnp.take(target, pixel, axis=1)
    error = colour_sum.T - wanted
    return (jnp.sum(mask * jnp.sum(error * error, 0)), jnp.sum(mask))


def split_heads(matrix):
    return matrix.reshape(matrix.shape[0], -1, group_heads, HEAD_DIM).transpose(1, 0, 2, 3)


def merge_heads(groups):
    return groups.transpose(1, 0, 2, 3).reshape(groups.shape[1], -1)


def attend_fwd(query, keys, values):

    def one_group(operands):
        query_part, key_part, value_part = operands
        scores = jnp.einsum(
            "qhd,khd->hqk", query_part, key_part, preferred_element_type=jnp.float32
        ) * HEAD_DIM ** (-0.5)
        top = jnp.max(scores, -1, keepdims=True)
        log_total = top + jnp.log(jnp.sum(jnp.exp(scores - top), -1, keepdims=True))
        shares = jnp.exp(scores - log_total).astype(jnp.bfloat16)
        final_output = jnp.einsum(
            "hqk,khd->qhd", shares, value_part, preferred_element_type=jnp.float32
        )
        return (final_output, log_total[..., 0])

    final_output, log_total = lax.map(
        one_group, (split_heads(query), split_heads(keys), split_heads(values))
    )
    return (merge_heads(final_output), log_total)


def attend_bwd(query, keys, values, log_total, grad_out):

    def one_group(operands):
        query_part, key_part, value_part, total_part, grad_part = operands
        scores = jnp.einsum(
            "qhd,khd->hqk", query_part, key_part, preferred_element_type=jnp.float32
        ) * HEAD_DIM ** (-0.5)
        shares = jnp.exp(scores - total_part[..., None])
        grad_shares = jnp.einsum(
            "qhd,khd->hqk", grad_part, value_part, preferred_element_type=jnp.float32
        )
        grad_scores = (
            shares * (grad_shares - jnp.sum(grad_shares * shares, -1, keepdims=True))
        ).astype(jnp.bfloat16)
        grad_query = jnp.einsum(
            "hqk,khd->qhd", grad_scores, key_part, preferred_element_type=jnp.float32
        ) * HEAD_DIM ** (-0.5)
        grad_keys = jnp.einsum(
            "hqk,qhd->khd", grad_scores, query_part, preferred_element_type=jnp.float32
        ) * HEAD_DIM ** (-0.5)
        grad_values = jnp.einsum(
            "hqk,qhd->khd",
            shares.astype(jnp.bfloat16),
            grad_part,
            preferred_element_type=jnp.float32,
        )
        return (grad_query, grad_keys, grad_values)

    grads = lax.map(
        one_group,
        (
            split_heads(query),
            split_heads(keys),
            split_heads(values),
            log_total,
            split_heads(grad_out),
        ),
    )
    return (merge_heads(grads[0]), merge_heads(grads[1]), merge_heads(grads[2]))


def shards(
    weights,
    blocks,
    stat_left,
    stat_right,
    root_left,
    root_right,
    first_moment,
    second_moment,
    image,
    camera,
    samples,
    ray_pixel,
    target,
    valid,
):
    strips = lax.axis_size("strip")
    place = lax.axis_index("strip")
    plane_rows = PR * strips
    full_flat = lax.all_gather(weights.astype(jnp.bfloat16), ("dp", "strip"), axis=0, tiled=True)
    full_blocks = lax.all_gather(blocks.astype(jnp.bfloat16), "dp", axis=0, tiled=True)
    params = unflatten(full_flat, plane_rows)
    mlp_one, mlp_two = unblock(full_blocks)
    picture = image[0]
    cells_read = samples[0].reshape(3, -1)
    pixel = ray_pixel[0]
    onehot = (lax.iota(jnp.int32, NCAM) == camera[0]).astype(jnp.float32)
    mods = jnp.einsum("c,cjd->jd", onehot, params["modulate"].astype(jnp.float32))
    row_start = place * PR
    own_rows = lax.dynamic_slice_in_dim(params["triplane"], row_start, PR, 1)
    stream0 = own_rows.reshape(-1, D).astype(jnp.float32)
    hidden1, norm_one = jax.vjp(norm_mod, stream0, mods[0], mods[1])
    hidden1 = hidden1.astype(jnp.bfloat16)
    query1 = product(hidden1, params["query_cross"]).astype(jnp.bfloat16)
    image_kv = product(picture, params["keyval_cross"]).astype(jnp.bfloat16)
    cross_out, total_one = attend_fwd(query1, image_kv[:, :D], image_kv[:, D:])
    cross_out = cross_out.astype(jnp.bfloat16)
    stream1 = stream0 + product(cross_out, params["out_cross"])
    hidden2, norm_two = jax.vjp(norm_mod, stream1, mods[2], mods[3])
    hidden2 = hidden2.astype(jnp.bfloat16)
    qkv = product(hidden2, params["qkv_self"]).astype(jnp.bfloat16)
    kv_all = lax.all_gather(qkv[:, D:], "strip", axis=0, tiled=True)
    self_out, total_two = attend_fwd(qkv[:, :D], kv_all[:, :D], kv_all[:, D:])
    self_out = self_out.astype(jnp.bfloat16)
    stream2 = stream1 + product(self_out, params["out_self"])
    hidden3, norm_three = jax.vjp(norm_mod, stream2, mods[4], mods[5])
    hidden3 = hidden3.astype(jnp.bfloat16)
    up_value = product(hidden3, mlp_one)
    act, gelu_back = jax.vjp(gelu_tanh, up_value)
    act = act.astype(jnp.bfloat16)
    stream3 = stream2 + product(act, mlp_two)
    grid = stream3.astype(jnp.bfloat16).reshape(3, PR, -1, D)
    padded = with_halo(grid, (("strip", 1),), 1)
    ydc = jnp.einsum("prcd,dk->prck", padded, params["deconv"], preferred_element_type=jnp.float32)
    feature, assemble_back = jax.vjp(assemble, ydc)
    whole = lax.all_gather(feature.astype(jnp.bfloat16), "strip", axis=1, tiled=True)
    cells = whole.reshape(3, -1, CH)
    point = (
        jnp.take(cells[0], cells_read[0], axis=0).astype(jnp.float32)
        + jnp.take(cells[1], cells_read[1], axis=0).astype(jnp.float32)
        + jnp.take(cells[2], cells_read[2], axis=0).astype(jnp.float32)
    )
    point = point.astype(jnp.bfloat16)
    inner_value = product(point, params["decode_in"])
    hidden, silu_back = jax.vjp(jax.nn.silu, inner_value)
    hidden = hidden.astype(jnp.bfloat16)
    output = product(hidden, params["decode_out"])
    rays = pixel.shape[0]

    def local_loss(values):
        return render_loss(values.reshape(S, rays, 4), pixel, target[0], valid[0])

    (loss_part, count_part), render_back = jax.vjp(local_loss, output)
    loss_sum, count = lax.psum((loss_part, count_part), ("dp", "strip"))
    factor = 1.0 / jnp.maximum(count, 1.0)
    loss = loss_sum * factor
    (grad_output,) = render_back((factor, jnp.zeros_like(count_part)))
    grad_output = grad_output.astype(jnp.bfloat16)
    grad_decode_out = weight_grad(hidden, grad_output)
    (grad_inner,) = silu_back(product_back(grad_output, params["decode_out"]))
    grad_inner = grad_inner.astype(jnp.bfloat16)
    grad_decode_in = weight_grad(point, grad_inner)
    grad_point = product_back(grad_inner, params["decode_in"])
    gradient_cell_grid = jnp.stack(
        [
            jax.ops.segment_sum(grad_point, cells_read[plane], num_segments=cells.shape[1])
            for plane in range(3)
        ]
    )
    grad_feature = lax.psum_scatter(
        gradient_cell_grid.reshape(whole.shape).astype(jnp.bfloat16),
        "strip",
        scatter_dimension=1,
        tiled=True,
    ).astype(jnp.float32)
    grad_feature = lax.optimization_barrier(grad_feature.astype(jnp.bfloat16)).astype(jnp.float32)
    (grad_ydc,) = assemble_back(grad_feature)
    grad_ydc = grad_ydc.astype(jnp.bfloat16)
    grad_deconv = weight_grad(padded.reshape(-1, D), grad_ydc.reshape(-1, 16 * CH))
    grad_padded = product_back(grad_ydc, params["deconv"])
    edges = jnp.concatenate([grad_padded[:, :1], grad_padded[:, -1:]], 1)
    beside = with_halo(edges.astype(jnp.bfloat16), (("strip", 1),), 1).astype(edges.dtype)
    grad_grid = grad_padded[:, 1:-1]
    grad_grid = grad_grid.at[:, 0].add(beside[:, 0]).at[:, -1].add(beside[:, -1])
    grad_stream = grad_grid.reshape(-1, D)
    grad_branch = grad_stream.astype(jnp.bfloat16)
    gradient_second_term = weight_grad(act, grad_branch)
    (grad_up,) = gelu_back(product_back(grad_branch, mlp_two))
    grad_up = grad_up.astype(jnp.bfloat16)
    gradient_first_term = weight_grad(hidden3, grad_up)
    grad_norm, grad_mod4, grad_mod5 = norm_three(product_back(grad_up, mlp_one))
    grad_stream = grad_stream + grad_norm
    grad_branch = grad_stream.astype(jnp.bfloat16)
    grad_out_self = weight_grad(self_out, grad_branch)
    grad_self = product_back(grad_branch, params["out_self"]).astype(jnp.bfloat16)
    grad_query2, grad_keys2, grad_values2 = attend_bwd(
        qkv[:, :D], kv_all[:, :D], kv_all[:, D:], total_two, grad_self
    )
    grad_kv_own = lax.psum_scatter(
        jnp.concatenate([grad_keys2, grad_values2], 1).astype(jnp.bfloat16),
        "strip",
        scatter_dimension=0,
        tiled=True,
    ).astype(jnp.float32)
    grad_qkv = jnp.concatenate([grad_query2, grad_kv_own], 1).astype(jnp.bfloat16)
    grad_qkv_self = weight_grad(hidden2, grad_qkv)
    grad_norm, grad_mod2, grad_mod3 = norm_two(product_back(grad_qkv, params["qkv_self"]))
    grad_stream = grad_stream + grad_norm
    grad_branch = grad_stream.astype(jnp.bfloat16)
    grad_out_cross = weight_grad(cross_out, grad_branch)
    grad_cross = product_back(grad_branch, params["out_cross"]).astype(jnp.bfloat16)
    grad_query1, grad_keys1, grad_values1 = attend_bwd(
        query1, image_kv[:, :D], image_kv[:, D:], total_one, grad_cross
    )
    grad_query1 = grad_query1.astype(jnp.bfloat16)
    grad_image_kv = jnp.concatenate([grad_keys1, grad_values1], 1).astype(jnp.bfloat16)
    grad_keyval = weight_grad(picture, grad_image_kv)
    grad_query_cross = weight_grad(hidden1, grad_query1)
    grad_norm, grad_mod0, grad_mod1 = norm_one(product_back(grad_query1, params["query_cross"]))
    grad_stream = grad_stream + grad_norm
    grad_mods = jnp.stack([grad_mod0, grad_mod1, grad_mod2, grad_mod3, grad_mod4, grad_mod5])
    grad_modulate = onehot[:, None, None] * grad_mods[None]
    grad_triplane = lax.dynamic_update_slice_in_dim(
        jnp.zeros((3, plane_rows, TC, D), jnp.float32),
        grad_stream.reshape(3, PR, TC, D),
        row_start,
        1,
    )
    pieces = [
        grad_query_cross,
        grad_keyval,
        grad_out_cross,
        grad_qkv_self,
        grad_out_self,
        grad_deconv,
        grad_decode_in,
        grad_decode_out,
        grad_modulate,
        grad_triplane,
    ]
    flat_grad = jnp.concatenate([piece.reshape(-1) for piece in pieces])
    flat_grad = jnp.pad(flat_grad, (0, full_flat.shape[0] - flat_grad.shape[0]))
    blocked_gradient = regroup_blocks(gradient_first_term, gradient_second_term)
    flat_sum, block_part = (
        lax.psum_scatter(flat_grad, ("dp", "strip"), scatter_dimension=0, tiled=True),
        lax.psum_scatter(blocked_gradient, ("dp", "strip"), scatter_dimension=0, tiled=True),
    )
    block_sum = lax.all_gather(block_part.astype(jnp.bfloat16), "strip", axis=0, tiled=True).astype(
        block_part.dtype
    )
    new_first = BETA_FIRST * first_moment + (1.0 - BETA_FIRST) * flat_sum
    new_second = BETA_SECOND * second_moment + (1.0 - BETA_SECOND) * flat_sum * flat_sum
    fix_first = 1.0 - BETA_FIRST**ADAM_STEP
    fix_second = 1.0 - BETA_SECOND**ADAM_STEP
    moved = new_first / fix_first / (jnp.sqrt(new_second / fix_second) + ADAM_EPS)
    new_weights = weights - ADAM_RATE * (moved + WEIGHT_DECAY * weights)
    new_left = STAT_DECAY * stat_left + (1.0 - STAT_DECAY) * jnp.einsum(
        "bij,bkj->bik", block_sum, block_sum, precision=HIGHEST_MODE
    )
    new_right = STAT_DECAY * stat_right + (1.0 - STAT_DECAY) * jnp.einsum(
        "bji,bjk->bik", block_sum, block_sum, precision=HIGHEST_MODE
    )
    half_step = jnp.einsum("bij,bjk->bik", block_sum, root_right, precision=HIGHEST_MODE)
    precond = jnp.einsum("bij,bjk->bik", root_left, half_step, precision=HIGHEST_MODE)
    block_rms = jnp.sqrt(jnp.mean(precond * precond, axis=(1, 2)) + RMS_EPS)
    new_blocks = blocks - SHAMPOO_RATE * precond / block_rms[:, None, None]
    return (
        loss,
        new_weights,
        new_first,
        new_second,
        new_blocks,
        block_sum,
        new_left,
        new_right,
        block_rms,
    )


def solution(mesh):
    placed = (
        P(("dp", "strip")),
        P("dp", None, None),
        P("dp", None, None),
        P("dp", None, None),
        P("dp", None, None),
        P("dp", None, None),
        P(("dp", "strip")),
        P(("dp", "strip")),
        P("dp", None, None),
        P("dp"),
        P("dp", None, None, "strip"),
        P("dp", "strip"),
        P("dp", None, None),
        P("dp", None),
    )
    return jax.shard_map(
        shards,
        mesh=mesh,
        in_specs=placed,
        out_specs=(
            P(),
            P(("dp", "strip")),
            P(("dp", "strip")),
            P(("dp", "strip")),
            P("dp", None, None),
            P("dp", None, None),
            P("dp", None, None),
            P("dp", None, None),
            P("dp"),
        ),
        check_vma=False,
    )
```

profile of v0, /device:TPU:1, one launch (start us, length us, event | category | flops | bytes accessed | tf_op | source)
XLA Modules:
  0.0 2791.5 jit_solution(2490259091087222152)
XLA Ops:
  21.1 243.1 %all-gather.12.cloned.1.call-done = bf16[32,1,342272]{2,1,0:T(2,128)(2,1)} async-done(((bf16[1,1,342272]{2,1,0:T(2,128)(2,1)}), bf16[32,1,342272]{2,1,0:T(2,128)(2,1)}) %all-gather.12.cloned.1.call-update) | async-done | bytes 21905424 | tf_op jit(solution)/shard_map/all_gather | solution.py:241
  264.2 451.3 %reduce.8 = bf16[32,342272]{1,0:T(8,128)(2,1)} reduce(bf16[32,1,342272]{2,1,0:T(2,128)(2,1)} %all-gather.12.cloned.1.call-done, bf16[]{:T(256)} %constant.300), dimensions={1}, to_apply=%all-gather.reduce_sub_computation | reduce | bytes 43810816 | tf_op jit(solution)/shard_map/all_gather | solution.py:241
  715.5 52.5 %reshape.737 = bf16[10952704]{0:T(1024)(128)(2,1)} reshape(bf16[32,342272]{1,0:T(8,128)(2,1)} %reduce.8) | data formatting | bytes 43810816
  791.7 15.5 slice.281
  851.3 20.9 while.54
  925.0 23.1 copy.148
  974.8 116.2 %while.55 = (s32[]{:T(128)}, bf16[4,768,4,64]{1,3,2,0:T(8,128)(2,1)}, f32[4,4,768]{2,1,0:T(4,128)S(1)}, bf16[4,1536,4,64]{1,3,2,0:T(8,128)(2,1)}, bf16[4,768,4,6...) while((s32[]{:T(128)}, bf16[4,768,4,64]{1,3,2,0:T(8,128)(2,1)}, ...), condition=%wide.region_11.12_spmd, body=%wide.region_8.11_spmd.sunk | while | flops 1245705216 | bytes 59476056 | solution.py:175
  1096.8 19.2 fusion.114
  1161.3 15.5 gather_fusion.4
  1176.8 15.0 gather_fusion.2
  1191.8 15.0 gather_fusion.3
  1217.3 38.5 %all-reduce.13 = (f32[]{:T(128)}, f32[]{:T(128)}) all-reduce(f32[]{:T(128)} %get-tuple-element.263, f32[]{:T(128)} %get-tuple-element.262), channel_id=1, replica_groups=mesh['dp'=16,'strip'=2] {'dp','strip'}, use_global_device_ids=true, to_apply=%region_18.20 | all-reduce | flops 2 | bytes 16 | tf_op jit(solution)/shard_map/psum | solution.py:295
  1261.1 22.9 scatter_custom_fusion.1
  1284.9 22.9 scatter_custom_fusion
  1307.8 23.6 scatter_custom_fusion.2
  1385.7 19.7 fusion.106
  1428.2 201.3 %while.56 = (s32[]{:T(128)}, bf16[4,768,4,64]{1,3,2,0:T(8,128)(2,1)}, bf16[4,1536,4,64]{1,3,2,0:T(8,128)(2,1)}, bf16[4,1536,4,64]{1,3,2,0:T(8,128)(2,1)}, bf16[4...) while((s32[]{:T(128)}, ...), condition=%wide.region_31.33_spmd, body=%wide.region_29.32_spmd.sunk | while | flops 3077108736 | bytes 269444416 | solution.py:209
  1697.1 18.3 copy.167
  1727.4 19.0 pad_maximum_fusion
  1771.8 41.1 %while.57 = (s32[]{:T(128)}, bf16[4,768,4,64]{1,3,2,0:T(8,128)(2,1)}, bf16[4,257,4,64]{1,3,2,0:T(8,128)(2,1)}, bf16[4,257,4,64]{1,3,2,0:T(8,128)(2,1)}, bf16[4,2...) while((s32[]{:T(128)}, ...), condition=%wide.region_37.39_spmd, body=%wide.region_35.38_spmd.sunk | while | flops 515015936 | bytes 55065908 | solution.py:209
  1906.9 54.1 %dynamic-update-slice.15 = f32[10949888]{0:T(1024)} dynamic-update-slice(f32[10949888]{0:T(1024)} %constant_dynamic-update-slice_fusion, f32[1572864]{0:T(1024)} %bitcast.518, s32[]{} %constant.311) | dynamic-update-slice | bytes 12582916 | tf_op jit(solution)/shard_map/concatenate | solution.py:382
  1961.0 32.8 %pad.56 = f32[10952704]{0:T(1024)} pad(f32[10949888]{0:T(1024)} %dynamic-update-slice.15, f32[]{:T(128)} %constant.242.clone.1), padding=0_2816 | pad | bytes 87610368 | tf_op jit(solution)/shard_map/jit(_pad)/pad | solution.py:383
  1997.5 109.7 %reduce-scatter.8.cloned.1.call-done = f32[16,128,128]{2,1,0:T(8,128)} async-done(((f32[512,128,128]{2,1,0:T(8,128)}), f32[16,128,128]{2,1,0:T(8,128)}) %reduce-scatter.8.cloned.1.call-update) | async-done | bytes 1048592 | tf_op jit(solution)/shard_map/reduce_scatter | solution.py:387
  2109.3 641.5 %all-reduce.16.cloned.1.call-done = f32[10952704]{0:T(1024)} async-done(((f32[10952704]{0:T(1024)}), f32[10952704]{0:T(1024)}) %all-reduce.16.cloned.1.call-update) | async-done | bytes 43810832
  (678 shorter events, 917.8 us)
Async XLA Ops:
  7.2 2760.3 %copy-start = (f32[32,128,128]{2,1,0:T(8,128)S(1)}, f32[32,128,128]{2,1,0:T(8,128)}, u32[]{:S(2)}) copy-start(f32[32,128,128]{2,1,0:T(8,128)} %param.32) | copy-start | bytes 6291460
  7.2 257.1 %all-gather.12.cloned.1.call-start = ((), (), s32[]{:S(2)}) async-start(), calls=%async_computation.8 | async-start | bytes 45179904 | tf_op jit(solution)/shard_map/all_gather | solution.py:241
  17.4 883.3 %all-gather.8.cloned.1.call-start = ((), (), s32[]{:S(2)}) async-start(), calls=%async_computation.4 | async-start | bytes 17825792 | tf_op jit(solution)/shard_map/all_gather | solution.py:242
  20.2 937.6 %all-gather.6.cloned.1.call-start = ((), (), s32[]{:S(2)}) async-start(), calls=%async_computation.3 | async-start | bytes 9437184 | tf_op jit(solution)/shard_map/all_gather | solution.py:263
  839.1 39.5 %copy-start.96 = (f32[1,1024]{1,0:T(1,128)}, f32[1,1024]{1,0:T(1,128)S(1)}, u32[]{:S(2)}) copy-start(f32[1,1024]{1,0:T(1,128)S(1)} %get-tuple-element.381) | copy-start | bytes 12292
  839.1 39.5 %copy-start.108 = (f32[1,1024]{1,0:T(1,128)}, f32[1,1024]{1,0:T(1,128)S(1)}, u32[]{:S(2)}) copy-start(f32[1,1024]{1,0:T(1,128)S(1)} %get-tuple-element.380) | copy-start | bytes 12292
  888.6 460.3 %reduce-scatter.10.cloned.1.call-start = ((), (), s32[]{:S(2)}) async-start(), calls=%async_computation.9 | async-start | bytes 1474560
  889.4 23.6 copy-start.68
  889.4 23.6 copy-start.69
  889.4 23.6 copy-start.70
  1096.1 19.9 copy-start.5
  1096.1 322.0 %copy-start.53 = (f32[768]{0:T(1024)}, f32[768]{0:T(1024)S(1)}, u32[]{:S(2)}) copy-start(f32[768]{0:T(1024)S(1)} %broadcast_multiply_fusion.2) | copy-start | bytes 9220
  1096.6 321.6 %copy-start.57 = (f32[768]{0:T(1024)}, f32[768]{0:T(1024)S(1)}, u32[]{:S(2)}) copy-start(f32[768]{0:T(1024)S(1)} %fusion.212) | copy-start | bytes 9220
  1129.7 18.4 collective-permute-start
  1131.0 17.1 collective-permute-start.1
  1339.1 407.4 %reduce-scatter.6.cloned.1.call-start = ((), (), s32[]{:S(2)}) async-start(), calls=%async_computation.5 | async-start | bytes 9437184 | tf_op jit(solution)/shard_map/reduce_scatter | solution.py:340
  1376.3 6.7 collective-permute-start.2
  1377.6 5.4 collective-permute-start.3
  1635.4 471.8 %reduce-scatter.8.cloned.1.call-start = ((), (), s32[]{:S(2)}) async-start(), calls=%async_computation.6 | async-start | bytes 34603008 | tf_op jit(solution)/shard_map/reduce_scatter | solution.py:387
  1746.4 1004.5 %all-reduce.16.cloned.1.call-start = ((), (), s32[]{:S(2)}) async-start(), calls=%async_computation.10 | async-start | bytes 87621632
  1771.8 41.1 %copy-start.72 = (f32[1,1024]{1,0:T(1,128)S(1)}, f32[1,1024]{1,0:T(1,128)}, u32[]{:S(2)}) copy-start(f32[1,1024]{1,0:T(1,128)} %copy-done.71) | copy-start | bytes 12292
  1771.8 41.1 %copy-start.78 = (f32[768]{0:T(1024)S(1)}, f32[768]{0:T(1024)}, u32[]{:S(2)}) copy-start(f32[768]{0:T(1024)} %copy-done.77) | copy-start | bytes 9220
  1993.9 769.8 %all-gather.10.cloned.1.call-start = ((), (), s32[]{:S(2)}) async-start(), calls=%async_computation.7 | async-start | bytes 1572864 | tf_op jit(solution)/shard_map/all_gather | solution.py:389
  1993.9 757.0 %copy-start.23 = (f32[342272]{0:T(1024)S(1)}, f32[342272]{0:T(1024)}, u32[]{:S(2)}) copy-start(f32[342272]{0:T(1024)} %param.28) | copy-start | bytes 4107268
  (168 other events, 807.6 us)
Sparse Core Ops, SparseCore 0:
  17.5 246.6 all-gather.11
  267.6 188.9 all-gather.7
  888.7 14.8 all-gather.5
  1339.2 9.5 reduce-scatter.9
  1635.6 15.5 reduce-scatter.5
  1746.5 360.6 reduce-scatter.7
  2113.6 637.2 all-reduce.15
  2753.1 10.5 all-gather.9
where the time goes:
time: 2800 us; the launch traced here: 2790 us
  waiting for transfers between devices  1010 us (36%)
  other arithmetic  698 us (25%)
  local copies, waits for them, and re-layouts  588 us (21%)
  matrix products  430 us (15%)
  blocking collectives  41.5 us (1%)
    unnamed x10, waiting for transfers between devices  645 us
    all_gather x1, other arithmetic, shards(): lax.all_gather(weights.astype(jnp.bfloat16), ('dp', 'strip'), axis=0, til...  451 us
    all_gather x1, waiting for transfers between devices, shards(): lax.all_gather(weights.astype(jnp.bfloat16), ('dp', 'strip'), axis=0, til...  243 us
    unnamed x249, local copies, waits for them, and re-layouts  156 us
    reduce_scatter x1, waiting for transfers between devices, shards(): lax.psum_scatter(blocked_gradient, ('dp', 'strip'), scatter_dimension=0,...  110 us
    dot_general x16, matrix products, one_group(): jnp.einsum('qhd,khd->hqk', query_part, key_part, preferred_element_type=j...  70.7 us
    scatter-add x3, other arithmetic, shards(): jax.ops.segment_sum(grad_point, cells_read[plane], num_segments=cells.sha...  69.4 us
    dot_general x9, matrix products, product_back(): lax.dot_general(left, right, (((left.ndim - 1,), (1,)), ((), ())), prefer...  64.5 us
  transfers between devices with their start and end apart: 12, of which 5 were waited for; matrix products, arithmetic and copies ran while one was open for 38% of the time, Pallas kernels for 0%

commit v1 on v0

--- a/solution.py
+++ b/solution.py
@@ -1,8 +1,11 @@
+import functools
 import math
 
 import jax
 import jax.numpy as jnp
 from jax import lax
+from jax.experimental import pallas as pl
+from jax.experimental.pallas import tpu as pltpu
 from jax.sharding import PartitionSpec as P
 
 D = 1024
@@ -45,58 +48,6 @@
     return block
 
 
-def segments(plane_rows):
-    return (
-        ("query_cross", (D, D)),
-        ("keyval_cross", (DI, 2 * D)),
-        ("out_cross", (D, D)),
-        ("qkv_self", (D, 3 * D)),
-        ("out_self", (D, D)),
-        ("deconv", (D, 16 * CH)),
-        ("decode_in", (CH, DEC_HID)),
-        ("decode_out", (DEC_HID, 4)),
-        ("modulate", (NCAM, 6, D)),
-        ("triplane", (3, plane_rows, TC, D)),
-    )
-
-
-def unflatten(flat, plane_rows):
-    parts = {}
-    offset = 0
-    for label, shape in segments(plane_rows):
-        length = math.prod(shape)
-        parts[label] = flat[offset : offset + length].reshape(shape)
-        offset += length
-    return parts
-
-
-def unblock(tiles):
-    rows_one, cols_one = (D // BLOCK, HID // BLOCK)
-    half = rows_one * cols_one
-    leading_value = (
-        tiles[:half].reshape(rows_one, cols_one, BLOCK, BLOCK).transpose(0, 2, 1, 3).reshape(D, HID)
-    )
-    trailing_value = (
-        tiles[half:].reshape(cols_one, rows_one, BLOCK, BLOCK).transpose(0, 2, 1, 3).reshape(HID, D)
-    )
-    return (leading_value, trailing_value)
-
-
-def regroup_blocks(leading_value, trailing_value):
-    rows_one, cols_one = (D // BLOCK, HID // BLOCK)
-    upper = (
-        leading_value.reshape(rows_one, BLOCK, cols_one, BLOCK)
-        .transpose(0, 2, 1, 3)
-        .reshape(-1, BLOCK, BLOCK)
-    )
-    lower = (
-        trailing_value.reshape(cols_one, BLOCK, rows_one, BLOCK)
-        .transpose(0, 2, 1, 3)
-        .reshape(-1, BLOCK, BLOCK)
-    )
-    return jnp.concatenate([upper, lower], 0)
-
-
 def product(left, right):
     return jnp.dot(left, right, preferred_element_type=jnp.float32)
 
@@ -136,17 +87,15 @@
     return jnp.stack([left_cols, right_cols], 4).reshape(planes, 2 * inner, 2 * cols, -1)
 
 
-def render_loss(output, pixel, target, valid):
+def render_loss(output, mask, wanted):
     sigma = jax.nn.softplus(output[..., 0])
     colour = jax.nn.sigmoid(output[..., 1:])
     absorb = 4.0 / S * sigma
     before = jnp.cumsum(absorb, 0) - absorb
     weight = jnp.exp(-before) * (1.0 - jnp.exp(-absorb))
     colour_sum = jnp.sum(weight[..., None] * colour, 0)
-    mask = jnp.take(valid, pixel).astype(jnp.float32)
-    wanted = jnp.take(target, pixel, axis=1)
     error = colour_sum.T - wanted
-    return (jnp.sum(mask * jnp.sum(error * error, 0)), jnp.sum(mask))
+    return jnp.sum(mask * jnp.sum(error * error, 0))
 
 
 def split_heads(matrix):
@@ -217,6 +166,453 @@
         ),
     )
     return (merge_heads(grads[0]), merge_heads(grads[1]), merge_heads(grads[2]))
+
+
+LANE = 1024
+MESH_ID = pl.DeviceIdType.MESH
+
+
+def places():
+    p = lax.axis_index("dp")
+    c = lax.axis_index("strip")
+    z = p // 4
+    flip_x = p + 1 - 2 * (p % 2)
+    flip_y = p + 2 - 4 * ((p // 2) % 2)
+    both = flip_x + flip_y - p
+    near = (1 - c) * flip_x + c * flip_y
+    far = (1 - c) * flip_y + c * flip_x
+    return p, c, z, near, far, both
+
+
+def along_z(line, z, k):
+    return ((z + k) % 4) * 4 + line % 4
+
+
+def enter(peers):
+    barrier = pltpu.get_barrier_semaphore()
+    for peer in peers:
+        pl.semaphore_signal(barrier, inc=1, device_id=peer, device_id_type=MESH_ID)
+    pl.semaphore_wait(barrier, len(peers))
+
+
+def flat_chunks(rows, n):
+    part = rows // n
+    return n, part, lambda p, c, j: (2 * p + c) * rows + j * part
+
+
+def block_chunk(p, c, k):
+    second = p // 8
+    return ((1 - second) * ((2 * c + k) * 8 + p) + second * (4 * p + 2 * c + k)) * BLOCK
+
+block_chunks = (2, BLOCK, block_chunk)
+
+
+ORDER = [("near", 0), ("z", 1), ("z", 3), ("far", 0), ("z", 2), ("near", 1), ("near", 3), ("near", 2)]
+ORDER += [("both", 0), ("far", 1), ("far", 3), ("far", 2), ("both", 1), ("both", 3), ("both", 2)]
+ORDER += [("core", i) for i in range(16)]
+
+def gather_kernel(layouts, stagger, *refs):
+    count = len(layouts)
+    sources = refs[:count]
+    fulls = refs[count : 2 * count]
+    send, recv, local = refs[2 * count :]
+    p, c, z, near, far, both = places()
+    zs = [along_z(p, z, k) for k in range(4)]
+    enter([(q, c) for q in zs[1:]] + [(near, c), (far, c), (p, 1 - c)])
+    jobs = [(a, j) for a, layout in enumerate(layouts) for j in range(layout[0])]
+
+    def target(owner, job):
+        a, j = jobs[job]
+        _, rows, place = layouts[a]
+        return fulls[a].at[pl.ds(pl.multiple_of(place(*owner, j), 8), rows)]
+
+    def source(job):
+        a, j = jobs[job]
+        rows = layouts[a][1]
+        return sources[a].at[pl.ds(j * rows, rows)]
+
+    started = []
+
+    def forward(owner, own, event, peer, job):
+        t = target(owner, job)
+        copy = pltpu.make_async_remote_copy(
+            source(job) if own else t, t, send.at[event, job], recv.at[event, job], device_id=peer, device_id_type=MESH_ID
+        )
+        copy.start()
+        started.append(copy)
+
+    def arrive(owner, event, job):
+        t = target(owner, job)
+        pltpu.make_async_remote_copy(
+            t, t, send.at[event, job], recv.at[event, job], device_id=(p, 1 - c), device_id_type=MESH_ID
+        ).wait_recv()
+
+    me = (p, c)
+
+    def begin(job):
+        forward(me, True, 3, (near, c), job)
+        for k in (1, 3, 2):
+            forward(me, True, 3 - k, (zs[k], c), job)
+        forward(me, True, 7, (far, c), job)
+        forward(me, True, 15, (p, 1 - c), job)
+        pltpu.make_async_copy(source(job), target(me, job), local.at[job]).start()
+
+    def take(kind, k, job):
+        if kind == "z":
+            owner = (zs[k], c)
+            arrive(owner, k - 1, job)
+            forward(owner, False, 3 + k, (near, c), job)
+            forward(owner, False, 7 + k, (far, c), job)
+            forward(owner, False, 15 + k, (p, 1 - c), job)
+        elif kind == "near":
+            owner = (along_z(near, z, k), c)
+            arrive(owner, 3 + k, job)
+            forward(owner, False, 11 + k, (far, c), job)
+            forward(owner, False, 19 + k, (p, 1 - c), job)
+        elif kind == "far":
+            owner = (along_z(far, z, k), c)
+            arrive(owner, 7 + k, job)
+            forward(owner, False, 23 + k, (p, 1 - c), job)
+        elif kind == "both":
+            owner = (along_z(both, z, k), c)
+            arrive(owner, 11 + k, job)
+            forward(owner, False, 27 + k, (p, 1 - c), job)
+        elif kind == "core":
+            line = (p, far, near, both)[k // 4]
+            arrive((along_z(line, z, k % 4), 1 - c), 15 + k, job)
+
+    steps = []
+    for job in range(len(jobs)):
+        steps.append((stagger * job, -1, job))
+        for i in range(len(ORDER)):
+            steps.append((stagger * job + i + 1, i, job))
+    for _, i, job in sorted(steps):
+        if i < 0:
+            begin(job)
+        else:
+            take(*ORDER[i], job)
+    for copy in started:
+        copy.wait_send()
+    for job in range(len(jobs)):
+        pltpu.make_async_copy(source(job), target(me, job), local.at[job]).wait()
+
+
+def gather_all(layouts, stagger, shards_in, name_id):
+    copies = sum(l[0] for l in layouts)
+    return pl.pallas_call(
+        functools.partial(gather_kernel, layouts, stagger),
+        out_shape=[jax.ShapeDtypeStruct((32 * s.shape[0],) + s.shape[1:], s.dtype) for s in shards_in],
+        in_specs=[pl.BlockSpec(memory_space=pl.ANY)] * len(shards_in),
+        out_specs=[pl.BlockSpec(memory_space=pl.ANY)] * len(shards_in),
+        scratch_shapes=[
+            pltpu.SemaphoreType.DMA((31, copies)),
+            pltpu.SemaphoreType.DMA((31, copies)),
+            pltpu.SemaphoreType.DMA((copies,)),
+        ],
+        compiler_params=pltpu.CompilerParams(collective_id=name_id, has_side_effects=True),
+        name="gather_all",
+    )(*shards_in)
+
+
+SUM_ORDER = [(3, 0), (3, 1), (3, 3), (3, 2), (2, 0), (2, 1), (2, 3), (2, 2)]
+SUM_ORDER += [(1, 1), (1, 3), (1, 2), (1, 0), (0, 1), (0, 3), (0, 2), (0, 0)]
+AHEAD = 3
+
+
+def scatter_kernel(layouts, shared, stagger, *refs):
+    count = len(layouts)
+    grads = refs[:count]
+    outs = refs[count : 2 * count]
+    scratch = refs[2 * count :]
+    p, c, z, near, far, both = places()
+    zs = [along_z(p, z, k) for k in range(4)]
+    enter([(q, c) for q in zs[1:]] + [(near, c), (far, c), (p, 1 - c)])
+    csend, crecv, bsend, brecv, load_sem, out_sem = scratch[:6]
+    buffers = [scratch[6 + 6 * a : 12 + 6 * a] for a in range(count)]
+    jobs = [(a, j) for a, layout in enumerate(layouts) for j in range(layout[0])]
+    lines = (p, near, far, both)
+    partner_lines = (p, far, near, both)
+
+    def view(job, ref, slot):
+        a, j = jobs[job]
+        rows = layouts[a][1]
+        return ref.at[slot, pl.ds(j * rows, rows)]
+
+    def piece(owner, job):
+        a, j = jobs[job]
+        _, rows, place = layouts[a]
+        return grads[a].at[pl.ds(pl.multiple_of(place(*owner, j), 8), rows)]
+
+    def to_core(i, job):
+        g, k = SUM_ORDER[i]
+        owner = (along_z(partner_lines[g], z, k), 1 - c)
+        rc = buffers[jobs[job][0]][0]
+        return pltpu.make_async_remote_copy(
+            piece(owner, job), view(job, rc, g * 4 + k), csend.at[i, job], crecv.at[i, job],
+            device_id=(p, 1 - c), device_id_type=MESH_ID,
+        )
+
+    def load(i, job):
+        g, k = SUM_ORDER[i]
+        own = buffers[jobs[job][0]][4]
+        return pltpu.make_async_copy(
+            piece((along_z(lines[g], z, k), c), job), view(job, own, i % AHEAD), load_sem.at[i, job]
+        )
+
+    def onward(i, job):
+        g, k = SUM_ORDER[i]
+        rc, rb, ra, rz = buffers[jobs[job][0]][:4]
+        if g == 3:
+            target, event, peer = view(job, rb, 4 + k), 4 + k, (far, c)
+        elif g == 2:
+            target, event, peer = view(job, rb, k), k, (far, c)
+        elif g == 1:
+            target, event, peer = view(job, ra, k), 8 + k, (near, c)
+        else:
+            target, event, peer = view(job, rz, 3 - k), 12 + 3 - k, (zs[k], c)
+        return pltpu.make_async_remote_copy(
+            view(job, rc, g * 4 + k), target, bsend.at[event, job], brecv.at[event, job],
+            device_id=peer, device_id_type=MESH_ID,
+        )
+
+    def landed(event, job):
+        rc, rb, ra, rz = buffers[jobs[job][0]][:4]
+        if event < 8:
+            target = view(job, rb, event)
+        elif event < 12:
+            target = view(job, ra, event - 8)
+        else:
+            target = view(job, rz, event - 12)
+        pltpu.make_async_remote_copy(
+            target, target, bsend.at[event, job], brecv.at[event, job], device_id=(p, 1 - c), device_id_type=MESH_ID
+        ).wait_recv()
+        return target
+
+    def add_up(parts, target):
+        rows = target.shape[0]
+        step = math.gcd(rows, 16)
+
+        @pl.loop(0, rows // step)
+        def _(n):
+            at = pl.ds(pl.multiple_of(n * step, step), step)
+            total = parts[0][at].astype(jnp.float32)
+            for part in parts[1:]:
+                total = total + part[at].astype(jnp.float32)
+            target[at] = total.astype(target.dtype)
+
+    def start(i, job):
+        to_core(i, job).start()
+        load(i, job).start()
+
+    def final_copies(job):
+        a, j = jobs[job]
+        rows = layouts[a][1]
+        done = view(job, buffers[a][5], 0)
+        if not shared[a]:
+            return [pltpu.make_async_copy(done, outs[a].at[pl.ds(j * rows, rows)], out_sem.at[job, 0])]
+        spot = outs[a].at[pl.ds(pl.multiple_of((c * layouts[a][0] + j) * rows, 8), rows)]
+        return [
+            pltpu.make_async_copy(done, spot, out_sem.at[job, 0]),
+            pltpu.make_async_remote_copy(
+                done, spot, out_sem.at[job, 1], out_sem.at[job, 2], device_id=(p, 1 - c), device_id_type=MESH_ID
+            ),
+        ]
+
+    def step(i, job):
+        g, k = SUM_ORDER[i]
+        rc, rb, ra, rz, own, done = buffers[jobs[job][0]]
+        load(i, job).wait()
+        to_core(i, job).wait_recv()
+        here = view(job, rc, g * 4 + k)
+        parts = [here, view(job, own, i % AHEAD)]
+        if g == 1:
+            parts.append(landed(4 + k, job))
+        if g == 0:
+            parts.append(landed(k, job))
+            parts.append(landed(8 + k, job))
+        if (g, k) == (0, 0):
+            parts += [landed(12 + n, job) for n in range(3)]
+            add_up(parts, view(job, done, 0))
+            for copy in final_copies(job):
+                copy.start()
+        else:
+            add_up(parts, here)
+            onward(i, job).start()
+        if i + AHEAD < 16:
+            start(i + AHEAD, job)
+
+    steps = []
+    for job in range(len(jobs)):
+        for i in range(-1, 16):
+            steps.append((stagger * job + i, job, i))
+    for _, job, i in sorted(steps):
+        if i < 0:
+            for n in range(AHEAD):
+                start(n, job)
+        else:
+            step(i, job)
+    for job in range(len(jobs)):
+        for i in range(16):
+            to_core(i, job).wait_send()
+            if i < 15:
+                onward(i, job).wait_send()
+        for copy in final_copies(job):
+            copy.wait()
+
+
+def scatter_sum(layouts, shared, stagger, grads, name_id):
+    jobs = sum(l[0] for l in layouts)
+    scratch = [
+        pltpu.SemaphoreType.DMA((16, jobs)),
+        pltpu.SemaphoreType.DMA((16, jobs)),
+        pltpu.SemaphoreType.DMA((15, jobs)),
+        pltpu.SemaphoreType.DMA((15, jobs)),
+        pltpu.SemaphoreType.DMA((16, jobs)),
+        pltpu.SemaphoreType.DMA((jobs, 3)),
+    ]
+    shapes = []
+    for layout, both_cores, grad in zip(layouts, shared, grads):
+        rows, width = layout[0] * layout[1], grad.shape[1]
+        for slots in (16, 8, 4, 3, AHEAD):
+            scratch.append(pltpu.VMEM((slots, rows, width), grad.dtype))
+        kind = grad.dtype if both_cores else jnp.float32
+        scratch.append(pltpu.VMEM((1, rows, width), kind))
+        shapes.append(jax.ShapeDtypeStruct(((2 if both_cores else 1) * rows, width), kind))
+    return pl.pallas_call(
+        functools.partial(scatter_kernel, layouts, shared, stagger),
+        out_shape=shapes,
+        in_specs=[pl.BlockSpec(memory_space=pl.ANY)] * len(grads),
+        out_specs=[pl.BlockSpec(memory_space=pl.ANY)] * len(grads),
+        scratch_shapes=scratch,
+        compiler_params=pltpu.CompilerParams(
+            collective_id=name_id, has_side_effects=True, vmem_limit_bytes=56 * 1024 * 1024
+        ),
+        name="scatter_sum",
+    )(*grads)
+
+
+WIDE = 1024
+TILE = 8 * WIDE
+GAP_AT = D * D + DI * 2 * D + D * D + D * 3 * D + D * D + D * 16 * CH + CH * DEC_HID + DEC_HID * 4
+GAP = -GAP_AT % TILE
+ROWS = {}
+_row = 0
+for _name, _rows in (
+    ("query_cross", D),
+    ("keyval_cross", 2 * DI),
+    ("out_cross", D),
+    ("qkv_self", 3 * D),
+    ("out_self", D),
+    ("deconv", 16 * CH),
+    ("decode", 8),
+    ("modulate", 6 * NCAM),
+):
+    ROWS[_name] = (_row, _row + _rows)
+    _row += _rows
+PLANE_ROW = _row
+
+
+def direct_links():
+    return lax.axis_size("dp") == 16 and lax.axis_size("strip") == 2
+
+
+def align(shard):
+    length = shard.shape[0]
+    rows = -(-length // TILE) * 8
+    size = rows * WIDE
+    extra = size - length
+    reach = -(-32 * extra // WIDE) * WIDE
+    place = lax.axis_index("dp") * 2 + lax.axis_index("strip")
+    shard = shard.astype(jnp.bfloat16)
+    following = lax.ppermute(shard[:reach], ("dp", "strip"), [(n + 1, n) for n in range(31)])
+    joined = jnp.concatenate([shard, following])
+    shift = place * extra
+    early = lax.dynamic_slice_in_dim(joined, shift, size)
+    late = lax.dynamic_slice_in_dim(joined, jnp.maximum(shift - GAP, 0), size)
+    at = place * size + lax.iota(jnp.int32, size)
+    return jnp.where(at < GAP_AT, early, late).reshape(rows, WIDE)
+
+
+def unalign(summed, length):
+    size = summed.size
+    extra = size - length
+    reach = -(-32 * extra // WIDE) * WIDE
+    place = lax.axis_index("dp") * 2 + lax.axis_index("strip")
+    summed = summed.reshape(-1)
+    before = lax.ppermute(summed[size - reach :], ("dp", "strip"), [(n, n + 1) for n in range(31)])
+    joined = jnp.concatenate([before, summed])
+    shift = reach - place * extra
+    early = lax.dynamic_slice_in_dim(joined, shift, length)
+    late = lax.dynamic_slice_in_dim(joined, shift + GAP, length)
+    at = place * length + lax.iota(jnp.int32, length)
+    return jnp.where(at < GAP_AT, early, late)
+
+
+def chunks_of(tiles):
+    return tiles.reshape(-1, 8, BLOCK, BLOCK).transpose(0, 2, 1, 3).reshape(-1, WIDE)
+
+
+def tiles_of(chunks):
+    return chunks.reshape(-1, BLOCK, 8, BLOCK).transpose(0, 2, 1, 3).reshape(-1, BLOCK, BLOCK)
+
+
+def panels_of(chunks):
+    half = chunks.shape[0] // 2
+    first = chunks[:half].reshape(D // BLOCK, HID // WIDE, BLOCK, WIDE).transpose(1, 0, 2, 3)
+    return jnp.concatenate([first.reshape(half, WIDE), chunks[half:]])
+
+
+def chunks_of_panels(panels):
+    half = panels.shape[0] // 2
+    first = panels[:half].reshape(HID // WIDE, D // BLOCK, BLOCK, WIDE).transpose(1, 0, 2, 3)
+    return jnp.concatenate([first.reshape(half, WIDE), panels[half:]])
+
+
+META = (1, 8, lambda p, c, j: (2 * p + c) * 8)
+
+
+def gather_weights(weights, blocks, part):
+    length = weights.shape[0]
+    if direct_links():
+        own = align(weights)
+        half = blocks.shape[0] // 2
+        tiles = lax.dynamic_slice_in_dim(blocks, lax.axis_index("strip") * half, half)
+        tiles = chunks_of(tiles.astype(jnp.bfloat16))
+        meta = jnp.full((8, 128), part, jnp.float32)
+        rows, panels, parts = gather_all(
+            [flat_chunks(own.shape[0], 3), block_chunks, META], 6, [own, tiles, meta], 0
+        )
+        return rows, panels, jnp.sum(parts[::8, 0])
+    flat = lax.all_gather(weights.astype(jnp.bfloat16), ("dp", "strip"), axis=0, tiled=True)
+    tiles = lax.all_gather(blocks.astype(jnp.bfloat16), "dp", axis=0, tiled=True)
+    rows = jnp.concatenate([flat[:GAP_AT], jnp.zeros((GAP,), flat.dtype), flat[GAP_AT:]])
+    rows = rows[: rows.shape[0] // TILE * TILE].reshape(-1, WIDE)
+    return rows, panels_of(chunks_of(tiles)), lax.psum(part, ("dp", "strip"))
+
+
+def reduce_grads(pieces, panels, part, length):
+    if direct_links():
+        rows = -(-length // TILE) * 8
+        total = sum(piece.shape[0] for piece in pieces)
+        pieces = pieces + [jnp.zeros((32 * rows - total, WIDE), jnp.bfloat16)]
+        meta = jnp.full((32 * 8, 128), part, jnp.float32)
+        summed, tiles, parts = scatter_sum(
+            [flat_chunks(rows, 1), block_chunks, META],
+            [False, True, False],
+            6,
+            [jnp.concatenate(pieces), panels, meta],
+            1,
+        )
+        return unalign(summed, length), tiles_of(tiles).astype(jnp.float32), parts[0, 0]
+    flat = jnp.concatenate(pieces).astype(jnp.float32).reshape(-1)
+    flat = jnp.concatenate([flat[:GAP_AT], flat[GAP_AT + GAP :]])
+    devices = lax.axis_size("dp") * lax.axis_size("strip")
+    flat = jnp.pad(flat, (0, devices * length - flat.shape[0]))
+    tiles = tiles_of(chunks_of_panels(panels)).astype(jnp.float32)
+    flat_sum = lax.psum_scatter(flat, ("dp", "strip"), scatter_dimension=0, tiled=True)
+    tile_sum = lax.psum_scatter(tiles, ("dp", "strip"), scatter_dimension=0, tiled=True)
+    tile_sum = lax.all_gather(tile_sum.astype(jnp.bfloat16), "strip", axis=0, tiled=True)
+    return flat_sum, tile_sum.astype(jnp.float32), lax.psum(part, ("dp", "strip"))
 
 
 def shards(
@@ -238,17 +634,26 @@
     strips = lax.axis_size("strip")
     place = lax.axis_index("strip")
     plane_rows = PR * strips
-    full_flat = lax.all_gather(weights.astype(jnp.bfloat16), ("dp", "strip"), axis=0, tiled=True)
-    full_blocks = lax.all_gather(blocks.astype(jnp.bfloat16), "dp", axis=0, tiled=True)
-    params = unflatten(full_flat, plane_rows)
-    mlp_one, mlp_two = unblock(full_blocks)
+    pixel = ray_pixel[0]
+    mask = jnp.take(valid[0], pixel).astype(jnp.float32)
+    wanted = jnp.take(target[0], pixel, axis=1)
+    rows, panels, count = gather_weights(weights, blocks, jnp.sum(mask))
+    panels = panels.reshape(-1, WIDE, WIDE)
+    first_panels = [panels[n] for n in range(HID // WIDE)]
+    second_panels = [panels[n] for n in range(HID // WIDE, 2 * HID // WIDE)]
+    params = {name: rows[low:high] for name, (low, high) in ROWS.items()}
+    params["keyval_cross"] = params["keyval_cross"].reshape(DI, 2 * D)
+    params["qkv_self"] = params["qkv_self"].reshape(D, 3 * D)
+    params["deconv"] = params["deconv"].reshape(D, 16 * CH)
+    decode = params["decode"].reshape(-1)
+    decode_in = decode[: CH * DEC_HID].reshape(CH, DEC_HID)
+    decode_out = decode[CH * DEC_HID : CH * DEC_HID + DEC_HID * 4].reshape(DEC_HID, 4)
     picture = image[0]
     cells_read = samples[0].reshape(3, -1)
-    pixel = ray_pixel[0]
-    onehot = (lax.iota(jnp.int32, NCAM) == camera[0]).astype(jnp.float32)
-    mods = jnp.einsum("c,cjd->jd", onehot, params["modulate"].astype(jnp.float32))
+    mods = lax.dynamic_slice_in_dim(params["modulate"], 6 * camera[0], 6).astype(jnp.float32)
     row_start = place * PR
-    own_rows = lax.dynamic_slice_in_dim(params["triplane"], row_start, PR, 1)
+    triplane = rows[PLANE_ROW : PLANE_ROW + 3 * plane_rows * TC].reshape(3, plane_rows, TC, D)
+    own_rows = lax.dynamic_slice_in_dim(triplane, row_start, PR, 1)
     stream0 = own_rows.reshape(-1, D).astype(jnp.float32)
     hidden1, norm_one = jax.vjp(norm_mod, stream0, mods[0], mods[1])
     hidden1 = hidden1.astype(jnp.bfloat16)
@@ -266,10 +671,13 @@
     stream2 = stream1 + product(self_out, params["out_self"])
     hidden3, norm_three = jax.vjp(norm_mod, stream2, mods[4], mods[5])
     hidden3 = hidden3.astype(jnp.bfloat16)
-    up_value = product(hidden3, mlp_one)
-    act, gelu_back = jax.vjp(gelu_tanh, up_value)
-    act = act.astype(jnp.bfloat16)
-    stream3 = stream2 + product(act, mlp_two)
+    stream3 = stream2
+    acts, gelu_backs = [], []
+    for first, second in zip(first_panels, second_panels):
+        act, gelu_back = jax.vjp(gelu_tanh, product(hidden3, first))
+        acts.append(act.astype(jnp.bfloat16))
+        gelu_backs.append(gelu_back)
+        stream3 = stream3 + product(acts[-1], second)
     grid = stream3.astype(jnp.bfloat16).reshape(3, PR, -1, D)
     padded = with_halo(grid, (("strip", 1),), 1)
     ydc = jnp.einsum("prcd,dk->prck", padded, params["deconv"], preferred_element_type=jnp.float32)
@@ -282,26 +690,24 @@
         + jnp.take(cells[2], cells_read[2], axis=0).astype(jnp.float32)
     )
     point = point.astype(jnp.bfloat16)
-    inner_value = product(point, params["decode_in"])
+    inner_value = product(point, decode_in)
     hidden, silu_back = jax.vjp(jax.nn.silu, inner_value)
     hidden = hidden.astype(jnp.bfloat16)
-    output = product(hidden, params["decode_out"])
+    output = product(hidden, decode_out)
     rays = pixel.shape[0]
 
     def local_loss(values):
-        return render_loss(values.reshape(S, rays, 4), pixel, target[0], valid[0])
-
-    (loss_part, count_part), render_back = jax.vjp(local_loss, output)
-    loss_sum, count = lax.psum((loss_part, count_part), ("dp", "strip"))
+        return render_loss(values.reshape(S, rays, 4), mask, wanted)
+
+    loss_part, render_back = jax.vjp(local_loss, output)
     factor = 1.0 / jnp.maximum(count, 1.0)
-    loss = loss_sum * factor
-    (grad_output,) = render_back((factor, jnp.zeros_like(count_part)))
+    (grad_output,) = render_back(factor)
     grad_output = grad_output.astype(jnp.bfloat16)
     grad_decode_out = weight_grad(hidden, grad_output)
-    (grad_inner,) = silu_back(product_back(grad_output, params["decode_out"]))
+    (grad_inner,) = silu_back(product_back(grad_output, decode_out))
     grad_inner = grad_inner.astype(jnp.bfloat16)
     grad_decode_in = weight_grad(point, grad_inner)
-    grad_point = product_back(grad_inner, params["decode_in"])
+    grad_point = product_back(grad_inner, decode_in)
     gradient_cell_grid = jnp.stack(
         [
             jax.ops.segment_sum(grad_point, cells_read[plane], num_segments=cells.shape[1])
@@ -325,11 +731,15 @@
     grad_grid = grad_grid.at[:, 0].add(beside[:, 0]).at[:, -1].add(beside[:, -1])
     grad_stream = grad_grid.reshape(-1, D)
     grad_branch = grad_stream.astype(jnp.bfloat16)
-    gradient_second_term = weight_grad(act, grad_branch)
-    (grad_up,) = gelu_back(product_back(grad_branch, mlp_two))
-    grad_up = grad_up.astype(jnp.bfloat16)
-    gradient_first_term = weight_grad(hidden3, grad_up)
-    grad_norm, grad_mod4, grad_mod5 = norm_three(product_back(grad_up, mlp_one))
+    grad_first, grad_second = [], []
+    grad_hidden3 = 0.0
+    for first, second, act, gelu_back in zip(first_panels, second_panels, acts, gelu_backs):
+        grad_second.append(weight_grad(act, grad_branch).astype(jnp.bfloat16))
+        (grad_up,) = gelu_back(product_back(grad_branch, second))
+        grad_up = grad_up.astype(jnp.bfloat16)
+        grad_first.append(weight_grad(hidden3, grad_up).astype(jnp.bfloat16))
+        grad_hidden3 = grad_hidden3 + product_back(grad_up, first)
+    grad_norm, grad_mod4, grad_mod5 = norm_three(grad_hidden3)
     grad_stream = grad_stream + grad_norm
     grad_branch = grad_stream.astype(jnp.bfloat16)
     grad_out_self = weight_grad(self_out, grad_branch)
@@ -360,13 +770,17 @@
     grad_norm, grad_mod0, grad_mod1 = norm_one(product_back(grad_query1, params["query_cross"]))
     grad_stream = grad_stream + grad_norm
     grad_mods = jnp.stack([grad_mod0, grad_mod1, grad_mod2, grad_mod3, grad_mod4, grad_mod5])
-    grad_modulate = onehot[:, None, None] * grad_mods[None]
+    grad_modulate = lax.dynamic_update_slice_in_dim(
+        jnp.zeros((6 * NCAM, D), jnp.bfloat16), grad_mods.astype(jnp.bfloat16), 6 * camera[0], 0
+    )
     grad_triplane = lax.dynamic_update_slice_in_dim(
-        jnp.zeros((3, plane_rows, TC, D), jnp.float32),
-        grad_stream.reshape(3, PR, TC, D),
+        jnp.zeros((3, plane_rows, TC, D), jnp.bfloat16),
+        grad_stream.astype(jnp.bfloat16).reshape(3, PR, TC, D),
         row_start,
         1,
     )
+    grad_decode = jnp.concatenate([grad_decode_in.reshape(-1), grad_decode_out.reshape(-1)])
+    grad_decode = jnp.pad(grad_decode, (0, GAP))
     pieces = [
         grad_query_cross,
         grad_keyval,
@@ -374,21 +788,14 @@
         grad_qkv_self,
         grad_out_self,
         grad_deconv,
-        grad_decode_in,
-        grad_decode_out,
+        grad_decode,
         grad_modulate,
         grad_triplane,
     ]
-    flat_grad = jnp.concatenate([piece.reshape(-1) for piece in pieces])
-    flat_grad = jnp.pad(flat_grad, (0, full_flat.shape[0] - flat_grad.shape[0]))
-    blocked_gradient = regroup_blocks(gradient_first_term, gradient_second_term)
-    flat_sum, block_part = (
-        lax.psum_scatter(flat_grad, ("dp", "strip"), scatter_dimension=0, tiled=True),
-        lax.psum_scatter(blocked_gradient, ("dp", "strip"), scatter_dimension=0, tiled=True),
-    )
-    block_sum = lax.all_gather(block_part.astype(jnp.bfloat16), "strip", axis=0, tiled=True).astype(
-        block_part.dtype
-    )
+    pieces = [piece.astype(jnp.bfloat16).reshape(-1, WIDE) for piece in pieces]
+    panel_grads = jnp.concatenate(grad_first + grad_second)
+    flat_sum, block_sum, loss_sum = reduce_grads(pieces, panel_grads, loss_part, weights.shape[0])
+    loss = loss_sum * factor
     new_first = BETA_FIRST * first_moment + (1.0 - BETA_FIRST) * flat_sum
     new_second = BETA_SECOND * second_moment + (1.0 - BETA_SECOND) * flat_sum * flat_sum
     fix_first = 1.0 - BETA_FIRST**ADAM_STEP

time: 2800 us -> 1420 us (0.51)
  waiting for transfers between devices: 1010 us -> 4.22 us
  other arithmetic: 698 us -> 228 us
  Pallas kernels: 0 us -> 371 us
  local copies, waits for them, and re-layouts: 588 us -> 273 us
  matrix products: 430 us -> 494 us
  blocking collectives: 41.5 us -> 2.93 us
    unnamed x10 -> x4, waiting for transfers between devices: 645 us -> 3.2 us
    all_gather x1 -> x0, other arithmetic: 451 us -> none  [shards(): lax.all_gather(weights.astype(jnp.bfloat16), ('dp', 'strip'), axis=0, til...]
    pallas_call x0 -> x2, Pallas kernels: none -> 371 us  [the longest x1 197 us: scatter_sum(): pl.pallas_call(functools.partial(scatter_kernel, layouts, shared, stagger...]
    all_gather x3 -> x0, waiting for transfers between devices: 251 us -> none  [the longest x1 243 us: shards(): lax.all_gather(weights.astype(jnp.bfloat16), ('dp', 'strip'), axis=0, til...]
    reduce_scatter x1 -> x0, waiting for transfers between devices: 110 us -> none  [shards(): lax.psum_scatter(blocked_gradient, ('dp', 'strip'), scatter_dimension=0,...]
    unnamed x249 -> x271, local copies, waits for them, and re-layouts: 156 us -> 53 us
    concatenate x1 -> x2, local copies, waits for them, and re-layouts: 54.1 us -> 0.73 us  [the longest x1 0.64 us: reduce_grads(): jnp.concatenate(pieces)]
    slice x19 -> x13, local copies, waits for them, and re-layouts: 65.1 us -> 25.2 us  [the longest x5 17 us: shards(): params = {name: rows[low:high] for name, (low, high) in ROWS.items()}]
  transfers between devices with their start and end apart: 12 -> 9, of which waited for: 5 -> 2; matrix products, arithmetic and copies ran while one was open for 38% -> 8% of each run, Pallas kernels for 0% -> 0%
where the time goes in v1:
time: 1420 us; the launch traced here: 1410 us
  matrix products  494 us (35%)
  Pallas kernels  371 us (26%)
  local copies, waits for them, and re-layouts  273 us (19%)
  other arithmetic  228 us (16%)
  between operations  19.1 us (1%)
    pallas_call x1, Pallas kernels, scatter_sum(): pl.pallas_call(functools.partial(scatter_kernel, layouts, shared, stagger...  197 us
    pallas_call x1, Pallas kernels, gather_all(): pl.pallas_call(functools.partial(gather_kernel, layouts, stagger), out_sh...  173 us
    dot_general x16, matrix products, one_group(): jnp.einsum('qhd,khd->hqk', query_part, key_part, preferred_element_type=j...  96.8 us
    dot_general x15, matrix products, product_back(): lax.dot_general(left, right, (((left.ndim - 1,), (1,)), ((), ())), prefer...  73.6 us
    scatter-add x3, other arithmetic, shards(): jax.ops.segment_sum(grad_point, cells_read[plane], num_segments=cells.sha...  68.7 us
    dot_general x16, matrix products, weight_grad(): lax.dot_general(left, right, (((0,), (0,)), ((), ())), preferred_element_...  63.6 us
    convert_element_type x8, other arithmetic, one_group(): grad_scores = (shares * (grad_shares - jnp.sum(grad_shares * shares, -1,...  60.7 us
    dot_general x8, matrix products, one_group(): jnp.einsum('qhd,khd->hqk', grad_part, value_part, preferred_element_type=...  57.7 us
  transfers between devices with their start and end apart: 9, of which 2 were waited for; matrix products, arithmetic and copies ran while one was open for 8% of the time, Pallas kernels for 0%

profile of v1, /device:TPU:1, one launch (start us, length us, event | category | flops | bytes accessed | tf_op | source)
XLA Modules:
  0.0 1407.6 jit_solution(16465120010464371886)
XLA Ops:
  22.6 173.3 %gather_all.1 = (bf16[10752,1024]{1,0:T(8,128)(2,1)}, bf16[8192,1024]{1,0:T(8,128)(2,1)}, f32[256,128]{1,0:T(8,128)}) custom-call(bf16[336,1024]{1,0:T(8,128)(2,1)} %reshape.573.refs_0_, bf16[256,1024]{1,0:T(8,128)(2,1)} %bitcast.503, f32[8,128]{1,0:T(8,128)} %broadcast_in_dim.118.refs_2_), custom_call_target="tpu_custom_call" | custom-call | tf_op jit(solution)/shard_map/gather_all/pallas_call | solution.py:302
  237.9 20.9 %while.54 = (s32[]{:T(128)}, bf16[4,768,4,64]{1,3,2,0:T(8,128)(2,1)}, f32[4,4,768]{2,1,0:T(4,128)S(1)}, bf16[4,257,4,64]{1,3,2,0:T(8,128)(2,1)}, bf16[4,768,4,64...) while((s32[]{:T(128)}, bf16[4,768,4,64]{1,3,2,0:T(8,128)(2,1)}, ...), condition=%wide.region_6.7_spmd, body=%wide.region_3.6_spmd.sunk | while | flops 208425984 | bytes 23816328 | solution.py:124
  340.2 116.7 %while.55 = (s32[]{:T(128)}, bf16[4,768,4,64]{1,3,2,0:T(8,128)(2,1)}, f32[4,4,768]{2,1,0:T(4,128)S(1)}, bf16[4,1536,4,64]{1,3,2,0:T(8,128)(2,1)}, bf16[4,768,4,6...) while((s32[]{:T(128)}, bf16[4,768,4,64]{1,3,2,0:T(8,128)(2,1)}, ...), condition=%wide.region_12.13_spmd, body=%wide.region_9.12_spmd.sunk | while | flops 1245705216 | bytes 59476048 | solution.py:124
  503.9 15.7 %gather_fusion.2 = bf16[4096,80]{1,0:T(8,128)(2,1)} fusion(bf16[2048,80]{1,0:T(8,128)(2,1)} %bitcast.466, s32[4096]{0:T(1024)S(1)} %copy-done.67), kind=kCustom, calls=%fused_computation.clone | custom fusion | bytes 1327104 | tf_op jit(solution)/shard_map/jit(_take)/gather | solution.py:688
  519.6 15.0 %gather_fusion.3 = bf16[4096,80]{1,0:T(8,128)(2,1)} fusion(bf16[2048,80]{1,0:T(8,128)(2,1)S(1)} %bitcast.465, s32[4096]{0:T(1024)S(1)} %copy-done.66), kind=kCustom, calls=%fused_computation.1.clone | custom fusion | bytes 1327104 | tf_op jit(solution)/shard_map/jit(_take)/gather | solution.py:689
  534.6 15.0 %gather_fusion.4 = bf16[4096,80]{1,0:T(8,128)(2,1)} fusion(bf16[2048,80]{1,0:T(8,128)(2,1)S(1)} %bitcast.464, s32[4096]{0:T(1024)S(1)} %copy-done.65), kind=kCustom, calls=%fused_computation.2.clone | custom fusion | bytes 1327104 | tf_op jit(solution)/shard_map/jit(_take)/gather | solution.py:690
  562.5 22.9 %scatter_custom_fusion = f32[2048,80]{1,0:T(8,128)S(1)} fusion(s32[4096]{0:T(1024)} %bitcast.531, f32[4096,80]{1,0:T(8,128)} %fusion.308, f32[]{:T(128)} %constant.277.clone.1), kind=kCustom, calls=%fused_computation.348 | custom fusion | flops 327680 | bytes 655872 | tf_op jit(solution)/shard_map/scatter-add | solution.py:713
  586.2 22.9 %scatter_custom_fusion.1 = f32[2048,80]{1,0:T(8,128)S(1)} fusion(s32[4096]{0:T(1024)} %bitcast.528, f32[4096,80]{1,0:T(8,128)} %fusion.308, f32[]{:T(128)} %constant.277.clone.1), kind=kCustom, calls=%fused_computation.346 | custom fusion | flops 327680 | bytes 655872 | tf_op jit(solution)/shard_map/scatter-add | solution.py:713
  610.0 22.9 %scatter_custom_fusion.2 = f32[2048,80]{1,0:T(8,128)S(1)} fusion(s32[4096]{0:T(1024)} %bitcast.525, f32[4096,80]{1,0:T(8,128)} %fusion.308, f32[]{:T(128)} %constant.277.clone.1), kind=kCustom, calls=%fused_computation.344 | custom fusion | flops 327680 | bytes 655872 | tf_op jit(solution)/shard_map/scatter-add | solution.py:713
  737.7 230.2 %while.56 = (s32[]{:T(128)}, bf16[4,768,4,64]{1,3,2,0:T(8,128)(2,1)}, bf16[4,1536,4,64]{1,3,2,0:T(8,128)(2,1)}, bf16[4,1536,4,64]{1,3,2,0:T(8,128)(2,1)}, bf16[4...) while((s32[]{:T(128)}, ...), condition=%wide.region_28.30_spmd, body=%wide.region_26.29_spmd.sunk | while | flops 3077108736 | bytes 250176832 | solution.py:158
  748.8 12.7 multiply_reduce_fusion.21
  761.5 14.4 %multiply_convert_fusion.17 = bf16[4,768,1536]{2,1,0:T(8,128)(2,1)S(1)} fusion(f32[4,768,1536]{2,1,0:T(8,128)} %get-tuple-element.606, f32[4,768,1536]{2,1,0:T(8,128)} %fusion.409, f32[4,768]{1,0:T(4,128)S(1)} %get-tuple-element.607, f32[4,768]{1,0:T(4,128)S(1)} %dynamic-slice_bitcast_fusion.4), kind=kLoop, calls=%fused_computation.46.clone.1 | loop fusion | flops 23592960 | bytes 47210496 | tf_op jit(solution)/shard_map/while/body/eval_jaxpr/convert_element_type | solution.py:143
  806.3 12.7 multiply_reduce_fusion.21
  819.0 14.4 %multiply_convert_fusion.17 = bf16[4,768,1536]{2,1,0:T(8,128)(2,1)S(1)} fusion(f32[4,768,1536]{2,1,0:T(8,128)} %get-tuple-element.606, f32[4,768,1536]{2,1,0:T(8,128)} %fusion.409, f32[4,768]{1,0:T(4,128)S(1)} %get-tuple-element.607, f32[4,768]{1,0:T(4,128)S(1)} %dynamic-slice_bitcast_fusion.4), kind=kLoop, calls=%fused_computation.46.clone.1 | loop fusion | flops 23592960 | bytes 47210496 | tf_op jit(solution)/shard_map/while/body/eval_jaxpr/convert_element_type | solution.py:143
  852.8 10.4 fusion.409
  863.9 12.7 multiply_reduce_fusion.21
  876.6 14.4 %multiply_convert_fusion.17 = bf16[4,768,1536]{2,1,0:T(8,128)(2,1)S(1)} fusion(f32[4,768,1536]{2,1,0:T(8,128)} %get-tuple-element.606, f32[4,768,1536]{2,1,0:T(8,128)} %fusion.409, f32[4,768]{1,0:T(4,128)S(1)} %get-tuple-element.607, f32[4,768]{1,0:T(4,128)S(1)} %dynamic-slice_bitcast_fusion.4), kind=kLoop, calls=%fused_computation.46.clone.1 | loop fusion | flops 23592960 | bytes 47210496 | tf_op jit(solution)/shard_map/while/body/eval_jaxpr/convert_element_type | solution.py:143
  910.3 10.4 fusion.409
  921.4 12.7 multiply_reduce_fusion.21
  934.1 14.4 %multiply_convert_fusion.17 = bf16[4,768,1536]{2,1,0:T(8,128)(2,1)S(1)} fusion(f32[4,768,1536]{2,1,0:T(8,128)} %get-tuple-element.606, f32[4,768,1536]{2,1,0:T(8,128)} %fusion.409, f32[4,768]{1,0:T(4,128)S(1)} %get-tuple-element.607, f32[4,768]{1,0:T(4,128)S(1)} %dynamic-slice_bitcast_fusion.4), kind=kLoop, calls=%fused_computation.46.clone.1 | loop fusion | flops 23592960 | bytes 47210496 | tf_op jit(solution)/shard_map/while/body/eval_jaxpr/convert_element_type | solution.py:143
  1026.5 10.4 multiply_reduce_fusion.5
  1049.4 42.1 %while.57 = (s32[]{:T(128)}, bf16[4,768,4,64]{1,3,2,0:T(8,128)(2,1)}, bf16[4,257,4,64]{1,3,2,0:T(8,128)(2,1)}, bf16[4,257,4,64]{1,3,2,0:T(8,128)(2,1)}, bf16[4,2...) while((s32[]{:T(128)}, ...), condition=%wide.region_34.36_spmd, body=%wide.region_32.35_spmd.sunk | while | flops 515015936 | bytes 50855156 | solution.py:158
  1111.3 10.8 reshape.599
  1169.0 197.4 %scatter_sum.1 = (f32[336,1024]{1,0:T(8,128)}, bf16[512,1024]{1,0:T(8,128)(2,1)}, f32[8,128]{1,0:T(8,128)}) custom-call(bf16[10752,1024]{1,0:T(8,128)(2,1)} %broadcast_dynamic-update-slice_fusion.refs_0_, bf16[8192,1024]{1,0:T(8,128)(2,1)} %convert_dynamic-update-slice_fusion.refs_1_, f32[256,128]{1,0:T(8,128)} %broadcast_in_dim.133.refs_2_), custom_call_target="tpu_custom_call" | custom-call | tf_op jit(solution)/shard_map/scatter_sum/pallas_call | solution.py:481
  (688 shorter events, 751.6 us)
Async XLA Ops:
  7.2 1363.2 %copy-start = (f32[32,128,128]{2,1,0:T(8,128)S(1)}, f32[32,128,128]{2,1,0:T(8,128)}, u32[]{:S(2)}) copy-start(f32[32,128,128]{2,1,0:T(8,128)} %param.32) | copy-start | bytes 6291460
  7.2 316.0 %all-gather.2.cloned.1.call-start = ((), (), s32[]{:S(2)}) async-start(), calls=%async_computation.2 | async-start | bytes 9437184 | tf_op jit(solution)/shard_map/all_gather | solution.py:668
  8.8 8.1 collective-permute-start
  214.6 61.6 %copy-start.82 = (f32[1,1024]{1,0:T(1,128)}, f32[1,1024]{1,0:T(1,128)S(1)}, u32[]{:S(2)}) copy-start(f32[1,1024]{1,0:T(1,128)S(1)} %get-tuple-element.384) | copy-start | bytes 12292
  214.7 61.6 %copy-start.97 = (f32[1,1024]{1,0:T(1,128)}, f32[1,1024]{1,0:T(1,128)S(1)}, u32[]{:S(2)}) copy-start(f32[1,1024]{1,0:T(1,128)S(1)} %get-tuple-element.383) | copy-start | bytes 12292
  288.8 361.0 %reduce-scatter.7.cloned.1.call-start = ((), (), s32[]{:S(2)}) async-start(), calls=%async_computation.4 | async-start | bytes 1474560
  487.6 4.4 collective-permute-start.1
  488.9 4.1 collective-permute-start.2
  640.5 386.0 %reduce-scatter.5.cloned.1.call-start = ((), (), s32[]{:S(2)}) async-start(), calls=%async_computation.3 | async-start | bytes 9437184 | tf_op jit(solution)/shard_map/reduce_scatter | solution.py:750
  677.4 6.7 collective-permute-start.3
  678.7 5.4 collective-permute-start.4
  761.4 29.3 %slice-start = ((s8[18874368]{0:T(1024)(128)(4,1)}), s8[4194304]{0:T(1024)(128)(4,1)S(1)}, s32[]{:S(2)}) async-start(s8[18874368]{0:T(1024)(128)(4,1)} %bitcast.462), calls=%async_computation.5 | async-start | bytes 8388608 | tf_op jit(solution)/shard_map/while
  761.4 29.3 %slice-start.1 = ((s8[18874368]{0:T(1024)(128)(4,1)}), s8[4194304]{0:T(1024)(128)(4,1)S(1)}, s32[]{:S(2)}) async-start(s8[18874368]{0:T(1024)(128)(4,1)} %bitcast.462), calls=%async_computation.6 | async-start | bytes 8388608 | tf_op jit(solution)/shard_map/while
  761.5 29.3 %slice-start.2 = ((s8[18874368]{0:T(1024)(128)(4,1)}), s8[4194304]{0:T(1024)(128)(4,1)S(1)}, s32[]{:S(2)}) async-start(s8[18874368]{0:T(1024)(128)(4,1)} %bitcast.462), calls=%async_computation.7 | async-start | bytes 8388608 | tf_op jit(solution)/shard_map/while
  761.5 29.3 %slice-start.3 = ((s8[18874368]{0:T(1024)(128)(4,1)}), s8[4194304]{0:T(1024)(128)(4,1)S(1)}, s32[]{:S(2)}) async-start(s8[18874368]{0:T(1024)(128)(4,1)} %bitcast.462), calls=%async_computation.8 | async-start | bytes 8388608 | tf_op jit(solution)/shard_map/while
  819.0 29.3 %slice-start = ((s8[18874368]{0:T(1024)(128)(4,1)}), s8[4194304]{0:T(1024)(128)(4,1)S(1)}, s32[]{:S(2)}) async-start(s8[18874368]{0:T(1024)(128)(4,1)} %bitcast.462), calls=%async_computation.5 | async-start | bytes 8388608 | tf_op jit(solution)/shard_map/while
  819.0 29.3 %slice-start.1 = ((s8[18874368]{0:T(1024)(128)(4,1)}), s8[4194304]{0:T(1024)(128)(4,1)S(1)}, s32[]{:S(2)}) async-start(s8[18874368]{0:T(1024)(128)(4,1)} %bitcast.462), calls=%async_computation.6 | async-start | bytes 8388608 | tf_op jit(solution)/shard_map/while
  819.0 29.3 %slice-start.2 = ((s8[18874368]{0:T(1024)(128)(4,1)}), s8[4194304]{0:T(1024)(128)(4,1)S(1)}, s32[]{:S(2)}) async-start(s8[18874368]{0:T(1024)(128)(4,1)} %bitcast.462), calls=%async_computation.7 | async-start | bytes 8388608 | tf_op jit(solution)/shard_map/while
  819.0 29.3 %slice-start.3 = ((s8[18874368]{0:T(1024)(128)(4,1)}), s8[4194304]{0:T(1024)(128)(4,1)S(1)}, s32[]{:S(2)}) async-start(s8[18874368]{0:T(1024)(128)(4,1)} %bitcast.462), calls=%async_computation.8 | async-start | bytes 8388608 | tf_op jit(solution)/shard_map/while
  934.1 29.3 %slice-start = ((s8[18874368]{0:T(1024)(128)(4,1)}), s8[4194304]{0:T(1024)(128)(4,1)S(1)}, s32[]{:S(2)}) async-start(s8[18874368]{0:T(1024)(128)(4,1)} %bitcast.462), calls=%async_computation.5 | async-start | bytes 8388608 | tf_op jit(solution)/shard_map/while
  934.1 29.3 %slice-start.1 = ((s8[18874368]{0:T(1024)(128)(4,1)}), s8[4194304]{0:T(1024)(128)(4,1)S(1)}, s32[]{:S(2)}) async-start(s8[18874368]{0:T(1024)(128)(4,1)} %bitcast.462), calls=%async_computation.6 | async-start | bytes 8388608 | tf_op jit(solution)/shard_map/while
  934.1 29.3 %slice-start.2 = ((s8[18874368]{0:T(1024)(128)(4,1)}), s8[4194304]{0:T(1024)(128)(4,1)S(1)}, s32[]{:S(2)}) async-start(s8[18874368]{0:T(1024)(128)(4,1)} %bitcast.462), calls=%async_computation.7 | async-start | bytes 8388608 | tf_op jit(solution)/shard_map/while
  1049.4 42.1 %copy-start.64 = (f32[768]{0:T(1024)S(1)}, f32[768]{0:T(1024)}, u32[]{:S(2)}) copy-start(f32[768]{0:T(1024)} %copy-done.63) | copy-start | bytes 9220
  1380.8 13.4 collective-permute-start.5
  (165 other events, 1055.7 us)
Sparse Core Ops, SparseCore 0:
  288.9 17.4 all-gather.1
  640.6 9.1 reduce-scatter.6
  973.8 15.6 reduce-scatter.4

commit v2 on v1

--- a/solution.py
+++ b/solution.py
@@ -87,85 +87,294 @@
     return jnp.stack([left_cols, right_cols], 4).reshape(planes, 2 * inner, 2 * cols, -1)
 
 
-def render_loss(output, mask, wanted):
-    sigma = jax.nn.softplus(output[..., 0])
-    colour = jax.nn.sigmoid(output[..., 1:])
-    absorb = 4.0 / S * sigma
-    before = jnp.cumsum(absorb, 0) - absorb
-    weight = jnp.exp(-before) * (1.0 - jnp.exp(-absorb))
-    colour_sum = jnp.sum(weight[..., None] * colour, 0)
-    error = colour_sum.T - wanted
-    return jnp.sum(mask * jnp.sum(error * error, 0))
-
-
-def split_heads(matrix):
-    return matrix.reshape(matrix.shape[0], -1, group_heads, HEAD_DIM).transpose(1, 0, 2, 3)
-
-
-def merge_heads(groups):
-    return groups.transpose(1, 0, 2, 3).reshape(groups.shape[1], -1)
-
-
-def attend_fwd(query, keys, values):
-
-    def one_group(operands):
-        query_part, key_part, value_part = operands
-        scores = jnp.einsum(
-            "qhd,khd->hqk", query_part, key_part, preferred_element_type=jnp.float32
-        ) * HEAD_DIM ** (-0.5)
-        top = jnp.max(scores, -1, keepdims=True)
-        log_total = top + jnp.log(jnp.sum(jnp.exp(scores - top), -1, keepdims=True))
-        shares = jnp.exp(scores - log_total).astype(jnp.bfloat16)
-        final_output = jnp.einsum(
-            "hqk,khd->qhd", shares, value_part, preferred_element_type=jnp.float32
-        )
-        return (final_output, log_total[..., 0])
-
-    final_output, log_total = lax.map(
-        one_group, (split_heads(query), split_heads(keys), split_heads(values))
-    )
-    return (merge_heads(final_output), log_total)
-
-
-def attend_bwd(query, keys, values, log_total, grad_out):
-
-    def one_group(operands):
-        query_part, key_part, value_part, total_part, grad_part = operands
-        scores = jnp.einsum(
-            "qhd,khd->hqk", query_part, key_part, preferred_element_type=jnp.float32
-        ) * HEAD_DIM ** (-0.5)
-        shares = jnp.exp(scores - total_part[..., None])
-        grad_shares = jnp.einsum(
-            "qhd,khd->hqk", grad_part, value_part, preferred_element_type=jnp.float32
-        )
-        grad_scores = (
-            shares * (grad_shares - jnp.sum(grad_shares * shares, -1, keepdims=True))
-        ).astype(jnp.bfloat16)
-        grad_query = jnp.einsum(
-            "hqk,khd->qhd", grad_scores, key_part, preferred_element_type=jnp.float32
-        ) * HEAD_DIM ** (-0.5)
-        grad_keys = jnp.einsum(
-            "hqk,qhd->khd", grad_scores, query_part, preferred_element_type=jnp.float32
-        ) * HEAD_DIM ** (-0.5)
-        grad_values = jnp.einsum(
-            "hqk,qhd->khd",
-            shares.astype(jnp.bfloat16),
-            grad_part,
-            preferred_element_type=jnp.float32,
-        )
-        return (grad_query, grad_keys, grad_values)
-
-    grads = lax.map(
-        one_group,
-        (
-            split_heads(query),
-            split_heads(keys),
-            split_heads(values),
-            log_total,
-            split_heads(grad_out),
+PAIR = 2 * HEAD_DIM
+LOG2E = math.log2(math.e)
+EXP_SCALE = HEAD_DIM ** (-0.5) * LOG2E
+
+
+def nt_dot(left, right):
+    return lax.dot_general(left, right, (((1,), (1,)), ((), ())), preferred_element_type=jnp.float32)
+
+
+def head_lanes(shape, head):
+    return lax.broadcasted_iota(jnp.int32, shape, len(shape) - 1) // HEAD_DIM == head
+
+
+def attend_fwd_kernel(real_keys, q_ref, k_ref, v_ref, o_ref, lse_ref):
+    query, keys = q_ref[...], k_ref[...]
+    values = v_ref[...].T
+    outs = []
+    for head in range(2):
+        own = jnp.where(head_lanes(query.shape, head), query, 0)
+        scores = nt_dot(keys, own)
+        if real_keys < keys.shape[0]:
+            at = lax.broadcasted_iota(jnp.int32, scores.shape, 0)
+            scores = jnp.where(at < real_keys, scores, -3e38)
+        top = jnp.max(scores, 0, keepdims=True)
+        raised = jnp.exp2((scores - top) * EXP_SCALE)
+        total = jnp.sum(raised, 0, keepdims=True)
+        shares = (raised * (1.0 / total)).astype(jnp.bfloat16)
+        outs.append(product(values[head * HEAD_DIM : (head + 1) * HEAD_DIM], shares))
+        lse_ref[0, head : head + 1] = top * EXP_SCALE + jnp.log2(total)
+    o_ref[...] = jnp.concatenate(outs, 0).T.astype(jnp.bfloat16)
+
+
+def attend_fwd(query, keys, values, key_col, value_col, real_keys, rows):
+    count, total_keys = query.shape[0], keys.shape[0]
+    pairs = D // PAIR
+    return pl.pallas_call(
+        functools.partial(attend_fwd_kernel, real_keys),
+        grid=(pairs, count // rows),
+        in_specs=[
+            pl.BlockSpec((rows, PAIR), lambda j, n: (n, j)),
+            pl.BlockSpec((total_keys, PAIR), lambda j, n: (0, key_col + j)),
+            pl.BlockSpec((total_keys, PAIR), lambda j, n: (0, value_col + j)),
+        ],
+        out_specs=[
+            pl.BlockSpec((rows, PAIR), lambda j, n: (n, j)),
+            pl.BlockSpec((1, 8, rows), lambda j, n: (j, 0, n)),
+        ],
+        out_shape=[
+            jax.ShapeDtypeStruct((count, D), jnp.bfloat16),
+            jax.ShapeDtypeStruct((pairs, 8, count), jnp.float32),
+        ],
+        compiler_params=pltpu.CompilerParams(vmem_limit_bytes=48 * 1024 * 1024),
+        cost_estimate=pl.CostEstimate(
+            flops=4 * count * total_keys * D, transcendentals=count * total_keys * 16, bytes_accessed=4 * D * (count + total_keys)
         ),
-    )
-    return (merge_heads(grads[0]), merge_heads(grads[1]), merge_heads(grads[2]))
+        name="attend_fwd",
+    )(query, keys, values)
+
+
+def attend_bwd_kernel(real_keys, chunk, q_ref, k_ref, v_ref, lse_ref, o_ref, g_ref, dq_ref, dk_ref, dv_ref, kt_ref, dk_sum, dv_sum):
+    step = pl.program_id(1)
+
+    @pl.when(step == 0)
+    def _():
+        kt_ref[...] = k_ref[...].T
+        dk_sum[...] = jnp.zeros_like(dk_sum)
+        dv_sum[...] = jnp.zeros_like(dv_sum)
+
+    query, grad = q_ref[...], g_ref[...]
+    mixed = (grad.astype(jnp.float32) * o_ref[...].astype(jnp.float32)).T
+    total_keys = k_ref.shape[0]
+    queries = [jnp.where(head_lanes(query.shape, head), query, 0) for head in range(2)]
+    grads = [jnp.where(head_lanes(grad.shape, head), grad, 0) for head in range(2)]
+    inner = [jnp.sum(mixed[head * HEAD_DIM : (head + 1) * HEAD_DIM], 0, keepdims=True) for head in range(2)]
+    grad_query = [jnp.zeros((HEAD_DIM, query.shape[0]), jnp.float32) for head in range(2)]
+    for at in range(0, total_keys, chunk):
+        part = pl.ds(at, chunk)
+        keys, values = k_ref[part], v_ref[part]
+        for head in range(2):
+            scores = nt_dot(keys, queries[head])
+            shares = jnp.exp2(scores * EXP_SCALE - lse_ref[0, head : head + 1])
+            if at + chunk > real_keys:
+                row = at + lax.broadcasted_iota(jnp.int32, shares.shape, 0)
+                shares = jnp.where(row < real_keys, shares, 0.0)
+            grad_shares = nt_dot(values, grads[head])
+            grad_scores = (shares * (grad_shares - inner[head])).astype(jnp.bfloat16)
+            dv_sum[part] += product(shares.astype(jnp.bfloat16), grads[head])
+            dk_sum[part] += product(grad_scores, queries[head])
+            grad_query[head] += product(
+                kt_ref[head * HEAD_DIM : (head + 1) * HEAD_DIM, part], grad_scores
+            )
+    scale = HEAD_DIM ** (-0.5)
+    dq_ref[...] = (jnp.concatenate(grad_query, 0) * scale).T.astype(jnp.bfloat16)
+
+    @pl.when(step == pl.num_programs(1) - 1)
+    def _():
+        dk_ref[...] = (dk_sum[...] * scale).astype(jnp.bfloat16)
+        dv_ref[...] = dv_sum[...].astype(jnp.bfloat16)
+
+
+def attend_bwd(query, keys, values, key_col, value_col, real_keys, rows, chunk, totals, out, grad):
+    count, total_keys = query.shape[0], keys.shape[0]
+    pairs = D // PAIR
+    by_query = pl.BlockSpec((rows, PAIR), lambda j, n: (n, j))
+    by_key = pl.BlockSpec((total_keys, PAIR), lambda j, n: (0, j))
+    return pl.pallas_call(
+        functools.partial(attend_bwd_kernel, real_keys, chunk),
+        grid=(pairs, count // rows),
+        in_specs=[
+            by_query,
+            pl.BlockSpec((total_keys, PAIR), lambda j, n: (0, key_col + j)),
+            pl.BlockSpec((total_keys, PAIR), lambda j, n: (0, value_col + j)),
+            pl.BlockSpec((1, 8, rows), lambda j, n: (j, 0, n)),
+            by_query,
+            by_query,
+        ],
+        out_specs=[by_query, by_key, by_key],
+        out_shape=[
+            jax.ShapeDtypeStruct((count, D), jnp.bfloat16),
+            jax.ShapeDtypeStruct((total_keys, D), jnp.bfloat16),
+            jax.ShapeDtypeStruct((total_keys, D), jnp.bfloat16),
+        ],
+        scratch_shapes=[
+            pltpu.VMEM((PAIR, total_keys), jnp.bfloat16),
+            pltpu.VMEM((total_keys, PAIR), jnp.float32),
+            pltpu.VMEM((total_keys, PAIR), jnp.float32),
+        ],
+        compiler_params=pltpu.CompilerParams(vmem_limit_bytes=48 * 1024 * 1024),
+        cost_estimate=pl.CostEstimate(
+            flops=10 * count * total_keys * D, transcendentals=count * total_keys * 16, bytes_accessed=8 * D * (count + total_keys)
+        ),
+        name="attend_bwd",
+    )(query, keys, values, totals, out, grad)
+
+
+GROUPS = 3
+
+
+def render_kernel(samples_ref, cells_ref, wanted_ref, mask_ref, factor_ref, win_ref, wout_ref,
+                  loss_ref, grad_ref, gin_ref, gout_ref,
+                  table, inner_all, hidden_all, point_all, out_all, gout_all, sums):
+    block = pl.program_id(0)
+    cells = cells_ref.shape[1]
+    group = table.shape[2]
+    rays = samples_ref.shape[2]
+    planes = cells_ref.shape[0]
+
+    @pl.when(block == 0)
+    def _():
+        loss_ref[...] = jnp.zeros_like(loss_ref)
+        gin_ref[...] = jnp.zeros_like(gin_ref)
+        gout_ref[...] = jnp.zeros_like(gout_ref)
+        sums[...] = jnp.zeros_like(sums)
+        table[...] = jnp.zeros_like(table)
+        for plane in range(planes):
+            turned = cells_ref[plane].T
+            for g in range(GROUPS):
+                width = min(group, cells - g * group)
+                table[plane, g * CH : (g + 1) * CH, :width] = turned[:CH, g * group : g * group + width]
+
+    step = 4
+    width = step * rays
+    win, wout = win_ref[...], wout_ref[...]
+
+    def places_read(plane, s):
+        rows = [samples_ref[plane, s + n : s + n + 1, :] for n in range(step)]
+        at = jnp.concatenate(rows, 1)
+        owner = at // group
+        within = at - owner * group
+        hot = lax.broadcasted_iota(jnp.int32, (group, width), 0) == within
+        return owner, jnp.where(hot, 1.0, 0.0).astype(jnp.bfloat16)
+
+    def tn_dot(left, right):
+        return lax.dot_general(left, right, (((0,), (0,)), ((), ())), preferred_element_type=jnp.float32)
+
+    for s in range(0, S, step):
+        here = pl.ds(s * rays, width)
+        point = jnp.zeros((CH, width), jnp.float32)
+        for plane in range(planes):
+            owner, hot = places_read(plane, s)
+            found = product(table[plane], hot)
+            value = found[:CH]
+            for g in range(1, GROUPS):
+                value = jnp.where(owner == g, found[g * CH : (g + 1) * CH], value)
+            point = point + value
+        point = point.astype(jnp.bfloat16)
+        inner = tn_dot(win, point)
+        hidden = (inner * jax.nn.sigmoid(inner)).astype(jnp.bfloat16)
+        out_all[:, here] = tn_dot(wout, hidden)
+        inner_all[:, here] = inner
+        hidden_all[:, here] = hidden
+        point_all[:, here] = point
+
+    factor = factor_ref[0]
+    mask = mask_ref[...]
+    row = lax.broadcasted_iota(jnp.int32, (8, rays), 0)
+    is_colour = (row >= 1) & (row <= 3)
+    before = jnp.zeros((1, rays), jnp.float32)
+    rgb = jnp.zeros((8, rays), jnp.float32)
+    kept = []
+    for s in range(S):
+        out = out_all[:, s * rays : (s + 1) * rays]
+        level = out[0:1]
+        absorb = (4.0 / S) * (jnp.maximum(level, 0.0) + jnp.log1p(jnp.exp(-jnp.abs(level))))
+        weight = jnp.exp(-before) * (1.0 - jnp.exp(-absorb))
+        before = before + absorb
+        colour = jax.nn.sigmoid(out)
+        rgb = rgb + weight * colour
+        kept.append((weight, jnp.exp(-before), colour))
+    error = jnp.where(is_colour, rgb - wanted_ref[...], 0.0)
+    loss_ref[...] += jnp.sum(mask * jnp.sum(error * error, 0, keepdims=True))
+    pull = error * (2.0 * factor * mask)
+    tail = jnp.zeros((1, rays), jnp.float32)
+    for s in reversed(range(S)):
+        weight, left_over, colour = kept[s]
+        to_weight = jnp.sum(pull * colour, 0, keepdims=True)
+        to_absorb = to_weight * left_over - tail
+        tail = tail + to_weight * weight
+        to_level = (4.0 / S) * to_absorb * colour[0:1]
+        to_colour = weight * pull * colour * (1.0 - colour)
+        gout_all[:, s * rays : (s + 1) * rays] = jnp.where(row == 0, to_level, to_colour).astype(jnp.bfloat16)
+
+    for s in range(0, S, step):
+        here = pl.ds(s * rays, width)
+        pulled = gout_all[:, here]
+        inner = inner_all[:, here]
+        gate = jax.nn.sigmoid(inner)
+        grad_inner = product(wout, pulled) * (gate * (1.0 + inner * (1.0 - gate)))
+        grad_inner = grad_inner.astype(jnp.bfloat16)
+        gout_ref[...] += nt_dot(hidden_all[:, here], pulled)
+        gin_ref[...] += nt_dot(point_all[:, here], grad_inner)
+        grad_point = product(win, grad_inner)
+        coarse = grad_point.astype(jnp.bfloat16).astype(jnp.float32)
+        fine = grad_point - coarse
+        for plane in range(planes):
+            owner, hot = places_read(plane, s)
+            rows = [jnp.where(owner == g, coarse, 0.0) for g in range(GROUPS)]
+            rows += [jnp.where(owner == g, fine, 0.0) for g in range(GROUPS)]
+            stacked = jnp.concatenate(rows, 0).astype(jnp.bfloat16)
+            added = nt_dot(stacked, hot)
+            sums[plane] += added[: GROUPS * CH] + added[GROUPS * CH :]
+
+    @pl.when(block == pl.num_programs(0) - 1)
+    def _():
+        for plane in range(planes):
+            for g in range(GROUPS):
+                count = min(group, cells - g * group)
+                part = sums[plane, g * CH : (g + 1) * CH, :count]
+                grad_ref[plane, :, g * group : g * group + count] = part.astype(jnp.bfloat16)
+
+
+def render(cells, samples, wanted, mask, factor, decode_in, decode_out, rays):
+    planes, count, _ = cells.shape
+    all_rays = samples.shape[2]
+    group = -(-count // (GROUPS * 128)) * 128
+    points = S * rays
+    whole = lambda *shape: pl.BlockSpec(shape, lambda n: (0,) * len(shape))
+    return pl.pallas_call(
+        render_kernel,
+        grid=(all_rays // rays,),
+        in_specs=[
+            pl.BlockSpec((planes, S, rays), lambda n: (0, 0, n)),
+            whole(*cells.shape),
+            pl.BlockSpec((8, rays), lambda n: (0, n)),
+            pl.BlockSpec((1, rays), lambda n: (0, n)),
+            pl.BlockSpec(memory_space=pltpu.SMEM),
+            whole(CH, DEC_HID),
+            whole(DEC_HID, 8),
+        ],
+        out_specs=[whole(8, 128), whole(planes, CH, count), whole(CH, DEC_HID), whole(DEC_HID, 8)],
+        out_shape=[
+            jax.ShapeDtypeStruct((8, 128), jnp.float32),
+            jax.ShapeDtypeStruct((planes, CH, count), jnp.bfloat16),
+            jax.ShapeDtypeStruct((CH, DEC_HID), jnp.float32),
+            jax.ShapeDtypeStruct((DEC_HID, 8), jnp.float32),
+        ],
+        scratch_shapes=[
+            pltpu.VMEM((planes, GROUPS * CH, group), jnp.bfloat16),
+            pltpu.VMEM((DEC_HID, points), jnp.float32),
+            pltpu.VMEM((DEC_HID, points), jnp.bfloat16),
+            pltpu.VMEM((CH, points), jnp.bfloat16),
+            pltpu.VMEM((8, points), jnp.float32),
+            pltpu.VMEM((8, points), jnp.bfloat16),
+            pltpu.VMEM((planes, GROUPS * CH, group), jnp.float32),
+        ],
+        compiler_params=pltpu.CompilerParams(vmem_limit_bytes=48 * 1024 * 1024),
+        name="render",
+    )(samples, cells, wanted, mask, factor, decode_in, decode_out)
 
 
 LANE = 1024
@@ -658,16 +867,18 @@
     hidden1, norm_one = jax.vjp(norm_mod, stream0, mods[0], mods[1])
     hidden1 = hidden1.astype(jnp.bfloat16)
     query1 = product(hidden1, params["query_cross"]).astype(jnp.bfloat16)
+    real_keys = picture.shape[0]
+    picture = jnp.pad(picture, ((0, -real_keys % 128), (0, 0)))
     image_kv = product(picture, params["keyval_cross"]).astype(jnp.bfloat16)
-    cross_out, total_one = attend_fwd(query1, image_kv[:, :D], image_kv[:, D:])
-    cross_out = cross_out.astype(jnp.bfloat16)
+    tokens = query1.shape[0]
+    cross_out, total_one = attend_fwd(query1, image_kv, image_kv, 0, D // PAIR, real_keys, tokens)
     stream1 = stream0 + product(cross_out, params["out_cross"])
     hidden2, norm_two = jax.vjp(norm_mod, stream1, mods[2], mods[3])
     hidden2 = hidden2.astype(jnp.bfloat16)
     qkv = product(hidden2, params["qkv_self"]).astype(jnp.bfloat16)
     kv_all = lax.all_gather(qkv[:, D:], "strip", axis=0, tiled=True)
-    self_out, total_two = attend_fwd(qkv[:, :D], kv_all[:, :D], kv_all[:, D:])
-    self_out = self_out.astype(jnp.bfloat16)
+    all_keys = kv_all.shape[0]
+    self_out, total_two = attend_fwd(qkv, kv_all, kv_all, 0, D // PAIR, all_keys, tokens)
     stream2 = stream1 + product(self_out, params["out_self"])
     hidden3, norm_three = jax.vjp(norm_mod, stream2, mods[4], mods[5])
     hidden3 = hidden3.astype(jnp.bfloat16)
@@ -684,38 +895,22 @@
     feature, assemble_back = jax.vjp(assemble, ydc)
     whole = lax.all_gather(feature.astype(jnp.bfloat16), "strip", axis=1, tiled=True)
     cells = whole.reshape(3, -1, CH)
-    point = (
-        jnp.take(cells[0], cells_read[0], axis=0).astype(jnp.float32)
-        + jnp.take(cells[1], cells_read[1], axis=0).astype(jnp.float32)
-        + jnp.take(cells[2], cells_read[2], axis=0).astype(jnp.float32)
-    )
-    point = point.astype(jnp.bfloat16)
-    inner_value = product(point, decode_in)
-    hidden, silu_back = jax.vjp(jax.nn.silu, inner_value)
-    hidden = hidden.astype(jnp.bfloat16)
-    output = product(hidden, decode_out)
     rays = pixel.shape[0]
-
-    def local_loss(values):
-        return render_loss(values.reshape(S, rays, 4), mask, wanted)
-
-    loss_part, render_back = jax.vjp(local_loss, output)
     factor = 1.0 / jnp.maximum(count, 1.0)
-    (grad_output,) = render_back(factor)
-    grad_output = grad_output.astype(jnp.bfloat16)
-    grad_decode_out = weight_grad(hidden, grad_output)
-    (grad_inner,) = silu_back(product_back(grad_output, decode_out))
-    grad_inner = grad_inner.astype(jnp.bfloat16)
-    grad_decode_in = weight_grad(point, grad_inner)
-    grad_point = product_back(grad_inner, decode_in)
-    gradient_cell_grid = jnp.stack(
-        [
-            jax.ops.segment_sum(grad_point, cells_read[plane], num_segments=cells.shape[1])
-            for plane in range(3)
-        ]
-    )
+    loss_part, grad_cells, grad_decode_in, grad_decode_out = render(
+        cells,
+        samples[0],
+        jnp.pad(wanted, ((1, 4), (0, 0))),
+        mask[None],
+        factor.reshape(1),
+        decode_in,
+        jnp.pad(decode_out, ((0, 0), (0, 4))),
+        rays,
+    )
+    loss_part = loss_part[0, 0]
+    grad_decode_out = grad_decode_out[:, :4]
     grad_feature = lax.psum_scatter(
-        gradient_cell_grid.reshape(whole.shape).astype(jnp.bfloat16),
+        grad_cells.transpose(0, 2, 1).reshape(whole.shape),
         "strip",
         scatter_dimension=1,
         tiled=True,
@@ -745,15 +940,12 @@
     grad_out_self = weight_grad(self_out, grad_branch)
     grad_self = product_back(grad_branch, params["out_self"]).astype(jnp.bfloat16)
     grad_query2, grad_keys2, grad_values2 = attend_bwd(
-        qkv[:, :D], kv_all[:, :D], kv_all[:, D:], total_two, grad_self
+        qkv, kv_all, kv_all, 0, D // PAIR, all_keys, tokens, 512, total_two, self_out, grad_self
     )
     grad_kv_own = lax.psum_scatter(
-        jnp.concatenate([grad_keys2, grad_values2], 1).astype(jnp.bfloat16),
-        "strip",
-        scatter_dimension=0,
-        tiled=True,
-    ).astype(jnp.float32)
-    grad_qkv = jnp.concatenate([grad_query2, grad_kv_own], 1).astype(jnp.bfloat16)
+        jnp.concatenate([grad_keys2, grad_values2], 1), "strip", scatter_dimension=0, tiled=True
+    )
+    grad_qkv = jnp.concatenate([grad_query2, grad_kv_own], 1)
     grad_qkv_self = weight_grad(hidden2, grad_qkv)
     grad_norm, grad_mod2, grad_mod3 = norm_two(product_back(grad_qkv, params["qkv_self"]))
     grad_stream = grad_stream + grad_norm
@@ -761,10 +953,9 @@
     grad_out_cross = weight_grad(cross_out, grad_branch)
     grad_cross = product_back(grad_branch, params["out_cross"]).astype(jnp.bfloat16)
     grad_query1, grad_keys1, grad_values1 = attend_bwd(
-        query1, image_kv[:, :D], image_kv[:, D:], total_one, grad_cross
-    )
-    grad_query1 = grad_query1.astype(jnp.bfloat16)
-    grad_image_kv = jnp.concatenate([grad_keys1, grad_values1], 1).astype(jnp.bfloat16)
+        query1, image_kv, image_kv, 0, D // PAIR, real_keys, tokens, 128, total_one, cross_out, grad_cross
+    )
+    grad_image_kv = jnp.concatenate([grad_keys1, grad_values1], 1)
     grad_keyval = weight_grad(picture, grad_image_kv)
     grad_query_cross = weight_grad(hidden1, grad_query1)
     grad_norm, grad_mod0, grad_mod1 = norm_one(product_back(grad_query1, params["query_cross"]))

time: 1420 us -> 984 us (0.69)
  matrix products: 494 us -> 196 us
  other arithmetic: 228 us -> 47.4 us
  Pallas kernels: 371 us -> 506 us
  local copies, waits for them, and re-layouts: 273 us -> 168 us
    dot_general x56 -> x0, matrix products: 291 us -> none  [the longest x16 96.8 us: one_group(): jnp.einsum('qhd,khd->hqk', query_part, key_part, preferred_element_type=j...]
    pallas_call x0 -> x5, Pallas kernels: none -> 135 us  [the longest x2 70.4 us: attend_bwd(): pl.pallas_call(functools.partial(attend_bwd_kernel, real_keys, chunk), gr...]
    scatter-add x3 -> x0, other arithmetic: 68.7 us -> none  [shards(): jax.ops.segment_sum(grad_point, cells_read[plane], num_segments=cells.sha...]
    convert_element_type x10 -> x1, other arithmetic: 67 us -> 0.01 us  [shards(): mask = jnp.take(valid[0], pixel).astype(jnp.float32)]
    gather x3 -> x0, local copies, waits for them, and re-layouts: 45.8 us -> none  [the longest x1 15.7 us: shards(): jnp.take(cells[0], cells_read[0], axis=0).astype(jnp.float32)]
    reduce_sum x11 -> x0, other arithmetic: 41.7 us -> none  [the longest x8 40.5 us: one_group(): log_total = top + jnp.log(jnp.sum(jnp.exp(scores - top), -1, keepdims=True))]
    slice x9 -> x2, local copies, waits for them, and re-layouts: 25.7 us -> 0.51 us  [the longest x1 0.51 us: shards(): loss_part = loss_part[0, 0]]
    dot_general x16 -> x14, matrix products: 63.6 us -> 56.3 us  [weight_grad(): lax.dot_general(left, right, (((0,), (0,)), ((), ())), preferred_element_...]
  transfers between devices with their start and end apart: 9 -> 9, of which waited for: 2 -> 3; matrix products, arithmetic and copies ran while one was open for 8% -> 10% of each run, Pallas kernels for 0% -> 0%
where the time goes in v2:
time: 984 us; the launch traced here: 972 us
  Pallas kernels  506 us (51%)
  matrix products  196 us (20%)
  local copies, waits for them, and re-layouts  168 us (17%)
  other arithmetic  47.4 us (5%)
  between operations  18.8 us (2%)
  waiting for transfers between devices  16.4 us (2%)
  starting transfers between devices  15.9 us (2%)
    pallas_call x1, Pallas kernels, scatter_sum(): pl.pallas_call(functools.partial(scatter_kernel, layouts, shared, stagger...  198 us
    pallas_call x1, Pallas kernels, gather_all(): pl.pallas_call(functools.partial(gather_kernel, layouts, stagger), out_sh...  173 us
    pallas_call x2, Pallas kernels, attend_bwd(): pl.pallas_call(functools.partial(attend_bwd_kernel, real_keys, chunk), gr...  70.4 us
    dot_general x13, matrix products, product_back(): lax.dot_general(left, right, (((left.ndim - 1,), (1,)), ((), ())), prefer...  69.2 us
    dot_general x14, matrix products, weight_grad(): lax.dot_general(left, right, (((0,), (0,)), ((), ())), preferred_element_...  56.3 us
    dot_general x13, matrix products, product(): return jnp.dot(left, right, preferred_element_type=jnp.float32)  53.2 us
    unnamed x212, local copies, waits for them, and re-layouts  52.5 us
    pallas_call x2, Pallas kernels, attend_fwd(): pl.pallas_call(functools.partial(attend_fwd_kernel, real_keys), grid=(pai...  45.5 us
  transfers between devices with their start and end apart: 9, of which 3 were waited for; matrix products, arithmetic and copies ran while one was open for 10% of the time, Pallas kernels for 0%

profile of v2, /device:TPU:1, one launch (start us, length us, event | category | flops | bytes accessed | tf_op | source)
XLA Modules:
  0.0 972.1 jit_solution(11746776717280045047)
XLA Ops:
  24.8 172.9 %gather_all.1 = (bf16[10752,1024]{1,0:T(8,128)(2,1)}, bf16[8192,1024]{1,0:T(8,128)(2,1)}, f32[256,128]{1,0:T(8,128)}) custom-call(bf16[336,1024]{1,0:T(8,128)(2,1)} %reshape.401.refs_0_, bf16[256,1024]{1,0:T(8,128)(2,1)} %bitcast.211, f32[8,128]{1,0:T(8,128)} %broadcast_in_dim.63.refs_2_), custom_call_target="tpu_custom_call" | custom-call | tf_op jit(solution)/shard_map/gather_all/pallas_call | solution.py:511
  198.7 6.1 slice.232
  216.7 10.4 %reshape.406 = bf16[1024,3072]{1,0:T(8,128)(2,1)} reshape(bf16[3072,1024]{1,0:T(8,128)(2,1)} %slice.232) | data formatting | bytes 12582912 | tf_op jit(solution)/shard_map/reshape | solution.py:855
  227.1 6.1 reshape.405
  241.0 10.9 %attend_fwd.2 = (bf16[768,1024]{1,0:T(8,128)(2,1)S(1)}, f32[8,8,768]{2,1,0:T(8,128)S(1)}) custom-call(bf16[768,1024]{1,0:T(8,128)(2,1)S(1)} %fusion.100.q_ref, bf16[384,2048]{1,0:T(8,128)(2,1)S(1)} %convolution_convert_fusion.3.k_ref.v_ref, bf16[384,2048]{1,0:T(8,128)(2,1)S(1)} %convolution_convert_fusion.3.k_ref.v_ref), custom_call_target="tpu_custom_call" | custom-call | flops 1207959552 | bytes 4718592 | tf_op jit(solution)/shard_map/attend_fwd/pallas_call | solution.py:125
  272.6 12.0 %all-gather.2.cloned.1.call-done.k_ref.v_ref = bf16[1536,2048]{1,0:T(8,128)(2,1)} async-done(((bf16[768,2048]{1,0:T(8,128)(2,1)}), bf16[1536,2048]{1,0:T(8,128)(2,1)}) %all-gather.2.cloned.1.call-update) | async-done | bytes 6291472 | tf_op jit(solution)/shard_map/all_gather | solution.py:879
  284.6 34.6 %attend_fwd.3 = (bf16[768,1024]{1,0:T(8,128)(2,1)S(1)}, f32[8,8,768]{2,1,0:T(8,128)S(1)}) custom-call(bf16[768,3072]{1,0:T(8,128)(2,1)} %copy-done.39, bf16[1536,2048]{1,0:T(8,128)(2,1)} %all-gather.2.cloned.1.call-done.k_ref.v_ref, bf16[1536,2048]{1,0:T(8,128)(2,1)} %all-gather.2.cloned.1.call-done.k_ref.v_ref), custom_call_target="tpu_custom_call" | custom-call | flops 4831838208 | bytes 9437184 | tf_op jit(solution)/shard_map/attend_fwd/pallas_call | solution.py:125
  372.6 5.7 reshape.408
  382.8 6.6 fusion.41
  395.7 18.7 %render.1 = (f32[8,128]{1,0:T(8,128)S(1)}, bf16[3,80,2048]{2,1,0:T(8,128)(2,1)S(1)}, f32[80,64]{1,0:T(8,128)S(1)}, f32[64,8]{1,0:T(8,128)S(1)}) custom-call(s32[3,16,256]{2,1,0:T(8,128)S(1)} %bitcast.181, bf16[3,2048,80]{2,1,0:T(8,128)(2,1)S(1)} %bitcast.179, f32[8,256]{1,0:T(8,128)S(1)} %pad.54.wanted_ref, f32[1,256]{1,0:T(1,128)S(1)} %fusion.143.mask_ref, ...), custom_call_target="tpu_custom_call" | custom-call | tf_op jit(solution)/shard_map/render/pallas_call | solution.py:347
  423.2 5.7 reshape.454
  446.0 7.2 convert_element_type.184
  482.8 5.8 fusion.6
  510.0 51.7 %attend_bwd.2 = (bf16[768,1024]{1,0:T(8,128)(2,1)S(1)}, bf16[1536,1024]{1,0:T(8,128)(2,1)}, bf16[1536,1024]{1,0:T(8,128)(2,1)}) custom-call(bf16[768,3072]{1,0:T(8,128)(2,1)} %copy-done.39, bf16[1536,2048]{1,0:T(8,128)(2,1)} %all-gather.2.cloned.1.call-done.k_ref.v_ref, bf16[1536,2048]{1,0:T(8,128)(2,1)} %all-gather.2.cloned.1.call-done.k_ref.v_ref, ...), custom_call_target="tpu_custom_call" | custom-call | flops 12079595520 | bytes 18874368 | tf_op jit(solution)/shard_map/attend_bwd/pallas_call | solution.py:195
  563.0 6.5 pad_maximum_fusion
  573.1 6.8 bitcast_convert_fusion
  579.9 6.4 reshape.418
  620.4 10.2 %multiply_reduce_fusion.1 = (bf16[1024]{0:T(1024)(128)(2,1)S(1)}, f32[768]{0:T(1024)S(1)}, bf16[1024]{0:T(1024)(128)(2,1)S(1)}, f32[768,1024]{1,0:T(8,128)S(1)}) fusion(f32[768,1024]{1,0:T(8,128)S(1)} %copy-done.23, f32[768]{0:T(1024)S(1)} %copy-done.70, f32[768]{0:T(1024)S(1)} %copy-done.62, f32[1024]{0:T(1024)S(1)} %bitcast.224, ...), kind=kOutput, calls=%fused_computation.73 | convolution fusion | flops 4838126592 | bytes 17318912 | tf_op jit(solution)/shard_map/dot_general | solution.py:56
  630.6 7.6 convolution_convert_fusion
  640.7 5.8 fusion.103.g_ref
  646.5 18.7 %attend_bwd.3 = (bf16[768,1024]{1,0:T(8,128)(2,1)S(1)}, bf16[384,1024]{1,0:T(8,128)(2,1)S(1)}, bf16[384,1024]{1,0:T(8,128)(2,1)S(1)}) custom-call(bf16[768,1024]{1,0:T(8,128)(2,1)S(1)} %copy-done.9, bf16[384,2048]{1,0:T(8,128)(2,1)} %copy-done.3, bf16[384,2048]{1,0:T(8,128)(2,1)} %copy-done.3, f32[8,8,768]{2,1,0:T(8,128)S(1)} %get-tuple-element.54.lse_ref, ...), custom_call_target="tpu_custom_call" | custom-call | flops 3019898880 | bytes 9437184 | tf_op jit(solution)/shard_map/attend_bwd/pallas_call | solution.py:195
  673.9 10.4 %reshape.417 = bf16[3072,1024]{1,0:T(8,128)(2,1)} reshape(bf16[1024,3072]{1,0:T(8,128)(2,1)} %convolution_convert_fusion) | data formatting | bytes 12582912 | tf_op jit(solution)/shard_map/reshape | solution.py:986
  697.1 6.0 reshape.416
  733.9 198.5 %scatter_sum.1 = (f32[336,1024]{1,0:T(8,128)}, bf16[512,1024]{1,0:T(8,128)(2,1)}, f32[8,128]{1,0:T(8,128)}) custom-call(bf16[10752,1024]{1,0:T(8,128)(2,1)} %broadcast_dynamic-update-slice_fusion.refs_0_, bf16[8192,1024]{1,0:T(8,128)(2,1)} %convert_dynamic-update-slice_fusion.refs_1_, f32[256,128]{1,0:T(8,128)} %broadcast_in_dim.76.refs_2_), custom_call_target="tpu_custom_call" | custom-call | tf_op jit(solution)/shard_map/scatter_sum/pallas_call | solution.py:690
  (379 shorter events, 322.1 us)
Async XLA Ops:
  7.2 940.5 %copy-start = (f32[32,128,128]{2,1,0:T(8,128)S(1)}, f32[32,128,128]{2,1,0:T(8,128)}, u32[]{:S(2)}) copy-start(f32[32,128,128]{2,1,0:T(8,128)} %param.22) | copy-start | bytes 6291460
  7.2 277.4 %all-gather.2.cloned.1.call-start = ((), (), s32[]{:S(2)}) async-start(), calls=%async_computation.2 | async-start | bytes 9437184 | tf_op jit(solution)/shard_map/all_gather | solution.py:879
  8.8 8.2 collective-permute-start
  211.9 21.4 %copy-start.58 = (f32[768]{0:T(1024)}, f32[768]{0:T(1024)S(1)}, u32[]{:S(2)}) copy-start(f32[768]{0:T(1024)S(1)} %div.92) | copy-start | bytes 9220
  216.7 16.7 %copy-start.54 = (f32[1,1024]{1,0:T(1,128)}, f32[1,1024]{1,0:T(1,128)S(1)}, u32[]{:S(2)}) copy-start(f32[1,1024]{1,0:T(1,128)S(1)} %get-tuple-element.153) | copy-start | bytes 12292
  216.7 40.7 %copy-start.67 = (f32[1,1024]{1,0:T(1,128)}, f32[1,1024]{1,0:T(1,128)S(1)}, u32[]{:S(2)}) copy-start(f32[1,1024]{1,0:T(1,128)S(1)} %get-tuple-element.151) | copy-start | bytes 12292
  216.7 40.7 %copy-start.72 = (f32[1,1024]{1,0:T(1,128)}, f32[1,1024]{1,0:T(1,128)S(1)}, u32[]{:S(2)}) copy-start(f32[1,1024]{1,0:T(1,128)S(1)} %get-tuple-element.150) | copy-start | bytes 12292
  267.5 165.4 %reduce-scatter.7.cloned.1.call-start = ((), (), s32[]{:S(2)}) async-start(), calls=%async_computation.4 | async-start | bytes 1474560
  284.6 34.7 %copy-start.22 = (f32[768,1024]{1,0:T(8,128)S(1)}, f32[768,1024]{1,0:T(8,128)}, u32[]{:S(2)}) copy-start(f32[768,1024]{1,0:T(8,128)} %copy-done.21) | copy-start | bytes 9437188
  323.3 31.1 %copy-start.15 = (f32[768,1024]{1,0:T(8,128)}, f32[768,1024]{1,0:T(8,128)S(1)}, u32[]{:S(2)}) copy-start(f32[768,1024]{1,0:T(8,128)S(1)} %get-tuple-element.157) | copy-start | bytes 9437188
  328.4 22.1 %copy-start.77 = (f32[768,1024]{1,0:T(8,128)}, f32[768,1024]{1,0:T(8,128)S(1)}, u32[]{:S(2)}) copy-start(f32[768,1024]{1,0:T(8,128)S(1)} %fusion.51) | copy-start | bytes 9437188
  332.9 13.9 %copy-start.80 = (f32[768,1024]{1,0:T(8,128)}, f32[768,1024]{1,0:T(8,128)S(1)}, u32[]{:S(2)}) copy-start(f32[768,1024]{1,0:T(8,128)S(1)} %fusion.61) | copy-start | bytes 9437188
  358.5 24.3 %collective-permute-start.1 = (bf16[3,1,32,1024]{3,2,1,0:T(8,128)(2,1)S(1)}, bf16[3,1,32,1024]{3,2,1,0:T(8,128)(2,1)}, u32[]{:S(2)}, u32[]{:S(2)}) collective-permute-start(bf16[3,1,32,1024]{3,2,1,0:T(8,128)(2,1)S(1)} %get-tuple-element.144), channel_id=1, source_target_pairs={{0,1},{2,3},{4,5},{6,7},{8,9},{10,11},{12,13},{14,15},{16,17},{18,... | collective-permute-start | bytes 589832 | tf_op jit(solution)/shard_map/ppermute | solution.py:43
  359.8 23.0 %collective-permute-start.2 = (bf16[3,1,32,1024]{3,2,1,0:T(8,128)(2,1)S(1)}, bf16[3,1,32,1024]{3,2,1,0:T(8,128)(2,1)}, u32[]{:S(2)}, u32[]{:S(2)}) collective-permute-start(bf16[3,1,32,1024]{3,2,1,0:T(8,128)(2,1)S(1)} %get-tuple-element.145), channel_id=1, source_target_pairs={{1,0},{3,2},{5,4},{7,6},{9,8},{11,10},{13,12},{15,14},{17,16},{19,... | collective-permute-start | bytes 589832 | tf_op jit(solution)/shard_map/ppermute | solution.py:46
  423.1 193.1 %reduce-scatter.5.cloned.1.call-start = ((), (), s32[]{:S(2)}) async-start(), calls=%async_computation.3 | async-start | bytes 9437184 | tf_op jit(solution)/shard_map/reduce_scatter | solution.py:945
  458.5 5.0 collective-permute-start.3
  459.8 4.1 collective-permute-start.4
  465.8 17.0 %copy-start.48 = (bf16[768,1024]{1,0:T(8,128)(2,1)}, bf16[768,1024]{1,0:T(8,128)(2,1)S(1)}, u32[]{:S(2)}) copy-start(bf16[768,1024]{1,0:T(8,128)(2,1)S(1)} %bitcast_convert_fusion.1) | copy-start | bytes 4718596
  471.5 24.6 %copy-start.86 = (bf16[768,1024]{1,0:T(8,128)(2,1)}, bf16[768,1024]{1,0:T(8,128)(2,1)S(1)}, u32[]{:S(2)}) copy-start(bf16[768,1024]{1,0:T(8,128)(2,1)S(1)} %fusion.27) | copy-start | bytes 4718596
  477.1 15.5 %copy-start.88 = (bf16[768,1024]{1,0:T(8,128)(2,1)}, bf16[768,1024]{1,0:T(8,128)(2,1)S(1)}, u32[]{:S(2)}) copy-start(bf16[768,1024]{1,0:T(8,128)(2,1)S(1)} %fusion.20) | copy-start | bytes 4718596
  646.5 18.7 %copy-start.19 = (bf16[1536,1024]{1,0:T(8,128)(2,1)S(1)}, bf16[1536,1024]{1,0:T(8,128)(2,1)}, u32[]{:S(2)}) copy-start(bf16[1536,1024]{1,0:T(8,128)(2,1)} %copy-done.18) | copy-start | bytes 9437188
  646.5 18.7 %copy-start.55 = (f32[1,1024]{1,0:T(1,128)S(1)}, f32[1,1024]{1,0:T(1,128)}, u32[]{:S(2)}) copy-start(f32[1,1024]{1,0:T(1,128)} %copy-done.54) | copy-start | bytes 12292
  646.5 18.7 %copy-start.59 = (f32[768]{0:T(1024)S(1)}, f32[768]{0:T(1024)}, u32[]{:S(2)}) copy-start(f32[768]{0:T(1024)} %copy-done.58) | copy-start | bytes 9220
  936.9 21.7 %collective-permute-start.5 = (f32[57344]{0:T(1024)}, f32[57344]{0:T(1024)}, u32[]{:S(2)}, u32[]{:S(2)}) collective-permute-start(f32[57344]{0:T(1024)} %bitcast.65), channel_id=1, source_target_pairs={{0,1},{1,2},{2,3},{3,4},{4,5},{5,6},{6,7},{7,8},{8,9},{9,10},{10,1... | collective-permute-start | bytes 688136 | tf_op jit(solution)/shard_map/ppermute | solution.py:751
  (81 other events, 406.3 us)
Sparse Core Ops, SparseCore 0:
  267.6 16.9 all-gather.1
  423.2 9.5 reduce-scatter.6
  569.6 15.8 reduce-scatter.4

commit v3 on v2

--- a/solution.py
+++ b/solution.py
@@ -32,20 +32,7 @@
 SHAMPOO_RATE = 0.01
 RMS_EPS = 1e-06
 HIGHEST_MODE = lax.Precision.HIGHEST
-group_heads = 4
-
-
-def with_halo(block, sides, width):
-    for axis, dim in sides:
-        count = lax.axis_size(axis)
-        forward = [(i, i + 1) for i in range(count - 1)]
-        backward = [(target, source) for source, target in forward]
-        low = lax.ppermute(
-            lax.slice_in_dim(block, block.shape[dim] - width, None, axis=dim), axis, forward
-        )
-        high = lax.ppermute(lax.slice_in_dim(block, 0, width, axis=dim), axis, backward)
-        block = jnp.concatenate([low, block, high], axis=dim)
-    return block
+WIDE = 1024
 
 
 def product(left, right):
@@ -88,6 +75,7 @@
 
 
 PAIR = 2 * HEAD_DIM
+BRIEF = pl.CostEstimate(flops=1000000, transcendentals=0, bytes_accessed=100000)
 LOG2E = math.log2(math.e)
 EXP_SCALE = HEAD_DIM ** (-0.5) * LOG2E
 
@@ -100,9 +88,15 @@
     return lax.broadcasted_iota(jnp.int32, shape, len(shape) - 1) // HEAD_DIM == head
 
 
-def attend_fwd_kernel(real_keys, q_ref, k_ref, v_ref, o_ref, lse_ref):
-    query, keys = q_ref[...], k_ref[...]
-    values = v_ref[...].T
+def joined(refs, n):
+    parts = [ref[n] for ref in refs]
+    return parts[0] if len(parts) == 1 else jnp.concatenate(parts, 0)
+
+
+def attend_fwd_kernel(real_keys, sources, q_ref, *refs):
+    o_ref, lse_ref = refs[-2:]
+    query, keys = q_ref[...], joined(refs[:sources], 0)
+    values = joined(refs[:sources], 1).T
     outs = []
     for head in range(2):
         own = jnp.where(head_lanes(query.shape, head), query, 0)
@@ -119,52 +113,48 @@
     o_ref[...] = jnp.concatenate(outs, 0).T.astype(jnp.bfloat16)
 
 
-def attend_fwd(query, keys, values, key_col, value_col, real_keys, rows):
-    count, total_keys = query.shape[0], keys.shape[0]
-    pairs = D // PAIR
+def attend_fwd(query, sources, real_keys, span, earlier=()):
+    count = query.shape[0]
+    total_keys = sum(source.shape[1] for source in sources)
+    low, high = span
+    by_pair = pl.BlockSpec((count, PAIR), lambda j: (0, low + j))
+    work = count * total_keys * (high - low) * PAIR
     return pl.pallas_call(
-        functools.partial(attend_fwd_kernel, real_keys),
-        grid=(pairs, count // rows),
-        in_specs=[
-            pl.BlockSpec((rows, PAIR), lambda j, n: (n, j)),
-            pl.BlockSpec((total_keys, PAIR), lambda j, n: (0, key_col + j)),
-            pl.BlockSpec((total_keys, PAIR), lambda j, n: (0, value_col + j)),
-        ],
-        out_specs=[
-            pl.BlockSpec((rows, PAIR), lambda j, n: (n, j)),
-            pl.BlockSpec((1, 8, rows), lambda j, n: (j, 0, n)),
-        ],
+        functools.partial(attend_fwd_kernel, real_keys, len(sources)),
+        grid=(high - low,),
+        in_specs=[by_pair]
+        + [pl.BlockSpec((2, source.shape[1], PAIR), lambda j: (0, 0, low + j)) for source in sources]
+        + [pl.BlockSpec(memory_space=pl.ANY)] * len(earlier),
+        out_specs=[by_pair, pl.BlockSpec((1, 8, count), lambda j: (low + j, 0, 0))],
         out_shape=[
             jax.ShapeDtypeStruct((count, D), jnp.bfloat16),
-            jax.ShapeDtypeStruct((pairs, 8, count), jnp.float32),
+            jax.ShapeDtypeStruct((D // PAIR, 8, count), jnp.float32),
         ],
+        input_output_aliases={1 + len(sources) + n: n for n in range(len(earlier))},
         compiler_params=pltpu.CompilerParams(vmem_limit_bytes=48 * 1024 * 1024),
-        cost_estimate=pl.CostEstimate(
-            flops=4 * count * total_keys * D, transcendentals=count * total_keys * 16, bytes_accessed=4 * D * (count + total_keys)
-        ),
+        cost_estimate=BRIEF,
         name="attend_fwd",
-    )(query, keys, values)
-
-
-def attend_bwd_kernel(real_keys, chunk, q_ref, k_ref, v_ref, lse_ref, o_ref, g_ref, dq_ref, dk_ref, dv_ref, kt_ref, dk_sum, dv_sum):
-    step = pl.program_id(1)
-
-    @pl.when(step == 0)
-    def _():
-        kt_ref[...] = k_ref[...].T
-        dk_sum[...] = jnp.zeros_like(dk_sum)
-        dv_sum[...] = jnp.zeros_like(dv_sum)
-
+    )(query, *sources, *earlier)
+
+
+def attend_bwd_kernel(real_keys, chunk, sources, extra, q_ref, *refs):
+    kv_refs = refs[:sources]
+    lse_ref, o_ref, g_ref = refs[sources : sources + 3]
+    dq_ref, *grad_refs = refs[sources + 3 + extra : sources + 4 + extra + sources]
+    k_all, v_all, kt_ref, dk_sum, dv_sum = refs[sources + 4 + extra + sources :]
+    k_all[...] = joined(kv_refs, 0)
+    v_all[...] = joined(kv_refs, 1)
+    kt_ref[...] = k_all[...].T
     query, grad = q_ref[...], g_ref[...]
     mixed = (grad.astype(jnp.float32) * o_ref[...].astype(jnp.float32)).T
-    total_keys = k_ref.shape[0]
+    total_keys = k_all.shape[0]
     queries = [jnp.where(head_lanes(query.shape, head), query, 0) for head in range(2)]
     grads = [jnp.where(head_lanes(grad.shape, head), grad, 0) for head in range(2)]
     inner = [jnp.sum(mixed[head * HEAD_DIM : (head + 1) * HEAD_DIM], 0, keepdims=True) for head in range(2)]
     grad_query = [jnp.zeros((HEAD_DIM, query.shape[0]), jnp.float32) for head in range(2)]
     for at in range(0, total_keys, chunk):
         part = pl.ds(at, chunk)
-        keys, values = k_ref[part], v_ref[part]
+        keys, values = k_all[part], v_all[part]
         for head in range(2):
             scores = nt_dot(keys, queries[head])
             shares = jnp.exp2(scores * EXP_SCALE - lse_ref[0, head : head + 1])
@@ -173,66 +163,71 @@
                 shares = jnp.where(row < real_keys, shares, 0.0)
             grad_shares = nt_dot(values, grads[head])
             grad_scores = (shares * (grad_shares - inner[head])).astype(jnp.bfloat16)
-            dv_sum[part] += product(shares.astype(jnp.bfloat16), grads[head])
-            dk_sum[part] += product(grad_scores, queries[head])
+            to_values = product(shares.astype(jnp.bfloat16), grads[head])
+            to_keys = product(grad_scores, queries[head])
+            if head == 0:
+                dv_sum[part] = to_values
+                dk_sum[part] = to_keys
+            else:
+                dv_sum[part] += to_values
+                dk_sum[part] += to_keys
             grad_query[head] += product(
                 kt_ref[head * HEAD_DIM : (head + 1) * HEAD_DIM, part], grad_scores
             )
     scale = HEAD_DIM ** (-0.5)
     dq_ref[...] = (jnp.concatenate(grad_query, 0) * scale).T.astype(jnp.bfloat16)
-
-    @pl.when(step == pl.num_programs(1) - 1)
-    def _():
-        dk_ref[...] = (dk_sum[...] * scale).astype(jnp.bfloat16)
-        dv_ref[...] = dv_sum[...].astype(jnp.bfloat16)
-
-
-def attend_bwd(query, keys, values, key_col, value_col, real_keys, rows, chunk, totals, out, grad):
-    count, total_keys = query.shape[0], keys.shape[0]
-    pairs = D // PAIR
-    by_query = pl.BlockSpec((rows, PAIR), lambda j, n: (n, j))
-    by_key = pl.BlockSpec((total_keys, PAIR), lambda j, n: (0, j))
+    start = 0
+    for ref in grad_refs:
+        part = pl.ds(start, ref.shape[1])
+        ref[0] = (dk_sum[part] * scale).astype(jnp.bfloat16)
+        ref[1] = dv_sum[part].astype(jnp.bfloat16)
+        start += ref.shape[1]
+
+
+def attend_bwd(query, sources, real_keys, span, chunk, totals, out, grad, earlier=()):
+    count = query.shape[0]
+    total_keys = sum(source.shape[1] for source in sources)
+    low, high = span
+    by_pair = pl.BlockSpec((count, PAIR), lambda j: (0, low + j))
+    by_source = [pl.BlockSpec((2, source.shape[1], PAIR), lambda j: (0, 0, low + j)) for source in sources]
+    first = 1 + len(sources) + 3
+    work = count * total_keys * (high - low) * PAIR
     return pl.pallas_call(
-        functools.partial(attend_bwd_kernel, real_keys, chunk),
-        grid=(pairs, count // rows),
-        in_specs=[
-            by_query,
-            pl.BlockSpec((total_keys, PAIR), lambda j, n: (0, key_col + j)),
-            pl.BlockSpec((total_keys, PAIR), lambda j, n: (0, value_col + j)),
-            pl.BlockSpec((1, 8, rows), lambda j, n: (j, 0, n)),
-            by_query,
-            by_query,
-        ],
-        out_specs=[by_query, by_key, by_key],
-        out_shape=[
-            jax.ShapeDtypeStruct((count, D), jnp.bfloat16),
-            jax.ShapeDtypeStruct((total_keys, D), jnp.bfloat16),
-            jax.ShapeDtypeStruct((total_keys, D), jnp.bfloat16),
-        ],
+        functools.partial(attend_bwd_kernel, real_keys, chunk, len(sources), len(earlier)),
+        grid=(high - low,),
+        in_specs=[by_pair]
+        + by_source
+        + [pl.BlockSpec((1, 8, count), lambda j: (low + j, 0, 0)), by_pair, by_pair]
+        + [pl.BlockSpec(memory_space=pl.ANY)] * len(earlier),
+        out_specs=[by_pair] + by_source,
+        out_shape=[jax.ShapeDtypeStruct((count, D), jnp.bfloat16)]
+        + [jax.ShapeDtypeStruct(source.shape, jnp.bfloat16) for source in sources],
+        input_output_aliases={first + n: n for n in range(len(earlier))},
         scratch_shapes=[
+            pltpu.VMEM((total_keys, PAIR), jnp.bfloat16),
+            pltpu.VMEM((total_keys, PAIR), jnp.bfloat16),
             pltpu.VMEM((PAIR, total_keys), jnp.bfloat16),
             pltpu.VMEM((total_keys, PAIR), jnp.float32),
             pltpu.VMEM((total_keys, PAIR), jnp.float32),
         ],
         compiler_params=pltpu.CompilerParams(vmem_limit_bytes=48 * 1024 * 1024),
-        cost_estimate=pl.CostEstimate(
-            flops=10 * count * total_keys * D, transcendentals=count * total_keys * 16, bytes_accessed=8 * D * (count + total_keys)
-        ),
+        cost_estimate=BRIEF,
         name="attend_bwd",
-    )(query, keys, values, totals, out, grad)
+    )(query, *sources, totals, out, grad, *earlier)
 
 
 GROUPS = 3
 
 
-def render_kernel(samples_ref, cells_ref, wanted_ref, mask_ref, factor_ref, win_ref, wout_ref,
-                  loss_ref, grad_ref, gin_ref, gout_ref,
+def render_kernel(samples_ref, near_ref, far_ref, wanted_ref, mask_ref, factor_ref, win_ref, wout_ref,
+                  loss_ref, grad_ref, grad_far_ref, gin_ref, gout_ref,
                   table, inner_all, hidden_all, point_all, out_all, gout_all, sums):
     block = pl.program_id(0)
-    cells = cells_ref.shape[1]
+    half = near_ref.shape[1]
+    cells = 2 * half
     group = table.shape[2]
     rays = samples_ref.shape[2]
-    planes = cells_ref.shape[0]
+    planes = near_ref.shape[0]
 
     @pl.when(block == 0)
     def _():
@@ -242,7 +237,7 @@
         sums[...] = jnp.zeros_like(sums)
         table[...] = jnp.zeros_like(table)
         for plane in range(planes):
-            turned = cells_ref[plane].T
+            turned = jnp.concatenate([near_ref[plane], far_ref[plane]], 0).T
             for g in range(GROUPS):
                 width = min(group, cells - g * group)
                 table[plane, g * CH : (g + 1) * CH, :width] = turned[:CH, g * group : g * group + width]
@@ -333,13 +328,16 @@
     def _():
         for plane in range(planes):
             for g in range(GROUPS):
-                count = min(group, cells - g * group)
-                part = sums[plane, g * CH : (g + 1) * CH, :count]
-                grad_ref[plane, :, g * group : g * group + count] = part.astype(jnp.bfloat16)
-
-
-def render(cells, samples, wanted, mask, factor, decode_in, decode_out, rays):
-    planes, count, _ = cells.shape
+                for low, high, ref in ((0, half, grad_ref), (half, cells, grad_far_ref)):
+                    start, stop = max(g * group, low), min((g + 1) * group, high)
+                    if start < stop:
+                        part = sums[plane, g * CH : (g + 1) * CH, start - g * group : stop - g * group]
+                        ref[plane, :, start - low : stop - low] = part.astype(jnp.bfloat16)
+
+
+def render(near, far, samples, wanted, mask, factor, decode_in, decode_out, rays):
+    planes, half, _ = near.shape
+    count = 2 * half
     all_rays = samples.shape[2]
     group = -(-count // (GROUPS * 128)) * 128
     points = S * rays
@@ -349,17 +347,19 @@
         grid=(all_rays // rays,),
         in_specs=[
             pl.BlockSpec((planes, S, rays), lambda n: (0, 0, n)),
-            whole(*cells.shape),
+            whole(*near.shape),
+            whole(*far.shape),
             pl.BlockSpec((8, rays), lambda n: (0, n)),
             pl.BlockSpec((1, rays), lambda n: (0, n)),
             pl.BlockSpec(memory_space=pltpu.SMEM),
             whole(CH, DEC_HID),
             whole(DEC_HID, 8),
         ],
-        out_specs=[whole(8, 128), whole(planes, CH, count), whole(CH, DEC_HID), whole(DEC_HID, 8)],
+        out_specs=[whole(8, 128), whole(planes, CH, half), whole(planes, CH, half), whole(CH, DEC_HID), whole(DEC_HID, 8)],
         out_shape=[
             jax.ShapeDtypeStruct((8, 128), jnp.float32),
-            jax.ShapeDtypeStruct((planes, CH, count), jnp.bfloat16),
+            jax.ShapeDtypeStruct((planes, CH, half), jnp.bfloat16),
+            jax.ShapeDtypeStruct((planes, CH, half), jnp.bfloat16),
             jax.ShapeDtypeStruct((CH, DEC_HID), jnp.float32),
             jax.ShapeDtypeStruct((DEC_HID, 8), jnp.float32),
         ],
@@ -374,10 +374,9 @@
         ],
         compiler_params=pltpu.CompilerParams(vmem_limit_bytes=48 * 1024 * 1024),
         name="render",
-    )(samples, cells, wanted, mask, factor, decode_in, decode_out)
-
-
-LANE = 1024
+    )(samples, near, far, wanted, mask, factor, decode_in, decode_out)
+
+
 MESH_ID = pl.DeviceIdType.MESH
 
 
@@ -413,8 +412,6 @@
     second = p // 8
     return ((1 - second) * ((2 * c + k) * 8 + p) + second * (4 * p + 2 * c + k)) * BLOCK
 
-block_chunks = (2, BLOCK, block_chunk)
-
 
 ORDER = [("near", 0), ("z", 1), ("z", 3), ("far", 0), ("z", 2), ("near", 1), ("near", 3), ("near", 2)]
 ORDER += [("both", 0), ("far", 1), ("far", 3), ("far", 2), ("both", 1), ("both", 3), ("both", 2)]
@@ -422,12 +419,19 @@
 
 def gather_kernel(layouts, stagger, *refs):
     count = len(layouts)
-    sources = refs[:count]
-    fulls = refs[count : 2 * count]
-    send, recv, local = refs[2 * count :]
+    fulls = refs[count + 1 : 2 * count + 1]
+    line_full = refs[2 * count + 1]
+    send, recv, local, line_sems = refs[2 * count + 2 : 2 * count + 6]
+    held = refs[2 * count + 6 :]
+    brought = [pltpu.make_async_copy(s, h, local.at[n]) for n, (s, h) in enumerate(zip(refs[: count + 1], held))]
+    for copy in brought:
+        copy.start()
+    sources, line_source = held[:count], held[count]
     p, c, z, near, far, both = places()
     zs = [along_z(p, z, k) for k in range(4)]
     enter([(q, c) for q in zs[1:]] + [(near, c), (far, c), (p, 1 - c)])
+    for copy in brought:
+        copy.wait()
     jobs = [(a, j) for a, layout in enumerate(layouts) for j in range(layout[0])]
 
     def target(owner, job):
@@ -490,37 +494,63 @@
             line = (p, far, near, both)[k // 4]
             arrive((along_z(line, z, k % 4), 1 - c), 15 + k, job)
 
-    steps = []
+    lines = []
+    for k in (1, 3, 2):
+        lines.append(
+            pltpu.make_async_remote_copy(
+                line_source, line_full.at[4 - k], line_sems.at[k], line_sems.at[7 - k],
+                device_id=(zs[k], c), device_id_type=MESH_ID,
+            )
+        )
+    lines.append(pltpu.make_async_copy(line_source, line_full.at[0], line_sems.at[0]))
+
+    steps = [(stagger * len(jobs) - 4, -2, 0)]
     for job in range(len(jobs)):
         steps.append((stagger * job, -1, job))
         for i in range(len(ORDER)):
             steps.append((stagger * job + i + 1, i, job))
     for _, i, job in sorted(steps):
-        if i < 0:
+        if i == -2:
+            for copy in lines:
+                copy.start()
+        elif i < 0:
             begin(job)
         else:
             take(*ORDER[i], job)
+    for k in (1, 2, 3):
+        spot = line_full.at[k]
+        pltpu.make_async_remote_copy(
+            spot, spot, line_sems.at[k], line_sems.at[3 + k], device_id=(p, 1 - c), device_id_type=MESH_ID
+        ).wait_recv()
+    for copy in lines[:3]:
+        copy.wait_send()
+    lines[3].wait()
     for copy in started:
         copy.wait_send()
     for job in range(len(jobs)):
         pltpu.make_async_copy(source(job), target(me, job), local.at[job]).wait()
 
 
-def gather_all(layouts, stagger, shards_in, name_id):
+def gather_all(layouts, stagger, shards_in, line, name_id):
     copies = sum(l[0] for l in layouts)
+    everywhere = pl.BlockSpec(memory_space=pl.ANY)
+    shapes = [jax.ShapeDtypeStruct((32 * s.shape[0],) + s.shape[1:], s.dtype) for s in shards_in]
+    shapes.append(jax.ShapeDtypeStruct((4,) + line.shape, line.dtype))
     return pl.pallas_call(
         functools.partial(gather_kernel, layouts, stagger),
-        out_shape=[jax.ShapeDtypeStruct((32 * s.shape[0],) + s.shape[1:], s.dtype) for s in shards_in],
-        in_specs=[pl.BlockSpec(memory_space=pl.ANY)] * len(shards_in),
-        out_specs=[pl.BlockSpec(memory_space=pl.ANY)] * len(shards_in),
+        out_shape=shapes,
+        in_specs=[everywhere] * len(shapes),
+        out_specs=[everywhere] * len(shapes),
         scratch_shapes=[
             pltpu.SemaphoreType.DMA((31, copies)),
             pltpu.SemaphoreType.DMA((31, copies)),
             pltpu.SemaphoreType.DMA((copies,)),
-        ],
+            pltpu.SemaphoreType.DMA((7,)),
+        ]
+        + [pltpu.VMEM(a.shape, a.dtype) for a in (*shards_in, line)],
         compiler_params=pltpu.CompilerParams(collective_id=name_id, has_side_effects=True),
         name="gather_all",
-    )(*shards_in)
+    )(*shards_in, line)
 
 
 SUM_ORDER = [(3, 0), (3, 1), (3, 3), (3, 2), (2, 0), (2, 1), (2, 3), (2, 2)]
@@ -528,11 +558,14 @@
 AHEAD = 3
 
 
-def scatter_kernel(layouts, shared, stagger, *refs):
+def scatter_kernel(layouts, stagger, *refs):
     count = len(layouts)
     grads = refs[:count]
-    outs = refs[count : 2 * count]
-    scratch = refs[2 * count :]
+    line_grad = refs[count]
+    outs = refs[count + 1 : 2 * count + 1]
+    line_out = refs[2 * count + 1]
+    scratch = refs[2 * count + 2 :]
+    line_own, line_got, line_sum, line_sems = scratch[-4:]
     p, c, z, near, far, both = places()
     zs = [along_z(p, z, k) for k in range(4)]
     enter([(q, c) for q in zs[1:]] + [(near, c), (far, c), (p, 1 - c)])
@@ -616,16 +649,35 @@
     def final_copies(job):
         a, j = jobs[job]
         rows = layouts[a][1]
-        done = view(job, buffers[a][5], 0)
-        if not shared[a]:
-            return [pltpu.make_async_copy(done, outs[a].at[pl.ds(j * rows, rows)], out_sem.at[job, 0])]
-        spot = outs[a].at[pl.ds(pl.multiple_of((c * layouts[a][0] + j) * rows, 8), rows)]
-        return [
-            pltpu.make_async_copy(done, spot, out_sem.at[job, 0]),
+        return [pltpu.make_async_copy(view(job, buffers[a][5], 0), outs[a].at[pl.ds(j * rows, rows)], out_sem.at[job, 0])]
+
+    line_sends = [
+        pltpu.make_async_remote_copy(
+            line_grad.at[k], line_got.at[3 - k], line_sems.at[k], line_sems.at[7 - k],
+            device_id=(zs[k], c), device_id_type=MESH_ID,
+        )
+        for k in (1, 3, 2)
+    ]
+    line_load = pltpu.make_async_copy(line_grad.at[0], line_own, line_sems.at[0])
+    half = line_own.shape[0]
+    spot = line_out.at[pl.ds(pl.multiple_of(c * half, 8), half)]
+    line_stores = [
+        pltpu.make_async_copy(line_sum, spot, line_sems.at[7]),
+        pltpu.make_async_remote_copy(
+            line_sum, spot, line_sems.at[8], line_sems.at[9], device_id=(p, 1 - c), device_id_type=MESH_ID
+        ),
+    ]
+
+    def line_finish():
+        line_load.wait()
+        for k in (1, 2, 3):
+            target = line_got.at[k - 1]
             pltpu.make_async_remote_copy(
-                done, spot, out_sem.at[job, 1], out_sem.at[job, 2], device_id=(p, 1 - c), device_id_type=MESH_ID
-            ),
-        ]
+                target, target, line_sems.at[k], line_sems.at[3 + k], device_id=(p, 1 - c), device_id_type=MESH_ID
+            ).wait_recv()
+        add_up([line_own] + [line_got.at[n] for n in range(3)], line_sum)
+        for copy in line_stores:
+            copy.start()
 
     def step(i, job):
         g, k = SUM_ORDER[i]
@@ -650,12 +702,17 @@
         if i + AHEAD < 16:
             start(i + AHEAD, job)
 
-    steps = []
+    for copy in line_sends:
+        copy.start()
+    line_load.start()
+    steps = [(stagger * (len(jobs) - 1) + 11, -1, -2)]
     for job in range(len(jobs)):
         for i in range(-1, 16):
             steps.append((stagger * job + i, job, i))
     for _, job, i in sorted(steps):
-        if i < 0:
+        if i == -2:
+            line_finish()
+        elif i < 0:
             for n in range(AHEAD):
                 start(n, job)
         else:
@@ -667,9 +724,13 @@
                 onward(i, job).wait_send()
         for copy in final_copies(job):
             copy.wait()
-
-
-def scatter_sum(layouts, shared, stagger, grads, name_id):
+    for copy in line_sends:
+        copy.wait_send()
+    for copy in line_stores:
+        copy.wait()
+
+
+def scatter_sum(layouts, stagger, grads, line, name_id):
     jobs = sum(l[0] for l in layouts)
     scratch = [
         pltpu.SemaphoreType.DMA((16, jobs)),
@@ -680,81 +741,488 @@
         pltpu.SemaphoreType.DMA((jobs, 3)),
     ]
     shapes = []
-    for layout, both_cores, grad in zip(layouts, shared, grads):
+    for layout, grad in zip(layouts, grads):
         rows, width = layout[0] * layout[1], grad.shape[1]
         for slots in (16, 8, 4, 3, AHEAD):
             scratch.append(pltpu.VMEM((slots, rows, width), grad.dtype))
-        kind = grad.dtype if both_cores else jnp.float32
-        scratch.append(pltpu.VMEM((1, rows, width), kind))
-        shapes.append(jax.ShapeDtypeStruct(((2 if both_cores else 1) * rows, width), kind))
+        scratch.append(pltpu.VMEM((1, rows, width), jnp.float32))
+        shapes.append(jax.ShapeDtypeStruct((rows, width), jnp.float32))
+    piece = line.shape[1:]
+    scratch += [pltpu.VMEM(piece, line.dtype), pltpu.VMEM((3,) + piece, line.dtype), pltpu.VMEM(piece, line.dtype)]
+    scratch.append(pltpu.SemaphoreType.DMA((10,)))
+    shapes.append(jax.ShapeDtypeStruct((2 * piece[0], piece[1]), line.dtype))
+    everywhere = pl.BlockSpec(memory_space=pl.ANY)
     return pl.pallas_call(
-        functools.partial(scatter_kernel, layouts, shared, stagger),
+        functools.partial(scatter_kernel, layouts, stagger),
         out_shape=shapes,
-        in_specs=[pl.BlockSpec(memory_space=pl.ANY)] * len(grads),
-        out_specs=[pl.BlockSpec(memory_space=pl.ANY)] * len(grads),
+        in_specs=[everywhere] * len(shapes),
+        out_specs=[everywhere] * len(shapes),
         scratch_shapes=scratch,
         compiler_params=pltpu.CompilerParams(
-            collective_id=name_id, has_side_effects=True, vmem_limit_bytes=56 * 1024 * 1024
+            collective_id=name_id, has_side_effects=True, vmem_limit_bytes=48 * 1024 * 1024
         ),
         name="scatter_sum",
-    )(*grads)
-
-
-WIDE = 1024
+    )(*grads, line)
+
+
+GELU_A = math.sqrt(2.0 / math.pi)
+GELU_B = 0.044715
+
+
+def chunk_sources():
+    p, c, z, _, _, _ = places()
+    x, y = p % 2, (p // 2) % 2
+    out = []
+    for other in range(2):
+        core = (c + other) % 2
+        for g in range(4):
+            dx = (1 - core) * (g % 2) + core * (g // 2)
+            dy = (1 - core) * (g // 2) + core * (g % 2)
+            for k in range(4):
+                owner = ((z + k) % 4) * 4 + ((y + dy) % 2) * 2 + (x + dx) % 2
+                for half in range(2):
+                    out.append((other, g, k, half, block_chunk(owner, core, half) // BLOCK))
+    return out
+
+
+def panel_loads(refs, held, sems):
+    if len(refs) == 1:
+        for n in range(held.shape[0] // WIDE):
+            at = pl.ds(n * WIDE, WIDE)
+            pltpu.make_async_copy(refs[0].at[at], held.at[at], sems.at[n]).start()
+        return
+    for other, g, k, half, chunk in chunk_sources():
+        source = refs[other * 4 + g].at[k, pl.ds(half * BLOCK, BLOCK)]
+        target = held.at[pl.ds(pl.multiple_of(chunk * BLOCK, BLOCK), BLOCK)]
+        pltpu.make_async_copy(source, target, sems.at[chunk // 8]).start()
+
+
+def panel_ready(held, sems, n):
+    at = pl.ds(pl.multiple_of(n * WIDE, WIDE), WIDE)
+    pltpu.make_async_copy(held.at[at], held.at[at], sems.at[n]).wait()
+    return held.at[at]
+
+
+def mlp_fwd_kernel(count, *refs):
+    sources = refs[:count]
+    h_ref, s_ref, up_ref, act_ref, grid_ref, held, total, sems = refs[count:]
+    step = pl.program_id(0)
+    steps = pl.num_programs(0)
+
+    @pl.when(step == 0)
+    def _():
+        panel_loads(sources, held, sems)
+        total[...] = s_ref[...]
+
+    up = product(h_ref[...], panel_ready(held, sems, step)[...])
+    up_ref[0] = up
+    act = 0.5 * up * (1.0 + jnp.tanh(GELU_A * (up + GELU_B * up * up * up)))
+    act = act.astype(jnp.bfloat16)
+    act_ref[0] = act
+    total[...] += product(act, panel_ready(held, sems, steps + step)[...])
+
+    @pl.when(step == steps - 1)
+    def _():
+        grid_ref[...] = total[...].astype(jnp.bfloat16)
+
+
+def mlp_fwd(panels, hidden, stream):
+    rows = hidden.shape[0]
+    steps = HID // WIDE
+    whole = pl.BlockSpec((rows, WIDE), lambda n: (0, 0))
+    part = pl.BlockSpec((1, rows, WIDE), lambda n: (n, 0, 0))
+    return pl.pallas_call(
+        functools.partial(mlp_fwd_kernel, len(panels)),
+        grid=(steps,),
+        in_specs=[pl.BlockSpec(memory_space=pl.ANY)] * len(panels) + [whole, whole],
+        out_specs=[part, part, whole],
+        out_shape=[
+            jax.ShapeDtypeStruct((steps, rows, WIDE), jnp.float32),
+            jax.ShapeDtypeStruct((steps, rows, WIDE), jnp.bfloat16),
+            jax.ShapeDtypeStruct((rows, WIDE), jnp.bfloat16),
+        ],
+        scratch_shapes=[
+            pltpu.VMEM((2 * HID, WIDE), jnp.bfloat16),
+            pltpu.VMEM((rows, WIDE), jnp.float32),
+            pltpu.SemaphoreType.DMA((2 * steps,)),
+        ],
+        compiler_params=pltpu.CompilerParams(vmem_limit_bytes=56 * 1024 * 1024),
+        cost_estimate=BRIEF,
+        name="mlp_fwd",
+    )(*panels, hidden, stream)
+
+
+def mlp_bwd_kernel(count, *refs):
+    sources = refs[:count]
+    outs = 2 if count > 1 else 1
+    h_ref, g_ref, up_ref, act_ref = refs[count : count + 4]
+    dh_ref = refs[count + 4]
+    grads = refs[count + 5 : count + 5 + outs]
+    held, staged, sems, out_sem = refs[count + 5 + outs :]
+    step = pl.program_id(0)
+    steps = pl.num_programs(0)
+
+    @pl.when(step == 0)
+    def _():
+        panel_loads(sources, held, sems)
+        dh_ref[...] = jnp.zeros_like(dh_ref)
+
+    def tn_dot(left, right):
+        return lax.dot_general(left, right, (((0,), (0,)), ((), ())), preferred_element_type=jnp.float32)
+
+    def drain(side):
+        pltpu.make_async_copy(staged.at[side], staged.at[side], out_sem.at[side]).wait()
+
+    def store(side):
+        panel = side * steps + step
+        source = staged.at[side]
+        if count == 1:
+            at = pl.ds(pl.multiple_of(panel * WIDE, WIDE), WIDE)
+            pltpu.make_async_copy(source, grads[0].at[at], out_sem.at[side]).start()
+            return
+        p, c, z, _, _, _ = places()
+        for n in range(8):
+            if side == 0:
+                owner, core, half = n, step // 2, step % 2
+            else:
+                row = step * 8 + n
+                owner, core, half = 8 + row // 4, (n // 2) % 2, n % 2
+            dx = (owner % 2 + p % 2) % 2
+            dy = ((owner // 2) % 2 + (p // 2) % 2) % 2
+            g = (1 - core) * (dx + 2 * dy) + core * (dy + 2 * dx)
+            spot = g * 4 + (owner // 4 - z + 4) % 4
+            at = pl.ds(pl.multiple_of(half * BLOCK, BLOCK), BLOCK)
+            from_ref = source.at[pl.ds(n * BLOCK, BLOCK)]
+
+            @pl.when((core + c) % 2 == 0)
+            def _():
+                pltpu.make_async_copy(from_ref, grads[0].at[spot, at], out_sem.at[side]).start()
+
+            @pl.when((core + c) % 2 == 1)
+            def _():
+                pltpu.make_async_copy(from_ref, grads[1].at[spot, at], out_sem.at[side]).start()
+
+    pulled = g_ref[...]
+
+    @pl.when(step > 0)
+    def _():
+        drain(1)
+
+    staged[1] = tn_dot(act_ref[0], pulled).astype(jnp.bfloat16)
+    store(1)
+    grad_act = nt_dot(pulled, panel_ready(held, sems, steps + step)[...])
+    up = up_ref[0]
+    square = up * up
+    bend = jnp.tanh(GELU_A * up * (1.0 + GELU_B * square))
+    slope = 0.5 * (1.0 + bend) + 0.5 * GELU_A * up * (1.0 - bend * bend) * (1.0 + 3.0 * GELU_B * square)
+    grad_up = (grad_act * slope).astype(jnp.bfloat16)
+
+    @pl.when(step > 0)
+    def _():
+        drain(0)
+
+    staged[0] = tn_dot(h_ref[...], grad_up).astype(jnp.bfloat16)
+    store(0)
+    dh_ref[...] += nt_dot(grad_up, panel_ready(held, sems, step)[...])
+
+    @pl.when(step == steps - 1)
+    def _():
+        drain(0)
+        drain(1)
+
+
+def mlp_bwd(panels, hidden, grad, up, act):
+    rows = hidden.shape[0]
+    steps = HID // WIDE
+    whole = pl.BlockSpec((rows, WIDE), lambda n: (0, 0))
+    part = pl.BlockSpec((1, rows, WIDE), lambda n: (n, 0, 0))
+    if len(panels) == 1:
+        shapes = [jax.ShapeDtypeStruct((2 * HID, WIDE), jnp.bfloat16)]
+    else:
+        shapes = [jax.ShapeDtypeStruct((16, 2 * BLOCK, WIDE), jnp.bfloat16)] * 2
+    return pl.pallas_call(
+        functools.partial(mlp_bwd_kernel, len(panels)),
+        grid=(steps,),
+        in_specs=[pl.BlockSpec(memory_space=pl.ANY)] * len(panels) + [whole, whole, part, part],
+        out_specs=[whole] + [pl.BlockSpec(memory_space=pl.ANY)] * len(shapes),
+        out_shape=[jax.ShapeDtypeStruct((rows, WIDE), jnp.float32)] + shapes,
+        scratch_shapes=[
+            pltpu.VMEM((2 * HID, WIDE), jnp.bfloat16),
+            pltpu.VMEM((2, WIDE, WIDE), jnp.bfloat16),
+            pltpu.SemaphoreType.DMA((2 * steps,)),
+            pltpu.SemaphoreType.DMA((2,)),
+        ],
+        compiler_params=pltpu.CompilerParams(vmem_limit_bytes=58 * 1024 * 1024),
+        cost_estimate=BRIEF,
+        name="mlp_bwd",
+    )(*panels, hidden, grad, up, act)
+
+
+def panel_view(rows_ref, first, count, depth):
+    region = rows_ref.at[pl.ds(first, depth // 8 * count)]
+    return region.reshape(depth // 8, count, 8, WIDE)
+
+
+def project_kernel(first, count, depth, lead, x_ref, rows_ref, *rest):
+    outs, held, sems = rest[:-2], rest[-2], rest[-1]
+    step = pl.program_id(0)
+    panels = panel_view(rows_ref, first, count, depth)
+
+    @pl.when(step == 0)
+    def _():
+        for n in range(count):
+            pltpu.make_async_copy(panels.at[:, n], held.at[n], sems.at[n]).start()
+
+    pltpu.make_async_copy(held.at[step], held.at[step], sems.at[step]).wait()
+    result = product(x_ref[...], held[step].reshape(depth, WIDE)).astype(jnp.bfloat16)
+    if lead:
+
+        @pl.when(step == 0)
+        def _():
+            outs[0][...] = result
+
+        @pl.when(step > 0)
+        def _():
+            outs[1][0] = result
+
+    else:
+        outs[0][0] = result
+
+
+def project(x, rows, first, count, lead):
+    tokens, depth = x.shape
+    specs = [pl.BlockSpec((1, tokens, WIDE), lambda n: (jnp.maximum(n - lead, 0), 0, 0))]
+    shapes = [jax.ShapeDtypeStruct((count - lead, tokens, WIDE), jnp.bfloat16)]
+    if lead:
+        specs.insert(0, pl.BlockSpec((tokens, WIDE), lambda n: (0, 0)))
+        shapes.insert(0, jax.ShapeDtypeStruct((tokens, WIDE), jnp.bfloat16))
+    return pl.pallas_call(
+        functools.partial(project_kernel, first, count, depth, lead),
+        grid=(count,),
+        in_specs=[pl.BlockSpec((tokens, depth), lambda n: (0, 0)), pl.BlockSpec(memory_space=pl.ANY)],
+        out_specs=specs,
+        out_shape=shapes,
+        scratch_shapes=[pltpu.VMEM((count, depth // 8, 8, WIDE), jnp.bfloat16), pltpu.SemaphoreType.DMA((count,))],
+        compiler_params=pltpu.CompilerParams(vmem_limit_bytes=32 * 1024 * 1024),
+        cost_estimate=BRIEF,
+        name="project",
+    )(x, rows)
+
+
+def project_back_kernel(first, count, depth, lead_ref, g_ref, rows_ref, o_ref, held, sems):
+    step = pl.program_id(0)
+    panels = panel_view(rows_ref, first, count, depth)
+
+    @pl.when(step == 0)
+    def _():
+        for n in range(count):
+            pltpu.make_async_copy(panels.at[:, n], held.at[n], sems.at[n]).start()
+
+    pltpu.make_async_copy(held.at[step], held.at[step], sems.at[step]).wait()
+    grad = jnp.where(step == 0, lead_ref[...], g_ref[0])
+    back = nt_dot(grad, held[step].reshape(depth, WIDE))
+
+    @pl.when(step == 0)
+    def _():
+        o_ref[...] = back
+
+    @pl.when(step > 0)
+    def _():
+        o_ref[...] += back
+
+
+def project_back(lead, grads, rows, first, depth):
+    others, tokens, _ = grads.shape
+    count = others + 1
+    return pl.pallas_call(
+        functools.partial(project_back_kernel, first, count, depth),
+        grid=(count,),
+        in_specs=[
+            pl.BlockSpec((tokens, WIDE), lambda n: (0, 0)),
+            pl.BlockSpec((1, tokens, WIDE), lambda n: (jnp.maximum(n - 1, 0), 0, 0)),
+            pl.BlockSpec(memory_space=pl.ANY),
+        ],
+        out_specs=pl.BlockSpec((tokens, depth), lambda n: (0, 0)),
+        out_shape=jax.ShapeDtypeStruct((tokens, depth), jnp.float32),
+        scratch_shapes=[pltpu.VMEM((count, depth // 8, 8, WIDE), jnp.bfloat16), pltpu.SemaphoreType.DMA((count,))],
+        compiler_params=pltpu.CompilerParams(vmem_limit_bytes=32 * 1024 * 1024),
+        cost_estimate=BRIEF,
+        name="project_back",
+    )(lead, grads, rows)
+
+
+def weight_grads_kernel(products, copies, *refs):
+    arrays = refs[: len(refs) - 8]
+    out, left, right, staged, bounce, load_sem, store_sem, copy_sem = refs[len(refs) - 8 :]
+    step = pl.program_id(0)
+    steps = len(products)
+
+    def loads(n):
+        side, (a, a_pick), (b, b_pick), _, _ = products[n]
+        slot = n % 2
+        source_a = arrays[a] if a_pick is None else arrays[a].at[a_pick]
+        source_b = arrays[b] if b_pick is None else arrays[b].at[b_pick]
+        rows, deep = side
+        return [
+            pltpu.make_async_copy(source_a, left.at[slot, pl.ds(0, rows), pl.ds(0, deep)], load_sem.at[slot, 0]),
+            pltpu.make_async_copy(source_b, right.at[slot, pl.ds(0, rows)], load_sem.at[slot, 1]),
+        ]
+
+    def stores(n):
+        (rows, deep), _, _, first, panels = products[n]
+        slot = n % 2
+        count, at = panels
+        source = staged.at[slot, pl.ds(0, deep // 8)]
+        target = panel_view(out, first, count, deep).at[:, at]
+        return pltpu.make_async_copy(source, target, store_sem.at[slot])
+
+    def bounced(n):
+        a, first, count = copies[n]
+        held = bounce.at[pl.ds(sum(c[2] for c in copies[:n]), count)]
+        return (
+            pltpu.make_async_copy(arrays[a], held, copy_sem.at[n, 0]),
+            pltpu.make_async_copy(held, out.at[pl.ds(first, count)], copy_sem.at[n, 1]),
+        )
+
+    for n in range(steps):
+
+        @pl.when(step == n)
+        def _():
+            if n == 0:
+                for job in loads(0):
+                    job.start()
+                for m in range(len(copies)):
+                    bounced(m)[0].start()
+            if n == 1:
+                for m in range(len(copies)):
+                    bounced(m)[0].wait()
+                    bounced(m)[1].start()
+            if n + 1 < steps:
+                for job in loads(n + 1):
+                    job.start()
+            for job in loads(n):
+                job.wait()
+            if n >= 2:
+                stores(n - 2).wait()
+            rows, deep = products[n][0]
+            slot = n % 2
+            total = lax.dot_general(
+                left[slot, :rows, :deep], right[slot, :rows], (((0,), (0,)), ((), ())), preferred_element_type=jnp.float32
+            )
+            staged[slot, : deep // 8] = total.astype(jnp.bfloat16).reshape(deep // 8, 8, WIDE)
+            stores(n).start()
+            if n == steps - 1:
+                if n > 0:
+                    stores(n - 1).wait()
+                stores(n).wait()
+                for m in range(len(copies)):
+                    bounced(m)[1].wait()
+
+
+def weight_grads(arrays, products, copies, tile_rows):
+    rows = max(p[0][0] for p in products)
+    deep = max(p[0][1] for p in products)
+    everywhere = pl.BlockSpec(memory_space=pl.ANY)
+    return pl.pallas_call(
+        functools.partial(weight_grads_kernel, products, copies),
+        grid=(len(products),),
+        in_specs=[everywhere] * len(arrays),
+        out_specs=everywhere,
+        out_shape=jax.ShapeDtypeStruct((tile_rows, 8, WIDE), jnp.bfloat16),
+        scratch_shapes=[
+            pltpu.VMEM((2, rows, deep), jnp.bfloat16),
+            pltpu.VMEM((2, rows, WIDE), jnp.bfloat16),
+            pltpu.VMEM((2, deep // 8, 8, WIDE), jnp.bfloat16),
+            pltpu.VMEM((sum(c[2] for c in copies), 8, WIDE), jnp.bfloat16),
+            pltpu.SemaphoreType.DMA((2, 2)),
+            pltpu.SemaphoreType.DMA((2,)),
+            pltpu.SemaphoreType.DMA((len(copies), 2)),
+        ],
+        compiler_params=pltpu.CompilerParams(vmem_limit_bytes=40 * 1024 * 1024),
+        cost_estimate=BRIEF,
+        name="weight_grads",
+    )(*arrays)
+
+
 TILE = 8 * WIDE
-GAP_AT = D * D + DI * 2 * D + D * D + D * 3 * D + D * D + D * 16 * CH + CH * DEC_HID + DEC_HID * 4
-GAP = -GAP_AT % TILE
-ROWS = {}
-_row = 0
+KV_AT = D * D
+QKV_AT = KV_AT + DI * 2 * D + D * D
+GAP_AT = QKV_AT + D * 3 * D + D * D + D * 16 * CH + CH * DEC_HID + DEC_HID * 4
+QKV_GAP = -QKV_AT % (3 * TILE)
+END_GAP = -GAP_AT % TILE
+TILES = {}
+_tile = 0
 for _name, _rows in (
     ("query_cross", D),
     ("keyval_cross", 2 * DI),
     ("out_cross", D),
+    ("gap", QKV_GAP // WIDE),
     ("qkv_self", 3 * D),
     ("out_self", D),
     ("deconv", 16 * CH),
     ("decode", 8),
     ("modulate", 6 * NCAM),
+    ("triplane", 0),
 ):
-    ROWS[_name] = (_row, _row + _rows)
-    _row += _rows
-PLANE_ROW = _row
+    TILES[_name] = _tile
+    _tile += _rows // 8
 
 
 def direct_links():
     return lax.axis_size("dp") == 16 and lax.axis_size("strip") == 2
 
 
+def regroup(rows, first, back):
+    tile = first + lax.broadcasted_iota(jnp.int32, (rows.shape[0], 1), 0) // 8
+
+    def turned(panels):
+        shape = (-1, panels, 8, WIDE) if back else (-1, 8, panels, WIDE)
+        return rows.reshape(shape).transpose(0, 2, 1, 3).reshape(rows.shape)
+
+    in_kv = (tile >= TILES["keyval_cross"]) & (tile < TILES["out_cross"])
+    in_qkv = (tile >= TILES["qkv_self"]) & (tile < TILES["out_self"])
+    return jnp.where(in_kv, turned(2), jnp.where(in_qkv, turned(3), rows))
+
+
+def device_place():
+    return lax.axis_index("dp") * lax.axis_size("strip") + lax.axis_index("strip")
+
+
+def tile_rows(length):
+    return -(-length // (6 * TILE)) * 6
+
+
 def align(shard):
     length = shard.shape[0]
-    rows = -(-length // TILE) * 8
-    size = rows * WIDE
+    size = tile_rows(length) * TILE
     extra = size - length
     reach = -(-32 * extra // WIDE) * WIDE
-    place = lax.axis_index("dp") * 2 + lax.axis_index("strip")
+    place = device_place()
     shard = shard.astype(jnp.bfloat16)
-    following = lax.ppermute(shard[:reach], ("dp", "strip"), [(n + 1, n) for n in range(31)])
+    following = lax.ppermute(shard[:reach], AXES, [(n + 1, n) for n in range(31)])
     joined = jnp.concatenate([shard, following])
     shift = place * extra
-    early = lax.dynamic_slice_in_dim(joined, shift, size)
-    late = lax.dynamic_slice_in_dim(joined, jnp.maximum(shift - GAP, 0), size)
     at = place * size + lax.iota(jnp.int32, size)
-    return jnp.where(at < GAP_AT, early, late).reshape(rows, WIDE)
+    parts = [
+        lax.dynamic_slice_in_dim(joined, jnp.maximum(shift - gap, 0), size)
+        for gap in (0, QKV_GAP, QKV_GAP + END_GAP)
+    ]
+    rows = jnp.where(at < QKV_AT, parts[0], jnp.where(at < GAP_AT + QKV_GAP, parts[1], parts[2]))
+    return regroup(rows.reshape(-1, WIDE), place * (size // TILE), False)
 
 
 def unalign(summed, length):
     size = summed.size
     extra = size - length
     reach = -(-32 * extra // WIDE) * WIDE
-    place = lax.axis_index("dp") * 2 + lax.axis_index("strip")
-    summed = summed.reshape(-1)
-    before = lax.ppermute(summed[size - reach :], ("dp", "strip"), [(n, n + 1) for n in range(31)])
+    place = device_place()
+    summed = regroup(summed, place * (size // TILE), True).reshape(-1)
+    before = lax.ppermute(summed[size - reach :], AXES, [(n, n + 1) for n in range(31)])
     joined = jnp.concatenate([before, summed])
     shift = reach - place * extra
-    early = lax.dynamic_slice_in_dim(joined, shift, length)
-    late = lax.dynamic_slice_in_dim(joined, shift + GAP, length)
     at = place * length + lax.iota(jnp.int32, length)
-    return jnp.where(at < GAP_AT, early, late)
+    parts = [lax.dynamic_slice_in_dim(joined, shift + gap, length) for gap in (0, QKV_GAP, QKV_GAP + END_GAP)]
+    return jnp.where(at < QKV_AT, parts[0], jnp.where(at < GAP_AT, parts[1], parts[2]))
 
 
 def chunks_of(tiles):
@@ -778,6 +1246,17 @@
 
 
 META = (1, 8, lambda p, c, j: (2 * p + c) * 8)
+SWAP = ((0, 1), (1, 0))
+AXES = ("dp", "strip")
+
+
+def pairs_to(target):
+    return [(2 * p + c, sum(v * w for v, w in zip(target(p, c), (2, 1)))) for p in range(16) for c in range(2)]
+
+
+NEAR = pairs_to(lambda p, c: (p ^ (1 + c), c))
+FAR = pairs_to(lambda p, c: (p ^ (2 - c), c))
+CORE = pairs_to(lambda p, c: (p, 1 - c))
 
 
 def gather_weights(weights, blocks, part):
@@ -788,40 +1267,108 @@
         tiles = lax.dynamic_slice_in_dim(blocks, lax.axis_index("strip") * half, half)
         tiles = chunks_of(tiles.astype(jnp.bfloat16))
         meta = jnp.full((8, 128), part, jnp.float32)
-        rows, panels, parts = gather_all(
-            [flat_chunks(own.shape[0], 3), block_chunks, META], 6, [own, tiles, meta], 0
-        )
-        return rows, panels, jnp.sum(parts[::8, 0])
-    flat = lax.all_gather(weights.astype(jnp.bfloat16), ("dp", "strip"), axis=0, tiled=True)
+        rows, parts, line = gather_all([flat_chunks(own.shape[0], 3), META], 6, [own, meta], tiles, 0)
+        near = lax.ppermute(line, AXES, NEAR)
+        return rows, [line, near], jnp.sum(parts[::8, 0])
+    flat = lax.all_gather(weights.astype(jnp.bfloat16), AXES, axis=0, tiled=True)
     tiles = lax.all_gather(blocks.astype(jnp.bfloat16), "dp", axis=0, tiled=True)
-    rows = jnp.concatenate([flat[:GAP_AT], jnp.zeros((GAP,), flat.dtype), flat[GAP_AT:]])
-    rows = rows[: rows.shape[0] // TILE * TILE].reshape(-1, WIDE)
-    return rows, panels_of(chunks_of(tiles)), lax.psum(part, ("dp", "strip"))
-
-
-def reduce_grads(pieces, panels, part, length):
+    gaps = [jnp.zeros((QKV_GAP,), flat.dtype), jnp.zeros((END_GAP,), flat.dtype)]
+    rows = jnp.concatenate([flat[:QKV_AT], gaps[0], flat[QKV_AT:GAP_AT], gaps[1], flat[GAP_AT:]])
+    rows = jnp.pad(rows, (0, -rows.shape[0] % (6 * TILE))).reshape(-1, WIDE)
+    return regroup(rows, 0, False), [panels_of(chunks_of(tiles))], lax.psum(part, AXES)
+
+
+class Panels:
+    def __init__(self, parts):
+        self.parts = parts
+        self.staged = len(parts) > 1
+
+    def first(self, before):
+        if not self.staged:
+            return before
+        line, near = self.parts
+        near, before = lax.optimization_barrier((near, before))
+        self.parts = [line, near, lax.ppermute(line, AXES, FAR)]
+        return before
+
+    def second(self, before):
+        if not self.staged:
+            return before
+        line, near, far = self.parts
+        far, before = lax.optimization_barrier((far, before))
+        self.parts = [line, near, far, lax.ppermute(near, AXES, FAR)]
+        return before
+
+    def third(self, after):
+        if not self.staged:
+            return self.parts
+        line, near, far, both = self.parts
+        both, after = lax.optimization_barrier((both, after))
+        return [line, near, far, both] + [lax.ppermute(group, AXES, CORE) for group in (line, near, far, both)]
+
+
+class PanelSums:
+    def __init__(self, grads):
+        self.parts = grads
+        self.staged = len(grads) > 1
+        if self.staged:
+            self.mine = grads[0]
+            self.got = lax.ppermute(grads[1], AXES, CORE)
+
+    def added(self, g, *parts):
+        at = slice(4 * g, 4 * g + 4)
+        total = self.mine[at].astype(jnp.float32) + self.got[at].astype(jnp.float32)
+        for part in parts:
+            total = total + part.astype(jnp.float32)
+        return total.astype(jnp.bfloat16)
+
+    def first(self, before):
+        if not self.staged:
+            return before
+        both, self.far, before = lax.optimization_barrier((self.added(3), self.added(2), before))
+        self.to_near = lax.ppermute(both, AXES, FAR)
+        return before
+
+    def second(self, before):
+        if not self.staged:
+            return before
+        self.to_near, self.far, before = lax.optimization_barrier((self.to_near, self.far, before))
+        self.to_own = lax.ppermute(self.far, AXES, FAR)
+        return before
+
+    def third(self, before):
+        if not self.staged:
+            return before
+        near, self.to_own, before = lax.optimization_barrier((self.added(1, self.to_near), self.to_own, before))
+        self.last = lax.ppermute(near, AXES, NEAR)
+        return before
+
+    def fourth(self, before):
+        if not self.staged:
+            return before
+        self.last, before = lax.optimization_barrier((self.last, before))
+        self.parts = [self.added(0, self.to_own, self.last)]
+        return before
+
+
+def reduce_grads(rows, panels, part, length):
     if direct_links():
-        rows = -(-length // TILE) * 8
-        total = sum(piece.shape[0] for piece in pieces)
-        pieces = pieces + [jnp.zeros((32 * rows - total, WIDE), jnp.bfloat16)]
         meta = jnp.full((32 * 8, 128), part, jnp.float32)
-        summed, tiles, parts = scatter_sum(
-            [flat_chunks(rows, 1), block_chunks, META],
-            [False, True, False],
-            6,
-            [jnp.concatenate(pieces), panels, meta],
-            1,
+        summed, parts, tiles = scatter_sum(
+            [flat_chunks(rows.shape[0] // 32, 3), META], 6, [rows, meta], panels[0], 1
         )
         return unalign(summed, length), tiles_of(tiles).astype(jnp.float32), parts[0, 0]
-    flat = jnp.concatenate(pieces).astype(jnp.float32).reshape(-1)
-    flat = jnp.concatenate([flat[:GAP_AT], flat[GAP_AT + GAP :]])
+    flat = regroup(rows, 0, True).astype(jnp.float32).reshape(-1)
+    flat = jnp.concatenate(
+        [flat[:QKV_AT], flat[QKV_AT + QKV_GAP : GAP_AT + QKV_GAP], flat[GAP_AT + QKV_GAP + END_GAP :]]
+    )
     devices = lax.axis_size("dp") * lax.axis_size("strip")
-    flat = jnp.pad(flat, (0, devices * length - flat.shape[0]))
-    tiles = tiles_of(chunks_of_panels(panels)).astype(jnp.float32)
-    flat_sum = lax.psum_scatter(flat, ("dp", "strip"), scatter_dimension=0, tiled=True)
-    tile_sum = lax.psum_scatter(tiles, ("dp", "strip"), scatter_dimension=0, tiled=True)
+    flat = jnp.pad(flat, (0, max(0, devices * length - flat.shape[0])))[: devices * length]
+    tiles = tiles_of(chunks_of_panels(panels[0])).astype(jnp.float32)
+    flat_sum = lax.psum_scatter(flat, AXES, scatter_dimension=0, tiled=True)
+    tile_sum = lax.psum_scatter(tiles, AXES, scatter_dimension=0, tiled=True)
     tile_sum = lax.all_gather(tile_sum.astype(jnp.bfloat16), "strip", axis=0, tiled=True)
-    return flat_sum, tile_sum.astype(jnp.float32), lax.psum(part, ("dp", "strip"))
+    return flat_sum, tile_sum.astype(jnp.float32), lax.psum(part, AXES)
 
 
 def shards(
@@ -842,64 +1389,72 @@
 ):
     strips = lax.axis_size("strip")
     place = lax.axis_index("strip")
-    plane_rows = PR * strips
     pixel = ray_pixel[0]
     mask = jnp.take(valid[0], pixel).astype(jnp.float32)
     wanted = jnp.take(target[0], pixel, axis=1)
     rows, panels, count = gather_weights(weights, blocks, jnp.sum(mask))
-    panels = panels.reshape(-1, WIDE, WIDE)
-    first_panels = [panels[n] for n in range(HID // WIDE)]
-    second_panels = [panels[n] for n in range(HID // WIDE, 2 * HID // WIDE)]
-    params = {name: rows[low:high] for name, (low, high) in ROWS.items()}
-    params["keyval_cross"] = params["keyval_cross"].reshape(DI, 2 * D)
-    params["qkv_self"] = params["qkv_self"].reshape(D, 3 * D)
-    params["deconv"] = params["deconv"].reshape(D, 16 * CH)
-    decode = params["decode"].reshape(-1)
+    tiled = rows.reshape(-1, 8, WIDE)
+
+    def square(name):
+        return rows[TILES[name] * 8 : TILES[name] * 8 + D]
+
+    def plain(name, count):
+        return rows[TILES[name] * 8 : TILES[name] * 8 + count]
+
+    deconv = plain("deconv", 16 * CH).reshape(D, 16 * CH)
+    decode = plain("decode", 8).reshape(-1)
     decode_in = decode[: CH * DEC_HID].reshape(CH, DEC_HID)
     decode_out = decode[CH * DEC_HID : CH * DEC_HID + DEC_HID * 4].reshape(DEC_HID, 4)
     picture = image[0]
-    cells_read = samples[0].reshape(3, -1)
-    mods = lax.dynamic_slice_in_dim(params["modulate"], 6 * camera[0], 6).astype(jnp.float32)
-    row_start = place * PR
-    triplane = rows[PLANE_ROW : PLANE_ROW + 3 * plane_rows * TC].reshape(3, plane_rows, TC, D)
-    own_rows = lax.dynamic_slice_in_dim(triplane, row_start, PR, 1)
-    stream0 = own_rows.reshape(-1, D).astype(jnp.float32)
+    real_keys = picture.shape[0]
+    picture = jnp.pad(picture, ((0, -real_keys % 128), (0, 0)))
+    mods = lax.dynamic_slice_in_dim(plain("modulate", 6 * NCAM), 6 * camera[0], 6).astype(jnp.float32)
+    own_rows = PR * TC
+    stream0 = jnp.concatenate(
+        [
+            lax.dynamic_slice_in_dim(rows, TILES["triplane"] * 8 + (strips * plane + place) * own_rows, own_rows)
+            for plane in range(3)
+        ]
+    ).astype(jnp.float32)
     hidden1, norm_one = jax.vjp(norm_mod, stream0, mods[0], mods[1])
     hidden1 = hidden1.astype(jnp.bfloat16)
-    query1 = product(hidden1, params["query_cross"]).astype(jnp.bfloat16)
-    real_keys = picture.shape[0]
-    picture = jnp.pad(picture, ((0, -real_keys % 128), (0, 0)))
-    image_kv = product(picture, params["keyval_cross"]).astype(jnp.bfloat16)
+    query1 = product(hidden1, square("query_cross")).astype(jnp.bfloat16)
+    (image_kv,) = project(picture, tiled, TILES["keyval_cross"], 2, 0)
+    pairs = D // PAIR
     tokens = query1.shape[0]
-    cross_out, total_one = attend_fwd(query1, image_kv, image_kv, 0, D // PAIR, real_keys, tokens)
-    stream1 = stream0 + product(cross_out, params["out_cross"])
+    cross_out, total_one = attend_fwd(query1, [image_kv], real_keys, (0, pairs))
+    stream1 = stream0 + product(cross_out, square("out_cross"))
     hidden2, norm_two = jax.vjp(norm_mod, stream1, mods[2], mods[3])
     hidden2 = hidden2.astype(jnp.bfloat16)
-    qkv = product(hidden2, params["qkv_self"]).astype(jnp.bfloat16)
-    kv_all = lax.all_gather(qkv[:, D:], "strip", axis=0, tiled=True)
-    all_keys = kv_all.shape[0]
-    self_out, total_two = attend_fwd(qkv, kv_all, kv_all, 0, D // PAIR, all_keys, tokens)
-    stream2 = stream1 + product(self_out, params["out_self"])
+    panels = Panels(panels)
+    hidden2 = panels.first(hidden2)
+    query2, kv_own = project(hidden2, tiled, TILES["qkv_self"], 3, 1)
+    kv_both = [kv_own, lax.ppermute(kv_own, "strip", SWAP)]
+    all_keys = 2 * kv_own.shape[1]
+    early = attend_fwd(query2, kv_both, all_keys, (0, pairs // 2))
+    early = (panels.second(early[0]), early[1])
+    self_out, total_two = attend_fwd(query2, kv_both, all_keys, (pairs // 2, pairs), early)
+    panels = panels.third(self_out)
+    stream2 = stream1 + product(self_out, square("out_self"))
     hidden3, norm_three = jax.vjp(norm_mod, stream2, mods[4], mods[5])
     hidden3 = hidden3.astype(jnp.bfloat16)
-    stream3 = stream2
-    acts, gelu_backs = [], []
-    for first, second in zip(first_panels, second_panels):
-        act, gelu_back = jax.vjp(gelu_tanh, product(hidden3, first))
-        acts.append(act.astype(jnp.bfloat16))
-        gelu_backs.append(gelu_back)
-        stream3 = stream3 + product(acts[-1], second)
-    grid = stream3.astype(jnp.bfloat16).reshape(3, PR, -1, D)
-    padded = with_halo(grid, (("strip", 1),), 1)
-    ydc = jnp.einsum("prcd,dk->prck", padded, params["deconv"], preferred_element_type=jnp.float32)
+    up, act, grid = mlp_fwd(panels, hidden3, stream2)
+    grid = grid.reshape(3, PR, -1, D)
+    edge = lax.ppermute(jnp.where(place == 0, grid[:, -1:], grid[:, :1]), "strip", SWAP)
+    nothing = jnp.zeros_like(edge)
+    padded = jnp.concatenate(
+        [jnp.where(place == 0, nothing, edge), grid, jnp.where(place == 0, edge, nothing)], 1
+    )
+    ydc = jnp.einsum("prcd,dk->prck", padded, deconv, preferred_element_type=jnp.float32)
     feature, assemble_back = jax.vjp(assemble, ydc)
-    whole = lax.all_gather(feature.astype(jnp.bfloat16), "strip", axis=1, tiled=True)
-    cells = whole.reshape(3, -1, CH)
+    cells = feature.astype(jnp.bfloat16).reshape(3, -1, CH)
+    cells_far = lax.ppermute(cells, "strip", SWAP)
     rays = pixel.shape[0]
     factor = 1.0 / jnp.maximum(count, 1.0)
-    loss_part, grad_cells, grad_decode_in, grad_decode_out = render(
+    loss_part, grad_cells, grad_far, grad_decode_in, grad_decode_out = render(
         cells,
-        samples[0],
+        cells_far,
+        (samples[0] + place * cells.shape[1]) % (2 * cells.shape[1]),
         jnp.pad(wanted, ((1, 4), (0, 0))),
         mask[None],
         factor.reshape(1),
@@ -909,83 +1464,100 @@
     )
     loss_part = loss_part[0, 0]
     grad_decode_out = grad_decode_out[:, :4]
-    grad_feature = lax.psum_scatter(
-        grad_cells.transpose(0, 2, 1).reshape(whole.shape),
-        "strip",
-        scatter_dimension=1,
-        tiled=True,
-    ).astype(jnp.float32)
-    grad_feature = lax.optimization_barrier(grad_feature.astype(jnp.bfloat16)).astype(jnp.float32)
+    grad_cells = grad_cells.astype(jnp.float32) + lax.ppermute(grad_far, "strip", SWAP).astype(jnp.float32)
+    grad_feature = grad_cells.astype(jnp.bfloat16).transpose(0, 2, 1).reshape(feature.shape)
+    grad_feature = lax.optimization_barrier(grad_feature).astype(jnp.float32)
     (grad_ydc,) = assemble_back(grad_feature)
     grad_ydc = grad_ydc.astype(jnp.bfloat16)
     grad_deconv = weight_grad(padded.reshape(-1, D), grad_ydc.reshape(-1, 16 * CH))
-    grad_padded = product_back(grad_ydc, params["deconv"])
-    edges = jnp.concatenate([grad_padded[:, :1], grad_padded[:, -1:]], 1)
-    beside = with_halo(edges.astype(jnp.bfloat16), (("strip", 1),), 1).astype(edges.dtype)
+    grad_padded = product_back(grad_ydc, deconv)
+    beside = jnp.where(place == 0, grad_padded[:, -1], grad_padded[:, 0]).astype(jnp.bfloat16)
+    beside = lax.ppermute(beside, "strip", SWAP).astype(jnp.float32)
     grad_grid = grad_padded[:, 1:-1]
-    grad_grid = grad_grid.at[:, 0].add(beside[:, 0]).at[:, -1].add(beside[:, -1])
+    grad_grid = grad_grid.at[:, 0].add(jnp.where(place == 0, 0.0, beside))
+    grad_grid = grad_grid.at[:, -1].add(jnp.where(place == 0, beside, 0.0))
     grad_stream = grad_grid.reshape(-1, D)
     grad_branch = grad_stream.astype(jnp.bfloat16)
-    grad_first, grad_second = [], []
-    grad_hidden3 = 0.0
-    for first, second, act, gelu_back in zip(first_panels, second_panels, acts, gelu_backs):
-        grad_second.append(weight_grad(act, grad_branch).astype(jnp.bfloat16))
-        (grad_up,) = gelu_back(product_back(grad_branch, second))
-        grad_up = grad_up.astype(jnp.bfloat16)
-        grad_first.append(weight_grad(hidden3, grad_up).astype(jnp.bfloat16))
-        grad_hidden3 = grad_hidden3 + product_back(grad_up, first)
+    grad_hidden3, *panel_grads = mlp_bwd(panels, hidden3, grad_branch, up, act)
     grad_norm, grad_mod4, grad_mod5 = norm_three(grad_hidden3)
     grad_stream = grad_stream + grad_norm
-    grad_branch = grad_stream.astype(jnp.bfloat16)
-    grad_out_self = weight_grad(self_out, grad_branch)
-    grad_self = product_back(grad_branch, params["out_self"]).astype(jnp.bfloat16)
-    grad_query2, grad_keys2, grad_values2 = attend_bwd(
-        qkv, kv_all, kv_all, 0, D // PAIR, all_keys, tokens, 512, total_two, self_out, grad_self
+    grad_branch2 = grad_stream.astype(jnp.bfloat16)
+    grad_self = product_back(grad_branch2, square("out_self")).astype(jnp.bfloat16)
+    panel_sums = PanelSums(panel_grads)
+    grad_self = panel_sums.first(grad_self)
+    early = attend_bwd(query2, kv_both, all_keys, (0, pairs // 2), 512, total_two, self_out, grad_self)
+    early = (panel_sums.second(early[0]), *early[1:])
+    grad_query2, grad_kv_own, grad_kv_far = attend_bwd(
+        query2, kv_both, all_keys, (pairs // 2, pairs), 512, total_two, self_out, grad_self, early
     )
-    grad_kv_own = lax.psum_scatter(
-        jnp.concatenate([grad_keys2, grad_values2], 1), "strip", scatter_dimension=0, tiled=True
+    grad_kv_far = lax.ppermute(grad_kv_far, "strip", SWAP)
+    grad_query2 = panel_sums.third(grad_query2)
+    grad_kv = (grad_kv_own.astype(jnp.float32) + grad_kv_far.astype(jnp.float32)).astype(jnp.bfloat16)
+    grad_hidden2 = project_back(grad_query2, grad_kv, tiled, TILES["qkv_self"], D)
+    grad_norm, grad_mod2, grad_mod3 = norm_two(grad_hidden2)
+    grad_stream = grad_stream + grad_norm
+    grad_branch1 = grad_stream.astype(jnp.bfloat16)
+    grad_cross = product_back(grad_branch1, square("out_cross")).astype(jnp.bfloat16)
+    grad_query1, grad_image_kv = attend_bwd(
+        query1, [image_kv], real_keys, (0, pairs), 128, total_one, cross_out, grad_cross
     )
-    grad_qkv = jnp.concatenate([grad_query2, grad_kv_own], 1)
-    grad_qkv_self = weight_grad(hidden2, grad_qkv)
-    grad_norm, grad_mod2, grad_mod3 = norm_two(product_back(grad_qkv, params["qkv_self"]))
-    grad_stream = grad_stream + grad_norm
-    grad_branch = grad_stream.astype(jnp.bfloat16)
-    grad_out_cross = weight_grad(cross_out, grad_branch)
-    grad_cross = product_back(grad_branch, params["out_cross"]).astype(jnp.bfloat16)
-    grad_query1, grad_keys1, grad_values1 = attend_bwd(
-        query1, image_kv, image_kv, 0, D // PAIR, real_keys, tokens, 128, total_one, cross_out, grad_cross
-    )
-    grad_image_kv = jnp.concatenate([grad_keys1, grad_values1], 1)
-    grad_keyval = weight_grad(picture, grad_image_kv)
-    grad_query_cross = weight_grad(hidden1, grad_query1)
-    grad_norm, grad_mod0, grad_mod1 = norm_one(product_back(grad_query1, params["query_cross"]))
+    grad_query1 = panel_sums.fourth(grad_query1)
+    grad_norm, grad_mod0, grad_mod1 = norm_one(product_back(grad_query1, square("query_cross")))
     grad_stream = grad_stream + grad_norm
     grad_mods = jnp.stack([grad_mod0, grad_mod1, grad_mod2, grad_mod3, grad_mod4, grad_mod5])
     grad_modulate = lax.dynamic_update_slice_in_dim(
         jnp.zeros((6 * NCAM, D), jnp.bfloat16), grad_mods.astype(jnp.bfloat16), 6 * camera[0], 0
     )
     grad_triplane = lax.dynamic_update_slice_in_dim(
-        jnp.zeros((3, plane_rows, TC, D), jnp.bfloat16),
-        grad_stream.astype(jnp.bfloat16).reshape(3, PR, TC, D),
-        row_start,
+        jnp.zeros((3, strips, own_rows, D), jnp.bfloat16),
+        grad_stream.astype(jnp.bfloat16).reshape(3, 1, own_rows, D),
+        place,
         1,
     )
     grad_decode = jnp.concatenate([grad_decode_in.reshape(-1), grad_decode_out.reshape(-1)])
-    grad_decode = jnp.pad(grad_decode, (0, GAP))
-    pieces = [
-        grad_query_cross,
-        grad_keyval,
-        grad_out_cross,
-        grad_qkv_self,
-        grad_out_self,
-        grad_deconv,
-        grad_decode,
-        grad_modulate,
-        grad_triplane,
+    grad_decode = jnp.pad(grad_decode, (0, END_GAP))
+    total_tiles = tiled.shape[0]
+    end = TILES["triplane"] + 3 * strips * own_rows // 8
+    gap = TILES["qkv_self"] - TILES["gap"]
+    arrays = [
+        hidden1,
+        grad_query1,
+        picture,
+        grad_image_kv,
+        cross_out,
+        grad_branch1,
+        hidden2,
+        grad_query2,
+        grad_kv,
+        self_out,
+        grad_branch2,
     ]
-    pieces = [piece.astype(jnp.bfloat16).reshape(-1, WIDE) for piece in pieces]
-    panel_grads = jnp.concatenate(grad_first + grad_second)
-    flat_sum, block_sum, loss_sum = reduce_grads(pieces, panel_grads, loss_part, weights.shape[0])
+    tall, low = (tokens, D), (picture.shape[0], DI)
+    products = [
+        (tall, (9, None), (10, None), TILES["out_self"], (1, 0)),
+        (tall, (6, None), (7, None), TILES["qkv_self"], (3, 0)),
+        (tall, (6, None), (8, 0), TILES["qkv_self"], (3, 1)),
+        (tall, (6, None), (8, 1), TILES["qkv_self"], (3, 2)),
+        (tall, (4, None), (5, None), TILES["out_cross"], (1, 0)),
+        (low, (2, None), (3, 0), TILES["keyval_cross"], (2, 0)),
+        (low, (2, None), (3, 1), TILES["keyval_cross"], (2, 1)),
+        (tall, (0, None), (1, None), TILES["query_cross"], (1, 0)),
+    ]
+    copies = []
+    for piece, first in (
+        (grad_deconv, TILES["deconv"]),
+        (grad_decode, TILES["decode"]),
+        (grad_modulate, TILES["modulate"]),
+        (grad_triplane, TILES["triplane"]),
+        (jnp.zeros((gap, 8, WIDE), jnp.bfloat16), TILES["gap"]),
+        (jnp.zeros((total_tiles - end, 8, WIDE), jnp.bfloat16), end),
+    ):
+        piece = piece.astype(jnp.bfloat16).reshape(-1, 8, WIDE)
+        if piece.shape[0]:
+            copies.append((len(arrays), first, piece.shape[0]))
+            arrays.append(piece)
+    row_grads = weight_grads(arrays, products, copies, total_tiles).reshape(-1, WIDE)
+    flat_sum, block_sum, loss_sum = reduce_grads(row_grads, panel_sums.parts, loss_part, weights.shape[0])
     loss = loss_sum * factor
     new_first = BETA_FIRST * first_moment + (1.0 - BETA_FIRST) * flat_sum
     new_second = BETA_SECOND * second_moment + (1.0 - BETA_SECOND) * flat_sum * flat_sum

time: 984 us -> 792 us (0.80)
  matrix products: 196 us -> 57.1 us
  local copies, waits for them, and re-layouts: 168 us -> 118 us
  other arithmetic: 47.4 us -> 70 us
  between operations: 18.8 us -> 5.58 us
    dot_general x14 -> x1, matrix products: 56.3 us -> 6.6 us  [weight_grad(): lax.dot_general(left, right, (((0,), (0,)), ((), ())), preferred_element_...]
    dot_general x13 -> x4, matrix products: 69.2 us -> 20.5 us  [product_back(): lax.dot_general(left, right, (((left.ndim - 1,), (1,)), ((), ())), prefer...]
    pallas_call x1, Pallas kernels: 173 us -> 126 us  [gather_all(): pl.pallas_call(functools.partial(gather_kernel, layouts, stagger), out_sh...]
    dot_general x13 -> x3, matrix products: 53.2 us -> 12.8 us  [product(): return jnp.dot(left, right, preferred_element_type=jnp.float32)]
    pallas_call x5 -> x13, Pallas kernels: 314 us -> 353 us  [the longest x1 120 us: scatter_sum(): pl.pallas_call(functools.partial(scatter_kernel, layouts, stagger), out_s...]
    reshape x10, local copies, waits for them, and re-layouts: 54.4 us -> 31.8 us  [the longest x2 11.5 us: shards(): deconv = plain('deconv', 16 * CH).reshape(D, 16 * CH)]
    convert_element_type x2 -> x10, other arithmetic: 5.16 us -> 24 us  [the longest x3 14.4 us: added(): return total.astype(jnp.bfloat16)]
    unnamed x212 -> x186, local copies, waits for them, and re-layouts: 52.5 us -> 34 us
  transfers between devices with their start and end apart: 9 -> 19, of which waited for: 3 -> 7; matrix products, arithmetic and copies ran while one was open for 10% -> 13% of each run, Pallas kernels for 0% -> 13%
where the time goes in v3:
time: 792 us; the launch traced here: 781 us
  Pallas kernels  498 us (63%)
  local copies, waits for them, and re-layouts  118 us (15%)
  other arithmetic  70 us (9%)
  matrix products  57.1 us (7%)
  starting transfers between devices  17.9 us (2%)
  waiting for transfers between devices  14.6 us (2%)
    pallas_call x1, Pallas kernels, gather_all(): pl.pallas_call(functools.partial(gather_kernel, layouts, stagger), out_sh...  126 us
    pallas_call x1, Pallas kernels, scatter_sum(): pl.pallas_call(functools.partial(scatter_kernel, layouts, stagger), out_s...  120 us
    pallas_call x3, Pallas kernels, attend_bwd(): pl.pallas_call(functools.partial(attend_bwd_kernel, real_keys, chunk, len...  72.4 us
    pallas_call x3, Pallas kernels, attend_fwd(): pl.pallas_call(functools.partial(attend_fwd_kernel, real_keys, len(source...  46.7 us
    pallas_call x1, Pallas kernels, mlp_bwd(): pl.pallas_call(functools.partial(mlp_bwd_kernel, len(panels)), grid=(step...  45.4 us
    unnamed x186, local copies, waits for them, and re-layouts  34 us
    pallas_call x1, Pallas kernels, mlp_fwd(): pl.pallas_call(functools.partial(mlp_fwd_kernel, len(panels)), grid=(step...  28.8 us
    dot_general x4, matrix products, product_back(): lax.dot_general(left, right, (((left.ndim - 1,), (1,)), ((), ())), prefer...  20.5 us
  transfers between devices with their start and end apart: 19, of which 7 were waited for; matrix products, arithmetic and copies ran while one was open for 13% of the time, Pallas kernels for 13%

profile of v3, /device:TPU:1, one launch (start us, length us, event | category | flops | bytes accessed | tf_op | source)
XLA Modules:
  0.0 781.0 jit_solution(7337175148769987854)
XLA Ops:
  11.6 6.4 fusion.47
  26.4 126.3 %gather_all.1 = (bf16[10752,1024]{1,0:T(8,128)(2,1)}, f32[256,128]{1,0:T(8,128)}, bf16[4,256,1024]{2,1,0:T(8,128)(2,1)}) custom-call(bf16[336,1024]{1,0:T(8,128)(2,1)} %fusion.61.refs_0_, f32[8,128]{1,0:T(8,128)} %broadcast_in_dim.99.refs_1_, bf16[256,1024]{1,0:T(8,128)(2,1)} %bitcast.184), custom_call_target="tpu_custom_call" | custom-call | tf_op jit(solution)/shard_map/gather_all/pallas_call | solution.py:539
  165.2 10.9 %attend_fwd.3 = (bf16[768,1024]{1,0:T(8,128)(2,1)S(1)}, f32[8,8,768]{2,1,0:T(8,128)S(1)}) custom-call(bf16[768,1024]{1,0:T(8,128)(2,1)S(1)} %fusion.32.q_ref, bf16[2,384,1024]{2,1,0:T(8,128)(2,1)S(1)} %project.2.refs_0_), custom_call_target="tpu_custom_call" | custom-call | flops 1000000 | bytes 100000 | tf_op jit(solution)/shard_map/attend_fwd/pallas_call | solution.py:122
  182.2 8.4 %project.3 = (bf16[768,1024]{1,0:T(8,128)(2,1)S(1)}, bf16[2,768,1024]{2,1,0:T(8,128)(2,1)S(1)}) custom-call(bf16[768,1024]{1,0:T(8,128)(2,1)S(1)} %add_convert_fusion.8.x_ref.refs_6_, bf16[1344,8,1024]{2,1,0:T(8,128)(2,1)} %bitcast.162), custom_call_target="tpu_custom_call" | custom-call | flops 1000000 | bytes 100000 | tf_op jit(solution)/shard_map/project/pallas_call | solution.py:999
  200.9 17.8 %attend_fwd.4 = (bf16[768,1024]{1,0:T(8,128)(2,1)S(1)}, f32[8,8,768]{2,1,0:T(8,128)S(1)}) custom-call(bf16[768,1024]{1,0:T(8,128)(2,1)S(1)} %get-tuple-element.87.q_ref, bf16[2,768,1024]{2,1,0:T(8,128)(2,1)} %copy-done.1, bf16[2,768,1024]{2,1,0:T(8,128)(2,1)} %copy-done.38), custom_call_target="tpu_custom_call" | custom-call | flops 1000000 | bytes 100000 | tf_op jit(solution)/shard_map/attend_fwd/pallas_call | solution.py:122
  219.5 18.0 %attend_fwd.5 = (bf16[768,1024]{1,0:T(8,128)(2,1)S(1)}, f32[8,8,768]{2,1,0:T(8,128)S(1)}) custom-call(bf16[768,1024]{1,0:T(8,128)(2,1)S(1)} %get-tuple-element.87.q_ref, bf16[2,768,1024]{2,1,0:T(8,128)(2,1)} %copy-done.1, bf16[2,768,1024]{2,1,0:T(8,128)(2,1)} %copy-done.38, ...), custom_call_target="tpu_custom_call", output_to_operand_aliasing={{0}: (3, {}), {1}: (4, {})} | custom-call | flops 1000000 | bytes 100000 | tf_op jit(solution)/shard_map/attend_fwd/pallas_call | solution.py:122
  250.0 28.8 %mlp_fwd.1 = (f32[4,768,1024]{2,1,0:T(8,128)}, bf16[4,768,1024]{2,1,0:T(8,128)(2,1)}, bf16[768,1024]{1,0:T(8,128)(2,1)}) custom-call(bf16[4,256,1024]{2,1,0:T(8,128)(2,1)} %get-tuple-element.83.refs_0_, bf16[4,256,1024]{2,1,0:T(8,128)(2,1)} %copy-done.53, bf16[4,256,1024]{2,1,0:T(8,128)(2,1)} %collective-permute-done.2.refs_2_, ...), custom_call_target="tpu_custom_call" | custom-call | flops 1000000 | bytes 100000 | tf_op jit(solution)/shard_map/mlp_fwd/pallas_call | solution.py:834
  287.9 5.7 reshape.441
  298.6 6.6 fusion.13
  319.3 19.4 %render.1 = (f32[8,128]{1,0:T(8,128)S(1)}, bf16[3,80,1024]{2,1,0:T(8,128)(2,1)S(1)}, bf16[3,80,1024]{2,1,0:T(8,128)(2,1)}, f32[80,64]{1,0:T(8,128)S(1)}, f32[64,8]{1,0:T(8,128)S(1)}) custom-call(s32[3,16,256]{2,1,0:T(8,128)S(1)} %add_select_fusion.samples_ref, bf16[3,1024,80]{2,1,0:T(8,128)(2,1)S(1)} %bitcast.158, bf16[3,1024,80]{2,1,0:T(8,128)(2,1)S(1)} %copy-done.24, ...), custom_call_target="tpu_custom_call" | custom-call | tf_op jit(solution)/shard_map/render/pallas_call | solution.py:345
  339.5 5.8 reshape.491
  362.7 7.2 convert_element_type.166
  379.4 45.4 %mlp_bwd.1 = (f32[768,1024]{1,0:T(8,128)}, bf16[16,256,1024]{2,1,0:T(8,128)(2,1)}, bf16[16,256,1024]{2,1,0:T(8,128)(2,1)}) custom-call(bf16[4,256,1024]{2,1,0:T(8,128)(2,1)} %get-tuple-element.83.refs_0_, bf16[4,256,1024]{2,1,0:T(8,128)(2,1)} %copy-done.53, bf16[4,256,1024]{2,1,0:T(8,128)(2,1)} %collective-permute-done.2.refs_2_, ...), custom_call_target="tpu_custom_call" | custom-call | flops 1000000 | bytes 100000 | tf_op jit(solution)/shard_map/mlp_bwd/pallas_call | solution.py:943
  444.4 26.6 %attend_bwd.3 = (bf16[768,1024]{1,0:T(8,128)(2,1)S(1)}, bf16[2,768,1024]{2,1,0:T(8,128)(2,1)}, bf16[2,768,1024]{2,1,0:T(8,128)(2,1)}) custom-call(bf16[768,1024]{1,0:T(8,128)(2,1)S(1)} %copy-done.7, bf16[2,768,1024]{2,1,0:T(8,128)(2,1)} %copy-done.1, bf16[2,768,1024]{2,1,0:T(8,128)(2,1)} %copy-done.38, f32[8,8,768]{2,1,0:T(8,128)S(1)} %get-tuple-element.106.refs_2_, ...), custom_call_target="tpu_custom_call" | custom-call | flops 1000000 | bytes 100000 | tf_op jit(solution)/shard_map/attend_bwd/pallas_call | solution.py:195
  471.1 27.3 %attend_bwd.4 = (bf16[768,1024]{1,0:T(8,128)(2,1)S(1)}, bf16[2,768,1024]{2,1,0:T(8,128)(2,1)}, bf16[2,768,1024]{2,1,0:T(8,128)(2,1)}) custom-call(bf16[768,1024]{1,0:T(8,128)(2,1)S(1)} %copy-done.7, bf16[2,768,1024]{2,1,0:T(8,128)(2,1)} %copy-done.1, bf16[2,768,1024]{2,1,0:T(8,128)(2,1)} %copy-done.38, ...), custom_call_target="tpu_custom_call", output_to_operand_aliasing={{0}: (6, {}), {1}: (7, {}), {2}: (8, {})} | custom-call | flops 1000000 | bytes 100000 | tf_op jit(solution)/shard_map/attend_bwd/pallas_call | solution.py:195
  504.2 6.6 bitcast_convert_fusion
  510.8 5.8 reshape.450.refs_11_
  516.7 5.8 add_convert_fusion.3
  522.5 6.2 collective-permute-done.15
  533.4 9.1 %project_back.1 = f32[768,1024]{1,0:T(8,128)S(1)} custom-call(bf16[768,1024]{1,0:T(8,128)(2,1)S(1)} %copy-done.9, bf16[2,768,1024]{2,1,0:T(8,128)(2,1)S(1)} %add_convert_fusion.1.g_ref.refs_8_, bf16[1344,8,1024]{2,1,0:T(8,128)(2,1)} %bitcast.163), custom_call_target="tpu_custom_call" | custom-call | flops 1000000 | bytes 100000 | tf_op jit(solution)/shard_map/project_back/pallas_call | solution.py:1037
  551.1 18.5 %attend_bwd.5 = (bf16[768,1024]{1,0:T(8,128)(2,1)S(1)}, bf16[2,384,1024]{2,1,0:T(8,128)(2,1)S(1)}) custom-call(bf16[768,1024]{1,0:T(8,128)(2,1)S(1)} %copy-done.21, bf16[2,384,1024]{2,1,0:T(8,128)(2,1)} %copy-done.13, f32[8,8,768]{2,1,0:T(8,128)S(1)} %get-tuple-element.116.refs_1_, bf16[768,1024]{1,0:T(8,128)(2,1)} %copy-done.18, ...), custom_call_target="tpu_custom_call" | custom-call | flops 1000000 | bytes 100000 | tf_op jit(solution)/shard_map/attend_bwd/pallas_call | solution.py:195
  590.2 18.2 %weight_grads.1 = bf16[1344,8,1024]{2,1,0:T(8,128)(2,1)} custom-call(bf16[768,1024]{1,0:T(8,128)(2,1)S(1)} %copy-done.17, bf16[768,1024]{1,0:T(8,128)(2,1)S(1)} %copy-done.26, bf16[384,768]{1,0:T(8,128)(2,1)S(1)} %copy-done.23, bf16[2,384,1024]{2,1,0:T(8,128)(2,1)S(1)} %copy-done.28, bf16[768,1024]{1,0:T(8,128)(2,1)S(1)} %copy-done.19, ...), custom_call_target="tpu_custom_call" | custom-call | flops 1000000 | bytes 100000 | tf_op jit(solution)/shard_map/weight_grads/pallas_call | solution.py:1126
  608.3 5.5 add_convert_fusion.2.refs_2_
  614.5 119.7 %scatter_sum.1 = (f32[336,1024]{1,0:T(8,128)S(1)}, f32[8,128]{1,0:T(8,128)S(1)}, bf16[512,1024]{1,0:T(8,128)(2,1)S(1)}) custom-call(bf16[10752,1024]{1,0:T(8,128)(2,1)} %bitcast.164, f32[256,128]{1,0:T(8,128)S(1)} %broadcast_in_dim.115.refs_1_, bf16[4,256,1024]{2,1,0:T(8,128)(2,1)S(1)} %add_convert_fusion.2.refs_2_), custom_call_target="tpu_custom_call" | custom-call | tf_op jit(solution)/shard_map/scatter_sum/pallas_call | solution.py:755
  (359 shorter events, 219.3 us)
Async XLA Ops:
  0.6 737.8 %copy-start = (f32[32,128,128]{2,1,0:T(8,128)S(1)}, f32[32,128,128]{2,1,0:T(8,128)}, u32[]{:S(2)}) copy-start(f32[32,128,128]{2,1,0:T(8,128)} %param.22) | copy-start | bytes 6291460
  3.1 8.5 %collective-permute-start = (bf16[57344]{0:T(1024)(128)(2,1)S(1)}, bf16[57344]{0:T(1024)(128)(2,1)S(1)}, u32[]{:S(2)}, u32[]{:S(2)}) collective-permute-start(bf16[57344]{0:T(1024)(128)(2,1)S(1)} %slice.244), channel_id=1, source_target_pairs={{1,0},{2,1},{3,2},{4,3},{5,4},{6,5},{7,6},{8,7},{9,8},{10,9},{11,1... | collective-permute-start | bytes 344072 | tf_op jit(solution)/shard_map/ppermute | solution.py:1202
  11.5 145.9 %copy-start.22 = (bf16[384,768]{1,0:T(8,128)(2,1)}, bf16[384,768]{1,0:T(8,128)(2,1)S(1)}, u32[]{:S(2)}) copy-start(bf16[384,768]{1,0:T(8,128)(2,1)S(1)} %pad.52.x_ref.refs_2_) | copy-start | bytes 1769476
  156.7 25.5 %collective-permute-start.1 = (bf16[4,256,1024]{2,1,0:T(8,128)(2,1)}, bf16[4,256,1024]{2,1,0:T(8,128)(2,1)S(1)}, u32[]{:S(2)}, u32[]{:S(2)}) collective-permute-start(bf16[4,256,1024]{2,1,0:T(8,128)(2,1)} %get-tuple-element.83.refs_0_), channel_id=1, source_target_pairs={{0,2},{1,5},{2,0},{3,7},{4,6},{5,1},{6,4},{7,3},{8,10},{9,13},{10,... | collective-permute-start | bytes 6291464 | tf_op jit(solution)/shard_map/ppermute | solution.py:1271
  190.6 28.9 %copy-start.6 = (bf16[768,1024]{1,0:T(8,128)(2,1)}, bf16[768,1024]{1,0:T(8,128)(2,1)S(1)}, u32[]{:S(2)}) copy-start(bf16[768,1024]{1,0:T(8,128)(2,1)S(1)} %get-tuple-element.87.q_ref) | copy-start | bytes 4718596
  190.7 8.6 %collective-permute-start.3 = (bf16[2,768,1024]{2,1,0:T(8,128)(2,1)S(1)}, bf16[2,768,1024]{2,1,0:T(8,128)(2,1)S(1)}, u32[]{:S(2)}, u32[]{:S(2)}) collective-permute-start(bf16[2,768,1024]{2,1,0:T(8,128)(2,1)S(1)} %get-tuple-element.88.refs_0_), channel_id=1, source_target_pairs={{0,1},{1,0},{2,3},{3,2},{4,5},{5,4},{6,7},{7,6},{8,9},{9,8},{10,11... | collective-permute-start | bytes 9437192 | tf_op jit(solution)/shard_map/ppermute | solution.py:1432
  194.0 25.5 %collective-permute-start.2 = (bf16[4,256,1024]{2,1,0:T(8,128)(2,1)}, bf16[4,256,1024]{2,1,0:T(8,128)(2,1)}, u32[]{:S(2)}, u32[]{:S(2)}) collective-permute-start(bf16[4,256,1024]{2,1,0:T(8,128)(2,1)} %get-tuple-element.83.refs_0_), channel_id=1, source_target_pairs={{0,4},{1,3},{2,6},{3,1},{4,0},{5,7},{6,2},{7,5},{8,12},{9,11},{10,... | collective-permute-start | bytes 6291464 | tf_op jit(solution)/shard_map/ppermute | solution.py:1291
  195.1 46.9 %collective-permute-start.4 = (bf16[4,256,1024]{2,1,0:T(8,128)(2,1)}, bf16[4,256,1024]{2,1,0:T(8,128)(2,1)}, u32[]{:S(2)}, u32[]{:S(2)}) collective-permute-start(bf16[4,256,1024]{2,1,0:T(8,128)(2,1)} %copy-done.53), channel_id=1, source_target_pairs={{0,4},{1,3},{2,6},{3,1},{4,0},{5,7},{6,2},{7,5},{8,12},{9,11},{10,... | collective-permute-start | bytes 6291464 | tf_op jit(solution)/shard_map/ppermute | solution.py:1299
  195.5 54.5 %collective-permute-start.5 = (bf16[4,256,1024]{2,1,0:T(8,128)(2,1)}, bf16[4,256,1024]{2,1,0:T(8,128)(2,1)}, u32[]{:S(2)}, u32[]{:S(2)}) collective-permute-start(bf16[4,256,1024]{2,1,0:T(8,128)(2,1)} %get-tuple-element.83.refs_0_), channel_id=1, source_target_pairs={{0,1},{1,0},{2,3},{3,2},{4,5},{5,4},{6,7},{7,6},{8,9},{9,8},{10,11... | collective-permute-start | bytes 6291464 | tf_op jit(solution)/shard_map/ppermute | solution.py:1307
  196.1 53.9 %collective-permute-start.6 = (bf16[4,256,1024]{2,1,0:T(8,128)(2,1)}, bf16[4,256,1024]{2,1,0:T(8,128)(2,1)}, u32[]{:S(2)}, u32[]{:S(2)}) collective-permute-start(bf16[4,256,1024]{2,1,0:T(8,128)(2,1)} %copy-done.53), channel_id=1, source_target_pairs={{0,1},{1,0},{2,3},{3,2},{4,5},{5,4},{6,7},{7,6},{8,9},{9,8},{10,11... | collective-permute-start | bytes 6291464 | tf_op jit(solution)/shard_map/ppermute | solution.py:1307
  242.0 8.0 %collective-permute-start.8 = (bf16[4,256,1024]{2,1,0:T(8,128)(2,1)}, bf16[4,256,1024]{2,1,0:T(8,128)(2,1)}, u32[]{:S(2)}, u32[]{:S(2)}) collective-permute-start(bf16[4,256,1024]{2,1,0:T(8,128)(2,1)} %collective-permute-done.4.refs_3_), channel_id=1, source_target_pairs={{0,1},{1,0},{2,3},{3,2},{4,5},{5,4},{6,7},{7,6},{8,9},{9,8},{10,11... | collective-permute-start | bytes 6291464 | tf_op jit(solution)/shard_map/ppermute | solution.py:1307
  242.9 7.1 collective-permute-start.7
  250.0 30.0 %copy-start.77 = (f32[1,3,4096]{2,0,1:T(1,128)S(1)}, f32[1,3,4096]{2,0,1:T(1,128)}, u32[]{:S(2)}) copy-start(f32[1,3,4096]{2,0,1:T(1,128)} %param.30) | copy-start | bytes 147460
  279.9 18.6 %collective-permute-start.9 = (bf16[3,1,32,1024]{3,2,1,0:T(8,128)(2,1)S(1)}, bf16[3,1,32,1024]{3,2,1,0:T(8,128)(2,1)S(1)}, u32[]{:S(2)}, u32[]{:S(2)}) collective-permute-start(bf16[3,1,32,1024]{3,2,1,0:T(8,128)(2,1)S(1)} %slice_select_fusion.1), channel_id=1, source_target_pairs={{0,1},{1,0},{2,3},{3,2},{4,5},{5,4},{6,7},{7,6},{8,9},{9,8},{10,11... | collective-permute-start | bytes 589832 | tf_op jit(solution)/shard_map/ppermute | solution.py:1443
  309.0 7.0 collective-permute-start.10
  339.5 5.8 collective-permute-start.11
  375.1 1.6 collective-permute-start.12
  379.4 46.4 %copy-start.32 = (f32[768,1024]{1,0:T(8,128)S(1)}, f32[768,1024]{1,0:T(8,128)}, u32[]{:S(2)}) copy-start(f32[768,1024]{1,0:T(8,128)} %copy-done.31) | copy-start | bytes 9437188
  424.8 14.0 %collective-permute-start.13 = (bf16[16,256,1024]{2,1,0:T(8,128)(2,1)}, bf16[16,256,1024]{2,1,0:T(8,128)(2,1)S(1)}, u32[]{:S(2)}, u32[]{:S(2)}) collective-permute-start(bf16[16,256,1024]{2,1,0:T(8,128)(2,1)} %get-tuple-element.102), channel_id=1, source_target_pairs={{0,1},{1,0},{2,3},{3,2},{4,5},{5,4},{6,7},{7,6},{8,9},{9,8},{10,11... | collective-permute-start | bytes 25165832 | tf_op jit(solution)/shard_map/ppermute | solution.py:1316
  443.3 27.7 %collective-permute-start.14 = (bf16[4,256,1024]{2,1,0:T(8,128)(2,1)S(1)}, bf16[4,256,1024]{2,1,0:T(8,128)(2,1)S(1)}, u32[]{:S(2)}, u32[]{:S(2)}) collective-permute-start(bf16[4,256,1024]{2,1,0:T(8,128)(2,1)S(1)} %get-tuple-element.104), channel_id=1, source_target_pairs={{0,4},{1,3},{2,6},{3,1},{4,0},{5,7},{6,2},{7,5},{8,12},{9,11},{10,... | collective-permute-start | bytes 6291464 | tf_op jit(solution)/shard_map/ppermute | solution.py:1329
  499.6 30.2 %collective-permute-start.17 = (bf16[2,768,1024]{2,1,0:T(8,128)(2,1)}, bf16[2,768,1024]{2,1,0:T(8,128)(2,1)}, u32[]{:S(2)}, u32[]{:S(2)}) collective-permute-start(bf16[2,768,1024]{2,1,0:T(8,128)(2,1)} %get-tuple-element.119), channel_id=1, source_target_pairs={{0,1},{1,0},{2,3},{3,2},{4,5},{5,4},{6,7},{7,6},{8,9},{9,8},{10,11... | collective-permute-start | bytes 9437192 | tf_op jit(solution)/shard_map/ppermute | solution.py:1493
  503.3 25.5 %collective-permute-start.15 = (bf16[4,256,1024]{2,1,0:T(8,128)(2,1)}, bf16[4,256,1024]{2,1,0:T(8,128)(2,1)}, u32[]{:S(2)}, u32[]{:S(2)}) collective-permute-start(bf16[4,256,1024]{2,1,0:T(8,128)(2,1)} %get-tuple-element.110), channel_id=1, source_target_pairs={{0,4},{1,3},{2,6},{3,1},{4,0},{5,7},{6,2},{7,5},{8,12},{9,11},{10,... | collective-permute-start | bytes 6291464 | tf_op jit(solution)/shard_map/ppermute | solution.py:1336
  528.8 40.8 %collective-permute-start.16 = (bf16[4,256,1024]{2,1,0:T(8,128)(2,1)}, bf16[4,256,1024]{2,1,0:T(8,128)(2,1)}, u32[]{:S(2)}, u32[]{:S(2)}) collective-permute-start(bf16[4,256,1024]{2,1,0:T(8,128)(2,1)} %add_convert_fusion.3), channel_id=1, source_target_pairs={{0,2},{1,5},{2,0},{3,7},{4,6},{5,1},{6,4},{7,3},{8,10},{9,13},{10,... | collective-permute-start | bytes 6291464 | tf_op jit(solution)/shard_map/ppermute | solution.py:1343
  761.3 12.6 %collective-permute-start.18 = (f32[57344]{0:T(1024)}, f32[57344]{0:T(1024)S(1)}, u32[]{:S(2)}, u32[]{:S(2)}) collective-permute-start(f32[57344]{0:T(1024)} %bitcast.75), channel_id=1, source_target_pairs={{0,1},{1,2},{2,3},{3,4},{4,5},{5,6},{6,7},{7,8},{8,9},{9,10},{10,1... | collective-permute-start | bytes 688136 | tf_op jit(solution)/shard_map/ppermute | solution.py:1220
  (83 other events, 526.8 us)

commit v4 on v3

--- a/solution.py
+++ b/solution.py
@@ -59,19 +59,6 @@
 
 def gelu_tanh(value):
     return jax.nn.gelu(value, approximate=True)
-
-
-def assemble(ydc):
-    planes, rows, cols, _ = ydc.shape
-    inner = rows - 2
-    kernel = ydc.reshape(planes, rows, cols, 4, 4, -1)
-    even = kernel[:, 1 : inner + 1, :, 1] + kernel[:, 0:inner, :, 3]
-    odd = kernel[:, 1 : inner + 1, :, 2] + kernel[:, 2 : inner + 2, :, 0]
-    tall = jnp.stack([even, odd], 2)
-    wide = jnp.pad(tall, ((0, 0), (0, 0), (0, 0), (1, 1), (0, 0), (0, 0)))
-    left_cols = wide[:, :, :, 1 : cols + 1, 1] + wide[:, :, :, 0:cols, 3]
-    right_cols = wide[:, :, :, 1 : cols + 1, 2] + wide[:, :, :, 2 : cols + 2, 0]
-    return jnp.stack([left_cols, right_cols], 4).reshape(planes, 2 * inner, 2 * cols, -1)
 
 
 PAIR = 2 * HEAD_DIM
@@ -705,16 +692,18 @@
     for copy in line_sends:
         copy.start()
     line_load.start()
-    steps = [(stagger * (len(jobs) - 1) + 11, -1, -2)]
     for job in range(len(jobs)):
-        for i in range(-1, 16):
-            steps.append((stagger * job + i, job, i))
+        for n in range(AHEAD):
+            start(n, job)
+    steps = []
+    for job in range(len(jobs)):
+        begin = stagger * min(job, layouts[0][0] - 1)
+        for i in range(16):
+            steps.append((begin + i + 2 * (i // 4 - 1) * (i // 8), job, i))
+    steps.append((max(steps)[0] - 6, 0, -1))
     for _, job, i in sorted(steps):
-        if i == -2:
+        if i < 0:
             line_finish()
-        elif i < 0:
-            for n in range(AHEAD):
-                start(n, job)
         else:
             step(i, job)
     for job in range(len(jobs)):
@@ -958,6 +947,192 @@
     )(*panels, hidden, grad, up, act)
 
 
+SLOT = 128
+TAPS = 16
+
+
+def spread_deconv_kernel(first, rows_ref, o_ref, raw, flat, turned, sem):
+    load = pltpu.make_async_copy(rows_ref.at[pl.ds(first, raw.shape[0])], raw, sem)
+    load.start()
+    load.wait()
+    whole = raw[...].reshape(TAPS * CH, WIDE).astype(jnp.float32)
+    for n in range(WIDE // SLOT):
+        flat[n] = whole[:, n * SLOT : (n + 1) * SLOT]
+    lane = lax.broadcasted_iota(jnp.int32, (D // 4, SLOT), 1)
+
+    def block(i, j):
+        at = 10 * i + j
+        return flat[at % 8, pl.ds(at // 8, D // 4, stride=5), :]
+
+    for tap in range(TAPS):
+        j, start = divmod(tap * CH, SLOT)
+        for i in range(4):
+            part = block(i, j)
+            if start:
+                part = pltpu.roll(part, SLOT - start, 1)
+            if start + CH > SLOT:
+                part = jnp.where(lane < SLOT - start, part, pltpu.roll(block(i, j + 1), SLOT - start, 1))
+            turned[pl.ds(i, D // 4, stride=4), :] = jnp.where(lane < CH, part, 0.0)
+        o_ref[:, tap * SLOT : (tap + 1) * SLOT] = turned[...].astype(jnp.bfloat16)
+
+
+def spread_deconv(rows, first):
+    return pl.pallas_call(
+        functools.partial(spread_deconv_kernel, first),
+        in_specs=[pl.BlockSpec(memory_space=pl.ANY)],
+        out_specs=pl.BlockSpec(memory_space=pltpu.VMEM),
+        out_shape=jax.ShapeDtypeStruct((D, TAPS * SLOT), jnp.bfloat16),
+        scratch_shapes=[
+            pltpu.VMEM((TAPS * CH // 8, 8, WIDE), jnp.bfloat16),
+            pltpu.VMEM((WIDE // SLOT, TAPS * CH, SLOT), jnp.float32),
+            pltpu.VMEM((D, SLOT), jnp.float32),
+            pltpu.SemaphoreType.DMA,
+        ],
+        compiler_params=pltpu.CompilerParams(vmem_limit_bytes=32 * 1024 * 1024),
+        name="spread_deconv",
+    )(rows)
+
+
+def with_edges(own, edge):
+    place = lax.axis_index("strip")
+    above = jnp.where(place == 0, jnp.zeros_like(edge), edge)
+    below = jnp.where(place == 0, edge, jnp.zeros_like(edge))
+    return jnp.concatenate([above, own, below], 0)
+
+
+def moved(value, step):
+    column = lax.broadcasted_iota(jnp.int32, value.shape, 0) % TC
+    inside = (column + step >= 0) & (column + step < TC)
+    return jnp.where(inside, pltpu.roll(value, (-step) % value.shape[0], 0), 0.0)
+
+
+def deconv_fwd_kernel(grid_ref, edge_ref, w_ref, o_ref, taps, fine):
+    padded = with_edges(grid_ref[0], edge_ref[0])
+    rows = grid_ref.shape[1]
+    taps[...] = product(padded, w_ref[...])
+
+    def tap(kr, kc, r):
+        slot = kr * 4 + kc
+        return taps[pl.ds((r + 1) * TC, rows), slot * SLOT : (slot + 1) * SLOT]
+
+    for i in range(2):
+        for j in range(2):
+            total = tap(i + 1, j + 1, 0) + tap(3 - 3 * i, j + 1, 2 * i - 1)
+            side = tap(i + 1, 3 - 3 * j, 0) + tap(3 - 3 * i, 3 - 3 * j, 2 * i - 1)
+            total = total + moved(side, 2 * j - 1)
+            for a in range(rows // TC):
+                fine[pl.ds((2 * a + i) * 2 * TC + j, TC, stride=2), :] = total[a * TC : (a + 1) * TC]
+    o_ref[0] = fine[...].astype(jnp.bfloat16)
+
+
+def deconv_fwd(grid, edge, weights):
+    planes, rows, _ = grid.shape
+    return pl.pallas_call(
+        deconv_fwd_kernel,
+        grid=(planes,),
+        in_specs=[
+            pl.BlockSpec((1, rows, D), lambda n: (n, 0, 0)),
+            pl.BlockSpec((1, TC, D), lambda n: (n, 0, 0)),
+            pl.BlockSpec(weights.shape, lambda n: (0, 0)),
+        ],
+        out_specs=pl.BlockSpec((1, 4 * rows, SLOT), lambda n: (n, 0, 0)),
+        out_shape=jax.ShapeDtypeStruct((planes, 4 * rows, SLOT), jnp.bfloat16),
+        scratch_shapes=[
+            pltpu.VMEM((rows + 2 * TC, TAPS * SLOT), jnp.float32),
+            pltpu.VMEM((4 * rows, SLOT), jnp.float32),
+        ],
+        compiler_params=pltpu.CompilerParams(vmem_limit_bytes=40 * 1024 * 1024),
+        name="deconv_fwd",
+    )(grid, edge, weights)
+
+
+def deconv_bwd_kernel(own_ref, got_ref, grid_ref, edge_ref, w_ref, gx_ref, gedge_ref, gw_ref, fine, spread, tokens, sums, flat):
+    plane = pl.program_id(0)
+    rows = grid_ref.shape[1]
+    high = rows + 2 * TC
+    place = lax.axis_index("strip")
+    total = own_ref[0].astype(jnp.float32) + got_ref[0].astype(jnp.float32)
+    total = jnp.concatenate([total, jnp.zeros((SLOT - CH, total.shape[1]), jnp.float32)], 0)
+    fine[...] = total.T
+    here = pl.ds(plane * high, high)
+    tokens[here] = with_edges(grid_ref[0], edge_ref[0])
+    for i in range(2):
+        for j in range(2):
+            parts = [fine[pl.ds((2 * a + i) * 2 * TC + j, TC, stride=2), :] for a in range(rows // TC)]
+            part = jnp.concatenate(parts, 0)
+            for kr in (i + 1, 3 - 3 * i):
+                for kc in (j + 1, 3 - 3 * j):
+                    value = part if kc == j + 1 else moved(part, 1 - 2 * j)
+                    start = TC if kr == i + 1 else (0 if i == 0 else 2 * TC)
+                    pieces = [value]
+                    if start:
+                        pieces.insert(0, jnp.zeros((start, SLOT), jnp.float32))
+                    if high - rows - start:
+                        pieces.append(jnp.zeros((high - rows - start, SLOT), jnp.float32))
+                    slot = kr * 4 + kc
+                    spread[here, slot * SLOT : (slot + 1) * SLOT] = jnp.concatenate(pieces, 0).astype(jnp.bfloat16)
+    back = nt_dot(spread[here], w_ref[...])
+    gx_ref[0] = back[TC : TC + rows]
+    gedge_ref[0] = jnp.where(place == 0, back[TC + rows :], back[:TC]).astype(jnp.bfloat16)
+
+    @pl.when(plane == pl.num_programs(0) - 1)
+    def _():
+        wide = 512
+        for n in range(TAPS * SLOT // wide):
+            columns = slice(n * wide, (n + 1) * wide)
+            part = lax.dot_general(
+                tokens[...], spread[:, columns], (((0,), (0,)), ((), ())), preferred_element_type=jnp.float32
+            )
+            for m in range(wide // SLOT):
+                sums[n * (wide // SLOT) + m] = part[:, m * SLOT : (m + 1) * SLOT]
+        lane = lax.broadcasted_iota(jnp.int32, (D // 4, SLOT), 1)
+        for i in range(4):
+            for j in range(TAPS * CH // SLOT):
+                block = None
+                for tap in range(j * SLOT // CH, (j * SLOT + SLOT - 1) // CH + 1):
+                    part = sums[tap, pl.ds(i, D // 4, stride=4), :]
+                    shift = tap * CH - j * SLOT
+                    if shift % SLOT:
+                        part = pltpu.roll(part, shift % SLOT, 1)
+                    block = part if block is None else jnp.where(lane < shift, block, part)
+                at = 10 * i + j
+                flat[at % 8, pl.ds(at // 8, D // 4, stride=5), :] = block
+        whole = jnp.concatenate([flat[n] for n in range(WIDE // SLOT)], 1)
+        gw_ref[...] = whole.astype(jnp.bfloat16).reshape(gw_ref.shape)
+
+
+def deconv_bwd(own, got, grid, edge, weights):
+    planes, rows, _ = grid.shape
+    high = rows + 2 * TC
+    by_plane = lambda *shape: pl.BlockSpec((1,) + shape, lambda n: (n, 0, 0))
+    return pl.pallas_call(
+        deconv_bwd_kernel,
+        grid=(planes,),
+        in_specs=[
+            by_plane(*own.shape[1:]),
+            by_plane(*got.shape[1:]),
+            by_plane(rows, D),
+            by_plane(TC, D),
+            pl.BlockSpec(weights.shape, lambda n: (0, 0)),
+        ],
+        out_specs=[by_plane(rows, D), by_plane(TC, D), pl.BlockSpec((TAPS * CH // 8, 8, WIDE), lambda n: (0, 0, 0))],
+        out_shape=[
+            jax.ShapeDtypeStruct((planes, rows, D), jnp.float32),
+            jax.ShapeDtypeStruct((planes, TC, D), jnp.bfloat16),
+            jax.ShapeDtypeStruct((TAPS * CH // 8, 8, WIDE), jnp.bfloat16),
+        ],
+        scratch_shapes=[
+            pltpu.VMEM((4 * rows, SLOT), jnp.float32),
+            pltpu.VMEM((planes * high, TAPS * SLOT), jnp.bfloat16),
+            pltpu.VMEM((planes * high, D), jnp.bfloat16),
+            pltpu.VMEM((TAPS, D, SLOT), jnp.float32),
+            pltpu.VMEM((WIDE // SLOT, TAPS * CH, SLOT), jnp.float32),
+        ],
+        compiler_params=pltpu.CompilerParams(vmem_limit_bytes=56 * 1024 * 1024),
+        name="deconv_bwd",
+    )(own, got, grid, edge, weights)
+
+
 def panel_view(rows_ref, first, count, depth):
     region = rows_ref.at[pl.ds(first, depth // 8 * count)]
     return region.reshape(depth // 8, count, 8, WIDE)
@@ -1138,7 +1313,7 @@
             pltpu.SemaphoreType.DMA((2,)),
             pltpu.SemaphoreType.DMA((len(copies), 2)),
         ],
-        compiler_params=pltpu.CompilerParams(vmem_limit_bytes=40 * 1024 * 1024),
+        compiler_params=pltpu.CompilerParams(vmem_limit_bytes=60 * 1024 * 1024),
         cost_estimate=BRIEF,
         name="weight_grads",
     )(*arrays)
@@ -1184,45 +1359,208 @@
     return jnp.where(in_kv, turned(2), jnp.where(in_qkv, turned(3), rows))
 
 
-def device_place():
-    return lax.axis_index("dp") * lax.axis_size("strip") + lax.axis_index("strip")
-
-
 def tile_rows(length):
     return -(-length // (6 * TILE)) * 6
 
 
-def align(shard):
-    length = shard.shape[0]
-    size = tile_rows(length) * TILE
-    extra = size - length
-    reach = -(-32 * extra // WIDE) * WIDE
-    place = device_place()
-    shard = shard.astype(jnp.bfloat16)
-    following = lax.ppermute(shard[:reach], AXES, [(n + 1, n) for n in range(31)])
-    joined = jnp.concatenate([shard, following])
-    shift = place * extra
-    at = place * size + lax.iota(jnp.int32, size)
-    parts = [
-        lax.dynamic_slice_in_dim(joined, jnp.maximum(shift - gap, 0), size)
-        for gap in (0, QKV_GAP, QKV_GAP + END_GAP)
-    ]
-    rows = jnp.where(at < QKV_AT, parts[0], jnp.where(at < GAP_AT + QKV_GAP, parts[1], parts[2]))
-    return regroup(rows.reshape(-1, WIDE), place * (size // TILE), False)
-
-
-def unalign(summed, length):
-    size = summed.size
-    extra = size - length
-    reach = -(-32 * extra // WIDE) * WIDE
-    place = device_place()
-    summed = regroup(summed, place * (size // TILE), True).reshape(-1)
-    before = lax.ppermute(summed[size - reach :], AXES, [(n, n + 1) for n in range(31)])
-    joined = jnp.concatenate([before, summed])
-    shift = reach - place * extra
-    at = place * length + lax.iota(jnp.int32, length)
-    parts = [lax.dynamic_slice_in_dim(joined, shift + gap, length) for gap in (0, QKV_GAP, QKV_GAP + END_GAP)]
-    return jnp.where(at < QKV_AT, parts[0], jnp.where(at < GAP_AT, parts[1], parts[2]))
+LANES = 128
+TILE_LINES = TILE // LANES
+
+
+def tile_place(tile):
+    gap = QKV_GAP // LANES * jnp.where(tile >= TILES["gap"], 1, 0)
+    return gap + END_GAP // LANES * jnp.where(tile >= TILES["modulate"], 1, 0)
+
+
+def by_region(tile, work):
+    in_kv = (tile >= TILES["keyval_cross"]) & (tile < TILES["out_cross"])
+    in_qkv = (tile >= TILES["qkv_self"]) & (tile < TILES["out_self"])
+
+    @pl.when(in_kv)
+    def _():
+        work(2)
+
+    @pl.when(in_qkv)
+    def _():
+        work(3)
+
+    @pl.when(jnp.logical_not(in_kv | in_qkv))
+    def _():
+        work(1)
+
+
+def tile_lines(tile, first, panels):
+    panel = lax.rem(tile, panels)
+    return (tile - panel - first) * TILE_LINES + panel * 8
+
+
+def prepare_kernel(own_ref, next_ref, blocks_ref, o_ref, chunks_ref, lines, tiles, sem):
+    half = tiles.shape[0]
+    core = lax.axis_index("strip")
+    load = pltpu.make_async_copy(blocks_ref.at[pl.ds(core * half, half)], tiles, sem)
+    load.start()
+    place = lax.axis_index("dp") * 2 + core
+    count = own_ref.shape[0]
+    lines[:count] = own_ref[...]
+    lines[count : count + next_ref.shape[0]] = next_ref[...]
+    held = o_ref.shape[0] // 8
+    first = place * held
+    shift = place * (held * TILE_LINES - count)
+
+    @pl.loop(0, held // 2)
+    def _(n):
+        def work(panels):
+            rows = []
+            for m in range(2):
+                tile = first + 2 * n + m
+                start = tile_lines(tile, first, panels) + shift - tile_place(tile)
+                rows.append(jnp.concatenate([lines[pl.ds(start + j, 8, stride=8 * panels), :] for j in range(8)], 1))
+            o_ref[pl.ds(pl.multiple_of(16 * n, 16), 16)] = jnp.concatenate(rows, 0).astype(jnp.bfloat16)
+
+        by_region(first + 2 * n, work)
+
+    load.wait()
+    for n in range(half):
+        at, column = n // 8 * BLOCK, n % 8 * BLOCK
+        chunks_ref[at : at + BLOCK, column : column + BLOCK] = tiles[n].astype(jnp.bfloat16)
+
+
+def prepare(weights, blocks):
+    lines = weights.reshape(-1, LANES)
+    count = lines.shape[0]
+    held = tile_rows(weights.shape[0])
+    reach = -(-32 * (held * TILE_LINES - count) // 8) * 8
+    following = lax.ppermute(lines[:reach], AXES, [(n + 1, n) for n in range(31)])
+    half = blocks.shape[0] // 2
+    vmem = pl.BlockSpec(memory_space=pltpu.VMEM)
+    return pl.pallas_call(
+        prepare_kernel,
+        in_specs=[vmem, vmem, pl.BlockSpec(memory_space=pl.ANY)],
+        out_specs=[vmem, vmem],
+        out_shape=[
+            jax.ShapeDtypeStruct((held * 8, WIDE), jnp.bfloat16),
+            jax.ShapeDtypeStruct((half // 8 * BLOCK, WIDE), jnp.bfloat16),
+        ],
+        scratch_shapes=[
+            pltpu.VMEM((-(-(count + reach) // 8) * 8, LANES), jnp.float32),
+            pltpu.VMEM((half, BLOCK, BLOCK), jnp.float32),
+            pltpu.SemaphoreType.DMA,
+        ],
+        compiler_params=pltpu.CompilerParams(vmem_limit_bytes=16 * 1024 * 1024),
+        name="prepare",
+    )(lines, following, blocks)
+
+
+def ungroup_kernel(rows_ref, o_ref):
+    place = lax.axis_index("dp") * 2 + lax.axis_index("strip")
+    held = rows_ref.shape[0] // 8
+    first = place * held
+
+    @pl.loop(0, held)
+    def _(n):
+        def work(panels):
+            start = tile_lines(first + n, first, panels)
+            at = pl.ds(pl.multiple_of(8 * n, 8), 8)
+            for j in range(8):
+                o_ref[pl.ds(start + j, 8, stride=8 * panels), :] = rows_ref[at, j * LANES : (j + 1) * LANES]
+
+        by_region(first + n, work)
+
+
+def ungroup(rows):
+    vmem = pl.BlockSpec(memory_space=pltpu.VMEM)
+    return pl.pallas_call(
+        ungroup_kernel,
+        in_specs=[vmem],
+        out_specs=vmem,
+        out_shape=jax.ShapeDtypeStruct((rows.size // LANES, LANES), jnp.float32),
+        compiler_params=pltpu.CompilerParams(vmem_limit_bytes=16 * 1024 * 1024),
+        name="ungroup",
+    )(rows)
+
+
+def adam_kernel(before_ref, sum_ref, w_ref, first_ref, second_ref, nw_ref, nfirst_ref, nsecond_ref, lines):
+    place = lax.axis_index("dp") * 2 + lax.axis_index("strip")
+    reach, summed, count = before_ref.shape[0], sum_ref.shape[0], w_ref.shape[0]
+    lines[:reach] = before_ref[...]
+    lines[reach : reach + summed] = sum_ref[...]
+    shift = reach - place * (summed - count)
+    gaps = (0, QKV_GAP // LANES, (QKV_GAP + END_GAP) // LANES)
+
+    def update(at, rows):
+        parts = [lines[pl.ds(shift + at + gap, rows), :] for gap in gaps]
+        line = place * count + at + lax.broadcasted_iota(jnp.int32, (rows, LANES), 0)
+        grad = jnp.where(line < QKV_AT // LANES, parts[0], jnp.where(line < GAP_AT // LANES, parts[1], parts[2]))
+        here = pl.ds(at, rows)
+        weights = w_ref[here]
+        first = BETA_FIRST * first_ref[here] + (1.0 - BETA_FIRST) * grad
+        second = BETA_SECOND * second_ref[here] + (1.0 - BETA_SECOND) * grad * grad
+        nfirst_ref[here] = first
+        nsecond_ref[here] = second
+        fix_first = 1.0 - BETA_FIRST**ADAM_STEP
+        fix_second = 1.0 - BETA_SECOND**ADAM_STEP
+        step = first / fix_first / (jnp.sqrt(second / fix_second) + ADAM_EPS)
+        nw_ref[here] = weights - ADAM_RATE * (step + WEIGHT_DECAY * weights)
+
+    block = 32
+
+    @pl.loop(0, count // block)
+    def _(n):
+        update(pl.multiple_of(block * n, block), block)
+
+    if count % block:
+        update(count - count % block, count % block)
+
+
+def adam(rows, weights, first_moment, second_moment):
+    length = weights.shape[0]
+    count = length // LANES
+    summed = ungroup(rows)
+    reach = -(-32 * (summed.shape[0] - count) // 8) * 8
+    before = lax.ppermute(summed[summed.shape[0] - reach :], AXES, [(n, n + 1) for n in range(31)])
+    vmem = pl.BlockSpec(memory_space=pltpu.VMEM)
+    gap = (QKV_GAP + END_GAP) // LANES
+    results = pl.pallas_call(
+        adam_kernel,
+        in_specs=[vmem] * 5,
+        out_specs=[vmem] * 3,
+        out_shape=[jax.ShapeDtypeStruct((count, LANES), jnp.float32)] * 3,
+        scratch_shapes=[pltpu.VMEM((-(-(reach + summed.shape[0] + gap) // 8) * 8, LANES), jnp.float32)],
+        compiler_params=pltpu.CompilerParams(vmem_limit_bytes=32 * 1024 * 1024),
+        name="adam",
+    )(before, summed, *(a.reshape(count, LANES) for a in (weights, first_moment, second_moment)))
+    return [result.reshape(length) for result in results]
+
+
+def shampoo_kernel(tiles_ref, blocks_ref, sl_ref, sr_ref, rl_ref, rr_ref, nb_ref, g_ref, nl_ref, nr_ref, rms_ref):
+    for n in range(8):
+        grad = tiles_ref[:, n * BLOCK : (n + 1) * BLOCK]
+        wide = grad.astype(jnp.float32)
+        g_ref[n] = wide
+        nl_ref[n] = STAT_DECAY * sl_ref[n] + (1.0 - STAT_DECAY) * nt_dot(grad, grad)
+        square = lax.dot_general(grad, grad, (((0,), (0,)), ((), ())), preferred_element_type=jnp.float32)
+        nr_ref[n] = STAT_DECAY * sr_ref[n] + (1.0 - STAT_DECAY) * square
+        half = jnp.dot(wide, rr_ref[n], precision=HIGHEST_MODE, preferred_element_type=jnp.float32)
+        cond = jnp.dot(rl_ref[n], half, precision=HIGHEST_MODE, preferred_element_type=jnp.float32)
+        rms = jnp.sqrt(jnp.mean(cond * cond, axis=(0, 1), keepdims=True) + RMS_EPS)
+        nb_ref[n] = blocks_ref[n] - SHAMPOO_RATE * cond / rms
+        rms_ref[n : n + 1] = jnp.broadcast_to(rms, (1, LANES))
+
+
+def shampoo(chunks, blocks, stat_left, stat_right, root_left, root_right):
+    count = blocks.shape[0]
+    eight = pl.BlockSpec((8, BLOCK, BLOCK), lambda n: (n, 0, 0))
+    whole = jax.ShapeDtypeStruct(blocks.shape, jnp.float32)
+    *results, rms = pl.pallas_call(
+        shampoo_kernel,
+        grid=(count // 8,),
+        in_specs=[pl.BlockSpec((BLOCK, WIDE), lambda n: (n, 0))] + [eight] * 5,
+        out_specs=[eight] * 4 + [pl.BlockSpec((8, LANES), lambda n: (n, 0))],
+        out_shape=[whole] * 4 + [jax.ShapeDtypeStruct((count, LANES), jnp.float32)],
+        compiler_params=pltpu.CompilerParams(vmem_limit_bytes=60 * 1024 * 1024),
+        name="shampoo",
+    )(chunks, blocks, stat_left, stat_right, root_left, root_right)
+    return *results, rms[:, 0]
 
 
 def chunks_of(tiles):
@@ -1260,12 +1598,8 @@
 
 
 def gather_weights(weights, blocks, part):
-    length = weights.shape[0]
     if direct_links():
-        own = align(weights)
-        half = blocks.shape[0] // 2
-        tiles = lax.dynamic_slice_in_dim(blocks, lax.axis_index("strip") * half, half)
-        tiles = chunks_of(tiles.astype(jnp.bfloat16))
+        own, tiles = prepare(weights, blocks)
         meta = jnp.full((8, 128), part, jnp.float32)
         rows, parts, line = gather_all([flat_chunks(own.shape[0], 3), META], 6, [own, meta], tiles, 0)
         near = lax.ppermute(line, AXES, NEAR)
@@ -1315,8 +1649,7 @@
             self.mine = grads[0]
             self.got = lax.ppermute(grads[1], AXES, CORE)
 
-    def added(self, g, *parts):
-        at = slice(4 * g, 4 * g + 4)
+    def added(self, at, *parts):
         total = self.mine[at].astype(jnp.float32) + self.got[at].astype(jnp.float32)
         for part in parts:
             total = total + part.astype(jnp.float32)
@@ -1325,39 +1658,33 @@
     def first(self, before):
         if not self.staged:
             return before
-        both, self.far, before = lax.optimization_barrier((self.added(3), self.added(2), before))
-        self.to_near = lax.ppermute(both, AXES, FAR)
+        away, before = lax.optimization_barrier((self.added(slice(8, 16)), before))
+        self.away = lax.ppermute(away, AXES, FAR)
         return before
 
     def second(self, before):
         if not self.staged:
             return before
-        self.to_near, self.far, before = lax.optimization_barrier((self.to_near, self.far, before))
-        self.to_own = lax.ppermute(self.far, AXES, FAR)
+        self.away, before = lax.optimization_barrier((self.away, before))
+        near, before = lax.optimization_barrier((self.added(slice(4, 8), self.away[4:]), before))
+        self.last = lax.ppermute(near, AXES, NEAR)
         return before
 
     def third(self, before):
         if not self.staged:
             return before
-        near, self.to_own, before = lax.optimization_barrier((self.added(1, self.to_near), self.to_own, before))
-        self.last = lax.ppermute(near, AXES, NEAR)
+        self.last, before = lax.optimization_barrier((self.last, before))
+        self.parts = [self.added(slice(0, 4), self.away[:4], self.last)]
         return before
 
-    def fourth(self, before):
-        if not self.staged:
-            return before
-        self.last, before = lax.optimization_barrier((self.last, before))
-        self.parts = [self.added(0, self.to_own, self.last)]
-        return before
-
-
-def reduce_grads(rows, panels, part, length):
-    if direct_links():
-        meta = jnp.full((32 * 8, 128), part, jnp.float32)
-        summed, parts, tiles = scatter_sum(
-            [flat_chunks(rows.shape[0] // 32, 3), META], 6, [rows, meta], panels[0], 1
-        )
-        return unalign(summed, length), tiles_of(tiles).astype(jnp.float32), parts[0, 0]
+
+def reduce_grads(rows, panels, part):
+    meta = jnp.full((32 * 8, 128), part, jnp.float32)
+    summed, parts, tiles = scatter_sum([flat_chunks(rows.shape[0] // 32, 3), META], 6, [rows, meta], panels[0], 1)
+    return summed, tiles, parts[0, 0]
+
+
+def reduce_grads_plainly(rows, panels, part, length):
     flat = regroup(rows, 0, True).astype(jnp.float32).reshape(-1)
     flat = jnp.concatenate(
         [flat[:QKV_AT], flat[QKV_AT + QKV_GAP : GAP_AT + QKV_GAP], flat[GAP_AT + QKV_GAP + END_GAP :]]
@@ -1368,7 +1695,16 @@
     flat_sum = lax.psum_scatter(flat, AXES, scatter_dimension=0, tiled=True)
     tile_sum = lax.psum_scatter(tiles, AXES, scatter_dimension=0, tiled=True)
     tile_sum = lax.all_gather(tile_sum.astype(jnp.bfloat16), "strip", axis=0, tiled=True)
-    return flat_sum, tile_sum.astype(jnp.float32), lax.psum(part, AXES)
+    return flat_sum, chunks_of(tile_sum), lax.psum(part, AXES)
+
+
+def adam_plainly(grad, weights, first_moment, second_moment):
+    new_first = BETA_FIRST * first_moment + (1.0 - BETA_FIRST) * grad
+    new_second = BETA_SECOND * second_moment + (1.0 - BETA_SECOND) * grad * grad
+    fix_first = 1.0 - BETA_FIRST**ADAM_STEP
+    fix_second = 1.0 - BETA_SECOND**ADAM_STEP
+    moved = new_first / fix_first / (jnp.sqrt(new_second / fix_second) + ADAM_EPS)
+    return weights - ADAM_RATE * (moved + WEIGHT_DECAY * weights), new_first, new_second
 
 
 def shards(
@@ -1401,7 +1737,7 @@
     def plain(name, count):
         return rows[TILES[name] * 8 : TILES[name] * 8 + count]
 
-    deconv = plain("deconv", 16 * CH).reshape(D, 16 * CH)
+    deconv = spread_deconv(tiled, TILES["deconv"])
     decode = plain("decode", 8).reshape(-1)
     decode_in = decode[: CH * DEC_HID].reshape(CH, DEC_HID)
     decode_out = decode[CH * DEC_HID : CH * DEC_HID + DEC_HID * 4].reshape(DEC_HID, 4)
@@ -1439,15 +1775,9 @@
     hidden3, norm_three = jax.vjp(norm_mod, stream2, mods[4], mods[5])
     hidden3 = hidden3.astype(jnp.bfloat16)
     up, act, grid = mlp_fwd(panels, hidden3, stream2)
-    grid = grid.reshape(3, PR, -1, D)
-    edge = lax.ppermute(jnp.where(place == 0, grid[:, -1:], grid[:, :1]), "strip", SWAP)
-    nothing = jnp.zeros_like(edge)
-    padded = jnp.concatenate(
-        [jnp.where(place == 0, nothing, edge), grid, jnp.where(place == 0, edge, nothing)], 1
-    )
-    ydc = jnp.einsum("prcd,dk->prck", padded, deconv, preferred_element_type=jnp.float32)
-    feature, assemble_back = jax.vjp(assemble, ydc)
-    cells = feature.astype(jnp.bfloat16).reshape(3, -1, CH)
+    grid = grid.reshape(3, own_rows, D)
+    edge = lax.ppermute(jnp.where(place == 0, grid[:, -TC:], grid[:, :TC]), "strip", SWAP)
+    cells = deconv_fwd(grid, edge, deconv)
     cells_far = lax.ppermute(cells, "strip", SWAP)
     rays = pixel.shape[0]
     factor = 1.0 / jnp.maximum(count, 1.0)
@@ -1464,18 +1794,11 @@
     )
     loss_part = loss_part[0, 0]
     grad_decode_out = grad_decode_out[:, :4]
-    grad_cells = grad_cells.astype(jnp.float32) + lax.ppermute(grad_far, "strip", SWAP).astype(jnp.float32)
-    grad_feature = grad_cells.astype(jnp.bfloat16).transpose(0, 2, 1).reshape(feature.shape)
-    grad_feature = lax.optimization_barrier(grad_feature).astype(jnp.float32)
-    (grad_ydc,) = assemble_back(grad_feature)
-    grad_ydc = grad_ydc.astype(jnp.bfloat16)
-    grad_deconv = weight_grad(padded.reshape(-1, D), grad_ydc.reshape(-1, 16 * CH))
-    grad_padded = product_back(grad_ydc, deconv)
-    beside = jnp.where(place == 0, grad_padded[:, -1], grad_padded[:, 0]).astype(jnp.bfloat16)
+    grad_far = lax.ppermute(grad_far, "strip", SWAP)
+    grad_grid, beside, grad_deconv = deconv_bwd(grad_cells, grad_far, grid, edge, deconv)
     beside = lax.ppermute(beside, "strip", SWAP).astype(jnp.float32)
-    grad_grid = grad_padded[:, 1:-1]
-    grad_grid = grad_grid.at[:, 0].add(jnp.where(place == 0, 0.0, beside))
-    grad_grid = grad_grid.at[:, -1].add(jnp.where(place == 0, beside, 0.0))
+    grad_grid = grad_grid.at[:, :TC].add(jnp.where(place == 0, 0.0, beside))
+    grad_grid = grad_grid.at[:, -TC:].add(jnp.where(place == 0, beside, 0.0))
     grad_stream = grad_grid.reshape(-1, D)
     grad_branch = grad_stream.astype(jnp.bfloat16)
     grad_hidden3, *panel_grads = mlp_bwd(panels, hidden3, grad_branch, up, act)
@@ -1485,13 +1808,12 @@
     grad_self = product_back(grad_branch2, square("out_self")).astype(jnp.bfloat16)
     panel_sums = PanelSums(panel_grads)
     grad_self = panel_sums.first(grad_self)
-    early = attend_bwd(query2, kv_both, all_keys, (0, pairs // 2), 512, total_two, self_out, grad_self)
+    early = attend_bwd(query2, kv_both, all_keys, (0, pairs - 1), 512, total_two, self_out, grad_self)
     early = (panel_sums.second(early[0]), *early[1:])
     grad_query2, grad_kv_own, grad_kv_far = attend_bwd(
-        query2, kv_both, all_keys, (pairs // 2, pairs), 512, total_two, self_out, grad_self, early
+        query2, kv_both, all_keys, (pairs - 1, pairs), 512, total_two, self_out, grad_self, early
     )
     grad_kv_far = lax.ppermute(grad_kv_far, "strip", SWAP)
-    grad_query2 = panel_sums.third(grad_query2)
     grad_kv = (grad_kv_own.astype(jnp.float32) + grad_kv_far.astype(jnp.float32)).astype(jnp.bfloat16)
     grad_hidden2 = project_back(grad_query2, grad_kv, tiled, TILES["qkv_self"], D)
     grad_norm, grad_mod2, grad_mod3 = norm_two(grad_hidden2)
@@ -1501,7 +1823,7 @@
     grad_query1, grad_image_kv = attend_bwd(
         query1, [image_kv], real_keys, (0, pairs), 128, total_one, cross_out, grad_cross
     )
-    grad_query1 = panel_sums.fourth(grad_query1)
+    grad_query1 = panel_sums.third(grad_query1)
     grad_norm, grad_mod0, grad_mod1 = norm_one(product_back(grad_query1, square("query_cross")))
     grad_stream = grad_stream + grad_norm
     grad_mods = jnp.stack([grad_mod0, grad_mod1, grad_mod2, grad_mod3, grad_mod4, grad_mod5])
@@ -1557,31 +1879,23 @@
             copies.append((len(arrays), first, piece.shape[0]))
             arrays.append(piece)
     row_grads = weight_grads(arrays, products, copies, total_tiles).reshape(-1, WIDE)
-    flat_sum, block_sum, loss_sum = reduce_grads(row_grads, panel_sums.parts, loss_part, weights.shape[0])
+    if direct_links():
+        summed, chunks, loss_sum = reduce_grads(row_grads, panel_sums.parts, loss_part)
+        new_weights, new_first, new_second = adam(summed, weights, first_moment, second_moment)
+    else:
+        summed, chunks, loss_sum = reduce_grads_plainly(row_grads, panel_sums.parts, loss_part, weights.shape[0])
+        new_weights, new_first, new_second = adam_plainly(summed, weights, first_moment, second_moment)
+    new_blocks, block_grads, new_left, new_right, block_rms = shampoo(
+        chunks, blocks, stat_left, stat_right, root_left, root_right
+    )
     loss = loss_sum * factor
-    new_first = BETA_FIRST * first_moment + (1.0 - BETA_FIRST) * flat_sum
-    new_second = BETA_SECOND * second_moment + (1.0 - BETA_SECOND) * flat_sum * flat_sum
-    fix_first = 1.0 - BETA_FIRST**ADAM_STEP
-    fix_second = 1.0 - BETA_SECOND**ADAM_STEP
-    moved = new_first / fix_first / (jnp.sqrt(new_second / fix_second) + ADAM_EPS)
-    new_weights = weights - ADAM_RATE * (moved + WEIGHT_DECAY * weights)
-    new_left = STAT_DECAY * stat_left + (1.0 - STAT_DECAY) * jnp.einsum(
-        "bij,bkj->bik", block_sum, block_sum, precision=HIGHEST_MODE
-    )
-    new_right = STAT_DECAY * stat_right + (1.0 - STAT_DECAY) * jnp.einsum(
-        "bji,bjk->bik", block_sum, block_sum, precision=HIGHEST_MODE
-    )
-    half_step = jnp.einsum("bij,bjk->bik", block_sum, root_right, precision=HIGHEST_MODE)
-    precond = jnp.einsum("bij,bjk->bik", root_left, half_step, precision=HIGHEST_MODE)
-    block_rms = jnp.sqrt(jnp.mean(precond * precond, axis=(1, 2)) + RMS_EPS)
-    new_blocks = blocks - SHAMPOO_RATE * precond / block_rms[:, None, None]
     return (
         loss,
         new_weights,
         new_first,
         new_second,
         new_blocks,
-        block_sum,
+        block_grads,
         new_left,
         new_right,
         block_rms,

time: 792 us -> 714 us (0.902)
  local copies, waits for them, and re-layouts: 118 us -> 38.6 us
  Pallas kernels: 498 us -> 548 us
  matrix products: 57.1 us -> 27.7 us
  other arithmetic: 70 us -> 49.6 us
    pallas_call x0 -> x7, Pallas kernels: none -> 49.9 us  [the longest x1 16 us: deconv_bwd(): pl.pallas_call(deconv_bwd_kernel, grid=(planes,), in_specs=[by_plane(*own...]
    reshape x9 -> x0, local copies, waits for them, and re-layouts: 26.3 us -> none  [the longest x2 11.5 us: shards(): deconv = plain('deconv', 16 * CH).reshape(D, 16 * CH)]
    dot_general x6 -> x0, matrix products: 23.8 us -> none  [the longest x1 6.6 us: shards(): jnp.einsum('prcd,dk->prck', padded, deconv, preferred_element_type=jnp.fl...]
    unnamed x186 -> x123, local copies, waits for them, and re-layouts: 34 us -> 17.1 us
    convert_element_type x4 -> x0, local copies, waits for them, and re-layouts: 13.1 us -> none  [the longest x2 10.7 us: shards(): grad_ydc = grad_ydc.astype(jnp.bfloat16)]
    select_n x5 -> x1, other arithmetic: 10.6 us -> 1.05 us  [shards(): jnp.where(place == 0, grid[:, -TC:], grid[:, :TC])]
    dot_general x4 -> x3, matrix products: 20.5 us -> 15.3 us  [product_back(): lax.dot_general(left, right, (((left.ndim - 1,), (1,)), ((), ())), prefer...]
  transfers between devices with their start and end apart: 19 -> 18, of which waited for: 7 -> 10; matrix products, arithmetic and copies ran while one was open for 13% -> 8% of each run, Pallas kernels for 13% -> 21%
where the time goes in v4:
time: 714 us; the launch traced here: 704 us
  Pallas kernels  548 us (77%)
  other arithmetic  49.6 us (7%)
  local copies, waits for them, and re-layouts  38.6 us (5%)
  matrix products  27.7 us (4%)
  waiting for transfers between devices  18.5 us (3%)
  starting transfers between devices  16.7 us (2%)
    pallas_call x1, Pallas kernels, gather_all(): pl.pallas_call(functools.partial(gather_kernel, layouts, stagger), out_sh...  125 us
    pallas_call x1, Pallas kernels, scatter_sum(): pl.pallas_call(functools.partial(scatter_kernel, layouts, stagger), out_s...  117 us
    pallas_call x3, Pallas kernels, attend_bwd(): pl.pallas_call(functools.partial(attend_bwd_kernel, real_keys, chunk, len...  71.6 us
    pallas_call x3, Pallas kernels, attend_fwd(): pl.pallas_call(functools.partial(attend_fwd_kernel, real_keys, len(source...  46.8 us
    pallas_call x1, Pallas kernels, mlp_bwd(): pl.pallas_call(functools.partial(mlp_bwd_kernel, len(panels)), grid=(step...  45.2 us
    pallas_call x1, Pallas kernels, mlp_fwd(): pl.pallas_call(functools.partial(mlp_fwd_kernel, len(panels)), grid=(step...  29.4 us
    pallas_call x1, Pallas kernels, weight_grads(): pl.pallas_call(functools.partial(weight_grads_kernel, products, copies),...  22.5 us
    pallas_call x1, Pallas kernels, render(): pl.pallas_call(render_kernel, grid=(all_rays // rays,), in_specs=[pl.Bloc...  20.1 us
  transfers between devices with their start and end apart: 18, of which 10 were waited for; matrix products, arithmetic and copies ran while one was open for 8% of the time, Pallas kernels for 21%

profile of v4, /device:TPU:1, one launch (start us, length us, event | category | flops | bytes accessed | tf_op | source)
XLA Modules:
  0.0 704.4 jit_solution(5129605451456232028)
XLA Ops:
  15.3 125.3 %gather_all.1 = (bf16[10752,1024]{1,0:T(8,128)(2,1)}, f32[256,128]{1,0:T(8,128)}, bf16[4,256,1024]{2,1,0:T(8,128)(2,1)}) custom-call(bf16[336,1024]{1,0:T(8,128)(2,1)} %copy-done.24, f32[8,128]{1,0:T(8,128)} %broadcast_in_dim.71.refs_1_, bf16[256,1024]{1,0:T(8,128)(2,1)} %copy-done.25), custom_call_target="tpu_custom_call" | custom-call | tf_op jit(solution)/shard_map/gather_all/pallas_call | solution.py:526
  152.5 10.9 %attend_fwd.3 = (bf16[768,1024]{1,0:T(8,128)(2,1)S(1)}, f32[8,8,768]{2,1,0:T(8,128)S(1)}) custom-call(bf16[768,1024]{1,0:T(8,128)(2,1)S(1)} %fusion.28.q_ref, bf16[2,384,1024]{2,1,0:T(8,128)(2,1)S(1)} %project.2.refs_0_), custom_call_target="tpu_custom_call" | custom-call | flops 1000000 | bytes 100000 | tf_op jit(solution)/shard_map/attend_fwd/pallas_call | solution.py:109
  169.7 7.5 %project.3 = (bf16[768,1024]{1,0:T(8,128)(2,1)S(1)}, bf16[2,768,1024]{2,1,0:T(8,128)(2,1)S(1)}) custom-call(bf16[768,1024]{1,0:T(8,128)(2,1)S(1)} %add_convert_fusion.6.x_ref.refs_6_, bf16[1344,8,1024]{2,1,0:T(8,128)(2,1)} %bitcast.59), custom_call_target="tpu_custom_call" | custom-call | flops 1000000 | bytes 100000 | tf_op jit(solution)/shard_map/project/pallas_call | solution.py:1174
  187.9 18.1 %attend_fwd.4 = (bf16[768,1024]{1,0:T(8,128)(2,1)S(1)}, f32[8,8,768]{2,1,0:T(8,128)S(1)}) custom-call(bf16[768,1024]{1,0:T(8,128)(2,1)S(1)} %get-tuple-element.99.q_ref, bf16[2,768,1024]{2,1,0:T(8,128)(2,1)} %copy-done.2, bf16[2,768,1024]{2,1,0:T(8,128)(2,1)} %copy-done.33), custom_call_target="tpu_custom_call" | custom-call | flops 1000000 | bytes 100000 | tf_op jit(solution)/shard_map/attend_fwd/pallas_call | solution.py:109
  206.5 17.8 %attend_fwd.5 = (bf16[768,1024]{1,0:T(8,128)(2,1)S(1)}, f32[8,8,768]{2,1,0:T(8,128)S(1)}) custom-call(bf16[768,1024]{1,0:T(8,128)(2,1)S(1)} %get-tuple-element.99.q_ref, bf16[2,768,1024]{2,1,0:T(8,128)(2,1)} %copy-done.2, bf16[2,768,1024]{2,1,0:T(8,128)(2,1)} %copy-done.33, ...), custom_call_target="tpu_custom_call", output_to_operand_aliasing={{0}: (3, {}), {1}: (4, {})} | custom-call | flops 1000000 | bytes 100000 | tf_op jit(solution)/shard_map/attend_fwd/pallas_call | solution.py:109
  237.0 29.4 %mlp_fwd.1 = (f32[4,768,1024]{2,1,0:T(8,128)}, bf16[4,768,1024]{2,1,0:T(8,128)(2,1)}, bf16[768,1024]{1,0:T(8,128)(2,1)}) custom-call(bf16[4,256,1024]{2,1,0:T(8,128)(2,1)} %get-tuple-element.95.refs_0_, bf16[4,256,1024]{2,1,0:T(8,128)(2,1)} %collective-permute-done.1.refs_1_, bf16[4,256,1024]{2,1,0:T(8,128)(2,1)} %collective-permute-done.2.refs_2_, ...), custom_call_target="tpu_custom_call" | custom-call | flops 1000000 | bytes 100000 | tf_op jit(solution)/shard_map/mlp_fwd/pallas_call | solution.py:823
  267.6 6.1 spread_deconv.1.w_ref
  273.8 5.6 deconv_fwd.1.near_ref
  291.5 20.1 %render.1 = (f32[8,128]{1,0:T(8,128)S(1)}, bf16[3,80,1024]{2,1,0:T(8,128)(2,1)S(1)}, bf16[3,80,1024]{2,1,0:T(8,128)(2,1)S(1)}, f32[80,64]{1,0:T(8,128)S(1)}, f32[64,8]{1,0:T(8,128)S(1)}) custom-call(s32[3,16,256]{2,1,0:T(8,128)S(1)} %add_select_fusion.samples_ref, bf16[3,1024,128]{2,1,0:T(8,128)(2,1)} %deconv_fwd.1.near_ref, ...), custom_call_target="tpu_custom_call" | custom-call | tf_op jit(solution)/shard_map/render/pallas_call | solution.py:332
  315.0 16.0 %deconv_bwd.1 = (f32[3,256,1024]{2,1,0:T(8,128)}, bf16[3,32,1024]{2,1,0:T(8,128)(2,1)}, bf16[160,8,1024]{2,1,0:T(8,128)(2,1)}) custom-call(bf16[3,80,1024]{2,1,0:T(8,128)(2,1)} %copy-done.26, bf16[3,80,1024]{2,1,0:T(8,128)(2,1)} %copy-done.50, bf16[3,256,1024]{2,1,0:T(8,128)(2,1)} %bitcast.52, bf16[3,32,1024]{2,1,0:T(8,128)(2,1)} %copy-done.23, ...), custom_call_target="tpu_custom_call" | custom-call | tf_op jit(solution)/shard_map/deconv_bwd/pallas_call | solution.py:1108
  339.7 45.2 %mlp_bwd.1 = (f32[768,1024]{1,0:T(8,128)}, bf16[16,256,1024]{2,1,0:T(8,128)(2,1)}, bf16[16,256,1024]{2,1,0:T(8,128)(2,1)}) custom-call(bf16[4,256,1024]{2,1,0:T(8,128)(2,1)} %get-tuple-element.95.refs_0_, bf16[4,256,1024]{2,1,0:T(8,128)(2,1)} %collective-permute-done.1.refs_1_, bf16[4,256,1024]{2,1,0:T(8,128)(2,1)} %collective-permute-done.2.refs_2_, ...), custom_call_target="tpu_custom_call" | custom-call | flops 1000000 | bytes 100000 | tf_op jit(solution)/shard_map/mlp_bwd/pallas_call | solution.py:932
  394.4 5.4 fusion.34.refs_4_
  405.4 45.3 %attend_bwd.3 = (bf16[768,1024]{1,0:T(8,128)(2,1)S(1)}, bf16[2,768,1024]{2,1,0:T(8,128)(2,1)}, bf16[2,768,1024]{2,1,0:T(8,128)(2,1)}) custom-call(bf16[768,1024]{1,0:T(8,128)(2,1)S(1)} %get-tuple-element.99.q_ref, bf16[2,768,1024]{2,1,0:T(8,128)(2,1)} %copy-done.2, bf16[2,768,1024]{2,1,0:T(8,128)(2,1)} %copy-done.33, ...), custom_call_target="tpu_custom_call" | custom-call | flops 1000000 | bytes 100000 | tf_op jit(solution)/shard_map/attend_bwd/pallas_call | solution.py:182
  452.4 5.0 add_convert_fusion.3
  457.5 7.8 %attend_bwd.4 = (bf16[768,1024]{1,0:T(8,128)(2,1)S(1)}, bf16[2,768,1024]{2,1,0:T(8,128)(2,1)}, bf16[2,768,1024]{2,1,0:T(8,128)(2,1)}) custom-call(bf16[768,1024]{1,0:T(8,128)(2,1)S(1)} %get-tuple-element.99.q_ref, bf16[2,768,1024]{2,1,0:T(8,128)(2,1)} %copy-done.2, ...), custom_call_target="tpu_custom_call", output_to_operand_aliasing={{0}: (6, {}), {1}: (7, {}), {2}: (8, {})} | custom-call | flops 1000000 | bytes 100000 | tf_op jit(solution)/shard_map/attend_bwd/pallas_call | solution.py:182
  476.5 9.5 %project_back.1 = f32[768,1024]{1,0:T(8,128)S(1)} custom-call(bf16[768,1024]{1,0:T(8,128)(2,1)S(1)} %copy-done.7, bf16[2,768,1024]{2,1,0:T(8,128)(2,1)S(1)} %add_convert_fusion.1.g_ref.refs_8_, bf16[1344,8,1024]{2,1,0:T(8,128)(2,1)} %bitcast.61), custom_call_target="tpu_custom_call" | custom-call | flops 1000000 | bytes 100000 | tf_op jit(solution)/shard_map/project_back/pallas_call | solution.py:1212
  489.4 5.2 fusion.31.refs_3_
  494.6 18.5 %attend_bwd.5 = (bf16[768,1024]{1,0:T(8,128)(2,1)S(1)}, bf16[2,384,1024]{2,1,0:T(8,128)(2,1)S(1)}) custom-call(bf16[768,1024]{1,0:T(8,128)(2,1)S(1)} %copy-done.16, bf16[2,384,1024]{2,1,0:T(8,128)(2,1)} %copy-done.9, f32[8,8,768]{2,1,0:T(8,128)S(1)} %copy-done.28, bf16[768,1024]{1,0:T(8,128)(2,1)} %copy-done.14, bf16[768,1024]{1,0:T(8,128)(2,1)} %fusion.31.refs_3_), custom_call_target="tpu_custom_call" | custom-call | flops 1000000 | bytes 100000 | tf_op jit(solution)/shard_map/attend_bwd/pallas_call | solution.py:182
  513.1 4.7 fusion.10
  527.6 22.5 %weight_grads.1 = bf16[1344,8,1024]{2,1,0:T(8,128)(2,1)} custom-call(bf16[768,1024]{1,0:T(8,128)(2,1)} %copy-done.47, bf16[768,1024]{1,0:T(8,128)(2,1)} %copy-done.18, bf16[384,768]{1,0:T(8,128)(2,1)} %copy-done.17, bf16[2,384,1024]{2,1,0:T(8,128)(2,1)} %copy-done.19, bf16[768,1024]{1,0:T(8,128)(2,1)} %copy-done.14, bf16[768,1024]{1,0:T(8,128)(2,1)} %copy-done.46, ...), custom_call_target="tpu_custom_call" | custom-call | flops 1000000 | bytes 100000 | tf_op jit(solution)/shard_map/weight_grads/pallas_call | solution.py:1301
  550.1 5.5 add_convert_fusion.2.refs_2_
  556.3 116.8 %scatter_sum.1 = (f32[336,1024]{1,0:T(8,128)S(1)}, f32[8,128]{1,0:T(8,128)S(1)}, bf16[512,1024]{1,0:T(8,128)(2,1)S(1)}) custom-call(bf16[10752,1024]{1,0:T(8,128)(2,1)} %bitcast.62, f32[256,128]{1,0:T(8,128)S(1)} %broadcast_in_dim.86.refs_1_, bf16[4,256,1024]{2,1,0:T(8,128)(2,1)S(1)} %add_convert_fusion.2.refs_2_), custom_call_target="tpu_custom_call" | custom-call | tf_op jit(solution)/shard_map/scatter_sum/pallas_call | solution.py:744
  679.0 15.2 %shampoo.1 = (f32[32,128,128]{2,1,0:T(8,128)}, f32[32,128,128]{2,1,0:T(8,128)}, f32[32,128,128]{2,1,0:T(8,128)}, f32[32,128,128]{2,1,0:T(8,128)}, f32[32,128]{1,0:T(8,128)}) custom-call(bf16[512,1024]{1,0:T(8,128)(2,1)} %copy-done.22, f32[32,128,128]{2,1,0:T(8,128)} %blocks_ref.3, f32[32,128,128]{2,1,0:T(8,128)} %sl_ref.1, f32[32,128,128]{2,1,0:T(8,128)} %sr_ref.1, ...), custom_call_target="tpu_custom_call" | custom-call | tf_op jit(solution)/shard_map/shampoo/pallas_call | solution.py:1554
  698.2 4.8 adam.1
  (248 shorter events, 131.0 us)
Async XLA Ops:
  1.8 8.2 %collective-permute-start = (f32[448,128]{1,0:T(8,128)S(1)}, f32[448,128]{1,0:T(8,128)S(1)}, u32[]{:S(2)}, u32[]{:S(2)}) collective-permute-start(f32[448,128]{1,0:T(8,128)S(1)} %slice_bitcast_fusion), channel_id=1, source_target_pairs={{1,0},{2,1},{3,2},{4,3},{5,4},{6,5},{7,6},{8,7},{9,8},{10,9},{11,1... | collective-permute-start | bytes 688136 | tf_op jit(solution)/shard_map/ppermute | solution.py:1433
  7.9 137.0 %copy-start.17 = (bf16[384,768]{1,0:T(8,128)(2,1)}, bf16[384,768]{1,0:T(8,128)(2,1)S(1)}, u32[]{:S(2)}) copy-start(bf16[384,768]{1,0:T(8,128)(2,1)S(1)} %pad.21.x_ref.refs_2_) | copy-start | bytes 1769476
  143.2 20.2 %copy-start.35 = (bf16[256,1024]{1,0:T(8,128)(2,1)}, bf16[256,1024]{1,0:T(8,128)(2,1)S(1)}, u32[]{:S(2)}) copy-start(bf16[256,1024]{1,0:T(8,128)(2,1)S(1)} %get-tuple-element.168) | copy-start | bytes 1572868
  143.2 20.2 %copy-start.37 = (bf16[256,1024]{1,0:T(8,128)(2,1)}, bf16[256,1024]{1,0:T(8,128)(2,1)S(1)}, u32[]{:S(2)}) copy-start(bf16[256,1024]{1,0:T(8,128)(2,1)S(1)} %get-tuple-element.169) | copy-start | bytes 1572868
  144.1 25.6 %collective-permute-start.1 = (bf16[4,256,1024]{2,1,0:T(8,128)(2,1)}, bf16[4,256,1024]{2,1,0:T(8,128)(2,1)}, u32[]{:S(2)}, u32[]{:S(2)}) collective-permute-start(bf16[4,256,1024]{2,1,0:T(8,128)(2,1)} %get-tuple-element.95.refs_0_), channel_id=1, source_target_pairs={{0,2},{1,5},{2,0},{3,7},{4,6},{5,1},{6,4},{7,3},{8,10},{9,13},{10,... | collective-permute-start | bytes 6291464 | tf_op jit(solution)/shard_map/ppermute | solution.py:1605
  177.2 9.1 %collective-permute-start.3 = (bf16[2,768,1024]{2,1,0:T(8,128)(2,1)S(1)}, bf16[2,768,1024]{2,1,0:T(8,128)(2,1)S(1)}, u32[]{:S(2)}, u32[]{:S(2)}) collective-permute-start(bf16[2,768,1024]{2,1,0:T(8,128)(2,1)S(1)} %get-tuple-element.100.refs_0_), channel_id=1, source_target_pairs={{0,1},{1,0},{2,3},{3,2},{4,5},{5,4},{6,7},{7,6},{8,9},{9,8},{10,11... | collective-permute-start | bytes 9437192 | tf_op jit(solution)/shard_map/ppermute | solution.py:1768
  181.0 25.5 %collective-permute-start.2 = (bf16[4,256,1024]{2,1,0:T(8,128)(2,1)}, bf16[4,256,1024]{2,1,0:T(8,128)(2,1)}, u32[]{:S(2)}, u32[]{:S(2)}) collective-permute-start(bf16[4,256,1024]{2,1,0:T(8,128)(2,1)} %get-tuple-element.95.refs_0_), channel_id=1, source_target_pairs={{0,4},{1,3},{2,6},{3,1},{4,0},{5,7},{6,2},{7,5},{8,12},{9,11},{10,... | collective-permute-start | bytes 6291464 | tf_op jit(solution)/shard_map/ppermute | solution.py:1625
  181.9 47.0 %collective-permute-start.4 = (bf16[4,256,1024]{2,1,0:T(8,128)(2,1)}, bf16[4,256,1024]{2,1,0:T(8,128)(2,1)}, u32[]{:S(2)}, u32[]{:S(2)}) collective-permute-start(bf16[4,256,1024]{2,1,0:T(8,128)(2,1)} %collective-permute-done.1.refs_1_), channel_id=1, source_target_pairs={{0,4},{1,3},{2,6},{3,1},{4,0},{5,7},{6,2},{7,5},{8,12},{9,11},{10,... | collective-permute-start | bytes 6291464 | tf_op jit(solution)/shard_map/ppermute | solution.py:1633
  182.4 54.0 %collective-permute-start.5 = (bf16[4,256,1024]{2,1,0:T(8,128)(2,1)}, bf16[4,256,1024]{2,1,0:T(8,128)(2,1)}, u32[]{:S(2)}, u32[]{:S(2)}) collective-permute-start(bf16[4,256,1024]{2,1,0:T(8,128)(2,1)} %get-tuple-element.95.refs_0_), channel_id=1, source_target_pairs={{0,1},{1,0},{2,3},{3,2},{4,5},{5,4},{6,7},{7,6},{8,9},{9,8},{10,11... | collective-permute-start | bytes 6291464 | tf_op jit(solution)/shard_map/ppermute | solution.py:1641
  183.1 53.4 %collective-permute-start.6 = (bf16[4,256,1024]{2,1,0:T(8,128)(2,1)}, bf16[4,256,1024]{2,1,0:T(8,128)(2,1)}, u32[]{:S(2)}, u32[]{:S(2)}) collective-permute-start(bf16[4,256,1024]{2,1,0:T(8,128)(2,1)} %collective-permute-done.1.refs_1_), channel_id=1, source_target_pairs={{0,1},{1,0},{2,3},{3,2},{4,5},{5,4},{6,7},{7,6},{8,9},{9,8},{10,11... | collective-permute-start | bytes 6291464 | tf_op jit(solution)/shard_map/ppermute | solution.py:1641
  224.3 233.2 %copy-start.5 = (bf16[768,1024]{1,0:T(8,128)(2,1)}, bf16[768,1024]{1,0:T(8,128)(2,1)S(1)}, u32[]{:S(2)}) copy-start(bf16[768,1024]{1,0:T(8,128)(2,1)S(1)} %get-tuple-element.105.refs_3_.refs_9_) | copy-start | bytes 4718596
  228.9 7.5 %collective-permute-start.8 = (bf16[4,256,1024]{2,1,0:T(8,128)(2,1)}, bf16[4,256,1024]{2,1,0:T(8,128)(2,1)}, u32[]{:S(2)}, u32[]{:S(2)}) collective-permute-start(bf16[4,256,1024]{2,1,0:T(8,128)(2,1)} %collective-permute-done.4.refs_3_), channel_id=1, source_target_pairs={{0,1},{1,0},{2,3},{3,2},{4,5},{5,4},{6,7},{7,6},{8,9},{9,8},{10,11... | collective-permute-start | bytes 6291464 | tf_op jit(solution)/shard_map/ppermute | solution.py:1641
  229.9 7.1 %collective-permute-start.7 = (bf16[4,256,1024]{2,1,0:T(8,128)(2,1)}, bf16[4,256,1024]{2,1,0:T(8,128)(2,1)}, u32[]{:S(2)}, u32[]{:S(2)}) collective-permute-start(bf16[4,256,1024]{2,1,0:T(8,128)(2,1)} %collective-permute-done.2.refs_2_), channel_id=1, source_target_pairs={{0,1},{1,0},{2,3},{3,2},{4,5},{5,4},{6,7},{7,6},{8,9},{9,8},{10,11... | collective-permute-start | bytes 6291464 | tf_op jit(solution)/shard_map/ppermute | solution.py:1641
  234.7 31.7 %copy-start.56 = (f32[768]{0:T(1024)}, f32[768]{0:T(1024)S(1)}, u32[]{:S(2)}) copy-start(f32[768]{0:T(1024)S(1)} %multiply_reduce_fusion.4) | copy-start | bytes 9220
  267.5 6.3 collective-permute-start.9
  279.4 12.1 %collective-permute-start.10 = (bf16[3,1024,128]{2,1,0:T(8,128)(2,1)}, bf16[3,1024,128]{2,1,0:T(8,128)(2,1)}, u32[]{:S(2)}, u32[]{:S(2)}) collective-permute-start(bf16[3,1024,128]{2,1,0:T(8,128)(2,1)} %deconv_fwd.1.near_ref), channel_id=1, source_target_pairs={{0,1},{1,0},{2,3},{3,2},{4,5},{5,4},{6,7},{7,6},{8,9},{9,8},{10,11... | collective-permute-start | bytes 2359304 | tf_op jit(solution)/shard_map/ppermute | solution.py:1781
  312.4 1.9 collective-permute-start.11
  331.1 1.7 collective-permute-start.12
  384.9 14.9 %collective-permute-start.13 = (bf16[16,256,1024]{2,1,0:T(8,128)(2,1)}, bf16[16,256,1024]{2,1,0:T(8,128)(2,1)S(1)}, u32[]{:S(2)}, u32[]{:S(2)}) collective-permute-start(bf16[16,256,1024]{2,1,0:T(8,128)(2,1)} %get-tuple-element.116), channel_id=1, source_target_pairs={{0,1},{1,0},{2,3},{3,2},{4,5},{5,4},{6,7},{7,6},{8,9},{9,8},{10,11... | collective-permute-start | bytes 25165832 | tf_op jit(solution)/shard_map/ppermute | solution.py:1650
  404.5 48.0 %collective-permute-start.14 = (bf16[8,256,1024]{2,1,0:T(8,128)(2,1)}, bf16[8,256,1024]{2,1,0:T(8,128)(2,1)}, u32[]{:S(2)}, u32[]{:S(2)}) collective-permute-start(bf16[8,256,1024]{2,1,0:T(8,128)(2,1)} %add_convert_fusion), channel_id=1, source_target_pairs={{0,4},{1,3},{2,6},{3,1},{4,0},{5,7},{6,2},{7,5},{8,12},{9,11},{10,... | collective-permute-start | bytes 12582920 | tf_op jit(solution)/shard_map/ppermute | solution.py:1662
  466.5 6.4 collective-permute-start.16
  468.8 44.3 %collective-permute-start.15 = (bf16[4,256,1024]{2,1,0:T(8,128)(2,1)}, bf16[4,256,1024]{2,1,0:T(8,128)(2,1)}, u32[]{:S(2)}, u32[]{:S(2)}) collective-permute-start(bf16[4,256,1024]{2,1,0:T(8,128)(2,1)} %add_convert_fusion.3), channel_id=1, source_target_pairs={{0,2},{1,5},{2,0},{3,7},{4,6},{5,1},{6,4},{7,3},{8,10},{9,13},{10,... | collective-permute-start | bytes 6291464 | tf_op jit(solution)/shard_map/ppermute | solution.py:1670
  674.2 21.4 %collective-permute-start.17 = (f32[448,128]{1,0:T(8,128)S(1)}, f32[448,128]{1,0:T(8,128)S(1)}, u32[]{:S(2)}, u32[]{:S(2)}) collective-permute-start(f32[448,128]{1,0:T(8,128)S(1)} %slice.210), channel_id=1, source_target_pairs={{0,1},{1,2},{2,3},{3,4},{4,5},{5,6},{6,7},{7,8},{8,9},{9,10},{10,1... | collective-permute-start | bytes 688136 | tf_op jit(solution)/shard_map/ppermute | solution.py:1520
  679.0 24.0 %copy-start.1 = (s32[1,4096]{1,0:T(1,128)S(1)}, s32[1,4096]{1,0:T(1,128)}, u32[]{:S(2)}) copy-start(s32[1,4096]{1,0:T(1,128)} %param.31) | copy-start | bytes 49156
  (55 other events, 315.2 us)

commit v5 on v4

--- a/solution.py
+++ b/solution.py
@@ -364,6 +364,43 @@
     )(samples, near, far, wanted, mask, factor, decode_in, decode_out)
 
 
+def pick_kernel(pixel_ref, valid_ref, target_ref, mask_ref, wanted_ref, count_ref):
+    pixels = valid_ref.shape[1]
+    rays = pixel_ref.shape[1]
+    hot = lax.broadcasted_iota(jnp.int32, (pixels, rays), 0) == pixel_ref[...]
+    hot = jnp.where(hot, 1.0, 0.0).astype(jnp.bfloat16)
+    rest = target_ref[...]
+    rows = [valid_ref[...].astype(jnp.float32)]
+    for _ in range(3):
+        part = rest.astype(jnp.bfloat16).astype(jnp.float32)
+        rows.append(part)
+        rest = rest - part
+    rows.append(jnp.zeros((6, pixels), jnp.float32))
+    found = product(jnp.concatenate(rows, 0).astype(jnp.bfloat16), hot)
+    mask = found[:1]
+    mask_ref[...] = mask
+    wanted_ref[...] = jnp.zeros_like(wanted_ref)
+    wanted_ref[1:4] = found[1:4] + found[4:7] + found[7:10]
+    count_ref[...] = jnp.broadcast_to(jnp.sum(mask, 1, keepdims=True), count_ref.shape)
+
+
+def pick(pixel, valid, target):
+    rays = pixel.shape[1]
+    vmem = pl.BlockSpec(memory_space=pltpu.VMEM)
+    return pl.pallas_call(
+        pick_kernel,
+        in_specs=[vmem] * 3,
+        out_specs=[vmem] * 3,
+        out_shape=[
+            jax.ShapeDtypeStruct((1, rays), jnp.float32),
+            jax.ShapeDtypeStruct((8, rays), jnp.float32),
+            jax.ShapeDtypeStruct((8, 128), jnp.float32),
+        ],
+        compiler_params=pltpu.CompilerParams(vmem_limit_bytes=24 * 1024 * 1024),
+        name="pick",
+    )(pixel, valid, target)
+
+
 MESH_ID = pl.DeviceIdType.MESH
 
 
@@ -491,11 +528,11 @@
         )
     lines.append(pltpu.make_async_copy(line_source, line_full.at[0], line_sems.at[0]))
 
-    steps = [(stagger * len(jobs) - 4, -2, 0)]
+    steps = [(2 * stagger + 2, -2, 0)]
     for job in range(len(jobs)):
-        steps.append((stagger * job, -1, job))
-        for i in range(len(ORDER)):
-            steps.append((stagger * job + i + 1, i, job))
+        begin_at = stagger * min(job, layouts[0][0] - 1)
+        for i in range(-1, len(ORDER)):
+            steps.append((begin_at + i + 1, i, job))
     for _, i, job in sorted(steps):
         if i == -2:
             for copy in lines:
@@ -548,11 +585,11 @@
 def scatter_kernel(layouts, stagger, *refs):
     count = len(layouts)
     grads = refs[:count]
-    line_grad = refs[count]
-    outs = refs[count + 1 : 2 * count + 1]
-    line_out = refs[2 * count + 1]
-    scratch = refs[2 * count + 2 :]
-    line_own, line_got, line_sum, line_sems = scratch[-4:]
+    line_grads = refs[count : count + 4]
+    outs = refs[count + 4 : 2 * count + 4]
+    line_out = refs[2 * count + 4]
+    scratch = refs[2 * count + 5 :]
+    line_parts, line_sums, line_got, line_sum, line_sems, line_load_sems = scratch[-6:]
     p, c, z, near, far, both = places()
     zs = [along_z(p, z, k) for k in range(4)]
     enter([(q, c) for q in zs[1:]] + [(near, c), (far, c), (p, 1 - c)])
@@ -638,15 +675,26 @@
         rows = layouts[a][1]
         return [pltpu.make_async_copy(view(job, buffers[a][5], 0), outs[a].at[pl.ds(j * rows, rows)], out_sem.at[job, 0])]
 
-    line_sends = [
-        pltpu.make_async_remote_copy(
-            line_grad.at[k], line_got.at[3 - k], line_sems.at[k], line_sems.at[7 - k],
+    line_loads = [
+        [pltpu.make_async_copy(ref.at[k], line_parts.at[k, n], line_load_sems.at[k, n]) for n, ref in enumerate(line_grads)]
+        for k in range(4)
+    ]
+    line_sends = {
+        k: pltpu.make_async_remote_copy(
+            line_sums.at[k], line_got.at[3 - k], line_sems.at[k], line_sems.at[7 - k],
             device_id=(zs[k], c), device_id_type=MESH_ID,
         )
         for k in (1, 3, 2)
-    ]
-    line_load = pltpu.make_async_copy(line_grad.at[0], line_own, line_sems.at[0])
-    half = line_own.shape[0]
+    }
+
+    def line_step(k):
+        for load_part in line_loads[k]:
+            load_part.wait()
+        add_up([line_parts.at[k, n] for n in range(4)], line_sums.at[k])
+        if k:
+            line_sends[k].start()
+
+    half = line_sum.shape[0]
     spot = line_out.at[pl.ds(pl.multiple_of(c * half, 8), half)]
     line_stores = [
         pltpu.make_async_copy(line_sum, spot, line_sems.at[7]),
@@ -656,13 +704,12 @@
     ]
 
     def line_finish():
-        line_load.wait()
         for k in (1, 2, 3):
             target = line_got.at[k - 1]
             pltpu.make_async_remote_copy(
                 target, target, line_sems.at[k], line_sems.at[3 + k], device_id=(p, 1 - c), device_id_type=MESH_ID
             ).wait_recv()
-        add_up([line_own] + [line_got.at[n] for n in range(3)], line_sum)
+        add_up([line_sums.at[0]] + [line_got.at[n] for n in range(3)], line_sum)
         for copy in line_stores:
             copy.start()
 
@@ -689,9 +736,9 @@
         if i + AHEAD < 16:
             start(i + AHEAD, job)
 
-    for copy in line_sends:
-        copy.start()
-    line_load.start()
+    for k in (1, 3, 2, 0):
+        for load_part in line_loads[k]:
+            load_part.start()
     for job in range(len(jobs)):
         for n in range(AHEAD):
             start(n, job)
@@ -701,9 +748,13 @@
         for i in range(16):
             steps.append((begin + i + 2 * (i // 4 - 1) * (i // 8), job, i))
     steps.append((max(steps)[0] - 6, 0, -1))
+    for n, k in enumerate((1, 3, 2, 0)):
+        steps.append((n, len(jobs), -2 - k))
     for _, job, i in sorted(steps):
-        if i < 0:
+        if i == -1:
             line_finish()
+        elif i < 0:
+            line_step(-2 - i)
         else:
             step(i, job)
     for job in range(len(jobs)):
@@ -713,13 +764,13 @@
                 onward(i, job).wait_send()
         for copy in final_copies(job):
             copy.wait()
-    for copy in line_sends:
+    for copy in line_sends.values():
         copy.wait_send()
     for copy in line_stores:
         copy.wait()
 
 
-def scatter_sum(layouts, stagger, grads, line, name_id):
+def scatter_sum(layouts, stagger, grads, lines, name_id):
     jobs = sum(l[0] for l in layouts)
     scratch = [
         pltpu.SemaphoreType.DMA((16, jobs)),
@@ -736,22 +787,28 @@
             scratch.append(pltpu.VMEM((slots, rows, width), grad.dtype))
         scratch.append(pltpu.VMEM((1, rows, width), jnp.float32))
         shapes.append(jax.ShapeDtypeStruct((rows, width), jnp.float32))
-    piece = line.shape[1:]
-    scratch += [pltpu.VMEM(piece, line.dtype), pltpu.VMEM((3,) + piece, line.dtype), pltpu.VMEM(piece, line.dtype)]
-    scratch.append(pltpu.SemaphoreType.DMA((10,)))
-    shapes.append(jax.ShapeDtypeStruct((2 * piece[0], piece[1]), line.dtype))
+    piece, kind = lines[-1].shape[1:], lines[-1].dtype
+    scratch += [
+        pltpu.VMEM((4, 4) + piece, kind),
+        pltpu.VMEM((4,) + piece, kind),
+        pltpu.VMEM((3,) + piece, kind),
+        pltpu.VMEM(piece, kind),
+        pltpu.SemaphoreType.DMA((10,)),
+        pltpu.SemaphoreType.DMA((4, 4)),
+    ]
+    shapes.append(jax.ShapeDtypeStruct((2 * piece[0], piece[1]), kind))
     everywhere = pl.BlockSpec(memory_space=pl.ANY)
     return pl.pallas_call(
         functools.partial(scatter_kernel, layouts, stagger),
         out_shape=shapes,
-        in_specs=[everywhere] * len(shapes),
+        in_specs=[everywhere] * (len(grads) + len(lines)),
         out_specs=[everywhere] * len(shapes),
         scratch_shapes=scratch,
         compiler_params=pltpu.CompilerParams(
             collective_id=name_id, has_side_effects=True, vmem_limit_bytes=48 * 1024 * 1024
         ),
         name="scatter_sum",
-    )(*grads, line)
+    )(*grads, *lines)
 
 
 GELU_A = math.sqrt(2.0 / math.pi)
@@ -1532,6 +1589,11 @@
     return [result.reshape(length) for result in results]
 
 
+def two_parts(value):
+    coarse = value.astype(jnp.bfloat16)
+    return coarse, (value - coarse.astype(jnp.float32)).astype(jnp.bfloat16)
+
+
 def shampoo_kernel(tiles_ref, blocks_ref, sl_ref, sr_ref, rl_ref, rr_ref, nb_ref, g_ref, nl_ref, nr_ref, rms_ref):
     for n in range(8):
         grad = tiles_ref[:, n * BLOCK : (n + 1) * BLOCK]
@@ -1540,8 +1602,12 @@
         nl_ref[n] = STAT_DECAY * sl_ref[n] + (1.0 - STAT_DECAY) * nt_dot(grad, grad)
         square = lax.dot_general(grad, grad, (((0,), (0,)), ((), ())), preferred_element_type=jnp.float32)
         nr_ref[n] = STAT_DECAY * sr_ref[n] + (1.0 - STAT_DECAY) * square
-        half = jnp.dot(wide, rr_ref[n], precision=HIGHEST_MODE, preferred_element_type=jnp.float32)
-        cond = jnp.dot(rl_ref[n], half, precision=HIGHEST_MODE, preferred_element_type=jnp.float32)
+        coarse, fine = two_parts(rr_ref[n])
+        half = product(grad, jnp.concatenate([coarse, fine], 1))
+        half_coarse, half_fine = two_parts(half[:, :BLOCK] + half[:, BLOCK:])
+        coarse, fine = two_parts(rl_ref[n])
+        cond = product(jnp.concatenate([coarse, fine], 1), jnp.concatenate([half_coarse, half_coarse], 0))
+        cond = cond + product(coarse, half_fine)
         rms = jnp.sqrt(jnp.mean(cond * cond, axis=(0, 1), keepdims=True) + RMS_EPS)
         nb_ref[n] = blocks_ref[n] - SHAMPOO_RATE * cond / rms
         rms_ref[n : n + 1] = jnp.broadcast_to(rms, (1, LANES))
@@ -1600,8 +1666,7 @@
 def gather_weights(weights, blocks, part):
     if direct_links():
         own, tiles = prepare(weights, blocks)
-        meta = jnp.full((8, 128), part, jnp.float32)
-        rows, parts, line = gather_all([flat_chunks(own.shape[0], 3), META], 6, [own, meta], tiles, 0)
+        rows, parts, line = gather_all([flat_chunks(own.shape[0], 3), META], 6, [own, part], tiles, 0)
         near = lax.ppermute(line, AXES, NEAR)
         return rows, [line, near], jnp.sum(parts[::8, 0])
     flat = lax.all_gather(weights.astype(jnp.bfloat16), AXES, axis=0, tiled=True)
@@ -1609,7 +1674,7 @@
     gaps = [jnp.zeros((QKV_GAP,), flat.dtype), jnp.zeros((END_GAP,), flat.dtype)]
     rows = jnp.concatenate([flat[:QKV_AT], gaps[0], flat[QKV_AT:GAP_AT], gaps[1], flat[GAP_AT:]])
     rows = jnp.pad(rows, (0, -rows.shape[0] % (6 * TILE))).reshape(-1, WIDE)
-    return regroup(rows, 0, False), [panels_of(chunks_of(tiles))], lax.psum(part, AXES)
+    return regroup(rows, 0, False), [panels_of(chunks_of(tiles))], lax.psum(part[0, 0], AXES)
 
 
 class Panels:
@@ -1674,13 +1739,13 @@
         if not self.staged:
             return before
         self.last, before = lax.optimization_barrier((self.last, before))
-        self.parts = [self.added(slice(0, 4), self.away[:4], self.last)]
+        self.parts = [self.mine, self.got, self.away, self.last]
         return before
 
 
 def reduce_grads(rows, panels, part):
     meta = jnp.full((32 * 8, 128), part, jnp.float32)
-    summed, parts, tiles = scatter_sum([flat_chunks(rows.shape[0] // 32, 3), META], 6, [rows, meta], panels[0], 1)
+    summed, parts, tiles = scatter_sum([flat_chunks(rows.shape[0] // 32, 3), META], 6, [rows, meta], panels, 1)
     return summed, tiles, parts[0, 0]
 
 
@@ -1725,10 +1790,8 @@
 ):
     strips = lax.axis_size("strip")
     place = lax.axis_index("strip")
-    pixel = ray_pixel[0]
-    mask = jnp.take(valid[0], pixel).astype(jnp.float32)
-    wanted = jnp.take(target[0], pixel, axis=1)
-    rows, panels, count = gather_weights(weights, blocks, jnp.sum(mask))
+    mask, wanted, own_count = pick(ray_pixel, valid, target[0])
+    rows, panels, count = gather_weights(weights, blocks, own_count)
     tiled = rows.reshape(-1, 8, WIDE)
 
     def square(name):
@@ -1743,7 +1806,7 @@
     decode_out = decode[CH * DEC_HID : CH * DEC_HID + DEC_HID * 4].reshape(DEC_HID, 4)
     picture = image[0]
     real_keys = picture.shape[0]
-    picture = jnp.pad(picture, ((0, -real_keys % 128), (0, 0)))
+    picture = jnp.pad(picture, ((0, -real_keys % 16), (0, 0)))
     mods = lax.dynamic_slice_in_dim(plain("modulate", 6 * NCAM), 6 * camera[0], 6).astype(jnp.float32)
     own_rows = PR * TC
     stream0 = jnp.concatenate(
@@ -1779,14 +1842,14 @@
     edge = lax.ppermute(jnp.where(place == 0, grid[:, -TC:], grid[:, :TC]), "strip", SWAP)
     cells = deconv_fwd(grid, edge, deconv)
     cells_far = lax.ppermute(cells, "strip", SWAP)
-    rays = pixel.shape[0]
+    rays = ray_pixel.shape[1]
     factor = 1.0 / jnp.maximum(count, 1.0)
     loss_part, grad_cells, grad_far, grad_decode_in, grad_decode_out = render(
         cells,
         cells_far,
         (samples[0] + place * cells.shape[1]) % (2 * cells.shape[1]),
-        jnp.pad(wanted, ((1, 4), (0, 0))),
-        mask[None],
+        wanted,
+        mask,
         factor.reshape(1),
         decode_in,
         jnp.pad(decode_out, ((0, 0), (0, 4))),
@@ -1821,7 +1884,7 @@
     grad_branch1 = grad_stream.astype(jnp.bfloat16)
     grad_cross = product_back(grad_branch1, square("out_cross")).astype(jnp.bfloat16)
     grad_query1, grad_image_kv = attend_bwd(
-        query1, [image_kv], real_keys, (0, pairs), 128, total_one, cross_out, grad_cross
+        query1, [image_kv], real_keys, (0, pairs), picture.shape[0], total_one, cross_out, grad_cross
     )
     grad_query1 = panel_sums.third(grad_query1)
     grad_norm, grad_mod0, grad_mod1 = norm_one(product_back(grad_query1, square("query_cross")))

time: 714 us -> 680 us (0.952)
  Pallas kernels: 548 us -> 524 us
  other arithmetic: 49.6 us -> 41.4 us
    pallas_call x1, Pallas kernels: 125 us -> 112 us  [gather_all(): pl.pallas_call(functools.partial(gather_kernel, layouts, stagger), out_sh...]
    convert_element_type x3 -> x2, other arithmetic: 14.6 us -> 9.07 us  [added(): return total.astype(jnp.bfloat16)]
    unnamed x123 -> x129, local copies, waits for them, and re-layouts: 17.1 us -> 19.5 us
  transfers between devices with their start and end apart: 18 -> 18, of which waited for: 10 -> 9; matrix products, arithmetic and copies ran while one was open for 8% -> 8% of each run, Pallas kernels for 21% -> 20%
where the time goes in v5:
time: 680 us; the launch traced here: 670 us
  Pallas kernels  524 us (77%)
  other arithmetic  41.4 us (6%)
  local copies, waits for them, and re-layouts  35.2 us (5%)
  matrix products  27.9 us (4%)
  starting transfers between devices  18.3 us (3%)
  waiting for transfers between devices  17.3 us (3%)
    pallas_call x1, Pallas kernels, scatter_sum(): pl.pallas_call(functools.partial(scatter_kernel, layouts, stagger), out_s...  116 us
    pallas_call x1, Pallas kernels, gather_all(): pl.pallas_call(functools.partial(gather_kernel, layouts, stagger), out_sh...  112 us
    pallas_call x3, Pallas kernels, attend_bwd(): pl.pallas_call(functools.partial(attend_bwd_kernel, real_keys, chunk, len...  66.3 us
    pallas_call x3, Pallas kernels, attend_fwd(): pl.pallas_call(functools.partial(attend_fwd_kernel, real_keys, len(source...  46.2 us
    pallas_call x1, Pallas kernels, mlp_bwd(): pl.pallas_call(functools.partial(mlp_bwd_kernel, len(panels)), grid=(step...  45.2 us
    pallas_call x1, Pallas kernels, mlp_fwd(): pl.pallas_call(functools.partial(mlp_fwd_kernel, len(panels)), grid=(step...  29.1 us
    pallas_call x1, Pallas kernels, weight_grads(): pl.pallas_call(functools.partial(weight_grads_kernel, products, copies),...  22.6 us
    pallas_call x1, Pallas kernels, render(): pl.pallas_call(render_kernel, grid=(all_rays // rays,), in_specs=[pl.Bloc...  20.1 us
  transfers between devices with their start and end apart: 18, of which 9 were waited for; matrix products, arithmetic and copies ran while one was open for 8% of the time, Pallas kernels for 20%

profile of v5, /device:TPU:1, one launch (start us, length us, event | category | flops | bytes accessed | tf_op | source)
XLA Modules:
  0.0 669.6 jit_solution(11664953875922406078)
XLA Ops:
  15.5 111.6 %gather_all.1 = (bf16[10752,1024]{1,0:T(8,128)(2,1)}, f32[256,128]{1,0:T(8,128)}, bf16[4,256,1024]{2,1,0:T(8,128)(2,1)}) custom-call(bf16[336,1024]{1,0:T(8,128)(2,1)} %copy-done.25, f32[8,128]{1,0:T(8,128)} %copy-done.31, bf16[256,1024]{1,0:T(8,128)(2,1)} %copy-done.26), custom_call_target="tpu_custom_call" | custom-call | tf_op jit(solution)/shard_map/gather_all/pallas_call | solution.py:563
  140.1 10.5 %attend_fwd.3 = (bf16[768,1024]{1,0:T(8,128)(2,1)S(1)}, f32[8,8,768]{2,1,0:T(8,128)S(1)}) custom-call(bf16[768,1024]{1,0:T(8,128)(2,1)S(1)} %fusion.28.q_ref, bf16[2,272,1024]{2,1,0:T(8,128)(2,1)S(1)} %project.2.refs_0_), custom_call_target="tpu_custom_call" | custom-call | flops 1000000 | bytes 100000 | tf_op jit(solution)/shard_map/attend_fwd/pallas_call | solution.py:109
  156.4 8.0 %project.3 = (bf16[768,1024]{1,0:T(8,128)(2,1)S(1)}, bf16[2,768,1024]{2,1,0:T(8,128)(2,1)S(1)}) custom-call(bf16[768,1024]{1,0:T(8,128)(2,1)S(1)} %add_convert_fusion.5.x_ref.refs_6_, bf16[1344,8,1024]{2,1,0:T(8,128)(2,1)} %bitcast.53), custom_call_target="tpu_custom_call" | custom-call | flops 1000000 | bytes 100000 | tf_op jit(solution)/shard_map/project/pallas_call | solution.py:1231
  173.4 17.9 %attend_fwd.4 = (bf16[768,1024]{1,0:T(8,128)(2,1)S(1)}, f32[8,8,768]{2,1,0:T(8,128)S(1)}) custom-call(bf16[768,1024]{1,0:T(8,128)(2,1)S(1)} %get-tuple-element.103.q_ref, bf16[2,768,1024]{2,1,0:T(8,128)(2,1)} %copy-done, bf16[2,768,1024]{2,1,0:T(8,128)(2,1)} %copy-done.37), custom_call_target="tpu_custom_call" | custom-call | flops 1000000 | bytes 100000 | tf_op jit(solution)/shard_map/attend_fwd/pallas_call | solution.py:109
  191.9 17.8 %attend_fwd.5 = (bf16[768,1024]{1,0:T(8,128)(2,1)S(1)}, f32[8,8,768]{2,1,0:T(8,128)S(1)}) custom-call(bf16[768,1024]{1,0:T(8,128)(2,1)S(1)} %get-tuple-element.103.q_ref, bf16[2,768,1024]{2,1,0:T(8,128)(2,1)} %copy-done, bf16[2,768,1024]{2,1,0:T(8,128)(2,1)} %copy-done.37, ...), custom_call_target="tpu_custom_call", output_to_operand_aliasing={{0}: (3, {}), {1}: (4, {})} | custom-call | flops 1000000 | bytes 100000 | tf_op jit(solution)/shard_map/attend_fwd/pallas_call | solution.py:109
  209.8 4.6 collective-permute-done.4.refs_3_
  222.5 29.1 %mlp_fwd.1 = (f32[4,768,1024]{2,1,0:T(8,128)}, bf16[4,768,1024]{2,1,0:T(8,128)(2,1)}, bf16[768,1024]{1,0:T(8,128)(2,1)}) custom-call(bf16[4,256,1024]{2,1,0:T(8,128)(2,1)} %get-tuple-element.99.refs_0_, bf16[4,256,1024]{2,1,0:T(8,128)(2,1)} %collective-permute-done.1.refs_1_, bf16[4,256,1024]{2,1,0:T(8,128)(2,1)} %collective-permute-done.2.refs_2_, ...), custom_call_target="tpu_custom_call" | custom-call | flops 1000000 | bytes 100000 | tf_op jit(solution)/shard_map/mlp_fwd/pallas_call | solution.py:880
  252.7 6.1 spread_deconv.1.w_ref
  258.9 5.8 deconv_fwd.1.near_ref
  271.7 20.1 %render.1 = (f32[8,128]{1,0:T(8,128)S(1)}, bf16[3,80,1024]{2,1,0:T(8,128)(2,1)S(1)}, bf16[3,80,1024]{2,1,0:T(8,128)(2,1)S(1)}, f32[80,64]{1,0:T(8,128)S(1)}, f32[64,8]{1,0:T(8,128)S(1)}) custom-call(s32[3,16,256]{2,1,0:T(8,128)S(1)} %add_select_fusion.samples_ref, bf16[3,1024,128]{2,1,0:T(8,128)(2,1)} %deconv_fwd.1.near_ref, ...), custom_call_target="tpu_custom_call" | custom-call | tf_op jit(solution)/shard_map/render/pallas_call | solution.py:332
  295.2 16.0 %deconv_bwd.1 = (f32[3,256,1024]{2,1,0:T(8,128)}, bf16[3,32,1024]{2,1,0:T(8,128)(2,1)}, bf16[160,8,1024]{2,1,0:T(8,128)(2,1)}) custom-call(bf16[3,80,1024]{2,1,0:T(8,128)(2,1)} %copy-done.27, bf16[3,80,1024]{2,1,0:T(8,128)(2,1)} %copy-done.54, bf16[3,256,1024]{2,1,0:T(8,128)(2,1)} %bitcast.45, bf16[3,32,1024]{2,1,0:T(8,128)(2,1)} %copy-done.24, ...), custom_call_target="tpu_custom_call" | custom-call | tf_op jit(solution)/shard_map/deconv_bwd/pallas_call | solution.py:1165
  319.8 45.2 %mlp_bwd.1 = (f32[768,1024]{1,0:T(8,128)}, bf16[16,256,1024]{2,1,0:T(8,128)(2,1)}, bf16[16,256,1024]{2,1,0:T(8,128)(2,1)}) custom-call(bf16[4,256,1024]{2,1,0:T(8,128)(2,1)} %get-tuple-element.99.refs_0_, bf16[4,256,1024]{2,1,0:T(8,128)(2,1)} %collective-permute-done.1.refs_1_, bf16[4,256,1024]{2,1,0:T(8,128)(2,1)} %collective-permute-done.2.refs_2_, ...), custom_call_target="tpu_custom_call" | custom-call | flops 1000000 | bytes 100000 | tf_op jit(solution)/shard_map/mlp_bwd/pallas_call | solution.py:989
  374.6 5.3 fusion.34.refs_4_
  386.0 45.3 %attend_bwd.3 = (bf16[768,1024]{1,0:T(8,128)(2,1)S(1)}, bf16[2,768,1024]{2,1,0:T(8,128)(2,1)}, bf16[2,768,1024]{2,1,0:T(8,128)(2,1)}) custom-call(bf16[768,1024]{1,0:T(8,128)(2,1)S(1)} %get-tuple-element.103.q_ref, bf16[2,768,1024]{2,1,0:T(8,128)(2,1)} %copy-done, bf16[2,768,1024]{2,1,0:T(8,128)(2,1)} %copy-done.37, ...), custom_call_target="tpu_custom_call" | custom-call | flops 1000000 | bytes 100000 | tf_op jit(solution)/shard_map/attend_bwd/pallas_call | solution.py:182
  432.6 5.0 add_convert_fusion.2
  437.6 7.9 %attend_bwd.4 = (bf16[768,1024]{1,0:T(8,128)(2,1)S(1)}, bf16[2,768,1024]{2,1,0:T(8,128)(2,1)}, bf16[2,768,1024]{2,1,0:T(8,128)(2,1)}) custom-call(bf16[768,1024]{1,0:T(8,128)(2,1)S(1)} %get-tuple-element.103.q_ref, bf16[2,768,1024]{2,1,0:T(8,128)(2,1)} %copy-done, ...), custom_call_target="tpu_custom_call", output_to_operand_aliasing={{0}: (6, {}), {1}: (7, {}), {2}: (8, {})} | custom-call | flops 1000000 | bytes 100000 | tf_op jit(solution)/shard_map/attend_bwd/pallas_call | solution.py:182
  456.7 9.3 %project_back.1 = f32[768,1024]{1,0:T(8,128)S(1)} custom-call(bf16[768,1024]{1,0:T(8,128)(2,1)S(1)} %copy-done.5, bf16[2,768,1024]{2,1,0:T(8,128)(2,1)S(1)} %add_convert_fusion.1.g_ref.refs_8_, bf16[1344,8,1024]{2,1,0:T(8,128)(2,1)} %bitcast.55), custom_call_target="tpu_custom_call" | custom-call | flops 1000000 | bytes 100000 | tf_op jit(solution)/shard_map/project_back/pallas_call | solution.py:1269
  469.5 5.1 fusion.31.refs_3_
  474.6 13.2 %attend_bwd.5 = (bf16[768,1024]{1,0:T(8,128)(2,1)S(1)}, bf16[2,272,1024]{2,1,0:T(8,128)(2,1)S(1)}) custom-call(bf16[768,1024]{1,0:T(8,128)(2,1)S(1)} %copy-done.15, bf16[2,272,1024]{2,1,0:T(8,128)(2,1)S(1)} %copy-done.8, f32[8,8,768]{2,1,0:T(8,128)S(1)} %copy-done.29, bf16[768,1024]{1,0:T(8,128)(2,1)} %copy-done.13, bf16[768,1024]{1,0:T(8,128)(2,1)} %fusion.31.refs_3_), custom_call_target="tpu_custom_call" | custom-call | flops 1000000 | bytes 100000 | tf_op jit(solution)/shard_map/attend_bwd/pallas_call | solution.py:182
  487.9 5.2 fusion.10
  503.1 22.6 %weight_grads.1 = bf16[1344,8,1024]{2,1,0:T(8,128)(2,1)} custom-call(bf16[768,1024]{1,0:T(8,128)(2,1)} %copy-done.51, bf16[768,1024]{1,0:T(8,128)(2,1)} %copy-done.19, bf16[272,768]{1,0:T(8,128)(2,1)} %copy-done.16, bf16[2,272,1024]{2,1,0:T(8,128)(2,1)} %copy-done.22, bf16[768,1024]{1,0:T(8,128)(2,1)} %copy-done.13, bf16[768,1024]{1,0:T(8,128)(2,1)} %copy-done.50, ...), custom_call_target="tpu_custom_call" | custom-call | flops 1000000 | bytes 100000 | tf_op jit(solution)/shard_map/weight_grads/pallas_call | solution.py:1358
  526.3 115.6 %scatter_sum.1 = (f32[336,1024]{1,0:T(8,128)S(1)}, f32[8,128]{1,0:T(8,128)S(1)}, bf16[512,1024]{1,0:T(8,128)(2,1)S(1)}) custom-call(bf16[10752,1024]{1,0:T(8,128)(2,1)} %bitcast.56, f32[256,128]{1,0:T(8,128)S(1)} %broadcast_in_dim.59.refs_1_, bf16[16,256,1024]{2,1,0:T(8,128)(2,1)} %get-tuple-element.121.refs_2_, bf16[16,256,1024]{2,1,0:T(8,128)(2,1)} %copy-done.39, ...), custom_call_target="tpu_custom_call" | custom-call | tf_op jit(solution)/shard_map/scatter_sum/pallas_call | solution.py:801
  647.9 11.3 %shampoo.1 = (f32[32,128,128]{2,1,0:T(8,128)}, f32[32,128,128]{2,1,0:T(8,128)}, f32[32,128,128]{2,1,0:T(8,128)}, f32[32,128,128]{2,1,0:T(8,128)}, f32[32,128]{1,0:T(8,128)}) custom-call(bf16[512,1024]{1,0:T(8,128)(2,1)} %copy-done.23, f32[32,128,128]{2,1,0:T(8,128)} %blocks_ref.3, f32[32,128,128]{2,1,0:T(8,128)} %sl_ref.1, f32[32,128,128]{2,1,0:T(8,128)} %sr_ref.1, ...), custom_call_target="tpu_custom_call" | custom-call | tf_op jit(solution)/shard_map/shampoo/pallas_call | solution.py:1620
  663.2 4.8 adam.1
  (244 shorter events, 120.8 us)
Async XLA Ops:
  1.6 8.2 %collective-permute-start = (f32[448,128]{1,0:T(8,128)S(1)}, f32[448,128]{1,0:T(8,128)S(1)}, u32[]{:S(2)}, u32[]{:S(2)}) collective-permute-start(f32[448,128]{1,0:T(8,128)S(1)} %slice_bitcast_fusion), channel_id=1, source_target_pairs={{1,0},{2,1},{3,2},{4,3},{5,4},{6,5},{7,6},{8,7},{9,8},{10,9},{11,1... | collective-permute-start | bytes 688136 | tf_op jit(solution)/shard_map/ppermute | solution.py:1490
  6.1 126.9 %copy-start.16 = (bf16[272,768]{1,0:T(8,128)(2,1)}, bf16[272,768]{1,0:T(8,128)(2,1)S(1)}, u32[]{:S(2)}) copy-start(bf16[272,768]{1,0:T(8,128)(2,1)S(1)} %pad.17.x_ref.refs_2_) | copy-start | bytes 1253380
  129.7 20.9 %copy-start.40 = (bf16[256,1024]{1,0:T(8,128)(2,1)}, bf16[256,1024]{1,0:T(8,128)(2,1)S(1)}, u32[]{:S(2)}) copy-start(bf16[256,1024]{1,0:T(8,128)(2,1)S(1)} %get-tuple-element.172) | copy-start | bytes 1572868
  129.7 20.9 %copy-start.42 = (bf16[256,1024]{1,0:T(8,128)(2,1)}, bf16[256,1024]{1,0:T(8,128)(2,1)S(1)}, u32[]{:S(2)}) copy-start(bf16[256,1024]{1,0:T(8,128)(2,1)S(1)} %get-tuple-element.173) | copy-start | bytes 1572868
  130.6 25.7 %collective-permute-start.1 = (bf16[4,256,1024]{2,1,0:T(8,128)(2,1)}, bf16[4,256,1024]{2,1,0:T(8,128)(2,1)}, u32[]{:S(2)}, u32[]{:S(2)}) collective-permute-start(bf16[4,256,1024]{2,1,0:T(8,128)(2,1)} %get-tuple-element.99.refs_0_), channel_id=1, source_target_pairs={{0,2},{1,5},{2,0},{3,7},{4,6},{5,1},{6,4},{7,3},{8,10},{9,13},{10,... | collective-permute-start | bytes 6291464 | tf_op jit(solution)/shard_map/ppermute | solution.py:1670
  164.4 7.3 %collective-permute-start.3 = (bf16[2,768,1024]{2,1,0:T(8,128)(2,1)S(1)}, bf16[2,768,1024]{2,1,0:T(8,128)(2,1)S(1)}, u32[]{:S(2)}, u32[]{:S(2)}) collective-permute-start(bf16[2,768,1024]{2,1,0:T(8,128)(2,1)S(1)} %get-tuple-element.104.refs_0_), channel_id=1, source_target_pairs={{0,1},{1,0},{2,3},{3,2},{4,5},{5,4},{6,7},{7,6},{8,9},{9,8},{10,11... | collective-permute-start | bytes 9437192 | tf_op jit(solution)/shard_map/ppermute | solution.py:1831
  166.4 25.5 %collective-permute-start.2 = (bf16[4,256,1024]{2,1,0:T(8,128)(2,1)}, bf16[4,256,1024]{2,1,0:T(8,128)(2,1)}, u32[]{:S(2)}, u32[]{:S(2)}) collective-permute-start(bf16[4,256,1024]{2,1,0:T(8,128)(2,1)} %get-tuple-element.99.refs_0_), channel_id=1, source_target_pairs={{0,4},{1,3},{2,6},{3,1},{4,0},{5,7},{6,2},{7,5},{8,12},{9,11},{10,... | collective-permute-start | bytes 6291464 | tf_op jit(solution)/shard_map/ppermute | solution.py:1690
  167.9 46.5 %collective-permute-start.4 = (bf16[4,256,1024]{2,1,0:T(8,128)(2,1)}, bf16[4,256,1024]{2,1,0:T(8,128)(2,1)}, u32[]{:S(2)}, u32[]{:S(2)}) collective-permute-start(bf16[4,256,1024]{2,1,0:T(8,128)(2,1)} %collective-permute-done.1.refs_1_), channel_id=1, source_target_pairs={{0,4},{1,3},{2,6},{3,1},{4,0},{5,7},{6,2},{7,5},{8,12},{9,11},{10,... | collective-permute-start | bytes 6291464 | tf_op jit(solution)/shard_map/ppermute | solution.py:1698
  167.9 54.0 %collective-permute-start.5 = (bf16[4,256,1024]{2,1,0:T(8,128)(2,1)}, bf16[4,256,1024]{2,1,0:T(8,128)(2,1)}, u32[]{:S(2)}, u32[]{:S(2)}) collective-permute-start(bf16[4,256,1024]{2,1,0:T(8,128)(2,1)} %get-tuple-element.99.refs_0_), channel_id=1, source_target_pairs={{0,1},{1,0},{2,3},{3,2},{4,5},{5,4},{6,7},{7,6},{8,9},{9,8},{10,11... | collective-permute-start | bytes 6291464 | tf_op jit(solution)/shard_map/ppermute | solution.py:1706
  168.6 53.4 %collective-permute-start.6 = (bf16[4,256,1024]{2,1,0:T(8,128)(2,1)}, bf16[4,256,1024]{2,1,0:T(8,128)(2,1)}, u32[]{:S(2)}, u32[]{:S(2)}) collective-permute-start(bf16[4,256,1024]{2,1,0:T(8,128)(2,1)} %collective-permute-done.1.refs_1_), channel_id=1, source_target_pairs={{0,1},{1,0},{2,3},{3,2},{4,5},{5,4},{6,7},{7,6},{8,9},{9,8},{10,11... | collective-permute-start | bytes 6291464 | tf_op jit(solution)/shard_map/ppermute | solution.py:1706
  209.8 227.9 %copy-start.3 = (bf16[768,1024]{1,0:T(8,128)(2,1)}, bf16[768,1024]{1,0:T(8,128)(2,1)S(1)}, u32[]{:S(2)}) copy-start(bf16[768,1024]{1,0:T(8,128)(2,1)S(1)} %get-tuple-element.109.refs_3_.refs_9_) | copy-start | bytes 4718596
  214.4 7.6 %collective-permute-start.8 = (bf16[4,256,1024]{2,1,0:T(8,128)(2,1)}, bf16[4,256,1024]{2,1,0:T(8,128)(2,1)}, u32[]{:S(2)}, u32[]{:S(2)}) collective-permute-start(bf16[4,256,1024]{2,1,0:T(8,128)(2,1)} %collective-permute-done.4.refs_3_), channel_id=1, source_target_pairs={{0,1},{1,0},{2,3},{3,2},{4,5},{5,4},{6,7},{7,6},{8,9},{9,8},{10,11... | collective-permute-start | bytes 6291464 | tf_op jit(solution)/shard_map/ppermute | solution.py:1706
  215.3 7.1 %collective-permute-start.7 = (bf16[4,256,1024]{2,1,0:T(8,128)(2,1)}, bf16[4,256,1024]{2,1,0:T(8,128)(2,1)}, u32[]{:S(2)}, u32[]{:S(2)}) collective-permute-start(bf16[4,256,1024]{2,1,0:T(8,128)(2,1)} %collective-permute-done.2.refs_2_), channel_id=1, source_target_pairs={{0,1},{1,0},{2,3},{3,2},{4,5},{5,4},{6,7},{7,6},{8,9},{9,8},{10,11... | collective-permute-start | bytes 6291464 | tf_op jit(solution)/shard_map/ppermute | solution.py:1706
  220.2 31.3 %copy-start.60 = (f32[768]{0:T(1024)}, f32[768]{0:T(1024)S(1)}, u32[]{:S(2)}) copy-start(f32[768]{0:T(1024)S(1)} %multiply_reduce_fusion.4) | copy-start | bytes 9220
  252.6 6.2 collective-permute-start.9
  264.8 6.9 %collective-permute-start.10 = (bf16[3,1024,128]{2,1,0:T(8,128)(2,1)}, bf16[3,1024,128]{2,1,0:T(8,128)(2,1)}, u32[]{:S(2)}, u32[]{:S(2)}) collective-permute-start(bf16[3,1024,128]{2,1,0:T(8,128)(2,1)} %deconv_fwd.1.near_ref), channel_id=1, source_target_pairs={{0,1},{1,0},{2,3},{3,2},{4,5},{5,4},{6,7},{7,6},{8,9},{9,8},{10,11... | collective-permute-start | bytes 2359304 | tf_op jit(solution)/shard_map/ppermute | solution.py:1844
  292.5 1.9 collective-permute-start.11
  311.1 1.7 collective-permute-start.12
  365.0 14.9 %collective-permute-start.13 = (bf16[16,256,1024]{2,1,0:T(8,128)(2,1)}, bf16[16,256,1024]{2,1,0:T(8,128)(2,1)S(1)}, u32[]{:S(2)}, u32[]{:S(2)}) collective-permute-start(bf16[16,256,1024]{2,1,0:T(8,128)(2,1)} %get-tuple-element.122), channel_id=1, source_target_pairs={{0,1},{1,0},{2,3},{3,2},{4,5},{5,4},{6,7},{7,6},{8,9},{9,8},{10,11... | collective-permute-start | bytes 25165832 | tf_op jit(solution)/shard_map/ppermute | solution.py:1715
  384.6 48.0 %collective-permute-start.14 = (bf16[8,256,1024]{2,1,0:T(8,128)(2,1)}, bf16[8,256,1024]{2,1,0:T(8,128)(2,1)}, u32[]{:S(2)}, u32[]{:S(2)}) collective-permute-start(bf16[8,256,1024]{2,1,0:T(8,128)(2,1)} %add_convert_fusion), channel_id=1, source_target_pairs={{0,4},{1,3},{2,6},{3,1},{4,0},{5,7},{6,2},{7,5},{8,12},{9,11},{10,... | collective-permute-start | bytes 12582920 | tf_op jit(solution)/shard_map/ppermute | solution.py:1727
  446.6 6.6 collective-permute-start.16
  449.0 38.8 %collective-permute-start.15 = (bf16[4,256,1024]{2,1,0:T(8,128)(2,1)}, bf16[4,256,1024]{2,1,0:T(8,128)(2,1)S(1)}, u32[]{:S(2)}, u32[]{:S(2)}) collective-permute-start(bf16[4,256,1024]{2,1,0:T(8,128)(2,1)} %add_convert_fusion.2), channel_id=1, source_target_pairs={{0,2},{1,5},{2,0},{3,7},{4,6},{5,1},{6,4},{7,3},{8,10},{9,13},{10,... | collective-permute-start | bytes 6291464 | tf_op jit(solution)/shard_map/ppermute | solution.py:1735
  503.1 23.3 %copy-start.18 = (bf16[4,256,1024]{2,1,0:T(8,128)(2,1)S(1)}, bf16[4,256,1024]{2,1,0:T(8,128)(2,1)}, u32[]{:S(2)}) copy-start(bf16[4,256,1024]{2,1,0:T(8,128)(2,1)} %copy-done.17) | copy-start | bytes 6291460
  643.0 17.5 %collective-permute-start.17 = (f32[448,128]{1,0:T(8,128)S(1)}, f32[448,128]{1,0:T(8,128)S(1)}, u32[]{:S(2)}, u32[]{:S(2)}) collective-permute-start(f32[448,128]{1,0:T(8,128)S(1)} %slice.193), channel_id=1, source_target_pairs={{0,1},{1,2},{2,3},{3,4},{4,5},{5,6},{6,7},{7,8},{8,9},{9,10},{10,1... | collective-permute-start | bytes 688136 | tf_op jit(solution)/shard_map/ppermute | solution.py:1577
  (58 other events, 290.6 us)

commit v6 on v5

--- a/solution.py
+++ b/solution.py
@@ -437,16 +437,17 @@
     return ((1 - second) * ((2 * c + k) * 8 + p) + second * (4 * p + 2 * c + k)) * BLOCK
 
 
-ORDER = [("near", 0), ("z", 1), ("z", 3), ("far", 0), ("z", 2), ("near", 1), ("near", 3), ("near", 2)]
-ORDER += [("both", 0), ("far", 1), ("far", 3), ("far", 2), ("both", 1), ("both", 3), ("both", 2)]
+ORDER = [("near", 0), ("z", 1), ("far", 0), ("z", 2), ("z", 3), ("near", 1), ("near", 2), ("near", 3)]
+ORDER += [("both", 0), ("far", 1), ("far", 2), ("far", 3), ("both", 1), ("both", 2), ("both", 3)]
 ORDER += [("core", i) for i in range(16)]
+
 
 def gather_kernel(layouts, stagger, *refs):
     count = len(layouts)
     fulls = refs[count + 1 : 2 * count + 1]
     line_full = refs[2 * count + 1]
-    send, recv, local, line_sems = refs[2 * count + 2 : 2 * count + 6]
-    held = refs[2 * count + 6 :]
+    send, recv, local, z_send, line_recv, line_send = refs[2 * count + 2 : 2 * count + 8]
+    held = refs[2 * count + 8 :]
     brought = [pltpu.make_async_copy(s, h, local.at[n]) for n, (s, h) in enumerate(zip(refs[: count + 1], held))]
     for copy in brought:
         copy.start()
@@ -457,26 +458,26 @@
     for copy in brought:
         copy.wait()
     jobs = [(a, j) for a, layout in enumerate(layouts) for j in range(layout[0])]
+    me = (p, c)
+    up, down = (p + 4, c), (p - 4, c)
 
     def target(owner, job):
         a, j = jobs[job]
         _, rows, place = layouts[a]
         return fulls[a].at[pl.ds(pl.multiple_of(place(*owner, j), 8), rows)]
 
-    def source(job):
+    def source(owner, job):
+        if owner is not me:
+            return target(owner, job)
         a, j = jobs[job]
         rows = layouts[a][1]
         return sources[a].at[pl.ds(j * rows, rows)]
 
-    started = []
-
-    def forward(owner, own, event, peer, job):
-        t = target(owner, job)
-        copy = pltpu.make_async_remote_copy(
-            source(job) if own else t, t, send.at[event, job], recv.at[event, job], device_id=peer, device_id_type=MESH_ID
+    def sending(owner, event, peer, job, sem=None):
+        return pltpu.make_async_remote_copy(
+            source(owner, job), target(owner, job), send.at[event, job] if sem is None else sem, recv.at[event, job],
+            device_id=peer, device_id_type=MESH_ID,
         )
-        copy.start()
-        started.append(copy)
 
     def arrive(owner, event, job):
         t = target(owner, job)
@@ -484,75 +485,157 @@
             t, t, send.at[event, job], recv.at[event, job], device_id=(p, 1 - c), device_id_type=MESH_ID
         ).wait_recv()
 
-    me = (p, c)
+    def sending_up(distance, job):
+        owner = me if distance == 1 else (zs[5 - distance], c)
+        return sending(owner, 3 - distance, up, job, z_send.at[0, distance - 1, job])
+
+    def sending_down(distance, job):
+        owner = me if distance == 1 else (zs[distance - 1], c)
+        return sending(owner, distance - 1, down, job, z_send.at[1, distance - 1, job])
+
+    def line_up(distance):
+        held_at = line_source if distance == 1 else line_full.at[5 - distance]
+        return pltpu.make_async_remote_copy(
+            held_at, line_full.at[4 - distance], line_send.at[0, distance - 1], line_recv.at[4 - distance],
+            device_id=up, device_id_type=MESH_ID,
+        )
+
+    def line_down(distance):
+        held_at = line_source if distance == 1 else line_full.at[distance - 1]
+        return pltpu.make_async_remote_copy(
+            held_at, line_full.at[distance], line_send.at[1, distance - 1], line_recv.at[distance],
+            device_id=down, device_id_type=MESH_ID,
+        )
+
+    def each_way(distance, work):
+        @pl.when(z + distance <= 3)
+        def _():
+            work(distance, True)
+
+        @pl.when(z >= distance)
+        def _():
+            work(4 - distance, False)
+
+    def pass_on(ups, downs, distance, *job):
+        if distance > 3:
+            return
+
+        @pl.when((z < 3) & (z >= distance - 1))
+        def _():
+            ups(distance, *job)
+
+        @pl.when((z > 0) & (z + distance - 1 <= 3))
+        def _():
+            downs(distance, *job)
 
     def begin(job):
-        forward(me, True, 3, (near, c), job)
-        for k in (1, 3, 2):
-            forward(me, True, 3 - k, (zs[k], c), job)
-        forward(me, True, 7, (far, c), job)
-        forward(me, True, 15, (p, 1 - c), job)
-        pltpu.make_async_copy(source(job), target(me, job), local.at[job]).start()
+        sending(me, 3, (near, c), job).start()
+
+        @pl.when(z < 3)
+        def _():
+            sending_up(1, job).start()
+
+        @pl.when(z > 0)
+        def _():
+            sending_down(1, job).start()
+
+        sending(me, 7, (far, c), job).start()
+        sending(me, 15, (p, 1 - c), job).start()
+        pltpu.make_async_copy(source(me, job), target(me, job), local.at[job]).start()
+
+    def take_z(k, above, job):
+        owner = (zs[k], c)
+        arrive(owner, k - 1, job)
+        distance = k if above else 4 - k
+        if distance < 3:
+
+            @pl.when(z > 0 if above else z < 3)
+            def _():
+                (sending_down if above else sending_up)(distance + 1, job).start()
+
+        sending(owner, 3 + k, (near, c), job).start()
+        sending(owner, 7 + k, (far, c), job).start()
+        sending(owner, 15 + k, (p, 1 - c), job).start()
 
     def take(kind, k, job):
-        if kind == "z":
-            owner = (zs[k], c)
-            arrive(owner, k - 1, job)
-            forward(owner, False, 3 + k, (near, c), job)
-            forward(owner, False, 7 + k, (far, c), job)
-            forward(owner, False, 15 + k, (p, 1 - c), job)
-        elif kind == "near":
+        if kind == "near":
             owner = (along_z(near, z, k), c)
             arrive(owner, 3 + k, job)
-            forward(owner, False, 11 + k, (far, c), job)
-            forward(owner, False, 19 + k, (p, 1 - c), job)
+            sending(owner, 11 + k, (far, c), job).start()
+            sending(owner, 19 + k, (p, 1 - c), job).start()
         elif kind == "far":
             owner = (along_z(far, z, k), c)
             arrive(owner, 7 + k, job)
-            forward(owner, False, 23 + k, (p, 1 - c), job)
+            sending(owner, 23 + k, (p, 1 - c), job).start()
         elif kind == "both":
             owner = (along_z(both, z, k), c)
             arrive(owner, 11 + k, job)
-            forward(owner, False, 27 + k, (p, 1 - c), job)
+            sending(owner, 27 + k, (p, 1 - c), job).start()
         elif kind == "core":
             line = (p, far, near, both)[k // 4]
             arrive((along_z(line, z, k % 4), 1 - c), 15 + k, job)
 
-    lines = []
-    for k in (1, 3, 2):
-        lines.append(
-            pltpu.make_async_remote_copy(
-                line_source, line_full.at[4 - k], line_sems.at[k], line_sems.at[7 - k],
-                device_id=(zs[k], c), device_id_type=MESH_ID,
-            )
-        )
-    lines.append(pltpu.make_async_copy(line_source, line_full.at[0], line_sems.at[0]))
-
-    steps = [(2 * stagger + 2, -2, 0)]
+    def line_arrive(k):
+        spot = line_full.at[k]
+        pltpu.make_async_remote_copy(
+            spot, spot, line_send.at[0, 0], line_recv.at[k], device_id=(p, 1 - c), device_id_type=MESH_ID
+        ).wait_recv()
+
+    def line_take(k, above):
+        line_arrive(k)
+        distance = k if above else 4 - k
+        if distance < 3:
+
+            @pl.when(z > 0 if above else z < 3)
+            def _():
+                (line_down if above else line_up)(distance + 1).start()
+
+    steps = [(2 * stagger + 2 + 3 * n, -2, n) for n in range(4)]
     for job in range(len(jobs)):
         begin_at = stagger * min(job, layouts[0][0] - 1)
         for i in range(-1, len(ORDER)):
             steps.append((begin_at + i + 1, i, job))
+    own_line = pltpu.make_async_copy(line_source, line_full.at[0], line_recv.at[0])
     for _, i, job in sorted(steps):
         if i == -2:
-            for copy in lines:
-                copy.start()
+            if job == 0:
+
+                @pl.when(z < 3)
+                def _():
+                    line_up(1).start()
+
+                @pl.when(z > 0)
+                def _():
+                    line_down(1).start()
+
+                own_line.start()
+            else:
+                each_way(job, line_take)
         elif i < 0:
             begin(job)
         else:
-            take(*ORDER[i], job)
-    for k in (1, 2, 3):
-        spot = line_full.at[k]
-        pltpu.make_async_remote_copy(
-            spot, spot, line_sems.at[k], line_sems.at[3 + k], device_id=(p, 1 - c), device_id_type=MESH_ID
-        ).wait_recv()
-    for copy in lines[:3]:
-        copy.wait_send()
-    lines[3].wait()
-    for copy in started:
-        copy.wait_send()
+            kind, k = ORDER[i]
+            if kind == "z":
+                each_way(k, lambda n, above: take_z(n, above, job))
+            elif kind == "core" or k == 0:
+                take(kind, k, job)
+            else:
+                each_way(k, lambda n, above: take(kind, n, job))
+    own_line.wait()
+    for distance in (1, 2, 3):
+        pass_on(lambda d: line_up(d).wait_send(), lambda d: line_down(d).wait_send(), distance)
     for job in range(len(jobs)):
-        pltpu.make_async_copy(source(job), target(me, job), local.at[job]).wait()
+        for distance in (1, 2, 3):
+            pass_on(lambda d, n: sending_up(d, n).wait_send(), lambda d, n: sending_down(d, n).wait_send(), distance, job)
+        for k in range(4):
+            owner = (zs[k], c) if k else me
+            sending(owner, 3 + k, (near, c), job).wait_send()
+            sending(owner, 7 + k, (far, c), job).wait_send()
+            sending((along_z(near, z, k), c), 11 + k, (far, c), job).wait_send()
+            sending(owner, 15 + k, (p, 1 - c), job).wait_send()
+            for line, first in ((near, 19), (far, 23), (both, 27)):
+                sending((along_z(line, z, k), c), first + k, (p, 1 - c), job).wait_send()
+        pltpu.make_async_copy(source(me, job), target(me, job), local.at[job]).wait()
 
 
 def gather_all(layouts, stagger, shards_in, line, name_id):
@@ -569,7 +652,9 @@
             pltpu.SemaphoreType.DMA((31, copies)),
             pltpu.SemaphoreType.DMA((31, copies)),
             pltpu.SemaphoreType.DMA((copies,)),
-            pltpu.SemaphoreType.DMA((7,)),
+            pltpu.SemaphoreType.DMA((2, 3, copies)),
+            pltpu.SemaphoreType.DMA((4,)),
+            pltpu.SemaphoreType.DMA((2, 3)),
         ]
         + [pltpu.VMEM(a.shape, a.dtype) for a in (*shards_in, line)],
         compiler_params=pltpu.CompilerParams(collective_id=name_id, has_side_effects=True),
@@ -815,29 +900,31 @@
 GELU_B = 0.044715
 
 
-def chunk_sources():
+def chunk_sources(first):
     p, c, z, _, _, _ = places()
     x, y = p % 2, (p // 2) % 2
     out = []
-    for other in range(2):
-        core = (c + other) % 2
-        for g in range(4):
-            dx = (1 - core) * (g % 2) + core * (g // 2)
-            dy = (1 - core) * (g // 2) + core * (g % 2)
-            for k in range(4):
-                owner = ((z + k) % 4) * 4 + ((y + dy) % 2) * 2 + (x + dx) % 2
-                for half in range(2):
+    for n in range(4):
+        owner_z = (first + n) % 4
+        k = (owner_z - z + 4) % 4
+        for half in range(2):
+            for other in range(2):
+                core = (c + other) % 2
+                for g in range(4):
+                    dx = (1 - core) * (g % 2) + core * (g // 2)
+                    dy = (1 - core) * (g // 2) + core * (g % 2)
+                    owner = owner_z * 4 + ((y + dy) % 2) * 2 + (x + dx) % 2
                     out.append((other, g, k, half, block_chunk(owner, core, half) // BLOCK))
     return out
 
 
-def panel_loads(refs, held, sems):
+def panel_loads(refs, held, sems, first):
     if len(refs) == 1:
         for n in range(held.shape[0] // WIDE):
             at = pl.ds(n * WIDE, WIDE)
             pltpu.make_async_copy(refs[0].at[at], held.at[at], sems.at[n]).start()
         return
-    for other, g, k, half, chunk in chunk_sources():
+    for other, g, k, half, chunk in chunk_sources(first):
         source = refs[other * 4 + g].at[k, pl.ds(half * BLOCK, BLOCK)]
         target = held.at[pl.ds(pl.multiple_of(chunk * BLOCK, BLOCK), BLOCK)]
         pltpu.make_async_copy(source, target, sems.at[chunk // 8]).start()
@@ -857,7 +944,7 @@
 
     @pl.when(step == 0)
     def _():
-        panel_loads(sources, held, sems)
+        panel_loads(sources, held, sems, 0)
         total[...] = s_ref[...]
 
     up = product(h_ref[...], panel_ready(held, sems, step)[...])
@@ -910,7 +997,7 @@
 
     @pl.when(step == 0)
     def _():
-        panel_loads(sources, held, sems)
+        panel_loads(sources, held, sems, 2)
         dh_ref[...] = jnp.zeros_like(dh_ref)
 
     def tn_dot(left, right):

time: 680 us -> 667 us (0.981)
  Pallas kernels: 524 us -> 515 us
  transfers between devices with their start and end apart: 18 -> 18, of which waited for: 9 -> 10; matrix products, arithmetic and copies ran while one was open for 8% -> 8% of each run, Pallas kernels for 20% -> 21%
where the time goes in v6:
time: 667 us; the launch traced here: 657 us
  Pallas kernels  515 us (77%)
  other arithmetic  41.4 us (6%)
  local copies, waits for them, and re-layouts  35.2 us (5%)
  matrix products  27.9 us (4%)
  waiting for transfers between devices  19.8 us (3%)
  starting transfers between devices  12.9 us (2%)
    pallas_call x1, Pallas kernels, scatter_sum(): pl.pallas_call(functools.partial(scatter_kernel, layouts, stagger), out_s...  117 us
    pallas_call x1, Pallas kernels, gather_all(): pl.pallas_call(functools.partial(gather_kernel, layouts, stagger), out_sh...  107 us
    pallas_call x3, Pallas kernels, attend_bwd(): pl.pallas_call(functools.partial(attend_bwd_kernel, real_keys, chunk, len...  66.3 us
    pallas_call x3, Pallas kernels, attend_fwd(): pl.pallas_call(functools.partial(attend_fwd_kernel, real_keys, len(source...  46.2 us
    pallas_call x1, Pallas kernels, mlp_bwd(): pl.pallas_call(functools.partial(mlp_bwd_kernel, len(panels)), grid=(step...  42.7 us
    pallas_call x1, Pallas kernels, mlp_fwd(): pl.pallas_call(functools.partial(mlp_fwd_kernel, len(panels)), grid=(step...  26.4 us
    pallas_call x1, Pallas kernels, weight_grads(): pl.pallas_call(functools.partial(weight_grads_kernel, products, copies),...  22.6 us
    pallas_call x1, Pallas kernels, render(): pl.pallas_call(render_kernel, grid=(all_rays // rays,), in_specs=[pl.Bloc...  20.1 us
  transfers between devices with their start and end apart: 18, of which 10 were waited for; matrix products, arithmetic and copies ran while one was open for 8% of the time, Pallas kernels for 21%

profile of v6, /device:TPU:1, one launch (start us, length us, event | category | flops | bytes accessed | tf_op | source)
XLA Modules:
  0.0 657.2 jit_solution(18213227230068322550)
XLA Ops:
  15.5 106.6 %gather_all.1 = (bf16[10752,1024]{1,0:T(8,128)(2,1)}, f32[256,128]{1,0:T(8,128)}, bf16[4,256,1024]{2,1,0:T(8,128)(2,1)}) custom-call(bf16[336,1024]{1,0:T(8,128)(2,1)} %copy-done.25, f32[8,128]{1,0:T(8,128)} %copy-done.31, bf16[256,1024]{1,0:T(8,128)(2,1)} %copy-done.26), custom_call_target="tpu_custom_call" | custom-call | tf_op jit(solution)/shard_map/gather_all/pallas_call | solution.py:646
  133.7 10.5 %attend_fwd.3 = (bf16[768,1024]{1,0:T(8,128)(2,1)S(1)}, f32[8,8,768]{2,1,0:T(8,128)S(1)}) custom-call(bf16[768,1024]{1,0:T(8,128)(2,1)S(1)} %fusion.28.q_ref, bf16[2,272,1024]{2,1,0:T(8,128)(2,1)S(1)} %project.2.refs_0_), custom_call_target="tpu_custom_call" | custom-call | flops 1000000 | bytes 100000 | tf_op jit(solution)/shard_map/attend_fwd/pallas_call | solution.py:109
  151.2 7.5 %project.3 = (bf16[768,1024]{1,0:T(8,128)(2,1)S(1)}, bf16[2,768,1024]{2,1,0:T(8,128)(2,1)S(1)}) custom-call(bf16[768,1024]{1,0:T(8,128)(2,1)S(1)} %add_convert_fusion.5.x_ref.refs_6_, bf16[1344,8,1024]{2,1,0:T(8,128)(2,1)} %bitcast.53), custom_call_target="tpu_custom_call" | custom-call | flops 1000000 | bytes 100000 | tf_op jit(solution)/shard_map/project/pallas_call | solution.py:1318
  166.5 17.9 %attend_fwd.4 = (bf16[768,1024]{1,0:T(8,128)(2,1)S(1)}, f32[8,8,768]{2,1,0:T(8,128)S(1)}) custom-call(bf16[768,1024]{1,0:T(8,128)(2,1)S(1)} %get-tuple-element.103.q_ref, bf16[2,768,1024]{2,1,0:T(8,128)(2,1)} %copy-done, bf16[2,768,1024]{2,1,0:T(8,128)(2,1)} %copy-done.37), custom_call_target="tpu_custom_call" | custom-call | flops 1000000 | bytes 100000 | tf_op jit(solution)/shard_map/attend_fwd/pallas_call | solution.py:109
  185.1 17.8 %attend_fwd.5 = (bf16[768,1024]{1,0:T(8,128)(2,1)S(1)}, f32[8,8,768]{2,1,0:T(8,128)S(1)}) custom-call(bf16[768,1024]{1,0:T(8,128)(2,1)S(1)} %get-tuple-element.103.q_ref, bf16[2,768,1024]{2,1,0:T(8,128)(2,1)} %copy-done, bf16[2,768,1024]{2,1,0:T(8,128)(2,1)} %copy-done.37, ...), custom_call_target="tpu_custom_call", output_to_operand_aliasing={{0}: (3, {}), {1}: (4, {})} | custom-call | flops 1000000 | bytes 100000 | tf_op jit(solution)/shard_map/attend_fwd/pallas_call | solution.py:109
  202.9 4.6 collective-permute-done.4.refs_3_
  215.6 26.4 %mlp_fwd.1 = (f32[4,768,1024]{2,1,0:T(8,128)}, bf16[4,768,1024]{2,1,0:T(8,128)(2,1)}, bf16[768,1024]{1,0:T(8,128)(2,1)}) custom-call(bf16[4,256,1024]{2,1,0:T(8,128)(2,1)} %get-tuple-element.99.refs_0_, bf16[4,256,1024]{2,1,0:T(8,128)(2,1)} %collective-permute-done.1.refs_1_, bf16[4,256,1024]{2,1,0:T(8,128)(2,1)} %collective-permute-done.2.refs_2_, ...), custom_call_target="tpu_custom_call" | custom-call | flops 1000000 | bytes 100000 | tf_op jit(solution)/shard_map/mlp_fwd/pallas_call | solution.py:967
  243.2 6.1 spread_deconv.1.w_ref
  249.3 5.8 deconv_fwd.1.near_ref
  262.1 20.1 %render.1 = (f32[8,128]{1,0:T(8,128)S(1)}, bf16[3,80,1024]{2,1,0:T(8,128)(2,1)S(1)}, bf16[3,80,1024]{2,1,0:T(8,128)(2,1)S(1)}, f32[80,64]{1,0:T(8,128)S(1)}, f32[64,8]{1,0:T(8,128)S(1)}) custom-call(s32[3,16,256]{2,1,0:T(8,128)S(1)} %add_select_fusion.samples_ref, bf16[3,1024,128]{2,1,0:T(8,128)(2,1)} %deconv_fwd.1.near_ref, ...), custom_call_target="tpu_custom_call" | custom-call | tf_op jit(solution)/shard_map/render/pallas_call | solution.py:332
  285.6 16.0 %deconv_bwd.1 = (f32[3,256,1024]{2,1,0:T(8,128)}, bf16[3,32,1024]{2,1,0:T(8,128)(2,1)}, bf16[160,8,1024]{2,1,0:T(8,128)(2,1)}) custom-call(bf16[3,80,1024]{2,1,0:T(8,128)(2,1)} %copy-done.27, bf16[3,80,1024]{2,1,0:T(8,128)(2,1)} %copy-done.54, bf16[3,256,1024]{2,1,0:T(8,128)(2,1)} %bitcast.45, bf16[3,32,1024]{2,1,0:T(8,128)(2,1)} %copy-done.24, ...), custom_call_target="tpu_custom_call" | custom-call | tf_op jit(solution)/shard_map/deconv_bwd/pallas_call | solution.py:1252
  310.2 42.7 %mlp_bwd.1 = (f32[768,1024]{1,0:T(8,128)}, bf16[16,256,1024]{2,1,0:T(8,128)(2,1)}, bf16[16,256,1024]{2,1,0:T(8,128)(2,1)}) custom-call(bf16[4,256,1024]{2,1,0:T(8,128)(2,1)} %get-tuple-element.99.refs_0_, bf16[4,256,1024]{2,1,0:T(8,128)(2,1)} %collective-permute-done.1.refs_1_, bf16[4,256,1024]{2,1,0:T(8,128)(2,1)} %collective-permute-done.2.refs_2_, ...), custom_call_target="tpu_custom_call" | custom-call | flops 1000000 | bytes 100000 | tf_op jit(solution)/shard_map/mlp_bwd/pallas_call | solution.py:1076
  362.0 5.3 fusion.34.refs_4_
  373.4 45.3 %attend_bwd.3 = (bf16[768,1024]{1,0:T(8,128)(2,1)S(1)}, bf16[2,768,1024]{2,1,0:T(8,128)(2,1)}, bf16[2,768,1024]{2,1,0:T(8,128)(2,1)}) custom-call(bf16[768,1024]{1,0:T(8,128)(2,1)S(1)} %get-tuple-element.103.q_ref, bf16[2,768,1024]{2,1,0:T(8,128)(2,1)} %copy-done, bf16[2,768,1024]{2,1,0:T(8,128)(2,1)} %copy-done.37, ...), custom_call_target="tpu_custom_call" | custom-call | flops 1000000 | bytes 100000 | tf_op jit(solution)/shard_map/attend_bwd/pallas_call | solution.py:182
  419.9 5.0 add_convert_fusion.2
  424.9 7.8 %attend_bwd.4 = (bf16[768,1024]{1,0:T(8,128)(2,1)S(1)}, bf16[2,768,1024]{2,1,0:T(8,128)(2,1)}, bf16[2,768,1024]{2,1,0:T(8,128)(2,1)}) custom-call(bf16[768,1024]{1,0:T(8,128)(2,1)S(1)} %get-tuple-element.103.q_ref, bf16[2,768,1024]{2,1,0:T(8,128)(2,1)} %copy-done, ...), custom_call_target="tpu_custom_call", output_to_operand_aliasing={{0}: (6, {}), {1}: (7, {}), {2}: (8, {})} | custom-call | flops 1000000 | bytes 100000 | tf_op jit(solution)/shard_map/attend_bwd/pallas_call | solution.py:182
  444.2 9.3 %project_back.1 = f32[768,1024]{1,0:T(8,128)S(1)} custom-call(bf16[768,1024]{1,0:T(8,128)(2,1)S(1)} %copy-done.5, bf16[2,768,1024]{2,1,0:T(8,128)(2,1)S(1)} %add_convert_fusion.1.g_ref.refs_8_, bf16[1344,8,1024]{2,1,0:T(8,128)(2,1)} %bitcast.55), custom_call_target="tpu_custom_call" | custom-call | flops 1000000 | bytes 100000 | tf_op jit(solution)/shard_map/project_back/pallas_call | solution.py:1356
  456.9 5.1 fusion.31.refs_3_
  462.1 13.2 %attend_bwd.5 = (bf16[768,1024]{1,0:T(8,128)(2,1)S(1)}, bf16[2,272,1024]{2,1,0:T(8,128)(2,1)S(1)}) custom-call(bf16[768,1024]{1,0:T(8,128)(2,1)S(1)} %copy-done.15, bf16[2,272,1024]{2,1,0:T(8,128)(2,1)S(1)} %copy-done.8, f32[8,8,768]{2,1,0:T(8,128)S(1)} %copy-done.29, bf16[768,1024]{1,0:T(8,128)(2,1)} %copy-done.13, bf16[768,1024]{1,0:T(8,128)(2,1)} %fusion.31.refs_3_), custom_call_target="tpu_custom_call" | custom-call | flops 1000000 | bytes 100000 | tf_op jit(solution)/shard_map/attend_bwd/pallas_call | solution.py:182
  475.4 5.2 fusion.10
  490.6 22.6 %weight_grads.1 = bf16[1344,8,1024]{2,1,0:T(8,128)(2,1)} custom-call(bf16[768,1024]{1,0:T(8,128)(2,1)} %copy-done.51, bf16[768,1024]{1,0:T(8,128)(2,1)} %copy-done.19, bf16[272,768]{1,0:T(8,128)(2,1)} %copy-done.16, bf16[2,272,1024]{2,1,0:T(8,128)(2,1)} %copy-done.22, bf16[768,1024]{1,0:T(8,128)(2,1)} %copy-done.13, bf16[768,1024]{1,0:T(8,128)(2,1)} %copy-done.50, ...), custom_call_target="tpu_custom_call" | custom-call | flops 1000000 | bytes 100000 | tf_op jit(solution)/shard_map/weight_grads/pallas_call | solution.py:1445
  513.8 116.8 %scatter_sum.1 = (f32[336,1024]{1,0:T(8,128)S(1)}, f32[8,128]{1,0:T(8,128)S(1)}, bf16[512,1024]{1,0:T(8,128)(2,1)S(1)}) custom-call(bf16[10752,1024]{1,0:T(8,128)(2,1)} %bitcast.56, f32[256,128]{1,0:T(8,128)S(1)} %broadcast_in_dim.59.refs_1_, bf16[16,256,1024]{2,1,0:T(8,128)(2,1)} %get-tuple-element.121.refs_2_, bf16[16,256,1024]{2,1,0:T(8,128)(2,1)} %copy-done.39, ...), custom_call_target="tpu_custom_call" | custom-call | tf_op jit(solution)/shard_map/scatter_sum/pallas_call | solution.py:886
  635.4 11.3 %shampoo.1 = (f32[32,128,128]{2,1,0:T(8,128)}, f32[32,128,128]{2,1,0:T(8,128)}, f32[32,128,128]{2,1,0:T(8,128)}, f32[32,128,128]{2,1,0:T(8,128)}, f32[32,128]{1,0:T(8,128)}) custom-call(bf16[512,1024]{1,0:T(8,128)(2,1)} %copy-done.23, f32[32,128,128]{2,1,0:T(8,128)} %blocks_ref.3, f32[32,128,128]{2,1,0:T(8,128)} %sl_ref.1, f32[32,128,128]{2,1,0:T(8,128)} %sr_ref.1, ...), custom_call_target="tpu_custom_call" | custom-call | tf_op jit(solution)/shard_map/shampoo/pallas_call | solution.py:1707
  650.8 4.8 adam.1
  (244 shorter events, 118.0 us)
Async XLA Ops:
  1.6 8.2 %collective-permute-start = (f32[448,128]{1,0:T(8,128)S(1)}, f32[448,128]{1,0:T(8,128)S(1)}, u32[]{:S(2)}, u32[]{:S(2)}) collective-permute-start(f32[448,128]{1,0:T(8,128)S(1)} %slice_bitcast_fusion), channel_id=1, source_target_pairs={{1,0},{2,1},{3,2},{4,3},{5,4},{6,5},{7,6},{8,7},{9,8},{10,9},{11,1... | collective-permute-start | bytes 688136 | tf_op jit(solution)/shard_map/ppermute | solution.py:1577
  6.1 120.5 %copy-start.16 = (bf16[272,768]{1,0:T(8,128)(2,1)}, bf16[272,768]{1,0:T(8,128)(2,1)S(1)}, u32[]{:S(2)}) copy-start(bf16[272,768]{1,0:T(8,128)(2,1)S(1)} %pad.17.x_ref.refs_2_) | copy-start | bytes 1253380
  124.7 19.6 %copy-start.40 = (bf16[256,1024]{1,0:T(8,128)(2,1)}, bf16[256,1024]{1,0:T(8,128)(2,1)S(1)}, u32[]{:S(2)}) copy-start(bf16[256,1024]{1,0:T(8,128)(2,1)S(1)} %get-tuple-element.172) | copy-start | bytes 1572868
  124.7 19.6 %copy-start.42 = (bf16[256,1024]{1,0:T(8,128)(2,1)}, bf16[256,1024]{1,0:T(8,128)(2,1)S(1)}, u32[]{:S(2)}) copy-start(bf16[256,1024]{1,0:T(8,128)(2,1)S(1)} %get-tuple-element.173) | copy-start | bytes 1572868
  125.6 25.6 %collective-permute-start.1 = (bf16[4,256,1024]{2,1,0:T(8,128)(2,1)}, bf16[4,256,1024]{2,1,0:T(8,128)(2,1)}, u32[]{:S(2)}, u32[]{:S(2)}) collective-permute-start(bf16[4,256,1024]{2,1,0:T(8,128)(2,1)} %get-tuple-element.99.refs_0_), channel_id=1, source_target_pairs={{0,2},{1,5},{2,0},{3,7},{4,6},{5,1},{6,4},{7,3},{8,10},{9,13},{10,... | collective-permute-start | bytes 6291464 | tf_op jit(solution)/shard_map/ppermute | solution.py:1757
  158.7 6.2 collective-permute-start.3
  159.6 25.5 %collective-permute-start.2 = (bf16[4,256,1024]{2,1,0:T(8,128)(2,1)}, bf16[4,256,1024]{2,1,0:T(8,128)(2,1)}, u32[]{:S(2)}, u32[]{:S(2)}) collective-permute-start(bf16[4,256,1024]{2,1,0:T(8,128)(2,1)} %get-tuple-element.99.refs_0_), channel_id=1, source_target_pairs={{0,4},{1,3},{2,6},{3,1},{4,0},{5,7},{6,2},{7,5},{8,12},{9,11},{10,... | collective-permute-start | bytes 6291464 | tf_op jit(solution)/shard_map/ppermute | solution.py:1777
  161.0 46.5 %collective-permute-start.4 = (bf16[4,256,1024]{2,1,0:T(8,128)(2,1)}, bf16[4,256,1024]{2,1,0:T(8,128)(2,1)}, u32[]{:S(2)}, u32[]{:S(2)}) collective-permute-start(bf16[4,256,1024]{2,1,0:T(8,128)(2,1)} %collective-permute-done.1.refs_1_), channel_id=1, source_target_pairs={{0,4},{1,3},{2,6},{3,1},{4,0},{5,7},{6,2},{7,5},{8,12},{9,11},{10,... | collective-permute-start | bytes 6291464 | tf_op jit(solution)/shard_map/ppermute | solution.py:1785
  161.1 54.0 %collective-permute-start.5 = (bf16[4,256,1024]{2,1,0:T(8,128)(2,1)}, bf16[4,256,1024]{2,1,0:T(8,128)(2,1)}, u32[]{:S(2)}, u32[]{:S(2)}) collective-permute-start(bf16[4,256,1024]{2,1,0:T(8,128)(2,1)} %get-tuple-element.99.refs_0_), channel_id=1, source_target_pairs={{0,1},{1,0},{2,3},{3,2},{4,5},{5,4},{6,7},{7,6},{8,9},{9,8},{10,11... | collective-permute-start | bytes 6291464 | tf_op jit(solution)/shard_map/ppermute | solution.py:1793
  161.7 53.4 %collective-permute-start.6 = (bf16[4,256,1024]{2,1,0:T(8,128)(2,1)}, bf16[4,256,1024]{2,1,0:T(8,128)(2,1)}, u32[]{:S(2)}, u32[]{:S(2)}) collective-permute-start(bf16[4,256,1024]{2,1,0:T(8,128)(2,1)} %collective-permute-done.1.refs_1_), channel_id=1, source_target_pairs={{0,1},{1,0},{2,3},{3,2},{4,5},{5,4},{6,7},{7,6},{8,9},{9,8},{10,11... | collective-permute-start | bytes 6291464 | tf_op jit(solution)/shard_map/ppermute | solution.py:1793
  202.9 222.0 %copy-start.3 = (bf16[768,1024]{1,0:T(8,128)(2,1)}, bf16[768,1024]{1,0:T(8,128)(2,1)S(1)}, u32[]{:S(2)}) copy-start(bf16[768,1024]{1,0:T(8,128)(2,1)S(1)} %get-tuple-element.109.refs_3_.refs_9_) | copy-start | bytes 4718596
  207.6 7.6 %collective-permute-start.8 = (bf16[4,256,1024]{2,1,0:T(8,128)(2,1)}, bf16[4,256,1024]{2,1,0:T(8,128)(2,1)}, u32[]{:S(2)}, u32[]{:S(2)}) collective-permute-start(bf16[4,256,1024]{2,1,0:T(8,128)(2,1)} %collective-permute-done.4.refs_3_), channel_id=1, source_target_pairs={{0,1},{1,0},{2,3},{3,2},{4,5},{5,4},{6,7},{7,6},{8,9},{9,8},{10,11... | collective-permute-start | bytes 6291464 | tf_op jit(solution)/shard_map/ppermute | solution.py:1793
  208.5 7.1 %collective-permute-start.7 = (bf16[4,256,1024]{2,1,0:T(8,128)(2,1)}, bf16[4,256,1024]{2,1,0:T(8,128)(2,1)}, u32[]{:S(2)}, u32[]{:S(2)}) collective-permute-start(bf16[4,256,1024]{2,1,0:T(8,128)(2,1)} %collective-permute-done.2.refs_2_), channel_id=1, source_target_pairs={{0,1},{1,0},{2,3},{3,2},{4,5},{5,4},{6,7},{7,6},{8,9},{9,8},{10,11... | collective-permute-start | bytes 6291464 | tf_op jit(solution)/shard_map/ppermute | solution.py:1793
  213.4 28.6 %copy-start.60 = (f32[768]{0:T(1024)}, f32[768]{0:T(1024)S(1)}, u32[]{:S(2)}) copy-start(f32[768]{0:T(1024)S(1)} %multiply_reduce_fusion.4) | copy-start | bytes 9220
  243.0 6.3 collective-permute-start.9
  255.2 6.9 %collective-permute-start.10 = (bf16[3,1024,128]{2,1,0:T(8,128)(2,1)}, bf16[3,1024,128]{2,1,0:T(8,128)(2,1)}, u32[]{:S(2)}, u32[]{:S(2)}) collective-permute-start(bf16[3,1024,128]{2,1,0:T(8,128)(2,1)} %deconv_fwd.1.near_ref), channel_id=1, source_target_pairs={{0,1},{1,0},{2,3},{3,2},{4,5},{5,4},{6,7},{7,6},{8,9},{9,8},{10,11... | collective-permute-start | bytes 2359304 | tf_op jit(solution)/shard_map/ppermute | solution.py:1931
  283.0 1.9 collective-permute-start.11
  301.6 1.7 collective-permute-start.12
  352.9 14.3 %collective-permute-start.13 = (bf16[16,256,1024]{2,1,0:T(8,128)(2,1)}, bf16[16,256,1024]{2,1,0:T(8,128)(2,1)S(1)}, u32[]{:S(2)}, u32[]{:S(2)}) collective-permute-start(bf16[16,256,1024]{2,1,0:T(8,128)(2,1)} %get-tuple-element.122), channel_id=1, source_target_pairs={{0,1},{1,0},{2,3},{3,2},{4,5},{5,4},{6,7},{7,6},{8,9},{9,8},{10,11... | collective-permute-start | bytes 25165832 | tf_op jit(solution)/shard_map/ppermute | solution.py:1802
  371.9 48.0 %collective-permute-start.14 = (bf16[8,256,1024]{2,1,0:T(8,128)(2,1)}, bf16[8,256,1024]{2,1,0:T(8,128)(2,1)}, u32[]{:S(2)}, u32[]{:S(2)}) collective-permute-start(bf16[8,256,1024]{2,1,0:T(8,128)(2,1)} %add_convert_fusion), channel_id=1, source_target_pairs={{0,4},{1,3},{2,6},{3,1},{4,0},{5,7},{6,2},{7,5},{8,12},{9,11},{10,... | collective-permute-start | bytes 12582920 | tf_op jit(solution)/shard_map/ppermute | solution.py:1814
  433.9 6.7 %collective-permute-start.16 = (bf16[2,768,1024]{2,1,0:T(8,128)(2,1)}, bf16[2,768,1024]{2,1,0:T(8,128)(2,1)S(1)}, u32[]{:S(2)}, u32[]{:S(2)}) collective-permute-start(bf16[2,768,1024]{2,1,0:T(8,128)(2,1)} %get-tuple-element.137), channel_id=1, source_target_pairs={{0,1},{1,0},{2,3},{3,2},{4,5},{5,4},{6,7},{7,6},{8,9},{9,8},{10,11... | collective-permute-start | bytes 9437192 | tf_op jit(solution)/shard_map/ppermute | solution.py:1966
  436.5 38.8 %collective-permute-start.15 = (bf16[4,256,1024]{2,1,0:T(8,128)(2,1)}, bf16[4,256,1024]{2,1,0:T(8,128)(2,1)S(1)}, u32[]{:S(2)}, u32[]{:S(2)}) collective-permute-start(bf16[4,256,1024]{2,1,0:T(8,128)(2,1)} %add_convert_fusion.2), channel_id=1, source_target_pairs={{0,2},{1,5},{2,0},{3,7},{4,6},{5,1},{6,4},{7,3},{8,10},{9,13},{10,... | collective-permute-start | bytes 6291464 | tf_op jit(solution)/shard_map/ppermute | solution.py:1822
  490.6 23.3 %copy-start.18 = (bf16[4,256,1024]{2,1,0:T(8,128)(2,1)S(1)}, bf16[4,256,1024]{2,1,0:T(8,128)(2,1)}, u32[]{:S(2)}) copy-start(bf16[4,256,1024]{2,1,0:T(8,128)(2,1)} %copy-done.17) | copy-start | bytes 6291460
  631.7 16.4 %collective-permute-start.17 = (f32[448,128]{1,0:T(8,128)S(1)}, f32[448,128]{1,0:T(8,128)S(1)}, u32[]{:S(2)}, u32[]{:S(2)}) collective-permute-start(f32[448,128]{1,0:T(8,128)S(1)} %slice.193), channel_id=1, source_target_pairs={{0,1},{1,2},{2,3},{3,4},{4,5},{5,6},{6,7},{7,8},{8,9},{9,10},{10,1... | collective-permute-start | bytes 688136 | tf_op jit(solution)/shard_map/ppermute | solution.py:1664
  (58 other events, 288.0 us)

commit v7 on v6

--- a/solution.py
+++ b/solution.py
@@ -692,7 +692,8 @@
     def piece(owner, job):
         a, j = jobs[job]
         _, rows, place = layouts[a]
-        return grads[a].at[pl.ds(pl.multiple_of(place(*owner, j), 8), rows)]
+        at = place(*owner, j)
+        return grads[a].at[pl.ds(at if isinstance(at, int) else pl.multiple_of(at, 8), rows)]
 
     def to_core(i, job):
         g, k = SUM_ORDER[i]
@@ -1371,8 +1372,9 @@
 
 
 def weight_grads_kernel(products, copies, *refs):
-    arrays = refs[: len(refs) - 8]
-    out, left, right, staged, bounce, load_sem, store_sem, copy_sem = refs[len(refs) - 8 :]
+    arrays = refs[: len(refs) - 9]
+    out, left, right, staged, bounce, nothing, load_sem, store_sem, copy_sem = refs[len(refs) - 9 :]
+    place = lax.axis_index("strip")
     step = pl.program_id(0)
     steps = len(products)
 
@@ -1395,13 +1397,18 @@
         target = panel_view(out, first, count, deep).at[:, at]
         return pltpu.make_async_copy(source, target, store_sem.at[slot])
 
-    def bounced(n):
-        a, first, count = copies[n]
-        held = bounce.at[pl.ds(sum(c[2] for c in copies[:n]), count)]
-        return (
-            pltpu.make_async_copy(arrays[a], held, copy_sem.at[n, 0]),
-            pltpu.make_async_copy(held, out.at[pl.ds(first, count)], copy_sem.at[n, 1]),
-        )
+    def bring(n):
+        a, start, count, _, _ = copies[n]
+        held = bounce.at[pl.ds(sum(c[2] for c in copies[:n] if c[0] is not None), count)]
+        return pltpu.make_async_copy(arrays[a].at[pl.ds(start, count)], held, copy_sem.at[n, 0])
+
+    def put(n):
+        a, _, count, first, step = copies[n]
+        if a is None:
+            held = nothing.at[pl.ds(0, count)]
+        else:
+            held = bounce.at[pl.ds(sum(c[2] for c in copies[:n] if c[0] is not None), count)]
+        return pltpu.make_async_copy(held, out.at[pl.ds(first + step * place, count)], copy_sem.at[n, 1])
 
     for n in range(steps):
 
@@ -1410,12 +1417,15 @@
             if n == 0:
                 for job in loads(0):
                     job.start()
+                nothing[...] = jnp.zeros_like(nothing)
                 for m in range(len(copies)):
-                    bounced(m)[0].start()
+                    if copies[m][0] is not None:
+                        bring(m).start()
             if n == 1:
                 for m in range(len(copies)):
-                    bounced(m)[0].wait()
-                    bounced(m)[1].start()
+                    if copies[m][0] is not None:
+                        bring(m).wait()
+                    put(m).start()
             if n + 1 < steps:
                 for job in loads(n + 1):
                     job.start()
@@ -1435,7 +1445,7 @@
                     stores(n - 1).wait()
                 stores(n).wait()
                 for m in range(len(copies)):
-                    bounced(m)[1].wait()
+                    put(m).wait()
 
 
 def weight_grads(arrays, products, copies, tile_rows):
@@ -1452,7 +1462,8 @@
             pltpu.VMEM((2, rows, deep), jnp.bfloat16),
             pltpu.VMEM((2, rows, WIDE), jnp.bfloat16),
             pltpu.VMEM((2, deep // 8, 8, WIDE), jnp.bfloat16),
-            pltpu.VMEM((sum(c[2] for c in copies), 8, WIDE), jnp.bfloat16),
+            pltpu.VMEM((sum(c[2] for c in copies if c[0] is not None), 8, WIDE), jnp.bfloat16),
+            pltpu.VMEM((max(c[2] for c in copies if c[0] is None), 8, WIDE), jnp.bfloat16),
             pltpu.SemaphoreType.DMA((2, 2)),
             pltpu.SemaphoreType.DMA((2,)),
             pltpu.SemaphoreType.DMA((len(copies), 2)),
@@ -1753,7 +1764,7 @@
 def gather_weights(weights, blocks, part):
     if direct_links():
         own, tiles = prepare(weights, blocks)
-        rows, parts, line = gather_all([flat_chunks(own.shape[0], 3), META], 6, [own, part], tiles, 0)
+        rows, parts, line = gather_all([flat_chunks(own.shape[0], 3), META], 4, [own, part], tiles, 0)
         near = lax.ppermute(line, AXES, NEAR)
         return rows, [line, near], jnp.sum(parts[::8, 0])
     flat = lax.all_gather(weights.astype(jnp.bfloat16), AXES, axis=0, tiled=True)
@@ -1785,12 +1796,13 @@
         self.parts = [line, near, far, lax.ppermute(near, AXES, FAR)]
         return before
 
-    def third(self, after):
+    def third(self, after, beside):
         if not self.staged:
-            return self.parts
+            return self.parts, beside
         line, near, far, both = self.parts
-        both, after = lax.optimization_barrier((both, after))
-        return [line, near, far, both] + [lax.ppermute(group, AXES, CORE) for group in (line, near, far, both)]
+        both, after, beside = lax.optimization_barrier((both, after, beside))
+        others = [lax.ppermute(group, AXES, CORE) for group in (line, near, far, both)]
+        return [line, near, far, both] + others, beside
 
 
 class PanelSums:
@@ -1831,8 +1843,8 @@
 
 
 def reduce_grads(rows, panels, part):
-    meta = jnp.full((32 * 8, 128), part, jnp.float32)
-    summed, parts, tiles = scatter_sum([flat_chunks(rows.shape[0] // 32, 3), META], 6, [rows, meta], panels, 1)
+    everyone = (1, 8, lambda p, c, j: 0)
+    summed, parts, tiles = scatter_sum([flat_chunks(rows.shape[0] // 32, 3), everyone], 6, [rows, part], panels, 1)
     return summed, tiles, parts[0, 0]
 
 
@@ -1847,7 +1859,7 @@
     flat_sum = lax.psum_scatter(flat, AXES, scatter_dimension=0, tiled=True)
     tile_sum = lax.psum_scatter(tiles, AXES, scatter_dimension=0, tiled=True)
     tile_sum = lax.all_gather(tile_sum.astype(jnp.bfloat16), "strip", axis=0, tiled=True)
-    return flat_sum, chunks_of(tile_sum), lax.psum(part, AXES)
+    return flat_sum, chunks_of(tile_sum), lax.psum(part[0, 0], AXES)
 
 
 def adam_plainly(grad, weights, first_moment, second_moment):
@@ -1920,7 +1932,7 @@
     early = attend_fwd(query2, kv_both, all_keys, (0, pairs // 2))
     early = (panels.second(early[0]), early[1])
     self_out, total_two = attend_fwd(query2, kv_both, all_keys, (pairs // 2, pairs), early)
-    panels = panels.third(self_out)
+    panels, deconv = panels.third(self_out, deconv)
     stream2 = stream1 + product(self_out, square("out_self"))
     hidden3, norm_three = jax.vjp(norm_mod, stream2, mods[4], mods[5])
     hidden3 = hidden3.astype(jnp.bfloat16)
@@ -1942,7 +1954,6 @@
         jnp.pad(decode_out, ((0, 0), (0, 4))),
         rays,
     )
-    loss_part = loss_part[0, 0]
     grad_decode_out = grad_decode_out[:, :4]
     grad_far = lax.ppermute(grad_far, "strip", SWAP)
     grad_grid, beside, grad_deconv = deconv_bwd(grad_cells, grad_far, grid, edge, deconv)
@@ -1980,12 +1991,6 @@
     grad_modulate = lax.dynamic_update_slice_in_dim(
         jnp.zeros((6 * NCAM, D), jnp.bfloat16), grad_mods.astype(jnp.bfloat16), 6 * camera[0], 0
     )
-    grad_triplane = lax.dynamic_update_slice_in_dim(
-        jnp.zeros((3, strips, own_rows, D), jnp.bfloat16),
-        grad_stream.astype(jnp.bfloat16).reshape(3, 1, own_rows, D),
-        place,
-        1,
-    )
     grad_decode = jnp.concatenate([grad_decode_in.reshape(-1), grad_decode_out.reshape(-1)])
     grad_decode = jnp.pad(grad_decode, (0, END_GAP))
     total_tiles = tiled.shape[0]
@@ -2015,19 +2020,28 @@
         (low, (2, None), (3, 1), TILES["keyval_cross"], (2, 1)),
         (tall, (0, None), (1, None), TILES["query_cross"], (1, 0)),
     ]
+    grad_tokens = grad_stream.astype(jnp.bfloat16)
     copies = []
     for piece, first in (
         (grad_deconv, TILES["deconv"]),
         (grad_decode, TILES["decode"]),
         (grad_modulate, TILES["modulate"]),
-        (grad_triplane, TILES["triplane"]),
-        (jnp.zeros((gap, 8, WIDE), jnp.bfloat16), TILES["gap"]),
-        (jnp.zeros((total_tiles - end, 8, WIDE), jnp.bfloat16), end),
+        (grad_tokens, None),
     ):
         piece = piece.astype(jnp.bfloat16).reshape(-1, 8, WIDE)
-        if piece.shape[0]:
-            copies.append((len(arrays), first, piece.shape[0]))
-            arrays.append(piece)
+        if first is None:
+            part = own_rows // 8
+            for plane in range(3):
+                first = TILES["triplane"] + 2 * plane * part
+                copies.append((len(arrays), plane * part, part, first, part))
+                copies.append((None, 0, part, first + part, -part))
+        else:
+            copies.append((len(arrays), 0, piece.shape[0], first, 0))
+        arrays.append(piece)
+    for first, count in ((TILES["gap"], gap), (end, total_tiles - end)):
+        part = own_rows // 8
+        for start in range(0, count, part):
+            copies.append((None, 0, min(part, count - start), first + start, 0))
     row_grads = weight_grads(arrays, products, copies, total_tiles).reshape(-1, WIDE)
     if direct_links():
         summed, chunks, loss_sum = reduce_grads(row_grads, panel_sums.parts, loss_part)

time: 667 us -> 657 us (0.985)
  Pallas kernels: 515 us -> 508 us
    unnamed x129 -> x121, local copies, waits for them, and re-layouts: 19.5 us -> 23.2 us
  transfers between devices with their start and end apart: 18 -> 18, of which waited for: 10 -> 9; matrix products, arithmetic and copies ran while one was open for 8% -> 8% of each run, Pallas kernels for 21% -> 21%
where the time goes in v7:
time: 657 us; the launch traced here: 648 us
  Pallas kernels  508 us (77%)
  other arithmetic  42.5 us (6%)
  local copies, waits for them, and re-layouts  35.8 us (5%)
  matrix products  27.9 us (4%)
  starting transfers between devices  14.5 us (2%)
  waiting for transfers between devices  13.7 us (2%)
    pallas_call x1, Pallas kernels, scatter_sum(): pl.pallas_call(functools.partial(scatter_kernel, layouts, stagger), out_s...  115 us
    pallas_call x1, Pallas kernels, gather_all(): pl.pallas_call(functools.partial(gather_kernel, layouts, stagger), out_sh...  103 us
    pallas_call x3, Pallas kernels, attend_bwd(): pl.pallas_call(functools.partial(attend_bwd_kernel, real_keys, chunk, len...  66.3 us
    pallas_call x3, Pallas kernels, attend_fwd(): pl.pallas_call(functools.partial(attend_fwd_kernel, real_keys, len(source...  46.5 us
    pallas_call x1, Pallas kernels, mlp_bwd(): pl.pallas_call(functools.partial(mlp_bwd_kernel, len(panels)), grid=(step...  42.7 us
    pallas_call x1, Pallas kernels, mlp_fwd(): pl.pallas_call(functools.partial(mlp_fwd_kernel, len(panels)), grid=(step...  26.4 us
    unnamed x121, local copies, waits for them, and re-layouts  23.2 us
    pallas_call x1, Pallas kernels, weight_grads(): pl.pallas_call(functools.partial(weight_grads_kernel, products, copies),...  22.6 us
  transfers between devices with their start and end apart: 18, of which 9 were waited for; matrix products, arithmetic and copies ran while one was open for 8% of the time, Pallas kernels for 21%

profile of v7, /device:TPU:1, one launch (start us, length us, event | category | flops | bytes accessed | tf_op | source)
XLA Modules:
  0.0 647.5 jit_solution(7791397230659336547)
XLA Ops:
  15.5 103.4 %gather_all.1 = (bf16[10752,1024]{1,0:T(8,128)(2,1)}, f32[256,128]{1,0:T(8,128)}, bf16[4,256,1024]{2,1,0:T(8,128)(2,1)}) custom-call(bf16[336,1024]{1,0:T(8,128)(2,1)} %copy-done.28, f32[8,128]{1,0:T(8,128)} %copy-done.34, bf16[256,1024]{1,0:T(8,128)(2,1)} %copy-done.29), custom_call_target="tpu_custom_call" | custom-call | tf_op jit(solution)/shard_map/gather_all/pallas_call | solution.py:646
  130.7 10.5 %attend_fwd.3 = (bf16[768,1024]{1,0:T(8,128)(2,1)S(1)}, f32[8,8,768]{2,1,0:T(8,128)S(1)}) custom-call(bf16[768,1024]{1,0:T(8,128)(2,1)S(1)} %fusion.28.q_ref, bf16[2,272,1024]{2,1,0:T(8,128)(2,1)S(1)} %project.2.refs_0_), custom_call_target="tpu_custom_call" | custom-call | flops 1000000 | bytes 100000 | tf_op jit(solution)/shard_map/attend_fwd/pallas_call | solution.py:109
  148.0 7.7 %project.3 = (bf16[768,1024]{1,0:T(8,128)(2,1)S(1)}, bf16[2,768,1024]{2,1,0:T(8,128)(2,1)S(1)}) custom-call(bf16[768,1024]{1,0:T(8,128)(2,1)S(1)} %add_convert_fusion.5.x_ref.refs_6_, bf16[1344,8,1024]{2,1,0:T(8,128)(2,1)} %bitcast.50), custom_call_target="tpu_custom_call" | custom-call | flops 1000000 | bytes 100000 | tf_op jit(solution)/shard_map/project/pallas_call | solution.py:1319
  158.0 6.0 spread_deconv.1.w_ref
  168.3 17.8 %attend_fwd.4 = (bf16[768,1024]{1,0:T(8,128)(2,1)S(1)}, f32[8,8,768]{2,1,0:T(8,128)S(1)}) custom-call(bf16[768,1024]{1,0:T(8,128)(2,1)S(1)} %get-tuple-element.104.q_ref, bf16[2,768,1024]{2,1,0:T(8,128)(2,1)} %copy-done, bf16[2,768,1024]{2,1,0:T(8,128)(2,1)} %copy-done.40), custom_call_target="tpu_custom_call" | custom-call | flops 1000000 | bytes 100000 | tf_op jit(solution)/shard_map/attend_fwd/pallas_call | solution.py:109
  186.1 18.2 %attend_fwd.5 = (bf16[768,1024]{1,0:T(8,128)(2,1)S(1)}, f32[8,8,768]{2,1,0:T(8,128)S(1)}) custom-call(bf16[768,1024]{1,0:T(8,128)(2,1)S(1)} %get-tuple-element.104.q_ref, bf16[2,768,1024]{2,1,0:T(8,128)(2,1)} %copy-done, bf16[2,768,1024]{2,1,0:T(8,128)(2,1)} %copy-done.40, ...), custom_call_target="tpu_custom_call", output_to_operand_aliasing={{0}: (3, {}), {1}: (4, {})} | custom-call | flops 1000000 | bytes 100000 | tf_op jit(solution)/shard_map/attend_fwd/pallas_call | solution.py:109
  212.6 26.4 %mlp_fwd.1 = (f32[4,768,1024]{2,1,0:T(8,128)}, bf16[4,768,1024]{2,1,0:T(8,128)(2,1)}, bf16[768,1024]{1,0:T(8,128)(2,1)}) custom-call(bf16[4,256,1024]{2,1,0:T(8,128)(2,1)} %get-tuple-element.100.refs_0_, bf16[4,256,1024]{2,1,0:T(8,128)(2,1)} %collective-permute-done.1.refs_1_, bf16[4,256,1024]{2,1,0:T(8,128)(2,1)} %collective-permute-done.2.refs_2_, ...), custom_call_target="tpu_custom_call" | custom-call | flops 1000000 | bytes 100000 | tf_op jit(solution)/shard_map/mlp_fwd/pallas_call | solution.py:968
  243.0 4.9 deconv_fwd.1.near_ref
  255.4 18.8 %render.1 = (f32[8,128]{1,0:T(8,128)S(1)}, bf16[3,80,1024]{2,1,0:T(8,128)(2,1)S(1)}, bf16[3,80,1024]{2,1,0:T(8,128)(2,1)S(1)}, f32[80,64]{1,0:T(8,128)S(1)}, f32[64,8]{1,0:T(8,128)S(1)}) custom-call(s32[3,16,256]{2,1,0:T(8,128)S(1)} %add_select_fusion.samples_ref, bf16[3,1024,128]{2,1,0:T(8,128)(2,1)S(1)} %deconv_fwd.1.near_ref, ...), custom_call_target="tpu_custom_call" | custom-call | tf_op jit(solution)/shard_map/render/pallas_call | solution.py:332
  277.6 16.0 %deconv_bwd.1 = (f32[3,256,1024]{2,1,0:T(8,128)}, bf16[3,32,1024]{2,1,0:T(8,128)(2,1)}, bf16[160,8,1024]{2,1,0:T(8,128)(2,1)}) custom-call(bf16[3,80,1024]{2,1,0:T(8,128)(2,1)} %copy-done.30, bf16[3,80,1024]{2,1,0:T(8,128)(2,1)} %copy-done.57, bf16[3,256,1024]{2,1,0:T(8,128)(2,1)} %bitcast.42, bf16[3,32,1024]{2,1,0:T(8,128)(2,1)} %copy-done.27, ...), custom_call_target="tpu_custom_call" | custom-call | tf_op jit(solution)/shard_map/deconv_bwd/pallas_call | solution.py:1253
  302.2 42.7 %mlp_bwd.1 = (f32[768,1024]{1,0:T(8,128)}, bf16[16,256,1024]{2,1,0:T(8,128)(2,1)}, bf16[16,256,1024]{2,1,0:T(8,128)(2,1)}) custom-call(bf16[4,256,1024]{2,1,0:T(8,128)(2,1)} %get-tuple-element.100.refs_0_, bf16[4,256,1024]{2,1,0:T(8,128)(2,1)} %collective-permute-done.1.refs_1_, bf16[4,256,1024]{2,1,0:T(8,128)(2,1)} %collective-permute-done.2.refs_2_, ...), custom_call_target="tpu_custom_call" | custom-call | flops 1000000 | bytes 100000 | tf_op jit(solution)/shard_map/mlp_bwd/pallas_call | solution.py:1077
  354.1 5.4 fusion.34.refs_4_
  364.6 45.3 %attend_bwd.3 = (bf16[768,1024]{1,0:T(8,128)(2,1)S(1)}, bf16[2,768,1024]{2,1,0:T(8,128)(2,1)}, bf16[2,768,1024]{2,1,0:T(8,128)(2,1)}) custom-call(bf16[768,1024]{1,0:T(8,128)(2,1)S(1)} %copy-done.5, bf16[2,768,1024]{2,1,0:T(8,128)(2,1)} %copy-done, bf16[2,768,1024]{2,1,0:T(8,128)(2,1)} %copy-done.40, f32[8,8,768]{2,1,0:T(8,128)S(1)} %get-tuple-element.127.refs_2_, ...), custom_call_target="tpu_custom_call" | custom-call | flops 1000000 | bytes 100000 | tf_op jit(solution)/shard_map/attend_bwd/pallas_call | solution.py:182
  412.0 5.0 add_convert_fusion.2
  417.1 7.8 %attend_bwd.4 = (bf16[768,1024]{1,0:T(8,128)(2,1)S(1)}, bf16[2,768,1024]{2,1,0:T(8,128)(2,1)}, bf16[2,768,1024]{2,1,0:T(8,128)(2,1)}) custom-call(bf16[768,1024]{1,0:T(8,128)(2,1)S(1)} %copy-done.5, bf16[2,768,1024]{2,1,0:T(8,128)(2,1)} %copy-done, bf16[2,768,1024]{2,1,0:T(8,128)(2,1)} %copy-done.40, ...), custom_call_target="tpu_custom_call", output_to_operand_aliasing={{0}: (6, {}), {1}: (7, {}), {2}: (8, {})} | custom-call | flops 1000000 | bytes 100000 | tf_op jit(solution)/shard_map/attend_bwd/pallas_call | solution.py:182
  432.7 4.5 add_convert_fusion.1.g_ref.refs_8_
  437.3 9.5 %project_back.1 = f32[768,1024]{1,0:T(8,128)S(1)} custom-call(bf16[768,1024]{1,0:T(8,128)(2,1)S(1)} %copy-done.8, bf16[2,768,1024]{2,1,0:T(8,128)(2,1)S(1)} %add_convert_fusion.1.g_ref.refs_8_, bf16[1344,8,1024]{2,1,0:T(8,128)(2,1)} %bitcast.52), custom_call_target="tpu_custom_call" | custom-call | flops 1000000 | bytes 100000 | tf_op jit(solution)/shard_map/project_back/pallas_call | solution.py:1357
  450.9 5.2 fusion.31.refs_3_
  456.1 13.2 %attend_bwd.5 = (bf16[768,1024]{1,0:T(8,128)(2,1)S(1)}, bf16[2,272,1024]{2,1,0:T(8,128)(2,1)S(1)}) custom-call(bf16[768,1024]{1,0:T(8,128)(2,1)S(1)} %copy-done.17, bf16[2,272,1024]{2,1,0:T(8,128)(2,1)S(1)} %copy-done.11, f32[8,8,768]{2,1,0:T(8,128)S(1)} %copy-done.32, bf16[768,1024]{1,0:T(8,128)(2,1)} %copy-done.18, bf16[768,1024]{1,0:T(8,128)(2,1)} %fusion.31.refs_3_), custom_call_target="tpu_custom_call" | custom-call | flops 1000000 | bytes 100000 | tf_op jit(solution)/shard_map/attend_bwd/pallas_call | solution.py:182
  469.4 5.2 fusion.10
  481.6 22.6 %weight_grads.1 = bf16[1344,8,1024]{2,1,0:T(8,128)(2,1)} custom-call(bf16[768,1024]{1,0:T(8,128)(2,1)} %copy-done.55, bf16[768,1024]{1,0:T(8,128)(2,1)} %copy-done.22, bf16[272,768]{1,0:T(8,128)(2,1)} %copy-done.19, bf16[2,272,1024]{2,1,0:T(8,128)(2,1)} %copy-done.25, bf16[768,1024]{1,0:T(8,128)(2,1)} %copy-done.18, bf16[768,1024]{1,0:T(8,128)(2,1)} %copy-done.54, ...), custom_call_target="tpu_custom_call" | custom-call | flops 1000000 | bytes 100000 | tf_op jit(solution)/shard_map/weight_grads/pallas_call | solution.py:1455
  504.3 115.1 %scatter_sum.1 = (f32[336,1024]{1,0:T(8,128)S(1)}, f32[8,128]{1,0:T(8,128)S(1)}, bf16[512,1024]{1,0:T(8,128)(2,1)S(1)}) custom-call(bf16[10752,1024]{1,0:T(8,128)(2,1)} %bitcast.53, f32[8,128]{1,0:T(8,128)S(1)} %get-tuple-element.146.refs_1_, bf16[16,256,1024]{2,1,0:T(8,128)(2,1)} %get-tuple-element.123.refs_2_, bf16[16,256,1024]{2,1,0:T(8,128)(2,1)} %copy-done.44, ...), custom_call_target="tpu_custom_call" | custom-call | tf_op jit(solution)/shard_map/scatter_sum/pallas_call | solution.py:887
  626.0 11.3 %shampoo.1 = (f32[32,128,128]{2,1,0:T(8,128)}, f32[32,128,128]{2,1,0:T(8,128)}, f32[32,128,128]{2,1,0:T(8,128)}, f32[32,128,128]{2,1,0:T(8,128)}, f32[32,128]{1,0:T(8,128)}) custom-call(bf16[512,1024]{1,0:T(8,128)(2,1)} %copy-done.26, f32[32,128,128]{2,1,0:T(8,128)} %blocks_ref.3, f32[32,128,128]{2,1,0:T(8,128)} %sl_ref.1, f32[32,128,128]{2,1,0:T(8,128)} %sr_ref.1, ...), custom_call_target="tpu_custom_call" | custom-call | tf_op jit(solution)/shard_map/shampoo/pallas_call | solution.py:1718
  641.4 4.8 adam.1
  (230 shorter events, 115.3 us)
Async XLA Ops:
  1.6 8.2 %collective-permute-start = (f32[448,128]{1,0:T(8,128)S(1)}, f32[448,128]{1,0:T(8,128)S(1)}, u32[]{:S(2)}, u32[]{:S(2)}) collective-permute-start(f32[448,128]{1,0:T(8,128)S(1)} %slice_bitcast_fusion), channel_id=1, source_target_pairs={{1,0},{2,1},{3,2},{4,3},{5,4},{6,5},{7,6},{8,7},{9,8},{10,9},{11,1... | collective-permute-start | bytes 688136 | tf_op jit(solution)/shard_map/ppermute | solution.py:1588
  6.1 117.5 %copy-start.19 = (bf16[272,768]{1,0:T(8,128)(2,1)}, bf16[272,768]{1,0:T(8,128)(2,1)S(1)}, u32[]{:S(2)}) copy-start(bf16[272,768]{1,0:T(8,128)(2,1)S(1)} %pad.17.x_ref.refs_2_) | copy-start | bytes 1253380
  121.4 19.8 %copy-start.45 = (bf16[256,1024]{1,0:T(8,128)(2,1)}, bf16[256,1024]{1,0:T(8,128)(2,1)S(1)}, u32[]{:S(2)}) copy-start(bf16[256,1024]{1,0:T(8,128)(2,1)S(1)} %get-tuple-element.174) | copy-start | bytes 1572868
  122.4 25.6 %collective-permute-start.1 = (bf16[4,256,1024]{2,1,0:T(8,128)(2,1)}, bf16[4,256,1024]{2,1,0:T(8,128)(2,1)}, u32[]{:S(2)}, u32[]{:S(2)}) collective-permute-start(bf16[4,256,1024]{2,1,0:T(8,128)(2,1)} %get-tuple-element.100.refs_0_), channel_id=1, source_target_pairs={{0,2},{1,5},{2,0},{3,7},{4,6},{5,1},{6,4},{7,3},{8,10},{9,13},{10,... | collective-permute-start | bytes 6291464 | tf_op jit(solution)/shard_map/ppermute | solution.py:1768
  155.6 30.5 %copy-start.4 = (bf16[768,1024]{1,0:T(8,128)(2,1)}, bf16[768,1024]{1,0:T(8,128)(2,1)S(1)}, u32[]{:S(2)}) copy-start(bf16[768,1024]{1,0:T(8,128)(2,1)S(1)} %get-tuple-element.104.q_ref) | copy-start | bytes 4718596
  155.7 11.0 %collective-permute-start.3 = (bf16[2,768,1024]{2,1,0:T(8,128)(2,1)S(1)}, bf16[2,768,1024]{2,1,0:T(8,128)(2,1)S(1)}, u32[]{:S(2)}, u32[]{:S(2)}) collective-permute-start(bf16[2,768,1024]{2,1,0:T(8,128)(2,1)S(1)} %get-tuple-element.105.refs_0_), channel_id=1, source_target_pairs={{0,1},{1,0},{2,3},{3,2},{4,5},{5,4},{6,7},{7,6},{8,9},{9,8},{10,11... | collective-permute-start | bytes 9437192 | tf_op jit(solution)/shard_map/ppermute | solution.py:1930
  156.6 29.6 %collective-permute-start.2 = (bf16[4,256,1024]{2,1,0:T(8,128)(2,1)}, bf16[4,256,1024]{2,1,0:T(8,128)(2,1)}, u32[]{:S(2)}, u32[]{:S(2)}) collective-permute-start(bf16[4,256,1024]{2,1,0:T(8,128)(2,1)} %get-tuple-element.100.refs_0_), channel_id=1, source_target_pairs={{0,4},{1,3},{2,6},{3,1},{4,0},{5,7},{6,2},{7,5},{8,12},{9,11},{10,... | collective-permute-start | bytes 6291464 | tf_op jit(solution)/shard_map/ppermute | solution.py:1788
  157.1 47.5 %collective-permute-start.4 = (bf16[4,256,1024]{2,1,0:T(8,128)(2,1)}, bf16[4,256,1024]{2,1,0:T(8,128)(2,1)}, u32[]{:S(2)}, u32[]{:S(2)}) collective-permute-start(bf16[4,256,1024]{2,1,0:T(8,128)(2,1)} %collective-permute-done.1.refs_1_), channel_id=1, source_target_pairs={{0,4},{1,3},{2,6},{3,1},{4,0},{5,7},{6,2},{7,5},{8,12},{9,11},{10,... | collective-permute-start | bytes 6291464 | tf_op jit(solution)/shard_map/ppermute | solution.py:1796
  166.0 46.0 %collective-permute-start.5 = (bf16[4,256,1024]{2,1,0:T(8,128)(2,1)}, bf16[4,256,1024]{2,1,0:T(8,128)(2,1)}, u32[]{:S(2)}, u32[]{:S(2)}) collective-permute-start(bf16[4,256,1024]{2,1,0:T(8,128)(2,1)} %get-tuple-element.100.refs_0_), channel_id=1, source_target_pairs={{0,1},{1,0},{2,3},{3,2},{4,5},{5,4},{6,7},{7,6},{8,9},{9,8},{10,11... | collective-permute-start | bytes 6291464 | tf_op jit(solution)/shard_map/ppermute | solution.py:1804
  166.7 45.4 %collective-permute-start.6 = (bf16[4,256,1024]{2,1,0:T(8,128)(2,1)}, bf16[4,256,1024]{2,1,0:T(8,128)(2,1)}, u32[]{:S(2)}, u32[]{:S(2)}) collective-permute-start(bf16[4,256,1024]{2,1,0:T(8,128)(2,1)} %collective-permute-done.1.refs_1_), channel_id=1, source_target_pairs={{0,1},{1,0},{2,3},{3,2},{4,5},{5,4},{6,7},{7,6},{8,9},{9,8},{10,11... | collective-permute-start | bytes 6291464 | tf_op jit(solution)/shard_map/ppermute | solution.py:1804
  204.4 212.7 %copy-start.6 = (bf16[768,1024]{1,0:T(8,128)(2,1)}, bf16[768,1024]{1,0:T(8,128)(2,1)S(1)}, u32[]{:S(2)}) copy-start(bf16[768,1024]{1,0:T(8,128)(2,1)S(1)} %get-tuple-element.110.refs_3_.refs_9_) | copy-start | bytes 4718596
  204.5 7.5 %collective-permute-start.8 = (bf16[4,256,1024]{2,1,0:T(8,128)(2,1)}, bf16[4,256,1024]{2,1,0:T(8,128)(2,1)}, u32[]{:S(2)}, u32[]{:S(2)}) collective-permute-start(bf16[4,256,1024]{2,1,0:T(8,128)(2,1)} %collective-permute-done.4.refs_3_), channel_id=1, source_target_pairs={{0,1},{1,0},{2,3},{3,2},{4,5},{5,4},{6,7},{7,6},{8,9},{9,8},{10,11... | collective-permute-start | bytes 6291464 | tf_op jit(solution)/shard_map/ppermute | solution.py:1804
  205.5 7.1 %collective-permute-start.7 = (bf16[4,256,1024]{2,1,0:T(8,128)(2,1)}, bf16[4,256,1024]{2,1,0:T(8,128)(2,1)}, u32[]{:S(2)}, u32[]{:S(2)}) collective-permute-start(bf16[4,256,1024]{2,1,0:T(8,128)(2,1)} %collective-permute-done.2.refs_2_), channel_id=1, source_target_pairs={{0,1},{1,0},{2,3},{3,2},{4,5},{5,4},{6,7},{7,6},{8,9},{9,8},{10,11... | collective-permute-start | bytes 6291464 | tf_op jit(solution)/shard_map/ppermute | solution.py:1804
  212.6 29.0 %copy-start.2 = (bf16[1024,2048]{1,0:T(8,128)(2,1)S(1)}, bf16[1024,2048]{1,0:T(8,128)(2,1)}, u32[]{:S(2)}) copy-start(bf16[1024,2048]{1,0:T(8,128)(2,1)} %copy-done.1) | copy-start | bytes 12582916
  240.1 1.5 collective-permute-start.9
  247.9 7.4 %collective-permute-start.10 = (bf16[3,1024,128]{2,1,0:T(8,128)(2,1)S(1)}, bf16[3,1024,128]{2,1,0:T(8,128)(2,1)S(1)}, u32[]{:S(2)}, u32[]{:S(2)}) collective-permute-start(bf16[3,1024,128]{2,1,0:T(8,128)(2,1)S(1)} %deconv_fwd.1.near_ref), channel_id=1, source_target_pairs={{0,1},{1,0},{2,3},{3,2},{4,5},{5,4},{6,7},{7,6},{8,9},{9,8},{10,11... | collective-permute-start | bytes 2359304 | tf_op jit(solution)/shard_map/ppermute | solution.py:1943
  274.9 1.9 collective-permute-start.11
  293.6 1.7 collective-permute-start.12
  344.9 14.6 %collective-permute-start.13 = (bf16[16,256,1024]{2,1,0:T(8,128)(2,1)}, bf16[16,256,1024]{2,1,0:T(8,128)(2,1)S(1)}, u32[]{:S(2)}, u32[]{:S(2)}) collective-permute-start(bf16[16,256,1024]{2,1,0:T(8,128)(2,1)} %get-tuple-element.124), channel_id=1, source_target_pairs={{0,1},{1,0},{2,3},{3,2},{4,5},{5,4},{6,7},{7,6},{8,9},{9,8},{10,11... | collective-permute-start | bytes 25165832 | tf_op jit(solution)/shard_map/ppermute | solution.py:1814
  364.1 48.0 %collective-permute-start.14 = (bf16[8,256,1024]{2,1,0:T(8,128)(2,1)}, bf16[8,256,1024]{2,1,0:T(8,128)(2,1)}, u32[]{:S(2)}, u32[]{:S(2)}) collective-permute-start(bf16[8,256,1024]{2,1,0:T(8,128)(2,1)} %add_convert_fusion), channel_id=1, source_target_pairs={{0,4},{1,3},{2,6},{3,1},{4,0},{5,7},{6,2},{7,5},{8,12},{9,11},{10,... | collective-permute-start | bytes 12582920 | tf_op jit(solution)/shard_map/ppermute | solution.py:1826
  426.1 6.6 %collective-permute-start.16 = (bf16[2,768,1024]{2,1,0:T(8,128)(2,1)}, bf16[2,768,1024]{2,1,0:T(8,128)(2,1)}, u32[]{:S(2)}, u32[]{:S(2)}) collective-permute-start(bf16[2,768,1024]{2,1,0:T(8,128)(2,1)} %get-tuple-element.139), channel_id=1, source_target_pairs={{0,1},{1,0},{2,3},{3,2},{4,5},{5,4},{6,7},{7,6},{8,9},{9,8},{10,11... | collective-permute-start | bytes 9437192 | tf_op jit(solution)/shard_map/ppermute | solution.py:1977
  428.0 41.4 %collective-permute-start.15 = (bf16[4,256,1024]{2,1,0:T(8,128)(2,1)}, bf16[4,256,1024]{2,1,0:T(8,128)(2,1)S(1)}, u32[]{:S(2)}, u32[]{:S(2)}) collective-permute-start(bf16[4,256,1024]{2,1,0:T(8,128)(2,1)} %add_convert_fusion.2), channel_id=1, source_target_pairs={{0,2},{1,5},{2,0},{3,7},{4,6},{5,1},{6,4},{7,3},{8,10},{9,13},{10,... | collective-permute-start | bytes 6291464 | tf_op jit(solution)/shard_map/ppermute | solution.py:1834
  481.6 22.6 %copy-start.21 = (bf16[4,256,1024]{2,1,0:T(8,128)(2,1)S(1)}, bf16[4,256,1024]{2,1,0:T(8,128)(2,1)}, u32[]{:S(2)}) copy-start(bf16[4,256,1024]{2,1,0:T(8,128)(2,1)} %copy-done.20) | copy-start | bytes 6291460
  620.5 18.2 %collective-permute-start.17 = (f32[448,128]{1,0:T(8,128)S(1)}, f32[448,128]{1,0:T(8,128)S(1)}, u32[]{:S(2)}, u32[]{:S(2)}) collective-permute-start(f32[448,128]{1,0:T(8,128)S(1)} %slice.189), channel_id=1, source_target_pairs={{0,1},{1,2},{2,3},{3,4},{4,5},{5,6},{6,7},{7,8},{8,9},{9,10},{10,1... | collective-permute-start | bytes 688136 | tf_op jit(solution)/shard_map/ppermute | solution.py:1675
  (54 other events, 277.8 us)

commit v8 on v7

--- a/solution.py
+++ b/solution.py
@@ -85,9 +85,9 @@
     query, keys = q_ref[...], joined(refs[:sources], 0)
     values = joined(refs[:sources], 1).T
     outs = []
-    for head in range(2):
-        own = jnp.where(head_lanes(query.shape, head), query, 0)
-        scores = nt_dot(keys, own)
+    heads = [jnp.where(head_lanes(query.shape, head), query, 0) for head in range(2)]
+    all_scores = [nt_dot(keys, own) for own in heads]
+    for head, scores in enumerate(all_scores):
         if real_keys < keys.shape[0]:
             at = lax.broadcasted_iota(jnp.int32, scores.shape, 0)
             scores = jnp.where(at < real_keys, scores, -3e38)
@@ -139,16 +139,22 @@
     grads = [jnp.where(head_lanes(grad.shape, head), grad, 0) for head in range(2)]
     inner = [jnp.sum(mixed[head * HEAD_DIM : (head + 1) * HEAD_DIM], 0, keepdims=True) for head in range(2)]
     grad_query = [jnp.zeros((HEAD_DIM, query.shape[0]), jnp.float32) for head in range(2)]
+    def opened(at):
+        part = pl.ds(at, chunk)
+        keys, values = k_all[part], v_all[part]
+        return [(nt_dot(keys, queries[head]), nt_dot(values, grads[head])) for head in range(2)]
+
+    ahead = opened(0)
     for at in range(0, total_keys, chunk):
         part = pl.ds(at, chunk)
-        keys, values = k_all[part], v_all[part]
-        for head in range(2):
-            scores = nt_dot(keys, queries[head])
+        now = ahead
+        if at + chunk < total_keys:
+            ahead = opened(at + chunk)
+        for head, (scores, grad_shares) in enumerate(now):
             shares = jnp.exp2(scores * EXP_SCALE - lse_ref[0, head : head + 1])
             if at + chunk > real_keys:
                 row = at + lax.broadcasted_iota(jnp.int32, shares.shape, 0)
                 shares = jnp.where(row < real_keys, shares, 0.0)
-            grad_shares = nt_dot(values, grads[head])
             grad_scores = (shares * (grad_shares - inner[head])).astype(jnp.bfloat16)
             to_values = product(shares.astype(jnp.bfloat16), grads[head])
             to_keys = product(grad_scores, queries[head])
@@ -1329,7 +1335,7 @@
     )(x, rows)
 
 
-def project_back_kernel(first, count, depth, lead_ref, g_ref, rows_ref, o_ref, held, sems):
+def project_back_kernel(first, count, depth, lead_ref, own_ref, far_ref, rows_ref, o_ref, sum_ref, held, sems):
     step = pl.program_id(0)
     panels = panel_view(rows_ref, first, count, depth)
 
@@ -1339,7 +1345,9 @@
             pltpu.make_async_copy(panels.at[:, n], held.at[n], sems.at[n]).start()
 
     pltpu.make_async_copy(held.at[step], held.at[step], sems.at[step]).wait()
-    grad = jnp.where(step == 0, lead_ref[...], g_ref[0])
+    both = (own_ref[0].astype(jnp.float32) + far_ref[0].astype(jnp.float32)).astype(jnp.bfloat16)
+    sum_ref[0] = both
+    grad = jnp.where(step == 0, lead_ref[...], both)
     back = nt_dot(grad, held[step].reshape(depth, WIDE))
 
     @pl.when(step == 0)
@@ -1351,24 +1359,29 @@
         o_ref[...] += back
 
 
-def project_back(lead, grads, rows, first, depth):
-    others, tokens, _ = grads.shape
+def project_back(lead, own, far, rows, first, depth):
+    others, tokens, _ = own.shape
     count = others + 1
+    panel = pl.BlockSpec((1, tokens, WIDE), lambda n: (jnp.maximum(n - 1, 0), 0, 0))
     return pl.pallas_call(
         functools.partial(project_back_kernel, first, count, depth),
         grid=(count,),
         in_specs=[
             pl.BlockSpec((tokens, WIDE), lambda n: (0, 0)),
-            pl.BlockSpec((1, tokens, WIDE), lambda n: (jnp.maximum(n - 1, 0), 0, 0)),
+            panel,
+            panel,
             pl.BlockSpec(memory_space=pl.ANY),
         ],
-        out_specs=pl.BlockSpec((tokens, depth), lambda n: (0, 0)),
-        out_shape=jax.ShapeDtypeStruct((tokens, depth), jnp.float32),
+        out_specs=[pl.BlockSpec((tokens, depth), lambda n: (0, 0)), panel],
+        out_shape=[
+            jax.ShapeDtypeStruct((tokens, depth), jnp.float32),
+            jax.ShapeDtypeStruct((others, tokens, WIDE), jnp.bfloat16),
+        ],
         scratch_shapes=[pltpu.VMEM((count, depth // 8, 8, WIDE), jnp.bfloat16), pltpu.SemaphoreType.DMA((count,))],
-        compiler_params=pltpu.CompilerParams(vmem_limit_bytes=32 * 1024 * 1024),
+        compiler_params=pltpu.CompilerParams(vmem_limit_bytes=44 * 1024 * 1024),
         cost_estimate=BRIEF,
         name="project_back",
-    )(lead, grads, rows)
+    )(lead, own, far, rows)
 
 
 def weight_grads_kernel(products, copies, *refs):
@@ -1693,21 +1706,27 @@
 
 
 def shampoo_kernel(tiles_ref, blocks_ref, sl_ref, sr_ref, rl_ref, rr_ref, nb_ref, g_ref, nl_ref, nr_ref, rms_ref):
-    for n in range(8):
-        grad = tiles_ref[:, n * BLOCK : (n + 1) * BLOCK]
-        wide = grad.astype(jnp.float32)
-        g_ref[n] = wide
+    count = blocks_ref.shape[0]
+    grads = [tiles_ref[:, n * BLOCK : (n + 1) * BLOCK] for n in range(count)]
+    halves = []
+    for n, grad in enumerate(grads):
+        coarse, fine = two_parts(rr_ref[n])
+        half = product(grad, jnp.concatenate([coarse, fine], 1))
+        halves.append(half[:, :BLOCK] + half[:, BLOCK:])
+    for n, grad in enumerate(grads):
+        g_ref[n] = grad.astype(jnp.float32)
         nl_ref[n] = STAT_DECAY * sl_ref[n] + (1.0 - STAT_DECAY) * nt_dot(grad, grad)
         square = lax.dot_general(grad, grad, (((0,), (0,)), ((), ())), preferred_element_type=jnp.float32)
         nr_ref[n] = STAT_DECAY * sr_ref[n] + (1.0 - STAT_DECAY) * square
-        coarse, fine = two_parts(rr_ref[n])
-        half = product(grad, jnp.concatenate([coarse, fine], 1))
-        half_coarse, half_fine = two_parts(half[:, :BLOCK] + half[:, BLOCK:])
+    conds = []
+    for n, half in enumerate(halves):
+        half_coarse, half_fine = two_parts(half)
         coarse, fine = two_parts(rl_ref[n])
         cond = product(jnp.concatenate([coarse, fine], 1), jnp.concatenate([half_coarse, half_coarse], 0))
-        cond = cond + product(coarse, half_fine)
+        conds.append(cond + product(coarse, half_fine))
+    for n, cond in enumerate(conds):
         rms = jnp.sqrt(jnp.mean(cond * cond, axis=(0, 1), keepdims=True) + RMS_EPS)
-        nb_ref[n] = blocks_ref[n] - SHAMPOO_RATE * cond / rms
+        nb_ref[n] = blocks_ref[n] - (SHAMPOO_RATE / rms) * cond
         rms_ref[n : n + 1] = jnp.broadcast_to(rms, (1, LANES))
 
 
@@ -1958,8 +1977,10 @@
     grad_far = lax.ppermute(grad_far, "strip", SWAP)
     grad_grid, beside, grad_deconv = deconv_bwd(grad_cells, grad_far, grid, edge, deconv)
     beside = lax.ppermute(beside, "strip", SWAP).astype(jnp.float32)
-    grad_grid = grad_grid.at[:, :TC].add(jnp.where(place == 0, 0.0, beside))
-    grad_grid = grad_grid.at[:, -TC:].add(jnp.where(place == 0, beside, 0.0))
+    rest = own_rows - TC
+    above = jnp.pad(jnp.where(place == 0, 0.0, beside), ((0, 0), (0, rest), (0, 0)))
+    below = jnp.pad(jnp.where(place == 0, beside, 0.0), ((0, 0), (rest, 0), (0, 0)))
+    grad_grid = grad_grid + above + below
     grad_stream = grad_grid.reshape(-1, D)
     grad_branch = grad_stream.astype(jnp.bfloat16)
     grad_hidden3, *panel_grads = mlp_bwd(panels, hidden3, grad_branch, up, act)
@@ -1975,8 +1996,7 @@
         query2, kv_both, all_keys, (pairs - 1, pairs), 512, total_two, self_out, grad_self, early
     )
     grad_kv_far = lax.ppermute(grad_kv_far, "strip", SWAP)
-    grad_kv = (grad_kv_own.astype(jnp.float32) + grad_kv_far.astype(jnp.float32)).astype(jnp.bfloat16)
-    grad_hidden2 = project_back(grad_query2, grad_kv, tiled, TILES["qkv_self"], D)
+    grad_hidden2, grad_kv = project_back(grad_query2, grad_kv_own, grad_kv_far, tiled, TILES["qkv_self"], D)
     grad_norm, grad_mod2, grad_mod3 = norm_two(grad_hidden2)
     grad_stream = grad_stream + grad_norm
     grad_branch1 = grad_stream.astype(jnp.bfloat16)

time: 657 us -> 648 us (0.986)
  other arithmetic: 42.5 us -> 34.6 us
    unnamed x121 -> x149, local copies, waits for them, and re-layouts: 23.2 us -> 24.6 us
  transfers between devices with their start and end apart: 18 -> 18, of which waited for: 9 -> 9; matrix products, arithmetic and copies ran while one was open for 8% -> 7% of each run, Pallas kernels for 21% -> 20%
where the time goes in v8:
time: 648 us; the launch traced here: 639 us
  Pallas kernels  502 us (77%)
  local copies, waits for them, and re-layouts  37.7 us (6%)
  other arithmetic  34.6 us (5%)
  matrix products  27.4 us (4%)
  waiting for transfers between devices  17.2 us (3%)
  starting transfers between devices  14.5 us (2%)
    pallas_call x1, Pallas kernels, scatter_sum(): pl.pallas_call(functools.partial(scatter_kernel, layouts, stagger), out_s...  115 us
    pallas_call x1, Pallas kernels, gather_all(): pl.pallas_call(functools.partial(gather_kernel, layouts, stagger), out_sh...  103 us
    pallas_call x3, Pallas kernels, attend_bwd(): pl.pallas_call(functools.partial(attend_bwd_kernel, real_keys, chunk, len...  66.2 us
    pallas_call x1, Pallas kernels, mlp_bwd(): pl.pallas_call(functools.partial(mlp_bwd_kernel, len(panels)), grid=(step...  42.5 us
    pallas_call x3, Pallas kernels, attend_fwd(): pl.pallas_call(functools.partial(attend_fwd_kernel, real_keys, len(source...  41.2 us
    pallas_call x1, Pallas kernels, mlp_fwd(): pl.pallas_call(functools.partial(mlp_fwd_kernel, len(panels)), grid=(step...  26.3 us
    unnamed x149, local copies, waits for them, and re-layouts  24.6 us
    pallas_call x1, Pallas kernels, weight_grads(): pl.pallas_call(functools.partial(weight_grads_kernel, products, copies),...  22.7 us
  transfers between devices with their start and end apart: 18, of which 9 were waited for; matrix products, arithmetic and copies ran while one was open for 7% of the time, Pallas kernels for 20%

profile of v8, /device:TPU:1, one launch (start us, length us, event | category | flops | bytes accessed | tf_op | source)
XLA Modules:
  0.0 638.7 jit_solution(8205251750956181781)
XLA Ops:
  15.5 103.4 %gather_all.1 = (bf16[10752,1024]{1,0:T(8,128)(2,1)}, f32[256,128]{1,0:T(8,128)}, bf16[4,256,1024]{2,1,0:T(8,128)(2,1)}) custom-call(bf16[336,1024]{1,0:T(8,128)(2,1)} %copy-done.27, f32[8,128]{1,0:T(8,128)} %copy-done.32, bf16[256,1024]{1,0:T(8,128)(2,1)} %copy-done.28), custom_call_target="tpu_custom_call" | custom-call | tf_op jit(solution)/shard_map/gather_all/pallas_call | solution.py:652
  131.4 8.7 %attend_fwd.3 = (bf16[768,1024]{1,0:T(8,128)(2,1)S(1)}, f32[8,8,768]{2,1,0:T(8,128)S(1)}) custom-call(bf16[768,1024]{1,0:T(8,128)(2,1)S(1)} %fusion.28.q_ref, bf16[2,272,1024]{2,1,0:T(8,128)(2,1)S(1)} %project.2.refs_0_), custom_call_target="tpu_custom_call" | custom-call | flops 1000000 | bytes 100000 | tf_op jit(solution)/shard_map/attend_fwd/pallas_call | solution.py:109
  148.6 7.6 %project.3 = (bf16[768,1024]{1,0:T(8,128)(2,1)S(1)}, bf16[2,768,1024]{2,1,0:T(8,128)(2,1)S(1)}) custom-call(bf16[768,1024]{1,0:T(8,128)(2,1)S(1)} %add_convert_fusion.4.x_ref.refs_6_, bf16[1344,8,1024]{2,1,0:T(8,128)(2,1)} %bitcast.50), custom_call_target="tpu_custom_call" | custom-call | flops 1000000 | bytes 100000 | tf_op jit(solution)/shard_map/project/pallas_call | solution.py:1325
  158.6 6.0 spread_deconv.1.w_ref
  168.9 16.1 %attend_fwd.4 = (bf16[768,1024]{1,0:T(8,128)(2,1)S(1)}, f32[8,8,768]{2,1,0:T(8,128)S(1)}) custom-call(bf16[768,1024]{1,0:T(8,128)(2,1)S(1)} %get-tuple-element.82.q_ref, bf16[2,768,1024]{2,1,0:T(8,128)(2,1)} %copy-done, bf16[2,768,1024]{2,1,0:T(8,128)(2,1)} %copy-done.38), custom_call_target="tpu_custom_call" | custom-call | flops 1000000 | bytes 100000 | tf_op jit(solution)/shard_map/attend_fwd/pallas_call | solution.py:109
  185.1 16.4 %attend_fwd.5 = (bf16[768,1024]{1,0:T(8,128)(2,1)S(1)}, f32[8,8,768]{2,1,0:T(8,128)S(1)}) custom-call(bf16[768,1024]{1,0:T(8,128)(2,1)S(1)} %get-tuple-element.82.q_ref, bf16[2,768,1024]{2,1,0:T(8,128)(2,1)} %copy-done, bf16[2,768,1024]{2,1,0:T(8,128)(2,1)} %copy-done.38, ...), custom_call_target="tpu_custom_call", output_to_operand_aliasing={{0}: (3, {}), {1}: (4, {})} | custom-call | flops 1000000 | bytes 100000 | tf_op jit(solution)/shard_map/attend_fwd/pallas_call | solution.py:109
  213.2 26.3 %mlp_fwd.1 = (f32[4,768,1024]{2,1,0:T(8,128)}, bf16[4,768,1024]{2,1,0:T(8,128)(2,1)}, bf16[768,1024]{1,0:T(8,128)(2,1)}) custom-call(bf16[4,256,1024]{2,1,0:T(8,128)(2,1)} %get-tuple-element.78.refs_0_, bf16[4,256,1024]{2,1,0:T(8,128)(2,1)} %collective-permute-done.1.refs_1_, bf16[4,256,1024]{2,1,0:T(8,128)(2,1)} %collective-permute-done.2.refs_2_, ...), custom_call_target="tpu_custom_call" | custom-call | flops 1000000 | bytes 100000 | tf_op jit(solution)/shard_map/mlp_fwd/pallas_call | solution.py:974
  243.5 5.1 deconv_fwd.1.near_ref
  253.8 19.8 %render.1 = (f32[8,128]{1,0:T(8,128)S(1)}, bf16[3,80,1024]{2,1,0:T(8,128)(2,1)S(1)}, bf16[3,80,1024]{2,1,0:T(8,128)(2,1)S(1)}, f32[80,64]{1,0:T(8,128)S(1)}, f32[64,8]{1,0:T(8,128)S(1)}) custom-call(s32[3,16,256]{2,1,0:T(8,128)S(1)} %add_select_fusion.samples_ref, bf16[3,1024,128]{2,1,0:T(8,128)(2,1)S(1)} %deconv_fwd.1.near_ref, ...), custom_call_target="tpu_custom_call" | custom-call | tf_op jit(solution)/shard_map/render/pallas_call | solution.py:338
  277.1 16.2 %deconv_bwd.1 = (f32[3,256,1024]{2,1,0:T(8,128)}, bf16[3,32,1024]{2,1,0:T(8,128)(2,1)}, bf16[160,8,1024]{2,1,0:T(8,128)(2,1)}) custom-call(bf16[3,80,1024]{2,1,0:T(8,128)(2,1)} %copy-done.29, bf16[3,80,1024]{2,1,0:T(8,128)(2,1)} %copy-done.54, bf16[3,256,1024]{2,1,0:T(8,128)(2,1)} %bitcast.42, bf16[3,32,1024]{2,1,0:T(8,128)(2,1)} %copy-done.26, ...), custom_call_target="tpu_custom_call" | custom-call | tf_op jit(solution)/shard_map/deconv_bwd/pallas_call | solution.py:1259
  300.3 42.5 %mlp_bwd.1 = (f32[768,1024]{1,0:T(8,128)}, bf16[16,256,1024]{2,1,0:T(8,128)(2,1)}, bf16[16,256,1024]{2,1,0:T(8,128)(2,1)}) custom-call(bf16[4,256,1024]{2,1,0:T(8,128)(2,1)} %get-tuple-element.78.refs_0_, bf16[4,256,1024]{2,1,0:T(8,128)(2,1)} %collective-permute-done.1.refs_1_, bf16[4,256,1024]{2,1,0:T(8,128)(2,1)} %collective-permute-done.2.refs_2_, ...), custom_call_target="tpu_custom_call" | custom-call | flops 1000000 | bytes 100000 | tf_op jit(solution)/shard_map/mlp_bwd/pallas_call | solution.py:1083
  343.3 4.6 multiply_reduce_fusion
  352.1 5.3 fusion.34.refs_4_
  362.5 45.2 %attend_bwd.3 = (bf16[768,1024]{1,0:T(8,128)(2,1)S(1)}, bf16[2,768,1024]{2,1,0:T(8,128)(2,1)}, bf16[2,768,1024]{2,1,0:T(8,128)(2,1)}) custom-call(bf16[768,1024]{1,0:T(8,128)(2,1)S(1)} %copy-done.4, bf16[2,768,1024]{2,1,0:T(8,128)(2,1)} %copy-done, bf16[2,768,1024]{2,1,0:T(8,128)(2,1)} %copy-done.38, f32[8,8,768]{2,1,0:T(8,128)S(1)} %get-tuple-element.105.refs_2_, ...), custom_call_target="tpu_custom_call" | custom-call | flops 1000000 | bytes 100000 | tf_op jit(solution)/shard_map/attend_bwd/pallas_call | solution.py:188
  410.0 5.0 add_convert_fusion.1
  415.0 7.8 %attend_bwd.4 = (bf16[768,1024]{1,0:T(8,128)(2,1)S(1)}, bf16[2,768,1024]{2,1,0:T(8,128)(2,1)}, bf16[2,768,1024]{2,1,0:T(8,128)(2,1)}) custom-call(bf16[768,1024]{1,0:T(8,128)(2,1)S(1)} %copy-done.4, bf16[2,768,1024]{2,1,0:T(8,128)(2,1)} %copy-done, bf16[2,768,1024]{2,1,0:T(8,128)(2,1)} %copy-done.38, ...), custom_call_target="tpu_custom_call", output_to_operand_aliasing={{0}: (6, {}), {1}: (7, {}), {2}: (8, {})} | custom-call | flops 1000000 | bytes 100000 | tf_op jit(solution)/shard_map/attend_bwd/pallas_call | solution.py:188
  429.5 10.3 %project_back.1 = (f32[768,1024]{1,0:T(8,128)S(1)}, bf16[2,768,1024]{2,1,0:T(8,128)(2,1)S(1)}) custom-call(bf16[768,1024]{1,0:T(8,128)(2,1)S(1)} %get-tuple-element.115.lead_ref.refs_7_, bf16[2,768,1024]{2,1,0:T(8,128)(2,1)} %get-tuple-element.116.own_ref, bf16[2,768,1024]{2,1,0:T(8,128)(2,1)} %collective-permute-done.16.far_ref, bf16[1344,8,1024]{2,1,0:T(8,128)(2,1)} %bitcast.52), custom_call_target="tpu_custom_call" | custom-call | flops 1000000 | bytes 100000 | tf_op jit(solution)/shard_map/project_back/pallas_call | solution.py:1366
  444.9 4.7 fusion.31.refs_3_
  449.7 13.2 %attend_bwd.5 = (bf16[768,1024]{1,0:T(8,128)(2,1)S(1)}, bf16[2,272,1024]{2,1,0:T(8,128)(2,1)S(1)}) custom-call(bf16[768,1024]{1,0:T(8,128)(2,1)S(1)} %copy-done.15, bf16[2,272,1024]{2,1,0:T(8,128)(2,1)S(1)} %copy-done.9, f32[8,8,768]{2,1,0:T(8,128)S(1)} %get-tuple-element.111.refs_1_, bf16[768,1024]{1,0:T(8,128)(2,1)} %copy-done.16, ...), custom_call_target="tpu_custom_call" | custom-call | flops 1000000 | bytes 100000 | tf_op jit(solution)/shard_map/attend_bwd/pallas_call | solution.py:188
  463.0 5.2 fusion.10
  475.3 22.7 %weight_grads.1 = bf16[1344,8,1024]{2,1,0:T(8,128)(2,1)} custom-call(bf16[768,1024]{1,0:T(8,128)(2,1)} %copy-done.52, bf16[768,1024]{1,0:T(8,128)(2,1)} %copy-done.21, bf16[272,768]{1,0:T(8,128)(2,1)} %copy-done.17, bf16[2,272,1024]{2,1,0:T(8,128)(2,1)} %copy-done.24, bf16[768,1024]{1,0:T(8,128)(2,1)} %copy-done.16, bf16[768,1024]{1,0:T(8,128)(2,1)} %copy-done.51, ...), custom_call_target="tpu_custom_call" | custom-call | flops 1000000 | bytes 100000 | tf_op jit(solution)/shard_map/weight_grads/pallas_call | solution.py:1468
  498.0 115.1 %scatter_sum.1 = (f32[336,1024]{1,0:T(8,128)S(1)}, f32[8,128]{1,0:T(8,128)S(1)}, bf16[512,1024]{1,0:T(8,128)(2,1)S(1)}) custom-call(bf16[10752,1024]{1,0:T(8,128)(2,1)} %bitcast.53, f32[8,128]{1,0:T(8,128)S(1)} %get-tuple-element.126.refs_1_, bf16[16,256,1024]{2,1,0:T(8,128)(2,1)} %get-tuple-element.101.refs_2_, bf16[16,256,1024]{2,1,0:T(8,128)(2,1)} %copy-done.42, ...), custom_call_target="tpu_custom_call" | custom-call | tf_op jit(solution)/shard_map/scatter_sum/pallas_call | solution.py:893
  619.8 8.5 %shampoo.1 = (f32[32,128,128]{2,1,0:T(8,128)}, f32[32,128,128]{2,1,0:T(8,128)}, f32[32,128,128]{2,1,0:T(8,128)}, f32[32,128,128]{2,1,0:T(8,128)}, f32[32,128]{1,0:T(8,128)}) custom-call(bf16[512,1024]{1,0:T(8,128)(2,1)} %copy-done.25, f32[32,128,128]{2,1,0:T(8,128)} %blocks_ref.3, f32[32,128,128]{2,1,0:T(8,128)} %sl_ref.1, f32[32,128,128]{2,1,0:T(8,128)} %sr_ref.1, ...), custom_call_target="tpu_custom_call" | custom-call | tf_op jit(solution)/shard_map/shampoo/pallas_call | solution.py:1737
  632.4 4.8 adam.1
  (257 shorter events, 112.6 us)
Async XLA Ops:
  1.6 8.2 %collective-permute-start = (f32[448,128]{1,0:T(8,128)S(1)}, f32[448,128]{1,0:T(8,128)S(1)}, u32[]{:S(2)}, u32[]{:S(2)}) collective-permute-start(f32[448,128]{1,0:T(8,128)S(1)} %slice_bitcast_fusion), channel_id=1, source_target_pairs={{1,0},{2,1},{3,2},{4,3},{5,4},{6,5},{7,6},{8,7},{9,8},{10,9},{11,1... | collective-permute-start | bytes 688136 | tf_op jit(solution)/shard_map/ppermute | solution.py:1601
  6.1 118.1 %copy-start.17 = (bf16[272,768]{1,0:T(8,128)(2,1)}, bf16[272,768]{1,0:T(8,128)(2,1)S(1)}, u32[]{:S(2)}) copy-start(bf16[272,768]{1,0:T(8,128)(2,1)S(1)} %pad.21.x_ref.refs_2_) | copy-start | bytes 1253380
  123.0 21.7 %copy-start.63 = (f32[1,1024]{1,0:T(1,128)}, f32[1,1024]{1,0:T(1,128)S(1)}, u32[]{:S(2)}) copy-start(f32[1,1024]{1,0:T(1,128)S(1)} %get-tuple-element.162) | copy-start | bytes 12292
  123.0 25.6 %collective-permute-start.1 = (bf16[4,256,1024]{2,1,0:T(8,128)(2,1)}, bf16[4,256,1024]{2,1,0:T(8,128)(2,1)}, u32[]{:S(2)}, u32[]{:S(2)}) collective-permute-start(bf16[4,256,1024]{2,1,0:T(8,128)(2,1)} %get-tuple-element.78.refs_0_), channel_id=1, source_target_pairs={{0,2},{1,5},{2,0},{3,7},{4,6},{5,1},{6,4},{7,3},{8,10},{9,13},{10,... | collective-permute-start | bytes 6291464 | tf_op jit(solution)/shard_map/ppermute | solution.py:1787
  156.2 28.8 %copy-start.3 = (bf16[768,1024]{1,0:T(8,128)(2,1)}, bf16[768,1024]{1,0:T(8,128)(2,1)S(1)}, u32[]{:S(2)}) copy-start(bf16[768,1024]{1,0:T(8,128)(2,1)S(1)} %get-tuple-element.82.q_ref) | copy-start | bytes 4718596
  156.2 11.0 %collective-permute-start.3 = (bf16[2,768,1024]{2,1,0:T(8,128)(2,1)S(1)}, bf16[2,768,1024]{2,1,0:T(8,128)(2,1)S(1)}, u32[]{:S(2)}, u32[]{:S(2)}) collective-permute-start(bf16[2,768,1024]{2,1,0:T(8,128)(2,1)S(1)} %get-tuple-element.83.refs_0_), channel_id=1, source_target_pairs={{0,1},{1,0},{2,3},{3,2},{4,5},{5,4},{6,7},{7,6},{8,9},{9,8},{10,11... | collective-permute-start | bytes 9437192 | tf_op jit(solution)/shard_map/ppermute | solution.py:1949
  157.1 27.9 %collective-permute-start.2 = (bf16[4,256,1024]{2,1,0:T(8,128)(2,1)}, bf16[4,256,1024]{2,1,0:T(8,128)(2,1)}, u32[]{:S(2)}, u32[]{:S(2)}) collective-permute-start(bf16[4,256,1024]{2,1,0:T(8,128)(2,1)} %get-tuple-element.78.refs_0_), channel_id=1, source_target_pairs={{0,4},{1,3},{2,6},{3,1},{4,0},{5,7},{6,2},{7,5},{8,12},{9,11},{10,... | collective-permute-start | bytes 6291464 | tf_op jit(solution)/shard_map/ppermute | solution.py:1807
  157.6 47.5 %collective-permute-start.4 = (bf16[4,256,1024]{2,1,0:T(8,128)(2,1)}, bf16[4,256,1024]{2,1,0:T(8,128)(2,1)}, u32[]{:S(2)}, u32[]{:S(2)}) collective-permute-start(bf16[4,256,1024]{2,1,0:T(8,128)(2,1)} %collective-permute-done.1.refs_1_), channel_id=1, source_target_pairs={{0,4},{1,3},{2,6},{3,1},{4,0},{5,7},{6,2},{7,5},{8,12},{9,11},{10,... | collective-permute-start | bytes 6291464 | tf_op jit(solution)/shard_map/ppermute | solution.py:1815
  166.6 46.0 %collective-permute-start.5 = (bf16[4,256,1024]{2,1,0:T(8,128)(2,1)}, bf16[4,256,1024]{2,1,0:T(8,128)(2,1)}, u32[]{:S(2)}, u32[]{:S(2)}) collective-permute-start(bf16[4,256,1024]{2,1,0:T(8,128)(2,1)} %get-tuple-element.78.refs_0_), channel_id=1, source_target_pairs={{0,1},{1,0},{2,3},{3,2},{4,5},{5,4},{6,7},{7,6},{8,9},{9,8},{10,11... | collective-permute-start | bytes 6291464 | tf_op jit(solution)/shard_map/ppermute | solution.py:1823
  167.2 45.4 %collective-permute-start.6 = (bf16[4,256,1024]{2,1,0:T(8,128)(2,1)}, bf16[4,256,1024]{2,1,0:T(8,128)(2,1)}, u32[]{:S(2)}, u32[]{:S(2)}) collective-permute-start(bf16[4,256,1024]{2,1,0:T(8,128)(2,1)} %collective-permute-done.1.refs_1_), channel_id=1, source_target_pairs={{0,1},{1,0},{2,3},{3,2},{4,5},{5,4},{6,7},{7,6},{8,9},{9,8},{10,11... | collective-permute-start | bytes 6291464 | tf_op jit(solution)/shard_map/ppermute | solution.py:1823
  201.4 213.6 %copy-start.5 = (bf16[768,1024]{1,0:T(8,128)(2,1)}, bf16[768,1024]{1,0:T(8,128)(2,1)S(1)}, u32[]{:S(2)}) copy-start(bf16[768,1024]{1,0:T(8,128)(2,1)S(1)} %get-tuple-element.88.refs_3_.refs_9_) | copy-start | bytes 4718596
  205.1 7.5 %collective-permute-start.8 = (bf16[4,256,1024]{2,1,0:T(8,128)(2,1)}, bf16[4,256,1024]{2,1,0:T(8,128)(2,1)}, u32[]{:S(2)}, u32[]{:S(2)}) collective-permute-start(bf16[4,256,1024]{2,1,0:T(8,128)(2,1)} %collective-permute-done.4.refs_3_), channel_id=1, source_target_pairs={{0,1},{1,0},{2,3},{3,2},{4,5},{5,4},{6,7},{7,6},{8,9},{9,8},{10,11... | collective-permute-start | bytes 6291464 | tf_op jit(solution)/shard_map/ppermute | solution.py:1823
  206.0 7.1 %collective-permute-start.7 = (bf16[4,256,1024]{2,1,0:T(8,128)(2,1)}, bf16[4,256,1024]{2,1,0:T(8,128)(2,1)}, u32[]{:S(2)}, u32[]{:S(2)}) collective-permute-start(bf16[4,256,1024]{2,1,0:T(8,128)(2,1)} %collective-permute-done.2.refs_2_), channel_id=1, source_target_pairs={{0,1},{1,0},{2,3},{3,2},{4,5},{5,4},{6,7},{7,6},{8,9},{9,8},{10,11... | collective-permute-start | bytes 6291464 | tf_op jit(solution)/shard_map/ppermute | solution.py:1823
  213.2 28.9 %copy-start.2 = (bf16[1024,2048]{1,0:T(8,128)(2,1)S(1)}, bf16[1024,2048]{1,0:T(8,128)(2,1)}, u32[]{:S(2)}) copy-start(bf16[1024,2048]{1,0:T(8,128)(2,1)} %copy-done.1) | copy-start | bytes 12582916
  240.6 1.5 collective-permute-start.9
  248.7 5.1 collective-permute-start.10
  274.4 1.9 collective-permute-start.11
  293.3 1.7 collective-permute-start.12
  342.8 14.6 %collective-permute-start.13 = (bf16[16,256,1024]{2,1,0:T(8,128)(2,1)}, bf16[16,256,1024]{2,1,0:T(8,128)(2,1)S(1)}, u32[]{:S(2)}, u32[]{:S(2)}) collective-permute-start(bf16[16,256,1024]{2,1,0:T(8,128)(2,1)} %get-tuple-element.102), channel_id=1, source_target_pairs={{0,1},{1,0},{2,3},{3,2},{4,5},{5,4},{6,7},{7,6},{8,9},{9,8},{10,11... | collective-permute-start | bytes 25165832 | tf_op jit(solution)/shard_map/ppermute | solution.py:1833
  362.0 48.0 %collective-permute-start.14 = (bf16[8,256,1024]{2,1,0:T(8,128)(2,1)}, bf16[8,256,1024]{2,1,0:T(8,128)(2,1)}, u32[]{:S(2)}, u32[]{:S(2)}) collective-permute-start(bf16[8,256,1024]{2,1,0:T(8,128)(2,1)} %add_convert_fusion), channel_id=1, source_target_pairs={{0,4},{1,3},{2,6},{3,1},{4,0},{5,7},{6,2},{7,5},{8,12},{9,11},{10,... | collective-permute-start | bytes 12582920 | tf_op jit(solution)/shard_map/ppermute | solution.py:1845
  422.9 6.6 %collective-permute-start.16 = (bf16[2,768,1024]{2,1,0:T(8,128)(2,1)}, bf16[2,768,1024]{2,1,0:T(8,128)(2,1)}, u32[]{:S(2)}, u32[]{:S(2)}) collective-permute-start(bf16[2,768,1024]{2,1,0:T(8,128)(2,1)} %get-tuple-element.117), channel_id=1, source_target_pairs={{0,1},{1,0},{2,3},{3,2},{4,5},{5,4},{6,7},{7,6},{8,9},{9,8},{10,11... | collective-permute-start | bytes 9437192 | tf_op jit(solution)/shard_map/ppermute | solution.py:1998
  426.7 36.2 %collective-permute-start.15 = (bf16[4,256,1024]{2,1,0:T(8,128)(2,1)}, bf16[4,256,1024]{2,1,0:T(8,128)(2,1)S(1)}, u32[]{:S(2)}, u32[]{:S(2)}) collective-permute-start(bf16[4,256,1024]{2,1,0:T(8,128)(2,1)} %add_convert_fusion.1), channel_id=1, source_target_pairs={{0,2},{1,5},{2,0},{3,7},{4,6},{5,1},{6,4},{7,3},{8,10},{9,13},{10,... | collective-permute-start | bytes 6291464 | tf_op jit(solution)/shard_map/ppermute | solution.py:1853
  475.3 22.7 %copy-start.20 = (bf16[4,256,1024]{2,1,0:T(8,128)(2,1)S(1)}, bf16[4,256,1024]{2,1,0:T(8,128)(2,1)}, u32[]{:S(2)}) copy-start(bf16[4,256,1024]{2,1,0:T(8,128)(2,1)} %copy-done.19) | copy-start | bytes 6291460
  614.2 15.5 %collective-permute-start.17 = (f32[448,128]{1,0:T(8,128)S(1)}, f32[448,128]{1,0:T(8,128)S(1)}, u32[]{:S(2)}, u32[]{:S(2)}) collective-permute-start(f32[448,128]{1,0:T(8,128)S(1)} %slice.138), channel_id=1, source_target_pairs={{0,1},{1,2},{2,3},{3,4},{4,5},{5,6},{6,7},{7,8},{8,9},{9,10},{10,1... | collective-permute-start | bytes 688136 | tf_op jit(solution)/shard_map/ppermute | solution.py:1688
  (68 other events, 418.4 us)

commit v9 on v8

--- a/solution.py
+++ b/solution.py
@@ -235,7 +235,7 @@
                 width = min(group, cells - g * group)
                 table[plane, g * CH : (g + 1) * CH, :width] = turned[:CH, g * group : g * group + width]
 
-    step = 4
+    step = 8
     width = step * rays
     win, wout = win_ref[...], wout_ref[...]
 
@@ -680,8 +680,9 @@
     outs = refs[count + 4 : 2 * count + 4]
     line_out = refs[2 * count + 4]
     scratch = refs[2 * count + 5 :]
-    line_parts, line_sums, line_got, line_sum, line_sems, line_load_sems = scratch[-6:]
+    line_parts, line_sums, line_got, line_sum, line_sems, line_load_sems, line_send, line_recv = scratch[-8:]
     p, c, z, near, far, both = places()
+    up, down = (p + 4, c), (p - 4, c)
     zs = [along_z(p, z, k) for k in range(4)]
     enter([(q, c) for q in zs[1:]] + [(near, c), (far, c), (p, 1 - c)])
     csend, crecv, bsend, brecv, load_sem, out_sem = scratch[:6]
@@ -758,6 +759,65 @@
                 total = total + part[at].astype(jnp.float32)
             target[at] = total.astype(target.dtype)
 
+    def flow(sums, got, sends, recvs, upwards, distance):
+        side = 0 if upwards else 1
+        return pltpu.make_async_remote_copy(
+            sums(distance if upwards else 4 - distance), got(3 * side + distance - 1),
+            sends(side, distance - 1), recvs(side, distance - 1),
+            device_id=up if upwards else down, device_id_type=MESH_ID,
+        )
+
+    def flow_landed(got, sends, recvs, upwards, left):
+        side = 0 if upwards else 1
+        spot = got(3 * side + left)
+        pltpu.make_async_remote_copy(
+            spot, spot, sends(side, left), recvs(side, left), device_id=(p, 1 - c), device_id_type=MESH_ID
+        ).wait_recv()
+        return spot
+
+    def flow_step(sums, got, sends, recvs, distance):
+        for upwards in (True, False):
+
+            @pl.when(z + distance <= 3 if upwards else z >= distance)
+            def _():
+                if distance < 3:
+
+                    @pl.when(z > 0 if upwards else z < 3)
+                    def _():
+                        here = sums(distance if upwards else 4 - distance)
+                        add_up([here, flow_landed(got, sends, recvs, upwards, distance)], here)
+
+                flow(sums, got, sends, recvs, upwards, distance).start()
+
+    def flow_finish(parts, got, sends, recvs, target):
+        @pl.when(z == 0)
+        def _():
+            add_up(parts + [flow_landed(got, sends, recvs, False, 0)], target)
+
+        @pl.when(z == 3)
+        def _():
+            add_up(parts + [flow_landed(got, sends, recvs, True, 0)], target)
+
+        @pl.when((z > 0) & (z < 3))
+        def _():
+            both_ways = [flow_landed(got, sends, recvs, way, 0) for way in (True, False)]
+            add_up(parts + both_ways, target)
+
+    def flow_sent(sums, got, sends, recvs):
+        for distance in (1, 2, 3):
+            for upwards in (True, False):
+
+                @pl.when(z + distance <= 3 if upwards else z >= distance)
+                def _():
+                    flow(sums, got, sends, recvs, upwards, distance).wait_send()
+
+    line_flow = (
+        lambda k: line_sums.at[k],
+        lambda slot: line_got.at[slot],
+        lambda side, n: line_send.at[side, n],
+        lambda side, n: line_recv.at[side, n],
+    )
+
     def start(i, job):
         to_core(i, job).start()
         load(i, job).start()
@@ -771,20 +831,10 @@
         [pltpu.make_async_copy(ref.at[k], line_parts.at[k, n], line_load_sems.at[k, n]) for n, ref in enumerate(line_grads)]
         for k in range(4)
     ]
-    line_sends = {
-        k: pltpu.make_async_remote_copy(
-            line_sums.at[k], line_got.at[3 - k], line_sems.at[k], line_sems.at[7 - k],
-            device_id=(zs[k], c), device_id_type=MESH_ID,
-        )
-        for k in (1, 3, 2)
-    }
-
     def line_step(k):
         for load_part in line_loads[k]:
             load_part.wait()
         add_up([line_parts.at[k, n] for n in range(4)], line_sums.at[k])
-        if k:
-            line_sends[k].start()
 
     half = line_sum.shape[0]
     spot = line_out.at[pl.ds(pl.multiple_of(c * half, 8), half)]
@@ -796,12 +846,7 @@
     ]
 
     def line_finish():
-        for k in (1, 2, 3):
-            target = line_got.at[k - 1]
-            pltpu.make_async_remote_copy(
-                target, target, line_sems.at[k], line_sems.at[3 + k], device_id=(p, 1 - c), device_id_type=MESH_ID
-            ).wait_recv()
-        add_up([line_sums.at[0]] + [line_got.at[n] for n in range(3)], line_sum)
+        flow_finish([line_sums.at[0]], *line_flow[1:], line_sum)
         for copy in line_stores:
             copy.start()
 
@@ -842,9 +887,13 @@
     steps.append((max(steps)[0] - 6, 0, -1))
     for n, k in enumerate((1, 3, 2, 0)):
         steps.append((n, len(jobs), -2 - k))
+    for n, distance in enumerate((3, 2, 1)):
+        steps.append((4 + 3 * n, len(jobs), -5 - distance))
     for _, job, i in sorted(steps):
         if i == -1:
             line_finish()
+        elif i < -5:
+            flow_step(*line_flow, -5 - i)
         elif i < 0:
             line_step(-2 - i)
         else:
@@ -856,8 +905,7 @@
                 onward(i, job).wait_send()
         for copy in final_copies(job):
             copy.wait()
-    for copy in line_sends.values():
-        copy.wait_send()
+    flow_sent(*line_flow)
     for copy in line_stores:
         copy.wait()
 
@@ -883,10 +931,12 @@
     scratch += [
         pltpu.VMEM((4, 4) + piece, kind),
         pltpu.VMEM((4,) + piece, kind),
-        pltpu.VMEM((3,) + piece, kind),
+        pltpu.VMEM((6,) + piece, kind),
         pltpu.VMEM(piece, kind),
         pltpu.SemaphoreType.DMA((10,)),
         pltpu.SemaphoreType.DMA((4, 4)),
+        pltpu.SemaphoreType.DMA((2, 3)),
+        pltpu.SemaphoreType.DMA((2, 3)),
     ]
     shapes.append(jax.ShapeDtypeStruct((2 * piece[0], piece[1]), kind))
     everywhere = pl.BlockSpec(memory_space=pl.ANY)

time: 648 us -> 645 us (level)
  no operation moved by 1% of the time
where the time goes in v9:
time: 645 us; the launch traced here: 636 us
  Pallas kernels  501 us (78%)
  local copies, waits for them, and re-layouts  37.7 us (6%)
  other arithmetic  34.6 us (5%)
  matrix products  27.4 us (4%)
  waiting for transfers between devices  17.2 us (3%)
  starting transfers between devices  12.9 us (2%)
    pallas_call x1, Pallas kernels, scatter_sum(): pl.pallas_call(functools.partial(scatter_kernel, layouts, stagger), out_s...  115 us
    pallas_call x1, Pallas kernels, gather_all(): pl.pallas_call(functools.partial(gather_kernel, layouts, stagger), out_sh...  103 us
    pallas_call x3, Pallas kernels, attend_bwd(): pl.pallas_call(functools.partial(attend_bwd_kernel, real_keys, chunk, len...  66.2 us
    pallas_call x1, Pallas kernels, mlp_bwd(): pl.pallas_call(functools.partial(mlp_bwd_kernel, len(panels)), grid=(step...  42.7 us
    pallas_call x3, Pallas kernels, attend_fwd(): pl.pallas_call(functools.partial(attend_fwd_kernel, real_keys, len(source...  41.2 us
    pallas_call x1, Pallas kernels, mlp_fwd(): pl.pallas_call(functools.partial(mlp_fwd_kernel, len(panels)), grid=(step...  26.3 us
    unnamed x149, local copies, waits for them, and re-layouts  24.6 us
    pallas_call x1, Pallas kernels, weight_grads(): pl.pallas_call(functools.partial(weight_grads_kernel, products, copies),...  22.7 us
  transfers between devices with their start and end apart: 18, of which 9 were waited for; matrix products, arithmetic and copies ran while one was open for 7% of the time, Pallas kernels for 20%

profile of v9, /device:TPU:1, one launch (start us, length us, event | category | flops | bytes accessed | tf_op | source)
XLA Modules:
  0.0 636.1 jit_solution(7074184763976541574)
XLA Ops:
  15.5 103.4 %gather_all.1 = (bf16[10752,1024]{1,0:T(8,128)(2,1)}, f32[256,128]{1,0:T(8,128)}, bf16[4,256,1024]{2,1,0:T(8,128)(2,1)}) custom-call(bf16[336,1024]{1,0:T(8,128)(2,1)} %copy-done.27, f32[8,128]{1,0:T(8,128)} %copy-done.32, bf16[256,1024]{1,0:T(8,128)(2,1)} %copy-done.28), custom_call_target="tpu_custom_call" | custom-call | tf_op jit(solution)/shard_map/gather_all/pallas_call | solution.py:652
  131.4 8.7 %attend_fwd.3 = (bf16[768,1024]{1,0:T(8,128)(2,1)S(1)}, f32[8,8,768]{2,1,0:T(8,128)S(1)}) custom-call(bf16[768,1024]{1,0:T(8,128)(2,1)S(1)} %fusion.28.q_ref, bf16[2,272,1024]{2,1,0:T(8,128)(2,1)S(1)} %project.2.refs_0_), custom_call_target="tpu_custom_call" | custom-call | flops 1000000 | bytes 100000 | tf_op jit(solution)/shard_map/attend_fwd/pallas_call | solution.py:109
  148.6 7.6 %project.3 = (bf16[768,1024]{1,0:T(8,128)(2,1)S(1)}, bf16[2,768,1024]{2,1,0:T(8,128)(2,1)S(1)}) custom-call(bf16[768,1024]{1,0:T(8,128)(2,1)S(1)} %add_convert_fusion.4.x_ref.refs_6_, bf16[1344,8,1024]{2,1,0:T(8,128)(2,1)} %bitcast.50), custom_call_target="tpu_custom_call" | custom-call | flops 1000000 | bytes 100000 | tf_op jit(solution)/shard_map/project/pallas_call | solution.py:1375
  158.6 6.0 spread_deconv.1.w_ref
  168.9 16.1 %attend_fwd.4 = (bf16[768,1024]{1,0:T(8,128)(2,1)S(1)}, f32[8,8,768]{2,1,0:T(8,128)S(1)}) custom-call(bf16[768,1024]{1,0:T(8,128)(2,1)S(1)} %get-tuple-element.82.q_ref, bf16[2,768,1024]{2,1,0:T(8,128)(2,1)} %copy-done, bf16[2,768,1024]{2,1,0:T(8,128)(2,1)} %copy-done.38), custom_call_target="tpu_custom_call" | custom-call | flops 1000000 | bytes 100000 | tf_op jit(solution)/shard_map/attend_fwd/pallas_call | solution.py:109
  185.1 16.4 %attend_fwd.5 = (bf16[768,1024]{1,0:T(8,128)(2,1)S(1)}, f32[8,8,768]{2,1,0:T(8,128)S(1)}) custom-call(bf16[768,1024]{1,0:T(8,128)(2,1)S(1)} %get-tuple-element.82.q_ref, bf16[2,768,1024]{2,1,0:T(8,128)(2,1)} %copy-done, bf16[2,768,1024]{2,1,0:T(8,128)(2,1)} %copy-done.38, ...), custom_call_target="tpu_custom_call", output_to_operand_aliasing={{0}: (3, {}), {1}: (4, {})} | custom-call | flops 1000000 | bytes 100000 | tf_op jit(solution)/shard_map/attend_fwd/pallas_call | solution.py:109
  213.2 26.3 %mlp_fwd.1 = (f32[4,768,1024]{2,1,0:T(8,128)}, bf16[4,768,1024]{2,1,0:T(8,128)(2,1)}, bf16[768,1024]{1,0:T(8,128)(2,1)}) custom-call(bf16[4,256,1024]{2,1,0:T(8,128)(2,1)} %get-tuple-element.78.refs_0_, bf16[4,256,1024]{2,1,0:T(8,128)(2,1)} %collective-permute-done.1.refs_1_, bf16[4,256,1024]{2,1,0:T(8,128)(2,1)} %collective-permute-done.2.refs_2_, ...), custom_call_target="tpu_custom_call" | custom-call | flops 1000000 | bytes 100000 | tf_op jit(solution)/shard_map/mlp_fwd/pallas_call | solution.py:1024
  243.5 5.1 deconv_fwd.1.near_ref
  253.8 18.4 %render.1 = (f32[8,128]{1,0:T(8,128)S(1)}, bf16[3,80,1024]{2,1,0:T(8,128)(2,1)S(1)}, bf16[3,80,1024]{2,1,0:T(8,128)(2,1)S(1)}, f32[80,64]{1,0:T(8,128)S(1)}, f32[64,8]{1,0:T(8,128)S(1)}) custom-call(s32[3,16,256]{2,1,0:T(8,128)S(1)} %add_select_fusion.samples_ref, bf16[3,1024,128]{2,1,0:T(8,128)(2,1)S(1)} %deconv_fwd.1.near_ref, ...), custom_call_target="tpu_custom_call" | custom-call | tf_op jit(solution)/shard_map/render/pallas_call | solution.py:338
  275.7 16.0 %deconv_bwd.1 = (f32[3,256,1024]{2,1,0:T(8,128)}, bf16[3,32,1024]{2,1,0:T(8,128)(2,1)}, bf16[160,8,1024]{2,1,0:T(8,128)(2,1)}) custom-call(bf16[3,80,1024]{2,1,0:T(8,128)(2,1)} %copy-done.29, bf16[3,80,1024]{2,1,0:T(8,128)(2,1)} %copy-done.54, bf16[3,256,1024]{2,1,0:T(8,128)(2,1)} %bitcast.42, bf16[3,32,1024]{2,1,0:T(8,128)(2,1)} %copy-done.26, ...), custom_call_target="tpu_custom_call" | custom-call | tf_op jit(solution)/shard_map/deconv_bwd/pallas_call | solution.py:1309
  298.7 42.7 %mlp_bwd.1 = (f32[768,1024]{1,0:T(8,128)}, bf16[16,256,1024]{2,1,0:T(8,128)(2,1)}, bf16[16,256,1024]{2,1,0:T(8,128)(2,1)}) custom-call(bf16[4,256,1024]{2,1,0:T(8,128)(2,1)} %get-tuple-element.78.refs_0_, bf16[4,256,1024]{2,1,0:T(8,128)(2,1)} %collective-permute-done.1.refs_1_, bf16[4,256,1024]{2,1,0:T(8,128)(2,1)} %collective-permute-done.2.refs_2_, ...), custom_call_target="tpu_custom_call" | custom-call | flops 1000000 | bytes 100000 | tf_op jit(solution)/shard_map/mlp_bwd/pallas_call | solution.py:1133
  341.9 4.6 multiply_reduce_fusion
  350.6 5.3 fusion.34.refs_4_
  361.1 45.2 %attend_bwd.3 = (bf16[768,1024]{1,0:T(8,128)(2,1)S(1)}, bf16[2,768,1024]{2,1,0:T(8,128)(2,1)}, bf16[2,768,1024]{2,1,0:T(8,128)(2,1)}) custom-call(bf16[768,1024]{1,0:T(8,128)(2,1)S(1)} %copy-done.4, bf16[2,768,1024]{2,1,0:T(8,128)(2,1)} %copy-done, bf16[2,768,1024]{2,1,0:T(8,128)(2,1)} %copy-done.38, f32[8,8,768]{2,1,0:T(8,128)S(1)} %get-tuple-element.105.refs_2_, ...), custom_call_target="tpu_custom_call" | custom-call | flops 1000000 | bytes 100000 | tf_op jit(solution)/shard_map/attend_bwd/pallas_call | solution.py:188
  408.6 5.0 add_convert_fusion.1
  413.6 7.8 %attend_bwd.4 = (bf16[768,1024]{1,0:T(8,128)(2,1)S(1)}, bf16[2,768,1024]{2,1,0:T(8,128)(2,1)}, bf16[2,768,1024]{2,1,0:T(8,128)(2,1)}) custom-call(bf16[768,1024]{1,0:T(8,128)(2,1)S(1)} %copy-done.4, bf16[2,768,1024]{2,1,0:T(8,128)(2,1)} %copy-done, bf16[2,768,1024]{2,1,0:T(8,128)(2,1)} %copy-done.38, ...), custom_call_target="tpu_custom_call", output_to_operand_aliasing={{0}: (6, {}), {1}: (7, {}), {2}: (8, {})} | custom-call | flops 1000000 | bytes 100000 | tf_op jit(solution)/shard_map/attend_bwd/pallas_call | solution.py:188
  428.1 10.3 %project_back.1 = (f32[768,1024]{1,0:T(8,128)S(1)}, bf16[2,768,1024]{2,1,0:T(8,128)(2,1)S(1)}) custom-call(bf16[768,1024]{1,0:T(8,128)(2,1)S(1)} %get-tuple-element.115.lead_ref.refs_7_, bf16[2,768,1024]{2,1,0:T(8,128)(2,1)} %get-tuple-element.116.own_ref, bf16[2,768,1024]{2,1,0:T(8,128)(2,1)} %collective-permute-done.16.far_ref, bf16[1344,8,1024]{2,1,0:T(8,128)(2,1)} %bitcast.52), custom_call_target="tpu_custom_call" | custom-call | flops 1000000 | bytes 100000 | tf_op jit(solution)/shard_map/project_back/pallas_call | solution.py:1416
  443.5 4.7 fusion.31.refs_3_
  448.2 13.2 %attend_bwd.5 = (bf16[768,1024]{1,0:T(8,128)(2,1)S(1)}, bf16[2,272,1024]{2,1,0:T(8,128)(2,1)S(1)}) custom-call(bf16[768,1024]{1,0:T(8,128)(2,1)S(1)} %copy-done.15, bf16[2,272,1024]{2,1,0:T(8,128)(2,1)S(1)} %copy-done.9, f32[8,8,768]{2,1,0:T(8,128)S(1)} %get-tuple-element.111.refs_1_, bf16[768,1024]{1,0:T(8,128)(2,1)} %copy-done.16, ...), custom_call_target="tpu_custom_call" | custom-call | flops 1000000 | bytes 100000 | tf_op jit(solution)/shard_map/attend_bwd/pallas_call | solution.py:188
  461.6 5.2 fusion.10
  473.9 22.7 %weight_grads.1 = bf16[1344,8,1024]{2,1,0:T(8,128)(2,1)} custom-call(bf16[768,1024]{1,0:T(8,128)(2,1)} %copy-done.52, bf16[768,1024]{1,0:T(8,128)(2,1)} %copy-done.21, bf16[272,768]{1,0:T(8,128)(2,1)} %copy-done.17, bf16[2,272,1024]{2,1,0:T(8,128)(2,1)} %copy-done.24, bf16[768,1024]{1,0:T(8,128)(2,1)} %copy-done.16, bf16[768,1024]{1,0:T(8,128)(2,1)} %copy-done.51, ...), custom_call_target="tpu_custom_call" | custom-call | flops 1000000 | bytes 100000 | tf_op jit(solution)/shard_map/weight_grads/pallas_call | solution.py:1518
  496.6 115.5 %scatter_sum.1 = (f32[336,1024]{1,0:T(8,128)S(1)}, f32[8,128]{1,0:T(8,128)S(1)}, bf16[512,1024]{1,0:T(8,128)(2,1)S(1)}) custom-call(bf16[10752,1024]{1,0:T(8,128)(2,1)} %bitcast.53, f32[8,128]{1,0:T(8,128)S(1)} %get-tuple-element.126.refs_1_, bf16[16,256,1024]{2,1,0:T(8,128)(2,1)} %get-tuple-element.101.refs_2_, bf16[16,256,1024]{2,1,0:T(8,128)(2,1)} %copy-done.42, ...), custom_call_target="tpu_custom_call" | custom-call | tf_op jit(solution)/shard_map/scatter_sum/pallas_call | solution.py:943
  617.1 8.5 %shampoo.1 = (f32[32,128,128]{2,1,0:T(8,128)}, f32[32,128,128]{2,1,0:T(8,128)}, f32[32,128,128]{2,1,0:T(8,128)}, f32[32,128,128]{2,1,0:T(8,128)}, f32[32,128]{1,0:T(8,128)}) custom-call(bf16[512,1024]{1,0:T(8,128)(2,1)} %copy-done.25, f32[32,128,128]{2,1,0:T(8,128)} %blocks_ref.3, f32[32,128,128]{2,1,0:T(8,128)} %sl_ref.1, f32[32,128,128]{2,1,0:T(8,128)} %sr_ref.1, ...), custom_call_target="tpu_custom_call" | custom-call | tf_op jit(solution)/shard_map/shampoo/pallas_call | solution.py:1787
  629.7 4.8 adam.1
  (257 shorter events, 111.0 us)
Async XLA Ops:
  1.6 8.2 %collective-permute-start = (f32[448,128]{1,0:T(8,128)S(1)}, f32[448,128]{1,0:T(8,128)S(1)}, u32[]{:S(2)}, u32[]{:S(2)}) collective-permute-start(f32[448,128]{1,0:T(8,128)S(1)} %slice_bitcast_fusion), channel_id=1, source_target_pairs={{1,0},{2,1},{3,2},{4,3},{5,4},{6,5},{7,6},{8,7},{9,8},{10,9},{11,1... | collective-permute-start | bytes 688136 | tf_op jit(solution)/shard_map/ppermute | solution.py:1651
  6.1 118.1 %copy-start.17 = (bf16[272,768]{1,0:T(8,128)(2,1)}, bf16[272,768]{1,0:T(8,128)(2,1)S(1)}, u32[]{:S(2)}) copy-start(bf16[272,768]{1,0:T(8,128)(2,1)S(1)} %pad.21.x_ref.refs_2_) | copy-start | bytes 1253380
  123.0 21.7 %copy-start.63 = (f32[1,1024]{1,0:T(1,128)}, f32[1,1024]{1,0:T(1,128)S(1)}, u32[]{:S(2)}) copy-start(f32[1,1024]{1,0:T(1,128)S(1)} %get-tuple-element.162) | copy-start | bytes 12292
  123.0 25.6 %collective-permute-start.1 = (bf16[4,256,1024]{2,1,0:T(8,128)(2,1)}, bf16[4,256,1024]{2,1,0:T(8,128)(2,1)}, u32[]{:S(2)}, u32[]{:S(2)}) collective-permute-start(bf16[4,256,1024]{2,1,0:T(8,128)(2,1)} %get-tuple-element.78.refs_0_), channel_id=1, source_target_pairs={{0,2},{1,5},{2,0},{3,7},{4,6},{5,1},{6,4},{7,3},{8,10},{9,13},{10,... | collective-permute-start | bytes 6291464 | tf_op jit(solution)/shard_map/ppermute | solution.py:1837
  156.2 28.8 %copy-start.3 = (bf16[768,1024]{1,0:T(8,128)(2,1)}, bf16[768,1024]{1,0:T(8,128)(2,1)S(1)}, u32[]{:S(2)}) copy-start(bf16[768,1024]{1,0:T(8,128)(2,1)S(1)} %get-tuple-element.82.q_ref) | copy-start | bytes 4718596
  156.2 11.0 %collective-permute-start.3 = (bf16[2,768,1024]{2,1,0:T(8,128)(2,1)S(1)}, bf16[2,768,1024]{2,1,0:T(8,128)(2,1)S(1)}, u32[]{:S(2)}, u32[]{:S(2)}) collective-permute-start(bf16[2,768,1024]{2,1,0:T(8,128)(2,1)S(1)} %get-tuple-element.83.refs_0_), channel_id=1, source_target_pairs={{0,1},{1,0},{2,3},{3,2},{4,5},{5,4},{6,7},{7,6},{8,9},{9,8},{10,11... | collective-permute-start | bytes 9437192 | tf_op jit(solution)/shard_map/ppermute | solution.py:1999
  157.2 27.9 %collective-permute-start.2 = (bf16[4,256,1024]{2,1,0:T(8,128)(2,1)}, bf16[4,256,1024]{2,1,0:T(8,128)(2,1)}, u32[]{:S(2)}, u32[]{:S(2)}) collective-permute-start(bf16[4,256,1024]{2,1,0:T(8,128)(2,1)} %get-tuple-element.78.refs_0_), channel_id=1, source_target_pairs={{0,4},{1,3},{2,6},{3,1},{4,0},{5,7},{6,2},{7,5},{8,12},{9,11},{10,... | collective-permute-start | bytes 6291464 | tf_op jit(solution)/shard_map/ppermute | solution.py:1857
  157.7 47.5 %collective-permute-start.4 = (bf16[4,256,1024]{2,1,0:T(8,128)(2,1)}, bf16[4,256,1024]{2,1,0:T(8,128)(2,1)}, u32[]{:S(2)}, u32[]{:S(2)}) collective-permute-start(bf16[4,256,1024]{2,1,0:T(8,128)(2,1)} %collective-permute-done.1.refs_1_), channel_id=1, source_target_pairs={{0,4},{1,3},{2,6},{3,1},{4,0},{5,7},{6,2},{7,5},{8,12},{9,11},{10,... | collective-permute-start | bytes 6291464 | tf_op jit(solution)/shard_map/ppermute | solution.py:1865
  166.6 46.0 %collective-permute-start.5 = (bf16[4,256,1024]{2,1,0:T(8,128)(2,1)}, bf16[4,256,1024]{2,1,0:T(8,128)(2,1)}, u32[]{:S(2)}, u32[]{:S(2)}) collective-permute-start(bf16[4,256,1024]{2,1,0:T(8,128)(2,1)} %get-tuple-element.78.refs_0_), channel_id=1, source_target_pairs={{0,1},{1,0},{2,3},{3,2},{4,5},{5,4},{6,7},{7,6},{8,9},{9,8},{10,11... | collective-permute-start | bytes 6291464 | tf_op jit(solution)/shard_map/ppermute | solution.py:1873
  167.3 45.4 %collective-permute-start.6 = (bf16[4,256,1024]{2,1,0:T(8,128)(2,1)}, bf16[4,256,1024]{2,1,0:T(8,128)(2,1)}, u32[]{:S(2)}, u32[]{:S(2)}) collective-permute-start(bf16[4,256,1024]{2,1,0:T(8,128)(2,1)} %collective-permute-done.1.refs_1_), channel_id=1, source_target_pairs={{0,1},{1,0},{2,3},{3,2},{4,5},{5,4},{6,7},{7,6},{8,9},{9,8},{10,11... | collective-permute-start | bytes 6291464 | tf_op jit(solution)/shard_map/ppermute | solution.py:1873
  201.4 212.2 %copy-start.5 = (bf16[768,1024]{1,0:T(8,128)(2,1)}, bf16[768,1024]{1,0:T(8,128)(2,1)S(1)}, u32[]{:S(2)}) copy-start(bf16[768,1024]{1,0:T(8,128)(2,1)S(1)} %get-tuple-element.88.refs_3_.refs_9_) | copy-start | bytes 4718596
  205.1 7.5 %collective-permute-start.8 = (bf16[4,256,1024]{2,1,0:T(8,128)(2,1)}, bf16[4,256,1024]{2,1,0:T(8,128)(2,1)}, u32[]{:S(2)}, u32[]{:S(2)}) collective-permute-start(bf16[4,256,1024]{2,1,0:T(8,128)(2,1)} %collective-permute-done.4.refs_3_), channel_id=1, source_target_pairs={{0,1},{1,0},{2,3},{3,2},{4,5},{5,4},{6,7},{7,6},{8,9},{9,8},{10,11... | collective-permute-start | bytes 6291464 | tf_op jit(solution)/shard_map/ppermute | solution.py:1873
  206.1 7.1 %collective-permute-start.7 = (bf16[4,256,1024]{2,1,0:T(8,128)(2,1)}, bf16[4,256,1024]{2,1,0:T(8,128)(2,1)}, u32[]{:S(2)}, u32[]{:S(2)}) collective-permute-start(bf16[4,256,1024]{2,1,0:T(8,128)(2,1)} %collective-permute-done.2.refs_2_), channel_id=1, source_target_pairs={{0,1},{1,0},{2,3},{3,2},{4,5},{5,4},{6,7},{7,6},{8,9},{9,8},{10,11... | collective-permute-start | bytes 6291464 | tf_op jit(solution)/shard_map/ppermute | solution.py:1873
  213.2 28.9 %copy-start.2 = (bf16[1024,2048]{1,0:T(8,128)(2,1)S(1)}, bf16[1024,2048]{1,0:T(8,128)(2,1)}, u32[]{:S(2)}) copy-start(bf16[1024,2048]{1,0:T(8,128)(2,1)} %copy-done.1) | copy-start | bytes 12582916
  240.6 1.5 collective-permute-start.9
  248.7 5.1 collective-permute-start.10
  273.0 1.9 collective-permute-start.11
  291.7 1.7 collective-permute-start.12
  341.4 14.6 %collective-permute-start.13 = (bf16[16,256,1024]{2,1,0:T(8,128)(2,1)}, bf16[16,256,1024]{2,1,0:T(8,128)(2,1)S(1)}, u32[]{:S(2)}, u32[]{:S(2)}) collective-permute-start(bf16[16,256,1024]{2,1,0:T(8,128)(2,1)} %get-tuple-element.102), channel_id=1, source_target_pairs={{0,1},{1,0},{2,3},{3,2},{4,5},{5,4},{6,7},{7,6},{8,9},{9,8},{10,11... | collective-permute-start | bytes 25165832 | tf_op jit(solution)/shard_map/ppermute | solution.py:1883
  360.6 48.0 %collective-permute-start.14 = (bf16[8,256,1024]{2,1,0:T(8,128)(2,1)}, bf16[8,256,1024]{2,1,0:T(8,128)(2,1)}, u32[]{:S(2)}, u32[]{:S(2)}) collective-permute-start(bf16[8,256,1024]{2,1,0:T(8,128)(2,1)} %add_convert_fusion), channel_id=1, source_target_pairs={{0,4},{1,3},{2,6},{3,1},{4,0},{5,7},{6,2},{7,5},{8,12},{9,11},{10,... | collective-permute-start | bytes 12582920 | tf_op jit(solution)/shard_map/ppermute | solution.py:1895
  421.5 6.6 %collective-permute-start.16 = (bf16[2,768,1024]{2,1,0:T(8,128)(2,1)}, bf16[2,768,1024]{2,1,0:T(8,128)(2,1)}, u32[]{:S(2)}, u32[]{:S(2)}) collective-permute-start(bf16[2,768,1024]{2,1,0:T(8,128)(2,1)} %get-tuple-element.117), channel_id=1, source_target_pairs={{0,1},{1,0},{2,3},{3,2},{4,5},{5,4},{6,7},{7,6},{8,9},{9,8},{10,11... | collective-permute-start | bytes 9437192 | tf_op jit(solution)/shard_map/ppermute | solution.py:2048
  425.3 36.2 %collective-permute-start.15 = (bf16[4,256,1024]{2,1,0:T(8,128)(2,1)}, bf16[4,256,1024]{2,1,0:T(8,128)(2,1)S(1)}, u32[]{:S(2)}, u32[]{:S(2)}) collective-permute-start(bf16[4,256,1024]{2,1,0:T(8,128)(2,1)} %add_convert_fusion.1), channel_id=1, source_target_pairs={{0,2},{1,5},{2,0},{3,7},{4,6},{5,1},{6,4},{7,3},{8,10},{9,13},{10,... | collective-permute-start | bytes 6291464 | tf_op jit(solution)/shard_map/ppermute | solution.py:1903
  473.9 22.7 %copy-start.20 = (bf16[4,256,1024]{2,1,0:T(8,128)(2,1)S(1)}, bf16[4,256,1024]{2,1,0:T(8,128)(2,1)}, u32[]{:S(2)}) copy-start(bf16[4,256,1024]{2,1,0:T(8,128)(2,1)} %copy-done.19) | copy-start | bytes 6291460
  613.2 13.8 %collective-permute-start.17 = (f32[448,128]{1,0:T(8,128)S(1)}, f32[448,128]{1,0:T(8,128)S(1)}, u32[]{:S(2)}, u32[]{:S(2)}) collective-permute-start(f32[448,128]{1,0:T(8,128)S(1)} %slice.138), channel_id=1, source_target_pairs={{0,1},{1,2},{2,3},{3,4},{4,5},{5,6},{6,7},{7,8},{8,9},{9,10},{10,1... | collective-permute-start | bytes 688136 | tf_op jit(solution)/shard_map/ppermute | solution.py:1738
  (68 other events, 418.2 us)
